TPU v7x, 128 devices: a whole 4x4x4 slice. The times are simulated.
128 devices in a mesh: pos: 8 (over x, core), head: 8 (over y_lo, z), chan: 2 (over y_hi).
Axes of the slice: x: 4, y: 4 (y_hi: 2, y_lo: 2; y = y_hi * 2 + y_lo), z: 4, core: 2. Of those that a mesh axis runs over, the one named last changes fastest.
Arguments:
- inputs_saved: bfloat16 [3, 32768, 1536], P(None, ('pos', 'head'), 'chan'), may hold values from -6 to 6
- conv_weight: bfloat16 [3, 3, 1536, 768], P(None, None, 'chan'), may hold values from -0.09375 to 0.09375
- expand_weight: bfloat16 [3, 768, 1536], P(None, None, 'chan'), may hold values from -0.21875 to 0.21875
- head_weight: bfloat16 [4096, 1536], P(('pos', 'head')), may hold values from -1.796875 to 1.796875
- batch_of: int32 [4096], P(('pos', 'head')), may hold values from 0 to 7
- erase_left: bfloat16 [1536, 64], replicated, may hold values from -0.15625 to 0.15625
- erase_right: bfloat16 [1536, 64], replicated, may hold values from -2.09375 to 2.09375
- bin_gradient: bfloat16 [4096, 32], P(('pos', 'head')), may hold values from -6 to 6
- cover_bins: int32 [4096, 32], P(('pos', 'head')), may hold values from 0 to 32767, as said below
Outputs:
- input_grad: bfloat16 [32768, 1536], P(('pos', 'head'), 'chan')
Inputs may be any that keep to these rules, and one draw needn't show every extreme that they name: `cover_bins`: of the 2048 entries of the experiments held by one device of pos and head, at most 64 name positions of any one device; in every draw some device's positions are named by exactly 64 entries of every device. Positions may repeat within an experiment.
All inputs are finite; a program needn't handle non-finite values.
Results may differ from a plain program's by a relative error of at most 0.0095.
Values may be sent and summed in bfloat16 or wider, within the bound.
No kernel may reach another device: no remote copies, remote signals or barrier semaphores. Data moves between devices by JAX's collectives and lax.ppermute only.
A program may use at most 128 MiB of HBM per device.

v0:
```python
import jax
import jax.numpy as jnp
from jax import lax
from jax.sharding import PartitionSpec as P

BASE_DILATION = 4
RANK = 8


def with_halo(block, sides, width):
    for axis, dim in sides:
        count = lax.axis_size(axis)
        forward = [(i, i + 1) for i in range(count - 1)]
        backward = [(target, source) for source, target in forward]
        low = lax.ppermute(
            lax.slice_in_dim(block, block.shape[dim] - width, None, axis=dim), axis, forward
        )
        high = lax.ppermute(lax.slice_in_dim(block, 0, width, axis=dim), axis, backward)
        block = jnp.concatenate([low, block, high], axis=dim)
    return block


def gelu_value(value):
    return 0.5 * value * (1.0 + jax.scipy.special.erf(value * 0.7071067811865476))


def gelu_slope(value):
    return (
        0.5 * (1.0 + jax.scipy.special.erf(value * 0.7071067811865476))
        + value * jnp.exp(-0.5 * value * value) * 0.3989422804014327
    )


def per_device(
    inputs_saved,
    conv_weight,
    expand_weight,
    head_weight,
    batch_of,
    erase_left,
    erase_right,
    bin_gradient,
    cover_bins,
):
    members = lax.axis_size(("pos", "head"))
    width_share = inputs_saved.shape[2]
    local_rows = inputs_saved.shape[1]
    exp_local = head_weight.shape[0]
    cover_count = bin_gradient.shape[1]
    chan_place = lax.axis_index("chan")
    projected = jnp.dot(head_weight, erase_left, preferred_element_type=jnp.float32)
    columns = jnp.arange(erase_left.shape[1]) // RANK
    chosen = (columns[None, :] == batch_of[:, None]).astype(jnp.float32)
    right_share = lax.dynamic_slice_in_dim(erase_right, chan_place * width_share, width_share, 0)
    weight_share = lax.dynamic_slice_in_dim(head_weight, chan_place * width_share, width_share, 1)
    removed_rows = jnp.dot(
        projected * chosen, right_share.astype(jnp.float32).T, precision=lax.Precision.HIGHEST
    )
    vectors = (weight_share.astype(jnp.float32) - removed_rows).astype(jnp.bfloat16)
    entry_list = exp_local * cover_count
    flat_bins = cover_bins.reshape(-1)
    flat_grad = bin_gradient.reshape(-1).astype(jnp.float32)
    target = flat_bins // local_rows
    offset = flat_bins % local_rows
    capacity = 2 * entry_list // members
    one_hot = (target[:, None] == jnp.arange(members)[None, :]).astype(jnp.int32)
    ranking = jnp.sum((jnp.cumsum(one_hot, axis=0) - 1) * one_hot, axis=1)
    slot_index = target * capacity + ranking
    owner = (
        jnp.full((members * capacity,), -1, jnp.int32)
        .at[slot_index]
        .set(jnp.arange(entry_list, dtype=jnp.int32))
    )
    filled = owner >= 0
    source = jnp.maximum(owner, 0)
    slot_weight = jnp.where(filled, flat_grad[source], 0.0)
    slot_place = jnp.where(filled, offset[source], 0).astype(jnp.float32)
    local_exp = source // cover_count
    contrib = slot_weight[:, None] * vectors[local_exp].astype(jnp.float32)
    got_values, got_place = (
        lax.all_to_all(
            contrib.reshape(members, capacity, width_share),
            ("pos", "head"),
            split_axis=0,
            concat_axis=0,
            tiled=True,
        ),
        lax.all_to_all(
            slot_place.reshape(members, capacity),
            ("pos", "head"),
            split_axis=0,
            concat_axis=0,
            tiled=True,
        ),
    )
    flat_values = got_values.reshape(-1, width_share)
    grad = jax.ops.segment_sum(
        flat_values, got_place.reshape(-1).astype(jnp.int32), num_segments=local_rows
    )
    taps = conv_weight.shape[1]
    layer_count = inputs_saved.shape[0]
    for block_level in reversed(range(layer_count)):
        dilation_factor = BASE_DILATION * 2**block_level
        saved = inputs_saved[block_level].astype(jnp.float32)
        act = gelu_value(saved).astype(jnp.bfloat16)
        act_pad = with_halo(act, ((("pos", "head"), 0),), dilation_factor)
        partial_result = jnp.zeros((local_rows, conv_weight.shape[3]), jnp.float32)
        for kernel_tap in range(taps):
            start = kernel_tap * dilation_factor
            partial_result = partial_result + jnp.dot(
                act_pad[start : start + local_rows],
                conv_weight[block_level, kernel_tap],
                preferred_element_type=jnp.float32,
            )
        grad_in = grad.astype(jnp.bfloat16)
        mid_part = lax.dot_general(
            grad_in,
            expand_weight[block_level],
            (((1,), (1,)), ((), ())),
            preferred_element_type=jnp.float32,
        )
        preceding_sum, mid_sum = lax.psum((partial_result, mid_part), "chan")
        grad_pre = (mid_sum * gelu_slope(preceding_sum)).astype(jnp.bfloat16)
        grad_pad = with_halo(grad_pre, ((("pos", "head"), 0),), dilation_factor)
        grad_act = jnp.zeros((local_rows, width_share), jnp.float32)
        for kernel_tap in range(taps):
            start = (taps - 1 - kernel_tap) * dilation_factor
            grad_act = grad_act + lax.dot_general(
                grad_pad[start : start + local_rows],
                conv_weight[block_level, kernel_tap],
                (((1,), (1,)), ((), ())),
                preferred_element_type=jnp.float32,
            )
        grad = grad + grad_act * gelu_slope(saved)
    return grad.astype(jnp.bfloat16)


def solution(mesh):
    return jax.shard_map(
        per_device,
        mesh=mesh,
        in_specs=(
            P(None, ("pos", "head"), "chan"),
            P(None, None, "chan", None),
            P(None, None, "chan"),
            P(("pos", "head"), None),
            P(("pos", "head")),
            P(),
            P(),
            P(("pos", "head"), None),
            P(("pos", "head"), None),
        ),
        out_specs=P(("pos", "head"), "chan"),
        check_vma=False,
    )
```

profile of v0, /device:TPU:8, one launch (start us, length us, event | category | flops | bytes accessed | tf_op | source)
XLA Modules:
  0.0 684.3 jit_solution(13553706354659303547)
XLA Ops:
  6.5 0.8 copy.10
  7.6 0.8 copy.15
  8.5 18.1 %reduce-window.6 = s32[64,16,128]{2,1,0:T(8,128)S(1)} reduce-window(s32[64,16,128]{2,1,0:T(8,128)S(1)} %fusion.183, s32[]{:T(128)} %constant.79.clone.1), window={size=1x1x128 pad=0_0x0_0x127_0}, to_apply=%region_0.1 | reduce-window | flops 16646144 | bytes 1048580 | tf_op jit(solution)/shard_map/reduce-window
  26.7 0.2 slice.191
  26.9 0.4 copy.16
  27.5 0.2 add_add_fusion.3
  27.7 0.2 fusion.182
  28.0 8.1 %scatter_custom_fusion = s32[4096]{0:T(1024)S(1)} fusion(s32[2048]{0:T(1024)S(1)} %bitcast.223, s32[2048]{0:T(1024)S(1)} %iota.16, s32[]{:T(128)} %constant.77.clone.1), kind=kCustom, calls=%fused_computation.240 | custom fusion | bytes 16388 | tf_op jit(solution)/shard_map/scatter | solution.py:72
  36.1 23.0 %gather_fusion.1 = f32[4096]{0:T(1024)S(1)} fusion(f32[2048]{0:T(1024)S(1)} %reshape.188, s32[4096]{0:T(1024)S(1)} %get-tuple-element.29), kind=kCustom, calls=%fused_computation.1 | custom fusion | bytes 49152 | tf_op jit(solution)/shard_map/gather | solution.py:76
  59.2 23.0 %gather_fusion = s32[4096]{0:T(1024)S(1)} fusion(s32[2048]{0:T(1024)S(1)} %get-tuple-element.30, s32[4096]{0:T(1024)S(1)} %get-tuple-element.29), kind=kCustom, calls=%fused_computation | custom fusion | bytes 49152 | tf_op jit(solution)/shard_map/gather | solution.py:77
  82.2 0.7 all_to_all.9
  82.9 9.8 %all-to-all-start = ((f32[64,1,64]{2,1,0:T(1,128)}), f32[64,1,64]{2,1,0:T(1,128)S(1)}, u32[]{:S(2)}, u32[]{:S(2)}) async-start(f32[64,1,64]{2,1,0:T(1,128)} %all_to_all.9), calls=%async_computation | async-start | bytes 65536 | tf_op jit(solution)/shard_map/all_to_all | solution.py:88
  92.8 0.2 convolution_select_fusion
  93.0 0.2 fusion.130
  93.3 17.8 %gather_fusion.2 = bf16[4096,768]{1,0:T(8,128)(2,1)} fusion(bf16[64,768]{1,0:T(8,128)(2,1)S(1)} %fusion.130, s32[4096]{0:T(1024)S(1)} %get-tuple-element.28), kind=kCustom, calls=%fused_computation.2 | custom fusion | bytes 12599296 | tf_op jit(solution)/shard_map/gather | solution.py:79
  111.1 8.3 %convert_multiply_fusion = f32[64,64,768]{2,1,0:T(8,128)} fusion(bf16[64,64,768]{2,1,0:T(8,128)(2,1)} %bitcast.218, f32[64,64]{1,0:T(8,128)S(1)} %mul.211), kind=kLoop, calls=%fused_computation.5 | loop fusion | flops 6291456 | bytes 18890752 | tf_op jit(solution)/shard_map/mul | solution.py:79
  119.4 9.0 %all-to-all-start.1 = ((f32[64,64,768]{2,1,0:T(8,128)}), f32[64,64,768]{2,1,0:T(8,128)}, u32[]{:S(2)}, u32[]{:S(2)}) async-start(f32[64,64,768]{2,1,0:T(8,128)} %convert_multiply_fusion), calls=%async_computation.1 | async-start | bytes 25165824 | tf_op jit(solution)/shard_map/all_to_all | solution.py:81
  128.4 2.9 fusion.60
  131.4 3.4 collective-permute-start
  134.8 4.8 collective-permute-start.1
  139.5 3.6 fusion.119
  143.3 153.5 %collective-permute-done = bf16[16,768]{1,0:T(8,128)(2,1)S(1)} collective-permute-done((bf16[16,768]{1,0:T(8,128)(2,1)S(1)}, bf16[16,768]{1,0:T(8,128)(2,1)S(1)}, u32[]{:S(2)}, u32[]{:S(2)}) %collective-permute-start) | collective-permute-done | bytes 24608 | tf_op jit(solution)/shard_map/ppermute | solution.py:15
  296.8 2.0 fusion.123
  298.9 3.3 add_add_fusion.2
  302.2 28.6 %scatter_custom_fusion.1 = f32[512,768]{1,0:T(8,128)S(1)} fusion(s32[4096]{0:T(1024)S(1)} %reshape.227, f32[4096,768]{1,0:T(8,128)} %bitcast.6, f32[]{:T(128)} %constant.76.clone.1), kind=kCustom, calls=%fused_computation.199 | custom fusion | flops 3145728 | bytes 1573376 | tf_op jit(solution)/shard_map/scatter-add | solution.py:97
  330.8 3.3 fusion.125
  334.2 1.9 collective-permute-start.4
  336.1 6.0 collective-permute-start.5
  342.2 2.4 fusion.101
  344.6 2.1 fusion.105
  346.7 3.3 add_add_fusion.1
  349.9 73.7 %all-reduce.11.cloned.1.call-done = (f32[512,768]{1,0:T(8,128)}, f32[512,768]{1,0:T(8,128)}) async-done(((f32[512,768]{1,0:T(8,128)}, f32[512,768]{1,0:T(8,128)}), (f32[512,768]{1,0:T(8,128)}, f32[512,768]{1,0:T(8,128)})) %all-reduce.11.cloned.1.call-update) | async-done | bytes 3145744 | tf_op jit(solution)/shard_map/psum | solution.py:122
  423.6 2.5 fusion.20
  426.2 5.7 collective-permute-start.2
  431.9 2.1 fusion.117
  434.0 1.9 collective-permute-start.3
  435.9 2.1 fusion.121
  438.0 3.8 collective-permute-done.3
  441.8 2.8 fusion.41
  444.6 1.2 copy-done.3
  445.8 3.4 fusion.107
  449.2 2.1 collective-permute-start.8
  451.3 6.3 collective-permute-start.9
  457.6 2.2 fusion.83
  459.8 2.1 fusion.87
  461.8 3.2 add_add_fusion
  465.1 75.0 %all-reduce.9.cloned.1.call-done = (f32[512,768]{1,0:T(8,128)}, f32[512,768]{1,0:T(8,128)}) async-done(((f32[512,768]{1,0:T(8,128)}, f32[512,768]{1,0:T(8,128)}), (f32[512,768]{1,0:T(8,128)}, f32[512,768]{1,0:T(8,128)})) %all-reduce.9.cloned.1.call-update) | async-done | bytes 3145744 | tf_op jit(solution)/shard_map/psum | solution.py:122
  540.1 2.5 fusion.26
  542.6 5.7 collective-permute-start.6
  548.3 2.1 fusion.99
  550.4 2.1 collective-permute-start.7
  552.5 2.1 fusion.103
  554.6 3.7 collective-permute-done.7
  558.3 2.5 fusion.54
  560.8 1.2 copy-done.5
  562.0 3.2 fusion.89
  565.3 90.9 %all-reduce.7.cloned.1.call-done = (f32[512,768]{1,0:T(8,128)}, f32[512,768]{1,0:T(8,128)}) async-done(((f32[512,768]{1,0:T(8,128)}, f32[512,768]{1,0:T(8,128)}), (f32[512,768]{1,0:T(8,128)}, f32[512,768]{1,0:T(8,128)})) %all-reduce.7.cloned.1.call-update) | async-done | bytes 3145744 | tf_op jit(solution)/shard_map/psum | solution.py:122
  656.2 2.5 fusion.32
  658.7 5.7 collective-permute-start.10
  664.4 2.1 fusion.81
  666.5 2.1 collective-permute-start.11
  668.6 2.1 fusion.85
  670.7 3.6 collective-permute-done.11
  674.3 3.5 fusion.68
  (59 shorter events, 1.2 us)
Async XLA Ops:
  6.5 86.5 %copy-start = (bf16[1536,64]{0,1:T(8,128)(2,1)S(1)}, bf16[1536,64]{0,1:T(8,128)(2,1)}, u32[]{:S(2)}) copy-start(bf16[1536,64]{0,1:T(8,128)(2,1)} %param.15) | copy-start | bytes 589828
  59.2 33.7 %copy-start.8 = (bf16[64,1536]{1,0:T(8,128)(2,1)S(1)}, bf16[64,1536]{1,0:T(8,128)(2,1)}, u32[]{:S(2)}) copy-start(bf16[64,1536]{1,0:T(8,128)(2,1)} %param.12) | copy-start | bytes 589828
  59.2 33.7 %copy-start.9 = (bf16[1536,64]{0,1:T(8,128)(2,1)S(1)}, bf16[1536,64]{0,1:T(8,128)(2,1)}, u32[]{:S(2)}) copy-start(bf16[1536,64]{0,1:T(8,128)(2,1)} %param.14) | copy-start | bytes 589828
  59.2 33.7 %copy-start.10 = (s32[64]{0:T(128)S(1)}, s32[64]{0:T(128)}, u32[]{:S(2)}) copy-start(s32[64]{0:T(128)} %param.13) | copy-start | bytes 772
  82.9 36.5 %all-to-all-start = ((f32[64,1,64]{2,1,0:T(1,128)}), f32[64,1,64]{2,1,0:T(1,128)S(1)}, u32[]{:S(2)}, u32[]{:S(2)}) async-start(f32[64,1,64]{2,1,0:T(1,128)} %all_to_all.9), calls=%async_computation | async-start | bytes 65536 | tf_op jit(solution)/shard_map/all_to_all | solution.py:88
  119.4 182.8 %all-to-all-start.1 = ((f32[64,64,768]{2,1,0:T(8,128)}), f32[64,64,768]{2,1,0:T(8,128)}, u32[]{:S(2)}, u32[]{:S(2)}) async-start(f32[64,64,768]{2,1,0:T(8,128)} %convert_multiply_fusion), calls=%async_computation.1 | async-start | bytes 25165824 | tf_op jit(solution)/shard_map/all_to_all | solution.py:81
  128.4 295.2 %all-reduce.11.cloned.1.call-start = ((), (), s32[]{:S(2)}) async-start(), calls=%async_computation.4 | async-start | bytes 6291456 | tf_op jit(solution)/shard_map/psum | solution.py:122
  131.4 165.5 %collective-permute-start = (bf16[16,768]{1,0:T(8,128)(2,1)S(1)}, bf16[16,768]{1,0:T(8,128)(2,1)S(1)}, u32[]{:S(2)}, u32[]{:S(2)}) collective-permute-start(bf16[16,768]{1,0:T(8,128)(2,1)S(1)} %get-tuple-element.27), channel_id=1, source_target_pairs={{0,2},{2,4},{4,6},{6,8},{8,10},{10,12},{12,14},{14,16},{16,18},{18... | collective-permute-start | bytes 73736 | tf_op jit(solution)/shard_map/ppermute | solution.py:15
  134.8 164.1 %collective-permute-start.1 = (bf16[16,768]{1,0:T(8,128)(2,1)S(1)}, bf16[16,768]{1,0:T(8,128)(2,1)S(1)}, u32[]{:S(2)}, u32[]{:S(2)}) collective-permute-start(bf16[16,768]{1,0:T(8,128)(2,1)S(1)} %get-tuple-element.26), channel_id=1, source_target_pairs={{2,0},{4,2},{6,4},{8,6},{10,8},{12,10},{14,12},{16,14},{18,16},{20... | collective-permute-start | bytes 73736 | tf_op jit(solution)/shard_map/ppermute | solution.py:18
  143.3 155.6 %copy-start.7 = (f32[512,768]{1,0:T(8,128)S(1)}, f32[512,768]{1,0:T(8,128)}, u32[]{:S(2)}) copy-start(f32[512,768]{1,0:T(8,128)} %fusion.119) | copy-start | bytes 4718596
  334.1 205.9 %all-reduce.9.cloned.1.call-start = ((), (), s32[]{:S(2)}) async-start(), calls=%async_computation.3 | async-start | bytes 6291456 | tf_op jit(solution)/shard_map/psum | solution.py:122
  334.2 10.4 %collective-permute-start.4 = (bf16[8,768]{1,0:T(8,128)(2,1)S(1)}, bf16[8,768]{1,0:T(8,128)(2,1)S(1)}, u32[]{:S(2)}, u32[]{:S(2)}) collective-permute-start(bf16[8,768]{1,0:T(8,128)(2,1)S(1)} %get-tuple-element.23), channel_id=1, source_target_pairs={{0,2},{2,4},{4,6},{6,8},{8,10},{10,12},{12,14},{14,16},{16,18},{18... | collective-permute-start | bytes 36872 | tf_op jit(solution)/shard_map/ppermute | solution.py:15
  336.1 10.5 %collective-permute-start.5 = (bf16[8,768]{1,0:T(8,128)(2,1)S(1)}, bf16[8,768]{1,0:T(8,128)(2,1)S(1)}, u32[]{:S(2)}, u32[]{:S(2)}) collective-permute-start(bf16[8,768]{1,0:T(8,128)(2,1)S(1)} %get-tuple-element.22), channel_id=1, source_target_pairs={{2,0},{4,2},{6,4},{8,6},{10,8},{12,10},{14,12},{16,14},{18,16},{20... | collective-permute-start | bytes 36872 | tf_op jit(solution)/shard_map/ppermute | solution.py:18
  426.2 9.8 %collective-permute-start.2 = (bf16[16,768]{1,0:T(8,128)(2,1)S(1)}, bf16[16,768]{1,0:T(8,128)(2,1)S(1)}, u32[]{:S(2)}, u32[]{:S(2)}) collective-permute-start(bf16[16,768]{1,0:T(8,128)(2,1)S(1)} %get-tuple-element.25), channel_id=1, source_target_pairs={{2,0},{4,2},{6,4},{8,6},{10,8},{12,10},{14,12},{16,14},{18,16},{20... | collective-permute-start | bytes 73736 | tf_op jit(solution)/shard_map/ppermute | solution.py:18
  434.0 7.8 %collective-permute-start.3 = (bf16[16,768]{1,0:T(8,128)(2,1)S(1)}, bf16[16,768]{1,0:T(8,128)(2,1)S(1)}, u32[]{:S(2)}, u32[]{:S(2)}) collective-permute-start(bf16[16,768]{1,0:T(8,128)(2,1)S(1)} %get-tuple-element.24), channel_id=1, source_target_pairs={{0,2},{2,4},{4,6},{6,8},{8,10},{10,12},{12,14},{14,16},{16,18},{18... | collective-permute-start | bytes 73736 | tf_op jit(solution)/shard_map/ppermute | solution.py:15
  444.6 1.2 copy-start.3
  449.1 8.4 %copy-start.2 = (bf16[3,512,768]{2,1,0:T(8,128)(2,1)S(1)}, bf16[3,512,768]{2,1,0:T(8,128)(2,1)}, u32[]{:S(2)}) copy-start(bf16[3,512,768]{2,1,0:T(8,128)(2,1)} %param.9) | copy-start | bytes 7077892
  449.2 207.0 %all-reduce.7.cloned.1.call-start = ((), (), s32[]{:S(2)}) async-start(), calls=%async_computation.2 | async-start | bytes 6291456 | tf_op jit(solution)/shard_map/psum | solution.py:122
  449.2 10.5 %collective-permute-start.8 = (bf16[4,768]{1,0:T(4,128)(2,1)S(1)}, bf16[4,768]{1,0:T(4,128)(2,1)S(1)}, u32[]{:S(2)}, u32[]{:S(2)}) collective-permute-start(bf16[4,768]{1,0:T(4,128)(2,1)S(1)} %get-tuple-element.19), channel_id=1, source_target_pairs={{0,2},{2,4},{4,6},{6,8},{8,10},{10,12},{12,14},{14,16},{16,18},{18... | collective-permute-start | bytes 18440 | tf_op jit(solution)/shard_map/ppermute | solution.py:15
  451.3 10.5 %collective-permute-start.9 = (bf16[4,768]{1,0:T(4,128)(2,1)S(1)}, bf16[4,768]{1,0:T(4,128)(2,1)S(1)}, u32[]{:S(2)}, u32[]{:S(2)}) collective-permute-start(bf16[4,768]{1,0:T(4,128)(2,1)S(1)} %get-tuple-element.18), channel_id=1, source_target_pairs={{2,0},{4,2},{6,4},{8,6},{10,8},{12,10},{14,12},{16,14},{18,16},{20... | collective-permute-start | bytes 18440 | tf_op jit(solution)/shard_map/ppermute | solution.py:18
  542.6 9.9 %collective-permute-start.6 = (bf16[8,768]{1,0:T(8,128)(2,1)S(1)}, bf16[8,768]{1,0:T(8,128)(2,1)S(1)}, u32[]{:S(2)}, u32[]{:S(2)}) collective-permute-start(bf16[8,768]{1,0:T(8,128)(2,1)S(1)} %get-tuple-element.21), channel_id=1, source_target_pairs={{2,0},{4,2},{6,4},{8,6},{10,8},{12,10},{14,12},{16,14},{18,16},{20... | collective-permute-start | bytes 36872 | tf_op jit(solution)/shard_map/ppermute | solution.py:18
  550.4 7.8 %copy-start.4 = (f32[512,768]{1,0:T(8,128)S(1)}, f32[512,768]{1,0:T(8,128)}, u32[]{:S(2)}) copy-start(f32[512,768]{1,0:T(8,128)} %copy-done.3) | copy-start | bytes 4718596
  550.4 7.8 %collective-permute-start.7 = (bf16[8,768]{1,0:T(8,128)(2,1)S(1)}, bf16[8,768]{1,0:T(8,128)(2,1)S(1)}, u32[]{:S(2)}, u32[]{:S(2)}) collective-permute-start(bf16[8,768]{1,0:T(8,128)(2,1)S(1)} %get-tuple-element.20), channel_id=1, source_target_pairs={{0,2},{2,4},{4,6},{6,8},{8,10},{10,12},{12,14},{14,16},{16,18},{18... | collective-permute-start | bytes 36872 | tf_op jit(solution)/shard_map/ppermute | solution.py:15
  560.8 1.2 copy-start.5
  658.7 9.9 %collective-permute-start.10 = (bf16[4,768]{1,0:T(4,128)(2,1)S(1)}, bf16[4,768]{1,0:T(4,128)(2,1)S(1)}, u32[]{:S(2)}, u32[]{:S(2)}) collective-permute-start(bf16[4,768]{1,0:T(4,128)(2,1)S(1)} %get-tuple-element.17), channel_id=1, source_target_pairs={{2,0},{4,2},{6,4},{8,6},{10,8},{12,10},{14,12},{16,14},{18,16},{20... | collective-permute-start | bytes 18440 | tf_op jit(solution)/shard_map/ppermute | solution.py:18
  666.5 7.8 %copy-start.6 = (f32[512,768]{1,0:T(8,128)S(1)}, f32[512,768]{1,0:T(8,128)}, u32[]{:S(2)}) copy-start(f32[512,768]{1,0:T(8,128)} %copy-done.5) | copy-start | bytes 4718596
  666.5 7.8 %collective-permute-start.11 = (bf16[4,768]{1,0:T(4,128)(2,1)S(1)}, bf16[4,768]{1,0:T(4,128)(2,1)S(1)}, u32[]{:S(2)}, u32[]{:S(2)}) collective-permute-start(bf16[4,768]{1,0:T(4,128)(2,1)S(1)} %get-tuple-element.16), channel_id=1, source_target_pairs={{0,2},{2,4},{4,6},{6,8},{8,10},{10,12},{12,14},{14,16},{16,18},{18... | collective-permute-start | bytes 18440 | tf_op jit(solution)/shard_map/ppermute | solution.py:15
  674.3 3.5 copy-start.1
Sparse Core Ops, SparseCore 0:
  334.3 89.3 all-reduce.10
  449.3 90.7 all-reduce.8
  565.4 90.7 all-reduce.6
where the time goes:
time: 686 us; the launch traced here: 684 us
  waiting for transfers between devices  404 us (59%)
  local copies, waits for them, and re-layouts  77.8 us (11%)
  starting transfers between devices  66.5 us (10%)
  other arithmetic  66.4 us (10%)
  matrix products  55.8 us (8%)
  between operations  13.7 us (2%)
    psum x3, waiting for transfers between devices, per_device(): preceding_sum, mid_sum = lax.psum((partial_result, mid_part), 'chan')  240 us
    ppermute x6, waiting for transfers between devices, with_halo(): lax.ppermute(lax.slice_in_dim(block, block.shape[dim] - width, None, axis...  165 us
    ppermute x6, starting transfers between devices, with_halo(): lax.ppermute(lax.slice_in_dim(block, 0, width, axis=dim), axis, backward)  34.2 us
    scatter-add x1, other arithmetic, per_device(): jax.ops.segment_sum(flat_values, got_place.reshape(-1).astype(jnp.int32),...  28.6 us
    dot_general x9, matrix products, per_device(): jnp.dot(act_pad[start:start + local_rows], conv_weight[block_level, kerne...  24.2 us
    gather x1, local copies, waits for them, and re-layouts, per_device(): slot_weight = jnp.where(filled, flat_grad[source], 0.0)  23 us
    gather x1, local copies, waits for them, and re-layouts, per_device(): slot_place = jnp.where(filled, offset[source], 0).astype(jnp.float32)  23 us
    dot_general x9, matrix products, per_device(): lax.dot_general(grad_pad[start:start + local_rows], conv_weight[block_lev...  21.3 us
  transfers between devices with their start and end apart: 17, of which 7 were waited for; matrix products, arithmetic and copies ran while one was open for 10% of the time, Pallas kernels for 0%

commit v1 on v0

v1 whole, which is shorter than its diff:
```python
import functools

import jax
import jax.numpy as jnp
from jax import lax
from jax.experimental import pallas as pl
from jax.experimental.pallas import tpu as pltpu
from jax.sharding import PartitionSpec as P

BASE_DILATION = 4
RANK = 8
SLOTS = 64
COLS = 256
GROUP_AXES = ("pos", "head")
HALO_IN = {2: 32, 1: 16, 0: 8, -1: 0}
HALO_SAVED = {2: 48, 1: 32, 0: 16}
F32 = jnp.float32
BF16 = jnp.bfloat16
NT = (((1,), (1,)), ((), ()))


def cost(flops, bytes_accessed, transcendentals=0):
    return pl.CostEstimate(
        flops=int(flops), bytes_accessed=int(bytes_accessed), transcendentals=int(transcendentals)
    )


def params():
    return pltpu.CompilerParams(vmem_limit_bytes=40 * 2**20)


def gelu_parts(value):
    half = 0.5 * (1.0 + lax.erf(value * 0.7071067811865476))
    return value * half, half + value * jnp.exp(-0.5 * value * value) * 0.3989422804014327


def vectors_kernel(place, weight, share, batch, left, right, out):
    projected = jnp.dot(weight[...], left[...], preferred_element_type=F32)
    column = lax.broadcasted_iota(jnp.int32, projected.shape, 1) // RANK
    kept = jnp.where(column == batch[...], projected, 0.0)
    removed = lax.dot_general(
        kept, right[...].astype(F32), NT, precision=lax.Precision.HIGHEST,
        preferred_element_type=F32,
    )
    out[...] = (share[...].astype(F32) - removed).astype(BF16)


def head_vectors(place, head_weight, batch_of, erase_left, erase_right, share):
    count, channels = head_weight.shape
    whole = lambda i, place: (0, 0)
    return pl.pallas_call(
        vectors_kernel,
        grid_spec=pltpu.PrefetchScalarGridSpec(
            num_scalar_prefetch=1,
            grid=(1,),
            in_specs=[
                pl.BlockSpec((count, channels), whole),
                pl.BlockSpec((count, share), lambda i, place: (0, place[0])),
                pl.BlockSpec((count, 1), whole),
                pl.BlockSpec(erase_left.shape, whole),
                pl.BlockSpec((share, erase_right.shape[1]), lambda i, place: (place[0], 0)),
            ],
            out_specs=pl.BlockSpec((count, share), whole),
        ),
        out_shape=jax.ShapeDtypeStruct((count, share), BF16),
        cost_estimate=cost(1e9, 1e6),
        compiler_params=params(),
        name="head_vectors",
    )(place, head_weight, head_weight, batch_of[:, None], erase_left, erase_right)


def bucket_kernel(rows, cover, bins, grads, out):
    chunks, lanes = bins.shape
    members = out.shape[0]
    before = (
        lax.broadcasted_iota(jnp.int32, (lanes, lanes), 0)
        < lax.broadcasted_iota(jnp.int32, (lanes, lanes), 1)
    ).astype(F32).astype(BF16)
    index = lax.broadcasted_iota(jnp.int32, (members, lanes), 0)
    lane = lax.broadcasted_iota(jnp.int32, (1, lanes), 1)
    base = jnp.zeros((members, 1), F32)
    total = jnp.zeros((members, 4 * SLOTS), F32)
    for chunk in range(chunks):
        place = bins[chunk : chunk + 1, :]
        target = place // rows
        offset = place - target * rows
        mine = jnp.where(target == index, 1.0, 0.0)
        mine_low = mine.astype(BF16)
        earlier = jnp.dot(mine_low, before, preferred_element_type=F32) + base
        rank = jnp.sum(mine * earlier, axis=0, keepdims=True).astype(jnp.int32)
        base = base + jnp.sum(mine, axis=1, keepdims=True)
        expert = chunk * (lanes // cover) + lane // cover
        high = offset // 256
        low = (offset - high * 256).astype(F32)
        code = (expert + high * SLOTS).astype(F32)
        value = grads[chunk : chunk + 1, :].astype(F32)
        hit = rank == index
        spread = jnp.concatenate(
            [jnp.where(hit, v, 0.0) for v in (low, code, value)] + [jnp.zeros_like(mine)], axis=0
        ).astype(BF16)
        total = total + lax.dot_general(mine_low, spread, NT, preferred_element_type=F32)
    out[...] = total.astype(BF16)


def bucket(cover_bins, bin_gradient, members, rows):
    cover = cover_bins.shape[1]
    entries = cover_bins.size
    return pl.pallas_call(
        functools.partial(bucket_kernel, rows, cover),
        out_shape=jax.ShapeDtypeStruct((members, 4 * SLOTS), BF16),
        cost_estimate=cost(1e8, 1e5),
        compiler_params=params(),
        name="bucket_entries",
    )(cover_bins.reshape(entries // 128, 128), bin_gradient.reshape(entries // 128, 128))


def spread_kernel(groups, fields, out):
    group = pl.program_id(0)
    low = fields[pl.ds(group, 1), :]
    code = fields[pl.ds(groups + group, 1), :]
    value = fields[pl.ds(2 * groups + group, 1), :]
    high = code >= SLOTS
    offset = (low + jnp.where(high, 256.0, 0.0)).astype(jnp.int32)
    slot = lax.broadcasted_iota(jnp.int32, code.shape, 1)
    column = (code - jnp.where(high, 1.0 * SLOTS, 0.0)).astype(jnp.int32) + slot // SLOTS * SLOTS
    rows = out.shape[0]
    width = out.shape[1]
    at_row = jnp.where(
        lax.broadcasted_iota(jnp.int32, (rows, width), 0) == offset, 1.0, 0.0
    ).astype(BF16)
    at_column = jnp.where(
        lax.broadcasted_iota(jnp.int32, (width, width), 0) == column, value, 0.0
    ).astype(BF16)
    out[...] = lax.dot_general(at_row, at_column, NT, preferred_element_type=F32).astype(BF16)


def spread_entries(fields, rows):
    groups = fields.shape[0] // 4
    width = fields.shape[1]
    return pl.pallas_call(
        functools.partial(spread_kernel, groups),
        grid=(groups,),
        in_specs=[pl.BlockSpec(fields.shape, lambda i: (0, 0))],
        out_specs=pl.BlockSpec((rows, width), lambda i: (0, i)),
        out_shape=jax.ShapeDtypeStruct((rows, groups * width), BF16),
        cost_estimate=cost(6e9, 8e6),
        compiler_params=params(),
        name="spread_entries",
    )(fields)


def pre_kernel(level, rows, saved, low, high, weight, own, send, slope, act):
    dilation = BASE_DILATION * 2**level
    halo = HALO_SAVED[level]
    inner = HALO_IN[level - 1]

    @pl.when(pl.program_id(0) == 0)
    def _():
        act[:halo, :] = gelu_parts(low[...].astype(F32))[0]
        act[halo + rows :, :] = gelu_parts(high[...].astype(F32))[0]
        value, _ = gelu_parts(saved[...].astype(F32))
        act[halo : halo + rows, :] = value

    total = None
    first = halo - HALO_IN[level] - dilation
    count = own.shape[0]
    for tap in range(weight.shape[0]):
        start = first + tap * dilation
        part = jnp.dot(
            act[start : start + count, :].astype(BF16), weight[tap], preferred_element_type=F32
        )
        total = part if total is None else total + part
    own[...] = total
    send[...] = total.astype(BF16)


def slope_kernel(mask, flags, own, other, out, *, halo, rows):
    value = own[...] + other[...].astype(F32)
    _, slope = gelu_parts(value)
    if mask:
        at = lax.broadcasted_iota(jnp.int32, value.shape, 0)
        outside = ((at < halo) & (flags[0] != 0)) | ((at >= halo + rows) & (flags[1] != 0))
        slope = jnp.where(outside, 0.0, slope)
    out[...] = slope


def pre_partial(level, saved, low, high, weights):
    rows, share = saved.shape
    count = rows + 2 * HALO_IN[level]
    halo = HALO_SAVED[level]
    taps, _, width = weights.shape
    fixed = lambda i: (0, 0)
    blocks = pl.BlockSpec((count, COLS), lambda i: (0, i))

    def body(saved, low, high, weight, own, send, act):
        pre_kernel(level, rows, saved, low, high, weight, own, send, None, act)

    return pl.pallas_call(
        body,
        grid=(width // COLS,),
        in_specs=[
            pl.BlockSpec((rows, share), fixed),
            pl.BlockSpec((halo, share), fixed),
            pl.BlockSpec((halo, share), fixed),
            pl.BlockSpec((taps, share, COLS), lambda i: (0, 0, i)),
        ],
        out_specs=[blocks, blocks],
        out_shape=[
            jax.ShapeDtypeStruct((count, width), F32),
            jax.ShapeDtypeStruct((count, width), BF16),
        ],
        scratch_shapes=[pltpu.VMEM((rows + 2 * halo, share), F32)],
        cost_estimate=cost(4e9, 8e6, 1e6),
        compiler_params=params(),
        name=f"pre_partial_{level}",
    )(saved, low, high, weights)


def pre_slope(level, flags, own, other, rows):
    count, width = own.shape
    blocks = pl.BlockSpec((count, COLS), lambda i, flags: (0, i))

    def body(flags, own, other, out):
        slope_kernel(True, flags, own, other, out, halo=HALO_IN[level], rows=rows)

    return pl.pallas_call(
        body,
        grid_spec=pltpu.PrefetchScalarGridSpec(
            num_scalar_prefetch=1, grid=(width // COLS,), in_specs=[blocks, blocks], out_specs=blocks
        ),
        out_shape=jax.ShapeDtypeStruct((count, width), F32),
        cost_estimate=cost(4e9, 5e6, 1e6),
        compiler_params=params(),
        name=f"pre_slope_{level}",
    )(flags, own, other)


def saved_slope(level, saved, low, high):
    rows, share = saved.shape
    halo = HALO_SAVED[level]
    inner = HALO_IN[level - 1]

    def body(saved, low, high, out):
        slope = lambda value: gelu_parts(value.astype(F32))[1]
        if inner:
            out[:inner, :] = slope(low[...])[halo - inner :]
            out[inner + rows :, :] = slope(high[...])[:inner]
        out[inner : inner + rows, :] = slope(saved[...])

    fixed = lambda i: (0, i)
    return pl.pallas_call(
        body,
        grid=(share // COLS,),
        in_specs=[
            pl.BlockSpec((rows, COLS), fixed),
            pl.BlockSpec((halo, COLS), fixed),
            pl.BlockSpec((halo, COLS), fixed),
        ],
        out_specs=pl.BlockSpec((rows + 2 * inner, COLS), fixed),
        out_shape=jax.ShapeDtypeStruct((rows + 2 * inner, share), F32),
        cost_estimate=cost(4e9, 3e6, 1e6),
        compiler_params=params(),
        name=f"saved_slope_{level}",
    )(saved, low, high)


def to_middle(step, grad, expand, own, send, middle):
    part = lax.dot_general(grad.astype(BF16), expand[...], NT, preferred_element_type=F32)

    @pl.when(step == 0)
    def _():
        middle[...] = part

    @pl.when(step > 0)
    def _():
        middle[...] += part

    @pl.when(step == pl.num_programs(0) - 1)
    def _():
        own[...] = middle[...]
        send[...] = middle[...].astype(BF16)


def top_kernel(spread, vectors, expand, grad, own, send, middle):
    top = jnp.dot(spread[...], vectors[...], preferred_element_type=F32)
    grad[...] = top
    to_middle(pl.program_id(0), top, expand, own, send, middle)


def top_gradient(spread, vectors, expand):
    count, depth = spread.shape
    share = vectors.shape[1]
    width = expand.shape[0]
    fixed = lambda i: (0, 0)
    blocks = lambda i: (0, i)
    return pl.pallas_call(
        top_kernel,
        grid=(share // COLS,),
        in_specs=[
            pl.BlockSpec((count, depth), fixed),
            pl.BlockSpec((depth, COLS), blocks),
            pl.BlockSpec((width, COLS), blocks),
        ],
        out_specs=[
            pl.BlockSpec((count, COLS), blocks),
            pl.BlockSpec((count, width), fixed),
            pl.BlockSpec((count, width), fixed),
        ],
        out_shape=[
            jax.ShapeDtypeStruct((count, share), F32),
            jax.ShapeDtypeStruct((count, width), F32),
            jax.ShapeDtypeStruct((count, width), BF16),
        ],
        scratch_shapes=[pltpu.VMEM((count, width), F32)],
        cost_estimate=cost(5e9, 14e6),
        compiler_params=params(),
        name="top_gradient",
    )(spread, vectors, expand)


def block_kernel(level, refs):
    last = level == 0
    if last:
        own, other, slope, weight, grad, outer, out, pre, shifted = refs
    else:
        own, other, slope, weight, grad, outer, expand, out, own_next, send, pre, shifted, middle = refs
    dilation = BASE_DILATION * 2**level
    count = out.shape[0]
    trim = HALO_IN[level] - HALO_IN[level - 1]
    taps = weight.shape[0]

    @pl.when(pl.program_id(0) == 0)
    def _():
        pre[...] = (own[...] + other[...].astype(F32)) * slope[...]
        for tap in range(taps):
            start = trim - (tap - 1) * dilation
            shifted[tap] = pre[start : start + count, :].astype(BF16)

    total = None
    for tap in range(taps):
        part = lax.dot_general(shifted[tap], weight[tap], NT, preferred_element_type=F32)
        total = part if total is None else total + part
    new = grad[trim : trim + count, :] + total * outer[...]
    if last:
        out[...] = new.astype(BF16)
    else:
        out[...] = new
        to_middle(pl.program_id(0), new, expand, own_next, send, middle)


def block_step(level, own, other, slope, weight, grad, outer, expand):
    count_in, width = own.shape
    count = outer.shape[0]
    taps, share, _ = weight.shape
    fixed = lambda i: (0, 0)
    blocks = lambda i: (0, i)
    last = level == 0
    in_specs = [
        pl.BlockSpec((count_in, width), fixed),
        pl.BlockSpec((count_in, width), fixed),
        pl.BlockSpec((count_in, width), fixed),
        pl.BlockSpec((taps, COLS, width), lambda i: (0, i, 0)),
        pl.BlockSpec((count_in, COLS), blocks),
        pl.BlockSpec((count, COLS), blocks),
    ]
    args = [own, other, slope, weight, grad, outer]
    out_specs = [pl.BlockSpec((count, COLS), blocks)]
    out_shape = [jax.ShapeDtypeStruct((count, share), BF16 if last else F32)]
    scratch = [pltpu.VMEM((count_in, width), F32), pltpu.VMEM((taps, count, width), BF16)]
    if not last:
        in_specs.append(pl.BlockSpec((width, COLS), blocks))
        args.append(expand)
        out_specs += [pl.BlockSpec((count, width), fixed)] * 2
        out_shape += [
            jax.ShapeDtypeStruct((count, width), F32),
            jax.ShapeDtypeStruct((count, width), BF16),
        ]
        scratch.append(pltpu.VMEM((count, width), F32))
    return pl.pallas_call(
        lambda *refs: block_kernel(level, refs),
        grid=(share // COLS,),
        in_specs=in_specs,
        out_specs=out_specs,
        out_shape=out_shape,
        scratch_shapes=scratch,
        cost_estimate=cost(5e9, 14e6),
        compiler_params=params(),
        name=f"block_step_{level}",
    )(*args)


def gather_vectors(vectors):
    count = vectors.shape[0]
    place = lax.axis_index("head")
    along, turn = place // 4, place % 4
    same = lambda steps: [(a * 4 + z, a * 4 + (z - steps) % 4) for a in range(2) for z in range(4)]
    parts = [vectors] + [lax.ppermute(vectors, "head", same(k)) for k in (1, 2, 3)]
    twice = jnp.concatenate(parts + parts, axis=0)
    ring = lax.dynamic_slice_in_dim(twice, (4 - turn) % 4 * count, 4 * count, 0)
    other = lax.ppermute(ring, "head", [(k, (k + 4) % 8) for k in range(8)])
    both = jnp.where(
        along == 0,
        jnp.concatenate([ring, other], axis=0),
        jnp.concatenate([other, ring], axis=0),
    )
    return lax.all_gather(both, "pos", tiled=True)


def per_device(
    inputs_saved,
    conv_weight,
    expand_weight,
    head_weight,
    batch_of,
    erase_left,
    erase_right,
    bin_gradient,
    cover_bins,
):
    members = lax.axis_size(GROUP_AXES)
    layers, rows, share = inputs_saved.shape
    member = lax.axis_index(GROUP_AXES)
    chan_place = lax.axis_index("chan")
    up = [(k, k + 1) for k in range(members - 1)]
    down = [(k + 1, k) for k in range(members - 1)]
    swap = [(0, 1), (1, 0)]
    levels = list(reversed(range(layers)))

    vectors = head_vectors(
        chan_place[None].astype(jnp.int32), head_weight, batch_of, erase_left, erase_right, share
    )
    gathered = gather_vectors(vectors)

    payload = bucket(cover_bins, bin_gradient, members, rows)
    arrived = lax.all_to_all(payload, GROUP_AXES, split_axis=0, concat_axis=0, tiled=True)
    fields = (
        arrived.reshape(members, 4, SLOTS).transpose(1, 0, 2).reshape(-1, COLS).astype(F32)
    )
    spread = spread_entries(fields, rows)
    reach = HALO_IN[layers - 1]
    spread_low = lax.ppermute(spread[rows - reach :], GROUP_AXES, up)
    spread_high = lax.ppermute(spread[:reach], GROUP_AXES, down)
    spread = jnp.concatenate([spread_low, spread, spread_high], axis=0)

    edge_low = jnp.concatenate([inputs_saved[n, rows - HALO_SAVED[n] :] for n in levels], axis=0)
    edge_high = jnp.concatenate([inputs_saved[n, : HALO_SAVED[n]] for n in levels], axis=0)
    edge_low = lax.ppermute(edge_low, GROUP_AXES, up)
    edge_high = lax.ppermute(edge_high, GROUP_AXES, down)
    flags = jnp.stack([member == 0, member == members - 1]).astype(jnp.int32)
    start = 0
    slopes, outers = {}, {}
    for n in levels:
        size = HALO_SAVED[n]
        low, high = edge_low[start : start + size], edge_high[start : start + size]
        start += size
        own, send = pre_partial(n, inputs_saved[n], low, high, conv_weight[n])
        other = lax.ppermute(send, "chan", swap)
        slopes[n] = pre_slope(n, flags, own, other, rows)
        outers[n] = saved_slope(n, inputs_saved[n], low, high)

    grad, own, send = top_gradient(spread, gathered, expand_weight[layers - 1])
    for n in levels:
        other = lax.ppermute(send, "chan", swap)
        outs = block_step(
            n, own, other, slopes[n], conv_weight[n], grad, outers[n],
            expand_weight[n - 1] if n else None,
        )
        if n:
            grad, own, send = outs
    return outs[0]


def solution(mesh):
    return jax.shard_map(
        per_device,
        mesh=mesh,
        in_specs=(
            P(None, ("pos", "head"), "chan"),
            P(None, None, "chan", None),
            P(None, None, "chan"),
            P(("pos", "head"), None),
            P(("pos", "head")),
            P(),
            P(),
            P(("pos", "head"), None),
            P(("pos", "head"), None),
        ),
        out_specs=P(("pos", "head"), "chan"),
        check_vma=False,
    )
```

time: 686 us -> 223 us (0.33)
  waiting for transfers between devices: 404 us -> 67 us
  other arithmetic: 66.4 us -> 7.33 us
  matrix products: 55.8 us -> 0 us
  Pallas kernels: 0 us -> 53.8 us
  local copies, waits for them, and re-layouts: 77.8 us -> 38.8 us
  starting transfers between devices: 66.5 us -> 39.4 us
    psum x3 -> x0, waiting for transfers between devices: 240 us -> none  [per_device(): preceding_sum, mid_sum = lax.psum((partial_result, mid_part), 'chan')]
    ppermute x12 -> x14, waiting for transfers between devices: 165 us -> 67 us  [the longest x6 50.5 us: per_device(): other = lax.ppermute(send, 'chan', swap)]
    gather x3 -> x0, local copies, waits for them, and re-layouts: 63.9 us -> none  [the longest x1 23 us: per_device(): slot_weight = jnp.where(filled, flat_grad[source], 0.0)]
    dot_general x23 -> x0, matrix products: 55.8 us -> none  [the longest x9 24.2 us: per_device(): jnp.dot(act_pad[start:start + local_rows], conv_weight[block_level, kerne...]
    pallas_call x0 -> x16, Pallas kernels: none -> 53.8 us  [the longest x3 18.1 us: block_step(): pl.pallas_call(lambda *refs: block_kernel(level, refs), grid=(share // CO...]
    scatter-add x1 -> x0, other arithmetic: 28.6 us -> none  [per_device(): jax.ops.segment_sum(flat_values, got_place.reshape(-1).astype(jnp.int32),...]
    another operation x2 -> x0, other arithmetic: 18.3 us -> none
    ppermute x12 -> x14, starting transfers between devices: 47.6 us -> 32.9 us  [the longest x6 11.1 us: per_device(): other = lax.ppermute(send, 'chan', swap)]
  transfers between devices with their start and end apart: 17 -> 16, of which waited for: 7 -> 9; matrix products, arithmetic and copies ran while one was open for 10% -> 14% of each run, Pallas kernels for 0% -> 22%
where the time goes in v1:
time: 223 us; the launch traced here: 220 us
  waiting for transfers between devices  67 us (30%)
  Pallas kernels  53.8 us (24%)
  starting transfers between devices  39.4 us (18%)
  local copies, waits for them, and re-layouts  38.8 us (17%)
  between operations  13.9 us (6%)
  other arithmetic  7.33 us (3%)
    ppermute x6, waiting for transfers between devices, per_device(): other = lax.ppermute(send, 'chan', swap)  50.5 us
    pallas_call x3, Pallas kernels, block_step(): pl.pallas_call(lambda *refs: block_kernel(level, refs), grid=(share // CO...  18.1 us
    unnamed x89, local copies, waits for them, and re-layouts  15.9 us
    ppermute x6, starting transfers between devices, per_device(): other = lax.ppermute(send, 'chan', swap)  11.1 us
    pallas_call x3, Pallas kernels, pre_partial(): pl.pallas_call(body, grid=(width // COLS,), in_specs=[pl.BlockSpec((rows,...  10.5 us
    ppermute x1, waiting for transfers between devices, gather_vectors(): other = lax.ppermute(ring, 'head', [(k, (k + 4) % 8) for k in range(8)])  10.2 us
    pallas_call x1, Pallas kernels, top_gradient(): pl.pallas_call(top_kernel, grid=(share // COLS,), in_specs=[pl.BlockSpec(...  8.72 us
    squeeze x2, local copies, waits for them, and re-layouts, per_device(): own, send = pre_partial(n, inputs_saved[n], low, high, conv_weight[n])  8.6 us
  transfers between devices with their start and end apart: 16, of which 9 were waited for; matrix products, arithmetic and copies ran while one was open for 14% of the time, Pallas kernels for 22%

profile of v1, /device:TPU:8, one launch (start us, length us, event | category | flops | bytes accessed | tf_op | source)
XLA Modules:
  0.0 220.2 jit_solution(5036657597559716323)
XLA Ops:
  6.5 1.1 copy.27.left
  7.7 1.2 copy.28.right
  8.8 0.7 copy.26.batch
  9.6 0.9 copy-done.17
  10.5 0.7 head_vectors.1
  11.2 4.1 %collective-permute-start.2 = (bf16[64,768]{1,0:T(8,128)(2,1)S(1)}, bf16[64,768]{1,0:T(8,128)(2,1)S(1)}, u32[]{:S(2)}, u32[]{:S(2)}) collective-permute-start(bf16[64,768]{1,0:T(8,128)(2,1)S(1)} %head_vectors.1), channel_id=1, source_target_pairs={{0,6},{2,0},{4,2},{6,4},{8,14},{10,8},{12,10},{14,12},{1,7},{3,1},... | collective-permute-start | bytes 294920 | tf_op jit(solution)/shard_map/ppermute | solution.py:397
  15.3 1.3 collective-permute-start.4
  16.6 2.9 %collective-permute-done.2 = bf16[64,768]{1,0:T(8,128)(2,1)S(1)} collective-permute-done((bf16[64,768]{1,0:T(8,128)(2,1)S(1)}, bf16[64,768]{1,0:T(8,128)(2,1)S(1)}, u32[]{:S(2)}, u32[]{:S(2)}) %collective-permute-start.2) | collective-permute-done | bytes 98336 | tf_op jit(solution)/shard_map/ppermute | solution.py:397
  19.5 2.7 %collective-permute-done.3 = bf16[64,768]{1,0:T(8,128)(2,1)S(1)} collective-permute-done((bf16[64,768]{1,0:T(8,128)(2,1)S(1)}, bf16[64,768]{1,0:T(8,128)(2,1)S(1)}, u32[]{:S(2)}, u32[]{:S(2)}) %collective-permute-start.3) | collective-permute-done | bytes 98336 | tf_op jit(solution)/shard_map/ppermute | solution.py:397
  23.6 10.2 %collective-permute-done.5 = bf16[256,768]{1,0:T(8,128)(2,1)S(1)} collective-permute-done((bf16[256,768]{1,0:T(8,128)(2,1)S(1)}, bf16[256,768]{1,0:T(8,128)(2,1)S(1)}, u32[]{:S(2)}, u32[]{:S(2)}) %collective-permute-start.5) | collective-permute-done | bytes 393248 | tf_op jit(solution)/shard_map/ppermute | solution.py:400
  33.8 1.2 maximum_select_fusion
  35.4 1.9 bucket_entries.1
  39.0 6.5 %all-to-all-start = ((bf16[64,2,128]{2,1,0:T(2,128)(2,1)}), bf16[64,2,128]{2,1,0:T(2,128)(2,1)}, u32[]{:S(2)}, u32[]{:S(2)}) async-start(bf16[64,2,128]{2,1,0:T(2,128)(2,1)} %reshape.20), calls=%async_computation | async-start | bytes 65536 | tf_op jit(solution)/shard_map/all_to_all | solution.py:435
  46.3 3.4 %collective-permute-start.7 = (bf16[96,768]{1,0:T(8,128)(2,1)}, bf16[96,768]{1,0:T(8,128)(2,1)}, u32[]{:S(2)}, u32[]{:S(2)}) collective-permute-start(bf16[96,768]{1,0:T(8,128)(2,1)} %pad_maximum_fusion.1), channel_id=1, source_target_pairs={{0,2},{2,4},{4,6},{6,8},{8,10},{10,12},{12,14},{14,16},{16,18},{18... | collective-permute-start | bytes 442376 | tf_op jit(solution)/shard_map/ppermute | solution.py:447
  50.3 4.6 %collective-permute-start.8 = (bf16[96,768]{1,0:T(8,128)(2,1)}, bf16[96,768]{1,0:T(8,128)(2,1)}, u32[]{:S(2)}, u32[]{:S(2)}) collective-permute-start(bf16[96,768]{1,0:T(8,128)(2,1)} %pad_maximum_fusion.2), channel_id=1, source_target_pairs={{2,0},{4,2},{6,4},{8,6},{10,8},{12,10},{14,12},{16,14},{18,16},{20... | collective-permute-start | bytes 442376 | tf_op jit(solution)/shard_map/ppermute | solution.py:448
  54.9 1.5 slice_bitcast_fusion.6
  56.4 1.4 copy-done.34
  57.8 1.9 slice_bitcast_fusion.3
  59.6 7.1 %slice_bitcast_fusion = (bf16[3,768,768]{2,1,0:T(8,128)(2,1)S(1)}, bf16[3,768,768]{2,1,0:T(8,128)(2,1)}, bf16[3,768,768]{2,1,0:T(8,128)(2,1)}) fusion(bf16[3,3,768,768]{3,2,1,0:T(8,128)(2,1)} %param.10), kind=kLoop, calls=%fused_computation.1 | loop fusion | bytes 21233664 | tf_op jit(solution)/shard_map/squeeze | solution.py:456
  66.9 1.4 reshape.21
  68.3 1.6 convert_reduce_fusion
  69.9 1.6 reshape.18
  71.5 1.6 copy.30
  73.1 1.6 reshape.17.fields
  74.7 0.8 copy-done.14
  75.6 4.7 %spread_entries.1 = bf16[512,4096]{1,0:T(8,128)(2,1)S(1)} custom-call(f32[64,256]{1,0:T(8,128)S(1)} %copy-done.14), custom_call_target="tpu_custom_call" | custom-call | flops 6000000000 | bytes 8000000 | tf_op jit(solution)/shard_map/spread_entries/pallas_call | solution.py:140
  80.3 1.9 collective-permute-start
  82.3 6.0 %collective-permute-start.1 = (bf16[32,4096]{1,0:T(8,128)(2,1)S(1)}, bf16[32,4096]{1,0:T(8,128)(2,1)S(1)}, u32[]{:S(2)}, u32[]{:S(2)}) collective-permute-start(bf16[32,4096]{1,0:T(8,128)(2,1)S(1)} %get-tuple-element.39), channel_id=1, source_target_pairs={{2,0},{4,2},{6,4},{8,6},{10,8},{12,10},{14,12},{16,14},{18,16},{20... | collective-permute-start | bytes 786440 | tf_op jit(solution)/shard_map/ppermute | solution.py:442
  88.3 0.9 slice.100.low
  89.2 0.9 slice.101.high
  90.1 4.1 %pre_partial_2.1 = (f32[576,768]{1,0:T(8,128)S(1)}, bf16[576,768]{1,0:T(8,128)(2,1)}) custom-call(bf16[512,768]{1,0:T(8,128)(2,1)S(1)} %copy-done.8, bf16[48,768]{1,0:T(8,128)(2,1)S(1)} %slice.100.low, bf16[48,768]{1,0:T(8,128)(2,1)S(1)} %slice.101.high, bf16[3,768,768]{2,1,0:T(8,128)(2,1)S(1)} %copy-done.2), custom_call_target="tpu_custom_call" | custom-call | flops 4000000000 | bytes 8000000 | tf_op jit(solution)/shard_map/pre_partial_2/pallas_call | solution.py:198
  94.2 1.2 copy-done.28
  95.4 2.3 %collective-permute-start.9 = (bf16[576,768]{1,0:T(8,128)(2,1)}, bf16[576,768]{1,0:T(8,128)(2,1)}, u32[]{:S(2)}, u32[]{:S(2)}) collective-permute-start(bf16[576,768]{1,0:T(8,128)(2,1)} %get-tuple-element.23), channel_id=1, source_target_pairs={{0,1},{1,0},{2,3},{3,2},{4,5},{5,4},{6,7},{7,6},{8,9},{9,8},{10,11... | collective-permute-start | bytes 2654216 | tf_op jit(solution)/shard_map/ppermute | solution.py:457
  97.7 1.4 slice.102.low
  99.1 1.4 slice.103.high
  100.5 2.5 %pad_maximum_fusion.spread = bf16[576,4096]{1,0:T(8,128)(2,1)} fusion(bf16[32,4096]{1,0:T(8,128)(2,1)S(1)} %collective-permute-done.1, bf16[512,4096]{1,0:T(8,128)(2,1)S(1)} %spread_entries.1, bf16[32,4096]{1,0:T(8,128)(2,1)S(1)} %collective-permute-done), kind=kLoop, calls=%fused_computation | loop fusion | flops 14155776 | bytes 9437184 | tf_op jit(solution)/shard_map/concatenate | solution.py:443
  103.0 2.3 %copy-done = bf16[576,4096]{1,0:T(8,128)(2,1)S(1)} copy-done((bf16[576,4096]{1,0:T(8,128)(2,1)S(1)}, bf16[576,4096]{1,0:T(8,128)(2,1)}, u32[]{:S(2)}) %copy-start) | copy-done | bytes 4718616
  105.3 1.3 copy-done.5
  106.6 8.7 %top_gradient.1 = (f32[576,768]{1,0:T(8,128)S(1)}, f32[576,768]{1,0:T(8,128)S(1)}, bf16[576,768]{1,0:T(8,128)(2,1)S(1)}) custom-call(bf16[576,4096]{1,0:T(8,128)(2,1)S(1)} %copy-done, bf16[4096,768]{1,0:T(8,128)(2,1)} %all-gather.2.cloned.1.call-done.vectors, bf16[768,768]{1,0:T(8,128)(2,1)S(1)} %copy-done.5), custom_call_target="tpu_custom_call" | custom-call | flops 5000000000 | bytes 14000000 | tf_op jit(solution)/shard_map/top_gradient/pallas_call | solution.py:296
  115.4 1.2 copy-done.18
  116.6 1.3 collective-permute-start.6
  117.9 3.2 %pre_partial_1.1 = (f32[544,768]{1,0:T(8,128)S(1)}, bf16[544,768]{1,0:T(8,128)(2,1)S(1)}) custom-call(bf16[512,768]{1,0:T(8,128)(2,1)S(1)} %copy-done.7, bf16[32,768]{1,0:T(8,128)(2,1)S(1)} %copy-done.15, bf16[32,768]{1,0:T(8,128)(2,1)S(1)} %copy-done.16, bf16[3,768,768]{2,1,0:T(8,128)(2,1)S(1)} %copy-done.1), custom_call_target="tpu_custom_call" | custom-call | flops 4000000000 | bytes 8000000 | tf_op jit(solution)/shard_map/pre_partial_1/pallas_call | solution.py:198
  121.1 2.5 %collective-permute-start.11 = (bf16[544,768]{1,0:T(8,128)(2,1)S(1)}, bf16[544,768]{1,0:T(8,128)(2,1)S(1)}, u32[]{:S(2)}, u32[]{:S(2)}) collective-permute-start(bf16[544,768]{1,0:T(8,128)(2,1)S(1)} %get-tuple-element.28), channel_id=1, source_target_pairs={{0,1},{1,0},{2,3},{3,2},{4,5},{5,4},{6,7},{7,6},{8,9},{9,8},{10,11... | collective-permute-start | bytes 2506760 | tf_op jit(solution)/shard_map/ppermute | solution.py:457
  123.7 0.7 slice.104.low
  124.4 0.7 slice.105.high
  125.2 0.9 saved_slope_2.1.refs_5_
  126.6 3.4 %pre_slope_2.1.refs_2_ = f32[576,768]{1,0:T(8,128)S(1)} custom-call(s32[2]{0:T(128)S(1)} %add_convert_fusion.flags, f32[576,768]{1,0:T(8,128)S(1)} %copy-done.29, bf16[576,768]{1,0:T(8,128)(2,1)} %collective-permute-done.9.other), custom_call_target="tpu_custom_call" | custom-call | flops 4000000000 | bytes 5000000 | tf_op jit(solution)/shard_map/pre_slope_2/pallas_call | solution.py:226
  130.1 10.6 %collective-permute-done.6.refs_1_ = bf16[576,768]{1,0:T(8,128)(2,1)S(1)} collective-permute-done((bf16[576,768]{1,0:T(8,128)(2,1)S(1)}, bf16[576,768]{1,0:T(8,128)(2,1)S(1)}, u32[]{:S(2)}, u32[]{:S(2)}) %collective-permute-start.6) | collective-permute-done | bytes 884768 | tf_op jit(solution)/shard_map/ppermute | solution.py:463
  140.7 1.5 copy-done.21
  142.1 6.9 %block_step_2.1 = (f32[544,768]{1,0:T(8,128)S(1)}, f32[544,768]{1,0:T(8,128)S(1)}, bf16[544,768]{1,0:T(8,128)(2,1)S(1)}) custom-call(f32[576,768]{1,0:T(8,128)S(1)} %copy-done.21, bf16[576,768]{1,0:T(8,128)(2,1)S(1)} %collective-permute-done.6.refs_1_, f32[576,768]{1,0:T(8,128)S(1)} %pre_slope_2.1.refs_2_, ...), custom_call_target="tpu_custom_call" | custom-call | flops 5000000000 | bytes 14000000 | tf_op jit(solution)/shard_map/block_step_2/pallas_call | solution.py:379
  149.1 1.3 collective-permute-start.10
  150.4 3.2 %pre_partial_0.1 = (f32[528,768]{1,0:T(8,128)S(1)}, bf16[528,768]{1,0:T(8,128)(2,1)S(1)}) custom-call(bf16[512,768]{1,0:T(8,128)(2,1)S(1)} %copy-done.6, bf16[16,768]{1,0:T(8,128)(2,1)S(1)} %slice.104.low, bf16[16,768]{1,0:T(8,128)(2,1)S(1)} %slice.105.high, bf16[3,768,768]{2,1,0:T(8,128)(2,1)S(1)} %get-tuple-element.35.weight.refs_3_), custom_call_target="tpu_custom_call" | custom-call | flops 4000000000 | bytes 8000000 | tf_op jit(solution)/shard_map/pre_partial_0/pallas_call | solution.py:198
  153.6 2.3 %collective-permute-start.13 = (bf16[528,768]{1,0:T(8,128)(2,1)S(1)}, bf16[528,768]{1,0:T(8,128)(2,1)S(1)}, u32[]{:S(2)}, u32[]{:S(2)}) collective-permute-start(bf16[528,768]{1,0:T(8,128)(2,1)S(1)} %get-tuple-element.33), channel_id=1, source_target_pairs={{0,1},{1,0},{2,3},{3,2},{4,5},{5,4},{6,7},{7,6},{8,9},{9,8},{10,11... | collective-permute-start | bytes 2433032 | tf_op jit(solution)/shard_map/ppermute | solution.py:457
  156.0 0.9 saved_slope_1.1.refs_5_
  156.9 1.7 collective-permute-done.11.other
  158.6 1.6 pre_slope_1.1.refs_2_
  160.2 16.3 %collective-permute-done.10.refs_1_ = bf16[544,768]{1,0:T(8,128)(2,1)S(1)} collective-permute-done((bf16[544,768]{1,0:T(8,128)(2,1)S(1)}, bf16[544,768]{1,0:T(8,128)(2,1)S(1)}, u32[]{:S(2)}, u32[]{:S(2)}) %collective-permute-start.10) | collective-permute-done | bytes 835616 | tf_op jit(solution)/shard_map/ppermute | solution.py:463
  176.5 6.7 %block_step_1.1 = (f32[528,768]{1,0:T(8,128)S(1)}, f32[528,768]{1,0:T(8,128)S(1)}, bf16[528,768]{1,0:T(8,128)(2,1)S(1)}) custom-call(f32[544,768]{1,0:T(8,128)S(1)} %copy-done.25, bf16[544,768]{1,0:T(8,128)(2,1)S(1)} %collective-permute-done.10.refs_1_, f32[544,768]{1,0:T(8,128)S(1)} %pre_slope_1.1.refs_2_, ...), custom_call_target="tpu_custom_call" | custom-call | flops 5000000000 | bytes 14000000 | tf_op jit(solution)/shard_map/block_step_1/pallas_call | solution.py:379
  183.3 1.3 collective-permute-start.12
  184.6 0.8 saved_slope_0.1.refs_5_
  185.4 8.4 %collective-permute-done.13.other = bf16[528,768]{1,0:T(8,128)(2,1)S(1)} collective-permute-done((bf16[528,768]{1,0:T(8,128)(2,1)S(1)}, bf16[528,768]{1,0:T(8,128)(2,1)S(1)}, u32[]{:S(2)}, u32[]{:S(2)}) %collective-permute-start.13) | collective-permute-done | bytes 811040 | tf_op jit(solution)/shard_map/ppermute | solution.py:457
  193.9 1.6 pre_slope_0.1.refs_2_
  195.4 13.5 %collective-permute-done.12.refs_1_ = bf16[528,768]{1,0:T(8,128)(2,1)S(1)} collective-permute-done((bf16[528,768]{1,0:T(8,128)(2,1)S(1)}, bf16[528,768]{1,0:T(8,128)(2,1)S(1)}, u32[]{:S(2)}, u32[]{:S(2)}) %collective-permute-start.12) | collective-permute-done | bytes 811040 | tf_op jit(solution)/shard_map/ppermute | solution.py:463
  209.0 4.4 %block_step_0.1 = bf16[512,768]{1,0:T(8,128)(2,1)} custom-call(f32[528,768]{1,0:T(8,128)S(1)} %get-tuple-element.30.refs_0_, bf16[528,768]{1,0:T(8,128)(2,1)S(1)} %collective-permute-done.12.refs_1_, f32[528,768]{1,0:T(8,128)S(1)} %pre_slope_0.1.refs_2_, bf16[3,768,768]{2,1,0:T(8,128)(2,1)S(1)} %get-tuple-element.35.weight.refs_3_, ...), custom_call_target="tpu_custom_call" | custom-call | flops 5000000000 | bytes 14000000 | tf_op jit(solution)/shard_map/block_step_0/pallas_call | solution.py:379
  (103 shorter events, 5.5 us)
Async XLA Ops:
  6.5 96.5 %all-gather.2.cloned.1.call-start = ((), (), s32[]{:S(2)}) async-start(), calls=%async_computation.1 | async-start | bytes 7077888 | tf_op jit(solution)/shard_map/all_gather | solution.py:406
  9.6 0.9 copy-start.17
  11.2 8.3 %collective-permute-start.2 = (bf16[64,768]{1,0:T(8,128)(2,1)S(1)}, bf16[64,768]{1,0:T(8,128)(2,1)S(1)}, u32[]{:S(2)}, u32[]{:S(2)}) collective-permute-start(bf16[64,768]{1,0:T(8,128)(2,1)S(1)} %head_vectors.1), channel_id=1, source_target_pairs={{0,6},{2,0},{4,2},{6,4},{8,14},{10,8},{12,10},{14,12},{1,7},{3,1},... | collective-permute-start | bytes 294920 | tf_op jit(solution)/shard_map/ppermute | solution.py:397
  15.3 6.9 %collective-permute-start.3 = (bf16[64,768]{1,0:T(8,128)(2,1)S(1)}, bf16[64,768]{1,0:T(8,128)(2,1)S(1)}, u32[]{:S(2)}, u32[]{:S(2)}) collective-permute-start(bf16[64,768]{1,0:T(8,128)(2,1)S(1)} %head_vectors.1), channel_id=1, source_target_pairs={{0,4},{2,6},{4,0},{6,2},{8,12},{10,14},{12,8},{14,10},{1,5},{3,7},... | collective-permute-start | bytes 294920 | tf_op jit(solution)/shard_map/ppermute | solution.py:397
  15.3 7.6 %collective-permute-start.4 = (bf16[64,768]{1,0:T(8,128)(2,1)S(1)}, bf16[64,768]{1,0:T(8,128)(2,1)S(1)}, u32[]{:S(2)}, u32[]{:S(2)}) collective-permute-start(bf16[64,768]{1,0:T(8,128)(2,1)S(1)} %head_vectors.1), channel_id=1, source_target_pairs={{0,2},{2,4},{4,6},{6,0},{8,10},{10,12},{12,14},{14,8},{1,3},{3,5},... | collective-permute-start | bytes 294920 | tf_op jit(solution)/shard_map/ppermute | solution.py:397
  16.6 18.4 %copy-start.36 = (s32[64,32]{0,1:T(8,128)S(1)}, s32[64,32]{0,1:T(8,128)}, u32[]{:S(2)}) copy-start(s32[64,32]{0,1:T(8,128)} %param.17) | copy-start | bytes 24580
  16.6 18.6 %copy-start.37 = (bf16[64,32]{0,1:T(8,128)(2,1)S(1)}, bf16[64,32]{0,1:T(8,128)(2,1)}, u32[]{:S(2)}) copy-start(bf16[64,32]{0,1:T(8,128)(2,1)} %param.16) | copy-start | bytes 12292
  22.9 22.6 %copy-start.35 = (bf16[3,512,768]{2,1,0:T(8,128)(2,1)S(1)}, bf16[3,512,768]{2,1,0:T(8,128)(2,1)}, u32[]{:S(2)}) copy-start(bf16[3,512,768]{2,1,0:T(8,128)(2,1)} %param.9) | copy-start | bytes 7077892
  23.0 10.8 %collective-permute-start.5 = (bf16[256,768]{1,0:T(8,128)(2,1)S(1)}, bf16[256,768]{1,0:T(8,128)(2,1)S(1)}, u32[]{:S(2)}, u32[]{:S(2)}) collective-permute-start(bf16[256,768]{1,0:T(8,128)(2,1)S(1)} %constant_dynamic-slice_fusion), channel_id=1, source_target_pairs={{0,8},{2,10},{4,12},{6,14},{8,0},{10,2},{12,4},{14,6},{1,9},{3,11}... | collective-permute-start | bytes 1179656 | tf_op jit(solution)/shard_map/ppermute | solution.py:400
  39.0 27.8 %all-to-all-start = ((bf16[64,2,128]{2,1,0:T(2,128)(2,1)}), bf16[64,2,128]{2,1,0:T(2,128)(2,1)}, u32[]{:S(2)}, u32[]{:S(2)}) async-start(bf16[64,2,128]{2,1,0:T(2,128)(2,1)} %reshape.20), calls=%async_computation | async-start | bytes 65536 | tf_op jit(solution)/shard_map/all_to_all | solution.py:435
  46.3 42.0 %collective-permute-start.7 = (bf16[96,768]{1,0:T(8,128)(2,1)}, bf16[96,768]{1,0:T(8,128)(2,1)}, u32[]{:S(2)}, u32[]{:S(2)}) collective-permute-start(bf16[96,768]{1,0:T(8,128)(2,1)} %pad_maximum_fusion.1), channel_id=1, source_target_pairs={{0,2},{2,4},{4,6},{6,8},{8,10},{10,12},{12,14},{14,16},{16,18},{18... | collective-permute-start | bytes 442376 | tf_op jit(solution)/shard_map/ppermute | solution.py:447
  50.3 38.9 %collective-permute-start.8 = (bf16[96,768]{1,0:T(8,128)(2,1)}, bf16[96,768]{1,0:T(8,128)(2,1)}, u32[]{:S(2)}, u32[]{:S(2)}) collective-permute-start(bf16[96,768]{1,0:T(8,128)(2,1)} %pad_maximum_fusion.2), channel_id=1, source_target_pairs={{2,0},{4,2},{6,4},{8,6},{10,8},{12,10},{14,12},{16,14},{18,16},{20... | collective-permute-start | bytes 442376 | tf_op jit(solution)/shard_map/ppermute | solution.py:448
  54.9 2.9 %copy-start.34 = (bf16[3,768,768]{2,1,0:T(8,128)(2,1)S(1)}, bf16[3,768,768]{2,1,0:T(8,128)(2,1)}, u32[]{:S(2)}) copy-start(bf16[3,768,768]{2,1,0:T(8,128)(2,1)} %param.11) | copy-start | bytes 10616836
  74.7 0.8 copy-start.14
  75.5 14.6 %copy-start.2 = (bf16[3,768,768]{2,1,0:T(8,128)(2,1)S(1)}, bf16[3,768,768]{2,1,0:T(8,128)(2,1)}, u32[]{:S(2)}) copy-start(bf16[3,768,768]{2,1,0:T(8,128)(2,1)} %get-tuple-element.36.weight.refs_3_) | copy-start | bytes 10616836
  75.6 14.6 %copy-start.8 = (bf16[512,768]{1,0:T(8,128)(2,1)S(1)}, bf16[512,768]{1,0:T(8,128)(2,1)}, u32[]{:S(2)}) copy-start(bf16[512,768]{1,0:T(8,128)(2,1)} %get-tuple-element.44.saved) | copy-start | bytes 2359300
  80.3 20.2 %collective-permute-start = (bf16[32,4096]{1,0:T(8,128)(2,1)S(1)}, bf16[32,4096]{1,0:T(8,128)(2,1)S(1)}, u32[]{:S(2)}, u32[]{:S(2)}) collective-permute-start(bf16[32,4096]{1,0:T(8,128)(2,1)S(1)} %get-tuple-element.38), channel_id=1, source_target_pairs={{0,2},{2,4},{4,6},{6,8},{8,10},{10,12},{12,14},{14,16},{16,18},{18... | collective-permute-start | bytes 786440 | tf_op jit(solution)/shard_map/ppermute | solution.py:441
  82.3 18.2 %collective-permute-start.1 = (bf16[32,4096]{1,0:T(8,128)(2,1)S(1)}, bf16[32,4096]{1,0:T(8,128)(2,1)S(1)}, u32[]{:S(2)}, u32[]{:S(2)}) collective-permute-start(bf16[32,4096]{1,0:T(8,128)(2,1)S(1)} %get-tuple-element.39), channel_id=1, source_target_pairs={{2,0},{4,2},{6,4},{8,6},{10,8},{12,10},{14,12},{16,14},{18,16},{20... | collective-permute-start | bytes 786440 | tf_op jit(solution)/shard_map/ppermute | solution.py:442
  89.2 5.0 %copy-start.10 = (bf16[48,768]{1,0:T(8,128)(2,1)}, bf16[48,768]{1,0:T(8,128)(2,1)S(1)}, u32[]{:S(2)}) copy-start(bf16[48,768]{1,0:T(8,128)(2,1)S(1)} %slice.100.low) | copy-start | bytes 221188
  90.1 4.1 %copy-start.12 = (bf16[48,768]{1,0:T(8,128)(2,1)}, bf16[48,768]{1,0:T(8,128)(2,1)S(1)}, u32[]{:S(2)}) copy-start(bf16[48,768]{1,0:T(8,128)(2,1)S(1)} %slice.101.high) | copy-start | bytes 221188
  94.2 1.2 copy-start.28
  95.4 30.7 %collective-permute-start.9 = (bf16[576,768]{1,0:T(8,128)(2,1)}, bf16[576,768]{1,0:T(8,128)(2,1)}, u32[]{:S(2)}, u32[]{:S(2)}) collective-permute-start(bf16[576,768]{1,0:T(8,128)(2,1)} %get-tuple-element.23), channel_id=1, source_target_pairs={{0,1},{1,0},{2,3},{3,2},{4,5},{5,4},{6,7},{7,6},{8,9},{9,8},{10,11... | collective-permute-start | bytes 2654216 | tf_op jit(solution)/shard_map/ppermute | solution.py:457
  103.0 2.3 %copy-start = (bf16[576,4096]{1,0:T(8,128)(2,1)S(1)}, bf16[576,4096]{1,0:T(8,128)(2,1)}, u32[]{:S(2)}) copy-start(bf16[576,4096]{1,0:T(8,128)(2,1)} %pad_maximum_fusion.spread) | copy-start | bytes 14155780
  105.3 1.3 copy-start.5
  106.6 11.2 %copy-start.1 = (bf16[3,768,768]{2,1,0:T(8,128)(2,1)S(1)}, bf16[3,768,768]{2,1,0:T(8,128)(2,1)}, u32[]{:S(2)}) copy-start(bf16[3,768,768]{2,1,0:T(8,128)(2,1)} %get-tuple-element.37.weight.refs_3_) | copy-start | bytes 10616836
  106.6 11.2 %copy-start.7 = (bf16[512,768]{1,0:T(8,128)(2,1)S(1)}, bf16[512,768]{1,0:T(8,128)(2,1)}, u32[]{:S(2)}) copy-start(bf16[512,768]{1,0:T(8,128)(2,1)} %get-tuple-element.45.saved) | copy-start | bytes 2359300
  106.6 11.2 %copy-start.15 = (bf16[32,768]{1,0:T(8,128)(2,1)S(1)}, bf16[32,768]{1,0:T(8,128)(2,1)}, u32[]{:S(2)}) copy-start(bf16[32,768]{1,0:T(8,128)(2,1)} %slice.102.low) | copy-start | bytes 147460
  106.6 11.2 %copy-start.16 = (bf16[32,768]{1,0:T(8,128)(2,1)S(1)}, bf16[32,768]{1,0:T(8,128)(2,1)}, u32[]{:S(2)}) copy-start(bf16[32,768]{1,0:T(8,128)(2,1)} %slice.103.high) | copy-start | bytes 147460
  115.4 1.2 copy-start.18
  116.6 4.6 %copy-start.20 = (f32[576,768]{1,0:T(8,128)}, f32[576,768]{1,0:T(8,128)S(1)}, u32[]{:S(2)}) copy-start(f32[576,768]{1,0:T(8,128)S(1)} %get-tuple-element.20.refs_0_) | copy-start | bytes 5308420
  116.6 24.1 %collective-permute-start.6 = (bf16[576,768]{1,0:T(8,128)(2,1)S(1)}, bf16[576,768]{1,0:T(8,128)(2,1)S(1)}, u32[]{:S(2)}, u32[]{:S(2)}) collective-permute-start(bf16[576,768]{1,0:T(8,128)(2,1)S(1)} %get-tuple-element.21), channel_id=1, source_target_pairs={{0,1},{1,0},{2,3},{3,2},{4,5},{5,4},{6,7},{7,6},{8,9},{9,8},{10,11... | collective-permute-start | bytes 2654216 | tf_op jit(solution)/shard_map/ppermute | solution.py:463
  117.8 7.3 %copy-start.9 = (bf16[512,768]{1,0:T(8,128)(2,1)S(1)}, bf16[512,768]{1,0:T(8,128)(2,1)}, u32[]{:S(2)}) copy-start(bf16[512,768]{1,0:T(8,128)(2,1)} %get-tuple-element.44.saved) | copy-start | bytes 2359300
  117.9 7.3 %copy-start.11 = (bf16[48,768]{1,0:T(8,128)(2,1)S(1)}, bf16[48,768]{1,0:T(8,128)(2,1)}, u32[]{:S(2)}) copy-start(bf16[48,768]{1,0:T(8,128)(2,1)} %copy-done.10) | copy-start | bytes 221188
  117.9 7.3 %copy-start.13 = (bf16[48,768]{1,0:T(8,128)(2,1)S(1)}, bf16[48,768]{1,0:T(8,128)(2,1)}, u32[]{:S(2)}) copy-start(bf16[48,768]{1,0:T(8,128)(2,1)} %copy-done.12) | copy-start | bytes 221188
  121.1 5.0 %copy-start.30 = (f32[544,768]{1,0:T(8,128)}, f32[544,768]{1,0:T(8,128)S(1)}, u32[]{:S(2)}) copy-start(f32[544,768]{1,0:T(8,128)S(1)} %get-tuple-element.27.own) | copy-start | bytes 5013508
  121.1 37.4 %collective-permute-start.11 = (bf16[544,768]{1,0:T(8,128)(2,1)S(1)}, bf16[544,768]{1,0:T(8,128)(2,1)S(1)}, u32[]{:S(2)}, u32[]{:S(2)}) collective-permute-start(bf16[544,768]{1,0:T(8,128)(2,1)S(1)} %get-tuple-element.28), channel_id=1, source_target_pairs={{0,1},{1,0},{2,3},{3,2},{4,5},{5,4},{6,7},{7,6},{8,9},{9,8},{10,11... | collective-permute-start | bytes 2506760 | tf_op jit(solution)/shard_map/ppermute | solution.py:457
  125.2 1.5 copy-start.29
  126.6 14.0 %copy-start.4 = (bf16[768,768]{1,0:T(8,128)(2,1)S(1)}, bf16[768,768]{1,0:T(8,128)(2,1)}, u32[]{:S(2)}) copy-start(bf16[768,768]{1,0:T(8,128)(2,1)} %get-tuple-element.42.refs_6_) | copy-start | bytes 3538948
  126.6 14.0 %copy-start.19 = (f32[576,768]{1,0:T(8,128)S(1)}, f32[576,768]{1,0:T(8,128)}, u32[]{:S(2)}) copy-start(f32[576,768]{1,0:T(8,128)} %copy-done.18) | copy-start | bytes 5308420
  140.7 1.5 copy-start.21
  142.1 8.3 %copy-start.6 = (bf16[512,768]{1,0:T(8,128)(2,1)S(1)}, bf16[512,768]{1,0:T(8,128)(2,1)}, u32[]{:S(2)}) copy-start(bf16[512,768]{1,0:T(8,128)(2,1)} %get-tuple-element.43.saved) | copy-start | bytes 2359300
  149.0 4.5 %copy-start.22 = (f32[544,768]{1,0:T(8,128)}, f32[544,768]{1,0:T(8,128)S(1)}, u32[]{:S(2)}) copy-start(f32[544,768]{1,0:T(8,128)S(1)} %get-tuple-element.29.refs_4_) | copy-start | bytes 5013508
  149.1 4.5 %copy-start.24 = (f32[544,768]{1,0:T(8,128)}, f32[544,768]{1,0:T(8,128)S(1)}, u32[]{:S(2)}) copy-start(f32[544,768]{1,0:T(8,128)S(1)} %get-tuple-element.25.refs_0_) | copy-start | bytes 5013508
  149.1 27.4 %collective-permute-start.10 = (bf16[544,768]{1,0:T(8,128)(2,1)S(1)}, bf16[544,768]{1,0:T(8,128)(2,1)S(1)}, u32[]{:S(2)}, u32[]{:S(2)}) collective-permute-start(bf16[544,768]{1,0:T(8,128)(2,1)S(1)} %get-tuple-element.26), channel_id=1, source_target_pairs={{0,1},{1,0},{2,3},{3,2},{4,5},{5,4},{6,7},{7,6},{8,9},{9,8},{10,11... | collective-permute-start | bytes 2506760 | tf_op jit(solution)/shard_map/ppermute | solution.py:463
  153.6 3.2 %copy-start.32 = (f32[528,768]{1,0:T(8,128)}, f32[528,768]{1,0:T(8,128)S(1)}, u32[]{:S(2)}) copy-start(f32[528,768]{1,0:T(8,128)S(1)} %get-tuple-element.32.own) | copy-start | bytes 4866052
  153.6 5.0 %copy-start.31 = (f32[544,768]{1,0:T(8,128)S(1)}, f32[544,768]{1,0:T(8,128)}, u32[]{:S(2)}) copy-start(f32[544,768]{1,0:T(8,128)} %copy-done.30) | copy-start | bytes 5013508
  153.6 40.2 %collective-permute-start.13 = (bf16[528,768]{1,0:T(8,128)(2,1)S(1)}, bf16[528,768]{1,0:T(8,128)(2,1)S(1)}, u32[]{:S(2)}, u32[]{:S(2)}) collective-permute-start(bf16[528,768]{1,0:T(8,128)(2,1)S(1)} %get-tuple-element.33), channel_id=1, source_target_pairs={{0,1},{1,0},{2,3},{3,2},{4,5},{5,4},{6,7},{7,6},{8,9},{9,8},{10,11... | collective-permute-start | bytes 2433032 | tf_op jit(solution)/shard_map/ppermute | solution.py:457
  158.6 17.9 %copy-start.3 = (bf16[768,768]{1,0:T(8,128)(2,1)S(1)}, bf16[768,768]{1,0:T(8,128)(2,1)}, u32[]{:S(2)}) copy-start(bf16[768,768]{1,0:T(8,128)(2,1)} %get-tuple-element.40.refs_6_) | copy-start | bytes 3538948
  158.6 17.9 %copy-start.23 = (f32[544,768]{1,0:T(8,128)S(1)}, f32[544,768]{1,0:T(8,128)}, u32[]{:S(2)}) copy-start(f32[544,768]{1,0:T(8,128)} %copy-done.22) | copy-start | bytes 5013508
  158.6 17.9 %copy-start.25 = (f32[544,768]{1,0:T(8,128)S(1)}, f32[544,768]{1,0:T(8,128)}, u32[]{:S(2)}) copy-start(f32[544,768]{1,0:T(8,128)} %copy-done.24) | copy-start | bytes 5013508
  183.2 2.2 copy-start.26
  183.2 10.6 %copy-start.33 = (f32[528,768]{1,0:T(8,128)S(1)}, f32[528,768]{1,0:T(8,128)}, u32[]{:S(2)}) copy-start(f32[528,768]{1,0:T(8,128)} %copy-done.32) | copy-start | bytes 4866052
  183.3 25.7 %collective-permute-start.12 = (bf16[528,768]{1,0:T(8,128)(2,1)S(1)}, bf16[528,768]{1,0:T(8,128)(2,1)S(1)}, u32[]{:S(2)}, u32[]{:S(2)}) collective-permute-start(bf16[528,768]{1,0:T(8,128)(2,1)S(1)} %get-tuple-element.31), channel_id=1, source_target_pairs={{0,1},{1,0},{2,3},{3,2},{4,5},{5,4},{6,7},{7,6},{8,9},{9,8},{10,11... | collective-permute-start | bytes 2433032 | tf_op jit(solution)/shard_map/ppermute | solution.py:463
  193.9 15.1 %copy-start.27 = (f32[528,768]{1,0:T(8,128)S(1)}, f32[528,768]{1,0:T(8,128)}, u32[]{:S(2)}) copy-start(f32[528,768]{1,0:T(8,128)} %copy-done.26) | copy-start | bytes 4866052
Sparse Core Ops, SparseCore 0:
  35.1 40.0 all-gather.1

commit v2 on v1

--- a/solution.py
+++ b/solution.py
@@ -14,6 +14,8 @@
 GROUP_AXES = ("pos", "head")
 HALO_IN = {2: 32, 1: 16, 0: 8, -1: 0}
 HALO_SAVED = {2: 48, 1: 32, 0: 16}
+EDGE_START = {1: 0, 0: 32, 2: 48}
+EDGE_ORDER = (1, 0, 2)
 F32 = jnp.float32
 BF16 = jnp.bfloat16
 NT = (((1,), (1,)), ((), ()))
@@ -69,7 +71,7 @@
     )(place, head_weight, head_weight, batch_of[:, None], erase_left, erase_right)
 
 
-def bucket_kernel(rows, cover, bins, grads, out):
+def bucket_kernel(rows, cover, place_of, bins, grads, out):
     chunks, lanes = bins.shape
     members = out.shape[0]
     before = (
@@ -77,9 +79,10 @@
         < lax.broadcasted_iota(jnp.int32, (lanes, lanes), 1)
     ).astype(F32).astype(BF16)
     index = lax.broadcasted_iota(jnp.int32, (members, lanes), 0)
+    slot = lax.broadcasted_iota(jnp.int32, (COLS, lanes), 0) - place_of[0] * SLOTS
     lane = lax.broadcasted_iota(jnp.int32, (1, lanes), 1)
     base = jnp.zeros((members, 1), F32)
-    total = jnp.zeros((members, 4 * SLOTS), F32)
+    total = jnp.zeros(out.shape, F32)
     for chunk in range(chunks):
         place = bins[chunk : chunk + 1, :]
         target = place // rows
@@ -94,31 +97,51 @@
         low = (offset - high * 256).astype(F32)
         code = (expert + high * SLOTS).astype(F32)
         value = grads[chunk : chunk + 1, :].astype(F32)
-        hit = rank == index
+        hit = rank == slot
         spread = jnp.concatenate(
-            [jnp.where(hit, v, 0.0) for v in (low, code, value)] + [jnp.zeros_like(mine)], axis=0
+            [jnp.where(hit, v, 0.0) for v in (low, code, value)], axis=0
         ).astype(BF16)
         total = total + lax.dot_general(mine_low, spread, NT, preferred_element_type=F32)
     out[...] = total.astype(BF16)
 
 
-def bucket(cover_bins, bin_gradient, members, rows):
+def bucket(place, cover_bins, bin_gradient, members, rows):
     cover = cover_bins.shape[1]
     entries = cover_bins.size
     return pl.pallas_call(
         functools.partial(bucket_kernel, rows, cover),
-        out_shape=jax.ShapeDtypeStruct((members, 4 * SLOTS), BF16),
+        in_specs=[
+            pl.BlockSpec(memory_space=pltpu.SMEM),
+            pl.BlockSpec(memory_space=pltpu.VMEM),
+            pl.BlockSpec(memory_space=pltpu.VMEM),
+        ],
+        out_shape=jax.ShapeDtypeStruct((members, 3 * COLS), BF16),
         cost_estimate=cost(1e8, 1e5),
         compiler_params=params(),
         name="bucket_entries",
-    )(cover_bins.reshape(entries // 128, 128), bin_gradient.reshape(entries // 128, 128))
-
-
-def spread_kernel(groups, fields, out):
+    )(place, cover_bins.reshape(entries // 128, 128), bin_gradient.reshape(entries // 128, 128))
+
+
+def spread_kernel(arrived, out, fields):
     group = pl.program_id(0)
-    low = fields[pl.ds(group, 1), :]
-    code = fields[pl.ds(groups + group, 1), :]
-    value = fields[pl.ds(2 * groups + group, 1), :]
+    together = COLS // SLOTS
+
+    @pl.when(group == 0)
+    def _():
+        members = arrived.shape[0]
+        shape = (members // together, members)
+        same = (
+            lax.broadcasted_iota(jnp.int32, shape, 1) // together
+            == lax.broadcasted_iota(jnp.int32, shape, 0)
+        )
+        fields[...] = jnp.dot(
+            jnp.where(same, 1.0, 0.0).astype(BF16), arrived[...], preferred_element_type=F32
+        )
+
+    row = fields[pl.ds(group, 1), :]
+    low = row[:, :COLS]
+    code = row[:, COLS : 2 * COLS]
+    value = row[:, 2 * COLS :]
     high = code >= SLOTS
     offset = (low + jnp.where(high, 256.0, 0.0)).astype(jnp.int32)
     slot = lax.broadcasted_iota(jnp.int32, code.shape, 1)
@@ -134,19 +157,20 @@
     out[...] = lax.dot_general(at_row, at_column, NT, preferred_element_type=F32).astype(BF16)
 
 
-def spread_entries(fields, rows):
-    groups = fields.shape[0] // 4
-    width = fields.shape[1]
-    return pl.pallas_call(
-        functools.partial(spread_kernel, groups),
+def spread_entries(arrived, rows):
+    groups = arrived.shape[0] * SLOTS // COLS
+    width = COLS
+    return pl.pallas_call(
+        spread_kernel,
         grid=(groups,),
-        in_specs=[pl.BlockSpec(fields.shape, lambda i: (0, 0))],
+        in_specs=[pl.BlockSpec(arrived.shape, lambda i: (0, 0))],
+        scratch_shapes=[pltpu.VMEM((groups, arrived.shape[1]), F32)],
         out_specs=pl.BlockSpec((rows, width), lambda i: (0, i)),
         out_shape=jax.ShapeDtypeStruct((rows, groups * width), BF16),
         cost_estimate=cost(6e9, 8e6),
         compiler_params=params(),
         name="spread_entries",
-    )(fields)
+    )(arrived)
 
 
 def pre_kernel(level, rows, saved, low, high, weight, own, send, slope, act):
@@ -184,12 +208,58 @@
     out[...] = slope
 
 
+def saved_specs(level, saved, columns=None):
+    rows, share = saved.shape[1:]
+    halo = HALO_SAVED[level]
+    at = EDGE_START[level] // halo
+    width = columns or share
+    col = (lambda i: i) if columns else (lambda i: 0)
+    return [
+        pl.BlockSpec((None, rows, width), lambda i: (level, 0, col(i))),
+        pl.BlockSpec((halo, width), lambda i: (at, col(i))),
+        pl.BlockSpec((halo, width), lambda i: (at, col(i))),
+    ]
+
+
+def cut_edges(saved):
+    levels, rows, share = saved.shape
+    count = sum(HALO_SAVED.values())
+
+    def body(*refs):
+        first, last = refs[-2:]
+        for k, level in enumerate(EDGE_ORDER):
+            start, size = EDGE_START[level], HALO_SAVED[level]
+            first[start : start + size, :] = refs[2 * k][...]
+            last[start : start + size, :] = refs[2 * k + 1][...]
+
+    specs = []
+    for level in EDGE_ORDER:
+        size = HALO_SAVED[level]
+        for start in (0, rows - size):
+            specs.append(
+                pl.BlockSpec(
+                    (None, pl.Element(size), pl.Element(share)),
+                    lambda i, level=level, start=start: (level, start, 0),
+                )
+            )
+    whole = pl.BlockSpec((count, share), lambda i: (0, 0))
+    return pl.pallas_call(
+        body,
+        grid=(1,),
+        in_specs=specs,
+        out_specs=[whole, whole],
+        out_shape=[jax.ShapeDtypeStruct((count, share), BF16)] * 2,
+        cost_estimate=cost(1e6, 6e5),
+        compiler_params=params(),
+        name="cut_edges",
+    )(*[saved] * len(specs))
+
+
 def pre_partial(level, saved, low, high, weights):
-    rows, share = saved.shape
+    rows, share = saved.shape[1:]
     count = rows + 2 * HALO_IN[level]
     halo = HALO_SAVED[level]
-    taps, _, width = weights.shape
-    fixed = lambda i: (0, 0)
+    _, taps, _, width = weights.shape
     blocks = pl.BlockSpec((count, COLS), lambda i: (0, i))
 
     def body(saved, low, high, weight, own, send, act):
@@ -198,12 +268,8 @@
     return pl.pallas_call(
         body,
         grid=(width // COLS,),
-        in_specs=[
-            pl.BlockSpec((rows, share), fixed),
-            pl.BlockSpec((halo, share), fixed),
-            pl.BlockSpec((halo, share), fixed),
-            pl.BlockSpec((taps, share, COLS), lambda i: (0, 0, i)),
-        ],
+        in_specs=saved_specs(level, saved)
+        + [pl.BlockSpec((None, taps, share, COLS), lambda i: (level, 0, 0, i))],
         out_specs=[blocks, blocks],
         out_shape=[
             jax.ShapeDtypeStruct((count, width), F32),
@@ -236,7 +302,7 @@
 
 
 def saved_slope(level, saved, low, high):
-    rows, share = saved.shape
+    rows, share = saved.shape[1:]
     halo = HALO_SAVED[level]
     inner = HALO_IN[level - 1]
 
@@ -247,16 +313,11 @@
             out[inner + rows :, :] = slope(high[...])[:inner]
         out[inner : inner + rows, :] = slope(saved[...])
 
-    fixed = lambda i: (0, i)
     return pl.pallas_call(
         body,
         grid=(share // COLS,),
-        in_specs=[
-            pl.BlockSpec((rows, COLS), fixed),
-            pl.BlockSpec((halo, COLS), fixed),
-            pl.BlockSpec((halo, COLS), fixed),
-        ],
-        out_specs=pl.BlockSpec((rows + 2 * inner, COLS), fixed),
+        in_specs=saved_specs(level, saved, COLS),
+        out_specs=pl.BlockSpec((rows + 2 * inner, COLS), lambda i: (0, i)),
         out_shape=jax.ShapeDtypeStruct((rows + 2 * inner, share), F32),
         cost_estimate=cost(4e9, 3e6, 1e6),
         compiler_params=params(),
@@ -290,7 +351,7 @@
 def top_gradient(spread, vectors, expand):
     count, depth = spread.shape
     share = vectors.shape[1]
-    width = expand.shape[0]
+    levels, width, _ = expand.shape
     fixed = lambda i: (0, 0)
     blocks = lambda i: (0, i)
     return pl.pallas_call(
@@ -299,7 +360,7 @@
         in_specs=[
             pl.BlockSpec((count, depth), fixed),
             pl.BlockSpec((depth, COLS), blocks),
-            pl.BlockSpec((width, COLS), blocks),
+            pl.BlockSpec((None, width, COLS), lambda i: (levels - 1, 0, i)),
         ],
         out_specs=[
             pl.BlockSpec((count, COLS), blocks),
@@ -351,7 +412,7 @@
 def block_step(level, own, other, slope, weight, grad, outer, expand):
     count_in, width = own.shape
     count = outer.shape[0]
-    taps, share, _ = weight.shape
+    _, taps, share, _ = weight.shape
     fixed = lambda i: (0, 0)
     blocks = lambda i: (0, i)
     last = level == 0
@@ -359,7 +420,7 @@
         pl.BlockSpec((count_in, width), fixed),
         pl.BlockSpec((count_in, width), fixed),
         pl.BlockSpec((count_in, width), fixed),
-        pl.BlockSpec((taps, COLS, width), lambda i: (0, i, 0)),
+        pl.BlockSpec((None, taps, COLS, width), lambda i: (level, 0, i, 0)),
         pl.BlockSpec((count_in, COLS), blocks),
         pl.BlockSpec((count, COLS), blocks),
     ]
@@ -368,7 +429,7 @@
     out_shape = [jax.ShapeDtypeStruct((count, share), BF16 if last else F32)]
     scratch = [pltpu.VMEM((count_in, width), F32), pltpu.VMEM((taps, count, width), BF16)]
     if not last:
-        in_specs.append(pl.BlockSpec((width, COLS), blocks))
+        in_specs.append(pl.BlockSpec((None, width, COLS), lambda i: (level - 1, 0, i)))
         args.append(expand)
         out_specs += [pl.BlockSpec((count, width), fixed)] * 2
         out_shape += [
@@ -389,15 +450,21 @@
     )(*args)
 
 
-def gather_vectors(vectors):
+def after(value, *earlier):
+    return lax.optimization_barrier((value, *earlier))[0]
+
+
+def gather_vectors(vectors, meanwhile, later):
     count = vectors.shape[0]
     place = lax.axis_index("head")
     along, turn = place // 4, place % 4
     same = lambda steps: [(a * 4 + z, a * 4 + (z - steps) % 4) for a in range(2) for z in range(4)]
-    parts = [vectors] + [lax.ppermute(vectors, "head", same(k)) for k in (1, 2, 3)]
+    parts = [lax.ppermute(vectors, "head", same(k)) for k in (1, 2, 3)]
+    parts = [after(vectors, *meanwhile)] + parts
     twice = jnp.concatenate(parts + parts, axis=0)
     ring = lax.dynamic_slice_in_dim(twice, (4 - turn) % 4 * count, 4 * count, 0)
     other = lax.ppermute(ring, "head", [(k, (k + 4) % 8) for k in range(8)])
+    ring = after(ring, *later)
     both = jnp.where(
         along == 0,
         jnp.concatenate([ring, other], axis=0),
@@ -429,41 +496,34 @@
     vectors = head_vectors(
         chan_place[None].astype(jnp.int32), head_weight, batch_of, erase_left, erase_right, share
     )
-    gathered = gather_vectors(vectors)
-
-    payload = bucket(cover_bins, bin_gradient, members, rows)
+    first, final = cut_edges(inputs_saved)
+    low = lax.ppermute(final, GROUP_AXES, up)
+    high = lax.ppermute(first, GROUP_AXES, down)
+    flags = jnp.stack([member == 0, member == members - 1]).astype(jnp.int32)
+    sends, owns, others = {}, {}, {}
+    for n in levels:
+        owns[n], sends[n] = pre_partial(n, inputs_saved, low, high, conv_weight)
+        others[n] = lax.ppermute(sends[n], "chan", swap)
+
+    payload = bucket(
+        (member % (COLS // SLOTS))[None].astype(jnp.int32), cover_bins, bin_gradient, members, rows
+    )
     arrived = lax.all_to_all(payload, GROUP_AXES, split_axis=0, concat_axis=0, tiled=True)
-    fields = (
-        arrived.reshape(members, 4, SLOTS).transpose(1, 0, 2).reshape(-1, COLS).astype(F32)
-    )
-    spread = spread_entries(fields, rows)
+    gathered = gather_vectors(vectors, (payload, low, high), (sends[levels[0]],))
+    spread = spread_entries(after(arrived, *sends.values()), rows)
     reach = HALO_IN[layers - 1]
     spread_low = lax.ppermute(spread[rows - reach :], GROUP_AXES, up)
     spread_high = lax.ppermute(spread[:reach], GROUP_AXES, down)
     spread = jnp.concatenate([spread_low, spread, spread_high], axis=0)
-
-    edge_low = jnp.concatenate([inputs_saved[n, rows - HALO_SAVED[n] :] for n in levels], axis=0)
-    edge_high = jnp.concatenate([inputs_saved[n, : HALO_SAVED[n]] for n in levels], axis=0)
-    edge_low = lax.ppermute(edge_low, GROUP_AXES, up)
-    edge_high = lax.ppermute(edge_high, GROUP_AXES, down)
-    flags = jnp.stack([member == 0, member == members - 1]).astype(jnp.int32)
-    start = 0
-    slopes, outers = {}, {}
-    for n in levels:
-        size = HALO_SAVED[n]
-        low, high = edge_low[start : start + size], edge_high[start : start + size]
-        start += size
-        own, send = pre_partial(n, inputs_saved[n], low, high, conv_weight[n])
-        other = lax.ppermute(send, "chan", swap)
-        slopes[n] = pre_slope(n, flags, own, other, rows)
-        outers[n] = saved_slope(n, inputs_saved[n], low, high)
-
-    grad, own, send = top_gradient(spread, gathered, expand_weight[layers - 1])
+    slopes = {n: pre_slope(n, flags, owns[n], others[n], rows) for n in levels}
+    outers = {n: saved_slope(n, inputs_saved, low, high) for n in levels}
+    spread = after(spread, others[levels[1]], slopes[levels[0]], *outers.values())
+
+    grad, own, send = top_gradient(spread, gathered, expand_weight)
     for n in levels:
         other = lax.ppermute(send, "chan", swap)
         outs = block_step(
-            n, own, other, slopes[n], conv_weight[n], grad, outers[n],
-            expand_weight[n - 1] if n else None,
+            n, own, other, slopes[n], conv_weight, grad, outers[n], expand_weight
         )
         if n:
             grad, own, send = outs

time: 223 us -> 220 us (0.987)
  local copies, waits for them, and re-layouts: 38.8 us -> 17.9 us
  waiting for transfers between devices: 67 us -> 84 us
  Pallas kernels: 53.8 us -> 59.1 us
    ppermute x1, waiting for transfers between devices: 0.01 us -> 13.4 us  [per_device(): spread_low = lax.ppermute(spread[rows - reach:], GROUP_AXES, up)]
    squeeze x6 -> x0, local copies, waits for them, and re-layouts: 10.5 us -> none  [the longest x2 8.6 us: per_device(): own, send = pre_partial(n, inputs_saved[n], low, high, conv_weight[n])]
    ppermute x6 -> x3, starting transfers between devices: 11.1 us -> 0.97 us  [per_device(): other = lax.ppermute(send, 'chan', swap)]
    ppermute x1, waiting for transfers between devices: 10.2 us -> 1.33 us  [gather_vectors(): other = lax.ppermute(ring, 'head', [(k, (k + 4) % 8) for k in range(8)])]
    all_to_all x1, waiting for transfers between devices: 0.01 us -> 7.27 us  [per_device(): lax.all_to_all(payload, GROUP_AXES, split_axis=0, concat_axis=0, tiled=True)]
    slice x6 -> x0, local copies, waits for them, and re-layouts: 6.12 us -> none  [per_device(): low, high = (edge_low[start:start + size], edge_high[start:start + size])]
    ppermute x5 -> x8, starting transfers between devices: 13.3 us -> 19.3 us  [the longest x3 6.78 us: per_device(): others[n] = lax.ppermute(sends[n], 'chan', swap)]
    pallas_call x8 -> x9, Pallas kernels: 19.7 us -> 25 us  [the longest x3 14.1 us: pre_partial(): pl.pallas_call(body, grid=(width // COLS,), in_specs=saved_specs(level, s...]
  transfers between devices with their start and end apart: 16 -> 16, of which waited for: 9 -> 7; matrix products, arithmetic and copies ran while one was open for 14% -> 3% of each run, Pallas kernels for 22% -> 17%
where the time goes in v2:
time: 220 us; the launch traced here: 219 us
  waiting for transfers between devices  84 us (38%)
  Pallas kernels  59.1 us (27%)
  starting transfers between devices  38.9 us (18%)
  local copies, waits for them, and re-layouts  17.9 us (8%)
  between operations  13.9 us (6%)
  other arithmetic  5.65 us (3%)
    ppermute x3, waiting for transfers between devices, per_device(): other = lax.ppermute(send, 'chan', swap)  52 us
    pallas_call x3, Pallas kernels, block_step(): pl.pallas_call(lambda *refs: block_kernel(level, refs), grid=(share // CO...  19.8 us
    unnamed x84, local copies, waits for them, and re-layouts  16.2 us
    pallas_call x3, Pallas kernels, pre_partial(): pl.pallas_call(body, grid=(width // COLS,), in_specs=saved_specs(level, s...  14.1 us
    ppermute x1, waiting for transfers between devices, per_device(): spread_low = lax.ppermute(spread[rows - reach:], GROUP_AXES, up)  13.4 us
    ppermute x3, waiting for transfers between devices, per_device(): others[n] = lax.ppermute(sends[n], 'chan', swap)  9.99 us
    all_to_all x1, starting transfers between devices, per_device(): lax.all_to_all(payload, GROUP_AXES, split_axis=0, concat_axis=0, tiled=True)  9.5 us
    pallas_call x1, Pallas kernels, top_gradient(): pl.pallas_call(top_kernel, grid=(share // COLS,), in_specs=[pl.BlockSpec(...  8.71 us
  transfers between devices with their start and end apart: 16, of which 7 were waited for; matrix products, arithmetic and copies ran while one was open for 3% of the time, Pallas kernels for 17%

profile of v2, /device:TPU:8, one launch (start us, length us, event | category | flops | bytes accessed | tf_op | source)
XLA Modules:
  0.0 219.5 jit_solution(13109530277355448041)
XLA Ops:
  6.5 1.7 copy-done
  8.2 4.0 %collective-permute-start = (bf16[96,768]{1,0:T(8,128)(2,1)S(1)}, bf16[96,768]{1,0:T(8,128)(2,1)S(1)}, u32[]{:S(2)}, u32[]{:S(2)}) collective-permute-start(bf16[96,768]{1,0:T(8,128)(2,1)S(1)} %get-tuple-element.26), channel_id=1, source_target_pairs={{0,2},{2,4},{4,6},{6,8},{8,10},{10,12},{12,14},{14,16},{16,18},{18... | collective-permute-start | bytes 442376 | tf_op jit(solution)/shard_map/ppermute | solution.py:500
  12.2 4.1 %collective-permute-start.1 = (bf16[96,768]{1,0:T(8,128)(2,1)S(1)}, bf16[96,768]{1,0:T(8,128)(2,1)S(1)}, u32[]{:S(2)}, u32[]{:S(2)}) collective-permute-start(bf16[96,768]{1,0:T(8,128)(2,1)S(1)} %get-tuple-element.27), channel_id=1, source_target_pairs={{2,0},{4,2},{6,4},{8,6},{10,8},{12,10},{14,12},{16,14},{18,16},{20... | collective-permute-start | bytes 442376 | tf_op jit(solution)/shard_map/ppermute | solution.py:501
  16.4 0.1 copy.29.batch
  16.5 0.2 copy.30.left
  16.7 0.2 copy.31.right
  17.0 0.7 head_vectors.1
  17.7 0.1 collective-permute-start.8
  17.8 3.4 %collective-permute-start.7 = (bf16[64,768]{1,0:T(8,128)(2,1)S(1)}, bf16[64,768]{1,0:T(8,128)(2,1)S(1)}, u32[]{:S(2)}, u32[]{:S(2)}) collective-permute-start(bf16[64,768]{1,0:T(8,128)(2,1)S(1)} %head_vectors.1), channel_id=1, source_target_pairs={{0,4},{2,6},{4,0},{6,2},{8,12},{10,14},{12,8},{14,10},{1,5},{3,7},... | collective-permute-start | bytes 294920 | tf_op jit(solution)/shard_map/ppermute | solution.py:462
  21.1 1.0 collective-permute-start.6
  22.1 0.1 copy.27
  22.2 0.1 reshape.9.grads
  22.3 0.1 copy.26
  22.4 0.1 reshape.8.bins
  22.5 3.3 %bucket_entries.1 = bf16[64,768]{1,0:T(8,128)(2,1)S(1)} custom-call(s32[1]{0:T(128)} %bitcast.place_of, s32[16,128]{1,0:T(8,128)S(1)} %reshape.8.bins, bf16[16,128]{1,0:T(8,128)(2,1)S(1)} %reshape.9.grads), custom_call_target="tpu_custom_call" | custom-call | flops 100000000 | bytes 100000 | tf_op jit(solution)/shard_map/bucket_entries/pallas_call | solution.py:111
  26.0 0.8 constant_dynamic-slice_fusion
  26.8 1.0 collective-permute-start.9
  27.8 0.9 copy-done.18
  28.7 0.9 copy-done.21
  29.6 4.7 %pre_partial_2.1 = (f32[576,768]{1,0:T(8,128)S(1)}, bf16[576,768]{1,0:T(8,128)(2,1)S(1)}) custom-call(bf16[3,512,768]{2,1,0:T(8,128)(2,1)S(1)} %copy-done.1, bf16[96,768]{1,0:T(8,128)(2,1)S(1)} %copy-done.18, bf16[96,768]{1,0:T(8,128)(2,1)S(1)} %copy-done.21, bf16[3,3,768,768]{3,2,1,0:T(8,128)(2,1)} %refs_3_.7), custom_call_target="tpu_custom_call" | custom-call | flops 4000000000 | bytes 8000000 | tf_op jit(solution)/shard_map/pre_partial_2/pallas_call | solution.py:268
  34.3 1.3 copy-done.24
  35.6 1.3 collective-permute-done.9
  36.9 2.4 %maximum_select_fusion = bf16[512,768]{1,0:T(8,128)(2,1)} fusion(bf16[256,768]{1,0:T(8,128)(2,1)} %collective-permute-done.9, bf16[256,768]{1,0:T(8,128)(2,1)} %constant_dynamic-slice_fusion, pred[]{:T(512)S(6)} %eq.15), kind=kLoop, calls=%fused_computation.1 | loop fusion | flops 3538944 | bytes 1572865 | tf_op jit(solution)/shard_map/jit(_where)/select_n | solution.py:468
  39.4 0.6 broadcast.4
  40.0 0.7 reduce
  40.7 0.7 reshape.10
  41.4 9.5 %all-to-all-start = ((bf16[64,2,384]{2,1,0:T(2,128)(2,1)}), bf16[64,2,384]{2,1,0:T(2,128)(2,1)S(1)}, u32[]{:S(2)}, u32[]{:S(2)}) async-start(bf16[64,2,384]{2,1,0:T(2,128)(2,1)} %reshape.10), calls=%async_computation | async-start | bytes 196608 | tf_op jit(solution)/shard_map/all_to_all | solution.py:511
  50.9 0.1 add_convert_fusion.flags
  50.9 7.3 %all-to-all-done = bf16[64,2,384]{2,1,0:T(2,128)(2,1)S(1)} async-done(((bf16[64,2,384]{2,1,0:T(2,128)(2,1)}), bf16[64,2,384]{2,1,0:T(2,128)(2,1)S(1)}, u32[]{:S(2)}, u32[]{:S(2)}) %all-to-all-start) | async-done | bytes 98336 | tf_op jit(solution)/shard_map/all_to_all | solution.py:511
  58.3 2.2 %collective-permute-start.5 = (bf16[576,768]{1,0:T(8,128)(2,1)S(1)}, bf16[576,768]{1,0:T(8,128)(2,1)S(1)}, u32[]{:S(2)}, u32[]{:S(2)}) collective-permute-start(bf16[576,768]{1,0:T(8,128)(2,1)S(1)} %get-tuple-element.28), channel_id=1, source_target_pairs={{0,1},{1,0},{2,3},{3,2},{4,5},{5,4},{6,7},{7,6},{8,9},{9,8},{10,11... | collective-permute-start | bytes 2654216 | tf_op jit(solution)/shard_map/ppermute | solution.py:506
  60.6 0.9 copy-done.19
  61.5 0.9 copy-done.22
  62.4 4.8 %pre_partial_1.1 = (f32[544,768]{1,0:T(8,128)S(1)}, bf16[544,768]{1,0:T(8,128)(2,1)S(1)}) custom-call(bf16[3,512,768]{2,1,0:T(8,128)(2,1)S(1)} %copy-done.1, bf16[96,768]{1,0:T(8,128)(2,1)S(1)} %copy-done.19, bf16[96,768]{1,0:T(8,128)(2,1)S(1)} %copy-done.22, bf16[3,3,768,768]{3,2,1,0:T(8,128)(2,1)} %refs_3_.7), custom_call_target="tpu_custom_call" | custom-call | flops 4000000000 | bytes 8000000 | tf_op jit(solution)/shard_map/pre_partial_1/pallas_call | solution.py:268
  67.2 1.2 copy-done.26
  68.3 1.3 collective-permute-start.4
  69.6 4.6 %pre_partial_0.1 = (f32[528,768]{1,0:T(8,128)S(1)}, bf16[528,768]{1,0:T(8,128)(2,1)S(1)}) custom-call(bf16[3,512,768]{2,1,0:T(8,128)(2,1)S(1)} %copy-done.1, bf16[96,768]{1,0:T(8,128)(2,1)S(1)} %copy-done.19, bf16[96,768]{1,0:T(8,128)(2,1)S(1)} %copy-done.23, bf16[3,3,768,768]{3,2,1,0:T(8,128)(2,1)} %refs_3_.7), custom_call_target="tpu_custom_call" | custom-call | flops 4000000000 | bytes 8000000 | tf_op jit(solution)/shard_map/pre_partial_0/pallas_call | solution.py:268
  74.3 5.0 %spread_entries.1 = bf16[512,4096]{1,0:T(8,128)(2,1)S(1)} custom-call(bf16[64,768]{1,0:T(8,128)(2,1)S(1)} %bitcast.10), custom_call_target="tpu_custom_call" | custom-call | flops 6000000000 | bytes 8000000 | tf_op jit(solution)/shard_map/spread_entries/pallas_call | solution.py:163
  79.3 2.6 %collective-permute-start.2 = (bf16[32,4096]{1,0:T(8,128)(2,1)S(1)}, bf16[32,4096]{1,0:T(8,128)(2,1)S(1)}, u32[]{:S(2)}, u32[]{:S(2)}) collective-permute-start(bf16[32,4096]{1,0:T(8,128)(2,1)S(1)} %get-tuple-element.47), channel_id=1, source_target_pairs={{0,2},{2,4},{4,6},{6,8},{8,10},{10,12},{12,14},{14,16},{16,18},{18... | collective-permute-start | bytes 786440 | tf_op jit(solution)/shard_map/ppermute | solution.py:515
  82.0 5.5 %collective-permute-start.3 = (bf16[32,4096]{1,0:T(8,128)(2,1)S(1)}, bf16[32,4096]{1,0:T(8,128)(2,1)S(1)}, u32[]{:S(2)}, u32[]{:S(2)}) collective-permute-start(bf16[32,4096]{1,0:T(8,128)(2,1)S(1)} %get-tuple-element.48), channel_id=1, source_target_pairs={{2,0},{4,2},{6,4},{8,6},{10,8},{12,10},{14,12},{16,14},{18,16},{20... | collective-permute-start | bytes 786440 | tf_op jit(solution)/shard_map/ppermute | solution.py:516
  87.5 0.8 saved_slope_0.1.refs_5_
  88.3 1.2 copy-done.10
  89.5 0.9 saved_slope_1.1.refs_5_
  90.4 1.2 copy-done.8
  91.6 0.9 saved_slope_2.1.refs_5_
  92.5 13.4 %collective-permute-done.2 = bf16[32,4096]{1,0:T(8,128)(2,1)S(1)} collective-permute-done((bf16[32,4096]{1,0:T(8,128)(2,1)S(1)}, bf16[32,4096]{1,0:T(8,128)(2,1)S(1)}, u32[]{:S(2)}, u32[]{:S(2)}) %collective-permute-start.2) | collective-permute-done | bytes 262176 | tf_op jit(solution)/shard_map/ppermute | solution.py:515
  105.9 2.5 %pad_maximum_fusion.spread = bf16[576,4096]{1,0:T(8,128)(2,1)} fusion(bf16[32,4096]{1,0:T(8,128)(2,1)S(1)} %collective-permute-done.3, bf16[512,4096]{1,0:T(8,128)(2,1)S(1)} %spread_entries.1, bf16[32,4096]{1,0:T(8,128)(2,1)S(1)} %collective-permute-done.2), kind=kLoop, calls=%fused_computation | loop fusion | flops 14155776 | bytes 9437184 | tf_op jit(solution)/shard_map/concatenate | solution.py:517
  108.4 1.7 pre_slope_2.1.refs_2_
  110.0 1.3 copy-done.4
  111.3 0.9 copy-done.12
  112.3 2.3 %copy-done.3 = bf16[576,4096]{1,0:T(8,128)(2,1)S(1)} copy-done((bf16[576,4096]{1,0:T(8,128)(2,1)S(1)}, bf16[576,4096]{1,0:T(8,128)(2,1)}, u32[]{:S(2)}) %copy-start.3) | copy-done | bytes 4718616
  114.6 8.7 %top_gradient.1 = (f32[576,768]{1,0:T(8,128)S(1)}, f32[576,768]{1,0:T(8,128)S(1)}, bf16[576,768]{1,0:T(8,128)(2,1)S(1)}) custom-call(bf16[576,4096]{1,0:T(8,128)(2,1)S(1)} %copy-done.3, bf16[4096,768]{1,0:T(8,128)(2,1)} %all-gather.2.cloned.1.call-done.vectors, bf16[3,768,768]{2,1,0:T(8,128)(2,1)S(1)} %copy-done.2), custom_call_target="tpu_custom_call" | custom-call | flops 5000000000 | bytes 14000000 | tf_op jit(solution)/shard_map/top_gradient/pallas_call | solution.py:357
  123.3 0.2 collective-permute-start.10
  123.6 21.6 %collective-permute-done.10.refs_1_ = bf16[576,768]{1,0:T(8,128)(2,1)S(1)} collective-permute-done((bf16[576,768]{1,0:T(8,128)(2,1)S(1)}, bf16[576,768]{1,0:T(8,128)(2,1)S(1)}, u32[]{:S(2)}, u32[]{:S(2)}) %collective-permute-start.10) | collective-permute-done | bytes 884768 | tf_op jit(solution)/shard_map/ppermute | solution.py:524
  145.2 7.0 %block_step_2.1 = (f32[544,768]{1,0:T(8,128)S(1)}, f32[544,768]{1,0:T(8,128)S(1)}, bf16[544,768]{1,0:T(8,128)(2,1)S(1)}) custom-call(f32[576,768]{1,0:T(8,128)S(1)} %get-tuple-element.36.refs_0_, bf16[576,768]{1,0:T(8,128)(2,1)S(1)} %collective-permute-done.10.refs_1_, f32[576,768]{1,0:T(8,128)S(1)} %copy-done.5, bf16[3,3,768,768]{3,2,1,0:T(8,128)(2,1)} %refs_3_.7, ...), custom_call_target="tpu_custom_call" | custom-call | flops 5000000000 | bytes 14000000 | tf_op jit(solution)/shard_map/block_step_2/pallas_call | solution.py:440
  152.2 0.4 collective-permute-start.11
  152.6 3.2 %collective-permute-start.13 = (bf16[528,768]{1,0:T(8,128)(2,1)S(1)}, bf16[528,768]{1,0:T(8,128)(2,1)S(1)}, u32[]{:S(2)}, u32[]{:S(2)}) collective-permute-start(bf16[528,768]{1,0:T(8,128)(2,1)S(1)} %copy-done.15), channel_id=1, source_target_pairs={{0,1},{1,0},{2,3},{3,2},{4,5},{5,4},{6,7},{7,6},{8,9},{9,8},{10,11... | collective-permute-start | bytes 2433032 | tf_op jit(solution)/shard_map/ppermute | solution.py:506
  155.9 1.6 pre_slope_1.1.refs_2_
  157.5 17.9 %collective-permute-done.11.refs_1_ = bf16[544,768]{1,0:T(8,128)(2,1)S(1)} collective-permute-done((bf16[544,768]{1,0:T(8,128)(2,1)S(1)}, bf16[544,768]{1,0:T(8,128)(2,1)S(1)}, u32[]{:S(2)}, u32[]{:S(2)}) %collective-permute-start.11) | collective-permute-done | bytes 835616 | tf_op jit(solution)/shard_map/ppermute | solution.py:524
  175.4 7.0 %block_step_1.1 = (f32[528,768]{1,0:T(8,128)S(1)}, f32[528,768]{1,0:T(8,128)S(1)}, bf16[528,768]{1,0:T(8,128)(2,1)S(1)}) custom-call(f32[544,768]{1,0:T(8,128)S(1)} %get-tuple-element.39.refs_0_, bf16[544,768]{1,0:T(8,128)(2,1)S(1)} %collective-permute-done.11.refs_1_, f32[544,768]{1,0:T(8,128)S(1)} %pre_slope_1.1.refs_2_, bf16[3,3,768,768]{3,2,1,0:T(8,128)(2,1)} %refs_3_.7, ...), custom_call_target="tpu_custom_call" | custom-call | flops 5000000000 | bytes 14000000 | tf_op jit(solution)/shard_map/block_step_1/pallas_call | solution.py:440
  182.4 0.4 collective-permute-start.12
  182.7 10.0 %collective-permute-done.13.other = bf16[528,768]{1,0:T(8,128)(2,1)S(1)} collective-permute-done((bf16[528,768]{1,0:T(8,128)(2,1)S(1)}, bf16[528,768]{1,0:T(8,128)(2,1)S(1)}, u32[]{:S(2)}, u32[]{:S(2)}) %collective-permute-start.13) | collective-permute-done | bytes 811040 | tf_op jit(solution)/shard_map/ppermute | solution.py:506
  192.7 1.6 pre_slope_0.1.refs_2_
  194.3 12.5 %collective-permute-done.12.refs_1_ = bf16[528,768]{1,0:T(8,128)(2,1)S(1)} collective-permute-done((bf16[528,768]{1,0:T(8,128)(2,1)S(1)}, bf16[528,768]{1,0:T(8,128)(2,1)S(1)}, u32[]{:S(2)}, u32[]{:S(2)}) %collective-permute-start.12) | collective-permute-done | bytes 811040 | tf_op jit(solution)/shard_map/ppermute | solution.py:524
  206.8 5.8 %block_step_0.1 = bf16[512,768]{1,0:T(8,128)(2,1)} custom-call(f32[528,768]{1,0:T(8,128)S(1)} %get-tuple-element.43.refs_0_, bf16[528,768]{1,0:T(8,128)(2,1)S(1)} %collective-permute-done.12.refs_1_, f32[528,768]{1,0:T(8,128)S(1)} %pre_slope_0.1.refs_2_, bf16[3,3,768,768]{3,2,1,0:T(8,128)(2,1)} %refs_3_.7, f32[528,768]{1,0:T(8,128)S(1)} %get-tuple-element.46.refs_4_, ...), custom_call_target="tpu_custom_call" | custom-call | flops 5000000000 | bytes 14000000 | tf_op jit(solution)/shard_map/block_step_0/pallas_call | solution.py:440
  (81 shorter events, 0.4 us)
Async XLA Ops:
  6.5 105.7 %all-gather.2.cloned.1.call-start = ((), (), s32[]{:S(2)}) async-start(), calls=%async_computation.1 | async-start | bytes 7077888 | tf_op jit(solution)/shard_map/all_gather | solution.py:473
  6.5 1.7 copy-start
  8.2 8.1 %copy-start.34 = (s32[64]{0:T(128)S(1)}, s32[64]{0:T(128)}, u32[]{:S(2)}) copy-start(s32[64]{0:T(128)} %param.13) | copy-start | bytes 772
  8.2 8.3 %copy-start.30 = (bf16[1536,64]{0,1:T(8,128)(2,1)S(1)}, bf16[1536,64]{0,1:T(8,128)(2,1)}, u32[]{:S(2)}) copy-start(bf16[1536,64]{0,1:T(8,128)(2,1)} %param.14) | copy-start | bytes 589828
  8.2 8.5 %copy-start.31 = (bf16[1536,64]{0,1:T(8,128)(2,1)S(1)}, bf16[1536,64]{0,1:T(8,128)(2,1)}, u32[]{:S(2)}) copy-start(bf16[1536,64]{0,1:T(8,128)(2,1)} %param.15) | copy-start | bytes 589828
  8.2 8.7 %copy-start.16 = (bf16[64,1536]{1,0:T(8,128)(2,1)S(1)}, bf16[64,1536]{1,0:T(8,128)(2,1)}, u32[]{:S(2)}) copy-start(bf16[64,1536]{1,0:T(8,128)(2,1)} %share.1) | copy-start | bytes 589828
  8.2 17.5 %collective-permute-start = (bf16[96,768]{1,0:T(8,128)(2,1)S(1)}, bf16[96,768]{1,0:T(8,128)(2,1)S(1)}, u32[]{:S(2)}, u32[]{:S(2)}) collective-permute-start(bf16[96,768]{1,0:T(8,128)(2,1)S(1)} %get-tuple-element.26), channel_id=1, source_target_pairs={{0,2},{2,4},{4,6},{6,8},{8,10},{10,12},{12,14},{14,16},{16,18},{18... | collective-permute-start | bytes 442376 | tf_op jit(solution)/shard_map/ppermute | solution.py:500
  12.2 13.6 %collective-permute-start.1 = (bf16[96,768]{1,0:T(8,128)(2,1)S(1)}, bf16[96,768]{1,0:T(8,128)(2,1)S(1)}, u32[]{:S(2)}, u32[]{:S(2)}) collective-permute-start(bf16[96,768]{1,0:T(8,128)(2,1)S(1)} %get-tuple-element.27), channel_id=1, source_target_pairs={{2,0},{4,2},{6,4},{8,6},{10,8},{12,10},{14,12},{16,14},{18,16},{20... | collective-permute-start | bytes 442376 | tf_op jit(solution)/shard_map/ppermute | solution.py:501
  16.9 5.2 %copy-start.33 = (bf16[64,32]{0,1:T(8,128)(2,1)S(1)}, bf16[64,32]{0,1:T(8,128)(2,1)}, u32[]{:S(2)}) copy-start(bf16[64,32]{0,1:T(8,128)(2,1)} %param.16) | copy-start | bytes 12292
  16.9 5.4 %copy-start.32 = (s32[64,32]{0,1:T(8,128)S(1)}, s32[64,32]{0,1:T(8,128)}, u32[]{:S(2)}) copy-start(s32[64,32]{0,1:T(8,128)} %param.17) | copy-start | bytes 24580
  17.7 10.1 %copy-start.1 = (bf16[3,512,768]{2,1,0:T(8,128)(2,1)S(1)}, bf16[3,512,768]{2,1,0:T(8,128)(2,1)}, u32[]{:S(2)}) copy-start(bf16[3,512,768]{2,1,0:T(8,128)(2,1)} %saved.11) | copy-start | bytes 7077892
  17.7 8.2 %collective-permute-start.8 = (bf16[64,768]{1,0:T(8,128)(2,1)S(1)}, bf16[64,768]{1,0:T(8,128)(2,1)S(1)}, u32[]{:S(2)}, u32[]{:S(2)}) collective-permute-start(bf16[64,768]{1,0:T(8,128)(2,1)S(1)} %head_vectors.1), channel_id=1, source_target_pairs={{0,2},{2,4},{4,6},{6,0},{8,10},{10,12},{12,14},{14,8},{1,3},{3,5},... | collective-permute-start | bytes 294920 | tf_op jit(solution)/shard_map/ppermute | solution.py:462
  17.8 8.1 %collective-permute-start.7 = (bf16[64,768]{1,0:T(8,128)(2,1)S(1)}, bf16[64,768]{1,0:T(8,128)(2,1)S(1)}, u32[]{:S(2)}, u32[]{:S(2)}) collective-permute-start(bf16[64,768]{1,0:T(8,128)(2,1)S(1)} %head_vectors.1), channel_id=1, source_target_pairs={{0,4},{2,6},{4,0},{6,2},{8,12},{10,14},{12,8},{14,10},{1,5},{3,7},... | collective-permute-start | bytes 294920 | tf_op jit(solution)/shard_map/ppermute | solution.py:462
  21.1 4.7 %collective-permute-start.6 = (bf16[64,768]{1,0:T(8,128)(2,1)S(1)}, bf16[64,768]{1,0:T(8,128)(2,1)S(1)}, u32[]{:S(2)}, u32[]{:S(2)}) collective-permute-start(bf16[64,768]{1,0:T(8,128)(2,1)S(1)} %head_vectors.1), channel_id=1, source_target_pairs={{0,6},{2,0},{4,2},{6,4},{8,14},{10,8},{12,10},{14,12},{1,7},{3,1},... | collective-permute-start | bytes 294920 | tf_op jit(solution)/shard_map/ppermute | solution.py:462
  25.8 1.9 copy-start.17
  25.8 1.9 copy-start.20
  26.8 10.2 %collective-permute-start.9 = (bf16[256,768]{1,0:T(8,128)(2,1)}, bf16[256,768]{1,0:T(8,128)(2,1)}, u32[]{:S(2)}, u32[]{:S(2)}) collective-permute-start(bf16[256,768]{1,0:T(8,128)(2,1)} %constant_dynamic-slice_fusion), channel_id=1, source_target_pairs={{0,8},{2,10},{4,12},{6,14},{8,0},{10,2},{12,4},{14,6},{1,9},{3,11}... | collective-permute-start | bytes 1179656 | tf_op jit(solution)/shard_map/ppermute | solution.py:466
  27.7 0.9 copy-start.18
  28.7 0.9 copy-start.21
  34.3 1.3 copy-start.24
  41.4 16.9 %all-to-all-start = ((bf16[64,2,384]{2,1,0:T(2,128)(2,1)}), bf16[64,2,384]{2,1,0:T(2,128)(2,1)S(1)}, u32[]{:S(2)}, u32[]{:S(2)}) async-start(bf16[64,2,384]{2,1,0:T(2,128)(2,1)} %reshape.10), calls=%async_computation | async-start | bytes 196608 | tf_op jit(solution)/shard_map/all_to_all | solution.py:511
  58.3 50.0 %collective-permute-start.5 = (bf16[576,768]{1,0:T(8,128)(2,1)S(1)}, bf16[576,768]{1,0:T(8,128)(2,1)S(1)}, u32[]{:S(2)}, u32[]{:S(2)}) collective-permute-start(bf16[576,768]{1,0:T(8,128)(2,1)S(1)} %get-tuple-element.28), channel_id=1, source_target_pairs={{0,1},{1,0},{2,3},{3,2},{4,5},{5,4},{6,7},{7,6},{8,9},{9,8},{10,11... | collective-permute-start | bytes 2654216 | tf_op jit(solution)/shard_map/ppermute | solution.py:506
  60.6 0.9 copy-start.19
  61.5 0.9 copy-start.22
  62.4 7.2 %copy-start.23 = (bf16[96,768]{1,0:T(8,128)(2,1)S(1)}, bf16[96,768]{1,0:T(8,128)(2,1)}, u32[]{:S(2)}) copy-start(bf16[96,768]{1,0:T(8,128)(2,1)} %copy-done.20) | copy-start | bytes 442372
  67.2 1.2 copy-start.26
  68.3 43.0 %collective-permute-start.4 = (bf16[544,768]{1,0:T(8,128)(2,1)S(1)}, bf16[544,768]{1,0:T(8,128)(2,1)S(1)}, u32[]{:S(2)}, u32[]{:S(2)}) collective-permute-start(bf16[544,768]{1,0:T(8,128)(2,1)S(1)} %get-tuple-element.29), channel_id=1, source_target_pairs={{0,1},{1,0},{2,3},{3,2},{4,5},{5,4},{6,7},{7,6},{8,9},{9,8},{10,11... | collective-permute-start | bytes 2506760 | tf_op jit(solution)/shard_map/ppermute | solution.py:506
  74.3 5.0 %copy-start.14 = (bf16[528,768]{1,0:T(8,128)(2,1)}, bf16[528,768]{1,0:T(8,128)(2,1)S(1)}, u32[]{:S(2)}) copy-start(bf16[528,768]{1,0:T(8,128)(2,1)S(1)} %get-tuple-element.30) | copy-start | bytes 2433028
  74.3 5.0 %copy-start.28 = (f32[528,768]{1,0:T(8,128)}, f32[528,768]{1,0:T(8,128)S(1)}, u32[]{:S(2)}) copy-start(f32[528,768]{1,0:T(8,128)S(1)} %get-tuple-element.45.own) | copy-start | bytes 4866052
  79.3 26.5 %collective-permute-start.2 = (bf16[32,4096]{1,0:T(8,128)(2,1)S(1)}, bf16[32,4096]{1,0:T(8,128)(2,1)S(1)}, u32[]{:S(2)}, u32[]{:S(2)}) collective-permute-start(bf16[32,4096]{1,0:T(8,128)(2,1)S(1)} %get-tuple-element.47), channel_id=1, source_target_pairs={{0,2},{2,4},{4,6},{6,8},{8,10},{10,12},{12,14},{14,16},{16,18},{18... | collective-permute-start | bytes 786440 | tf_op jit(solution)/shard_map/ppermute | solution.py:515
  82.0 23.9 %collective-permute-start.3 = (bf16[32,4096]{1,0:T(8,128)(2,1)S(1)}, bf16[32,4096]{1,0:T(8,128)(2,1)S(1)}, u32[]{:S(2)}, u32[]{:S(2)}) collective-permute-start(bf16[32,4096]{1,0:T(8,128)(2,1)S(1)} %get-tuple-element.48), channel_id=1, source_target_pairs={{2,0},{4,2},{6,4},{8,6},{10,8},{12,10},{14,12},{16,14},{18,16},{20... | collective-permute-start | bytes 786440 | tf_op jit(solution)/shard_map/ppermute | solution.py:516
  88.3 1.2 copy-start.10
  90.4 1.2 copy-start.8
  92.5 15.9 %copy-start.6 = (f32[544,768]{1,0:T(8,128)}, f32[544,768]{1,0:T(8,128)S(1)}, u32[]{:S(2)}) copy-start(f32[544,768]{1,0:T(8,128)S(1)} %saved_slope_2.1.refs_5_) | copy-start | bytes 5013508
  92.5 15.9 %copy-start.25 = (f32[576,768]{1,0:T(8,128)S(1)}, f32[576,768]{1,0:T(8,128)}, u32[]{:S(2)}) copy-start(f32[576,768]{1,0:T(8,128)} %copy-done.24) | copy-start | bytes 5308420
  108.3 3.9 %copy-start.2 = (bf16[3,768,768]{2,1,0:T(8,128)(2,1)S(1)}, bf16[3,768,768]{2,1,0:T(8,128)(2,1)}, u32[]{:S(2)}) copy-start(bf16[3,768,768]{2,1,0:T(8,128)(2,1)} %refs_6_.3) | copy-start | bytes 10616836
  110.0 1.3 copy-start.4
  111.3 0.9 copy-start.12
  112.3 2.3 %copy-start.3 = (bf16[576,4096]{1,0:T(8,128)(2,1)S(1)}, bf16[576,4096]{1,0:T(8,128)(2,1)}, u32[]{:S(2)}) copy-start(bf16[576,4096]{1,0:T(8,128)(2,1)} %pad_maximum_fusion.spread) | copy-start | bytes 14155780
  114.6 30.5 %copy-start.5 = (f32[576,768]{1,0:T(8,128)S(1)}, f32[576,768]{1,0:T(8,128)}, u32[]{:S(2)}) copy-start(f32[576,768]{1,0:T(8,128)} %copy-done.4) | copy-start | bytes 5308420
  114.6 30.5 %copy-start.7 = (f32[544,768]{1,0:T(8,128)S(1)}, f32[544,768]{1,0:T(8,128)}, u32[]{:S(2)}) copy-start(f32[544,768]{1,0:T(8,128)} %copy-done.6) | copy-start | bytes 5013508
  123.3 21.8 %collective-permute-start.10 = (bf16[576,768]{1,0:T(8,128)(2,1)S(1)}, bf16[576,768]{1,0:T(8,128)(2,1)S(1)}, u32[]{:S(2)}, u32[]{:S(2)}) collective-permute-start(bf16[576,768]{1,0:T(8,128)(2,1)S(1)} %get-tuple-element.37), channel_id=1, source_target_pairs={{0,1},{1,0},{2,3},{3,2},{4,5},{5,4},{6,7},{7,6},{8,9},{9,8},{10,11... | collective-permute-start | bytes 2654216 | tf_op jit(solution)/shard_map/ppermute | solution.py:524
  145.2 7.4 %copy-start.15 = (bf16[528,768]{1,0:T(8,128)(2,1)S(1)}, bf16[528,768]{1,0:T(8,128)(2,1)}, u32[]{:S(2)}) copy-start(bf16[528,768]{1,0:T(8,128)(2,1)} %copy-done.14) | copy-start | bytes 2433028
  145.2 10.7 %copy-start.13 = (bf16[544,768]{1,0:T(8,128)(2,1)S(1)}, bf16[544,768]{1,0:T(8,128)(2,1)}, u32[]{:S(2)}) copy-start(bf16[544,768]{1,0:T(8,128)(2,1)} %copy-done.12) | copy-start | bytes 2506756
  145.2 10.7 %copy-start.27 = (f32[544,768]{1,0:T(8,128)S(1)}, f32[544,768]{1,0:T(8,128)}, u32[]{:S(2)}) copy-start(f32[544,768]{1,0:T(8,128)} %copy-done.26) | copy-start | bytes 5013508
  152.2 23.1 %collective-permute-start.11 = (bf16[544,768]{1,0:T(8,128)(2,1)S(1)}, bf16[544,768]{1,0:T(8,128)(2,1)S(1)}, u32[]{:S(2)}, u32[]{:S(2)}) collective-permute-start(bf16[544,768]{1,0:T(8,128)(2,1)S(1)} %get-tuple-element.40), channel_id=1, source_target_pairs={{0,1},{1,0},{2,3},{3,2},{4,5},{5,4},{6,7},{7,6},{8,9},{9,8},{10,11... | collective-permute-start | bytes 2506760 | tf_op jit(solution)/shard_map/ppermute | solution.py:524
  152.6 40.1 %collective-permute-start.13 = (bf16[528,768]{1,0:T(8,128)(2,1)S(1)}, bf16[528,768]{1,0:T(8,128)(2,1)S(1)}, u32[]{:S(2)}, u32[]{:S(2)}) collective-permute-start(bf16[528,768]{1,0:T(8,128)(2,1)S(1)} %copy-done.15), channel_id=1, source_target_pairs={{0,1},{1,0},{2,3},{3,2},{4,5},{5,4},{6,7},{7,6},{8,9},{9,8},{10,11... | collective-permute-start | bytes 2433032 | tf_op jit(solution)/shard_map/ppermute | solution.py:506
  155.9 19.5 %copy-start.9 = (f32[528,768]{1,0:T(8,128)S(1)}, f32[528,768]{1,0:T(8,128)}, u32[]{:S(2)}) copy-start(f32[528,768]{1,0:T(8,128)} %copy-done.8) | copy-start | bytes 4866052
  175.4 17.4 %copy-start.29 = (f32[528,768]{1,0:T(8,128)S(1)}, f32[528,768]{1,0:T(8,128)}, u32[]{:S(2)}) copy-start(f32[528,768]{1,0:T(8,128)} %copy-done.28) | copy-start | bytes 4866052
  182.4 24.5 %collective-permute-start.12 = (bf16[528,768]{1,0:T(8,128)(2,1)S(1)}, bf16[528,768]{1,0:T(8,128)(2,1)S(1)}, u32[]{:S(2)}, u32[]{:S(2)}) collective-permute-start(bf16[528,768]{1,0:T(8,128)(2,1)S(1)} %get-tuple-element.44), channel_id=1, source_target_pairs={{0,1},{1,0},{2,3},{3,2},{4,5},{5,4},{6,7},{7,6},{8,9},{9,8},{10,11... | collective-permute-start | bytes 2433032 | tf_op jit(solution)/shard_map/ppermute | solution.py:524
  192.7 14.1 %copy-start.11 = (f32[512,768]{1,0:T(8,128)S(1)}, f32[512,768]{1,0:T(8,128)}, u32[]{:S(2)}) copy-start(f32[512,768]{1,0:T(8,128)} %copy-done.10) | copy-start | bytes 4718596
Sparse Core Ops, SparseCore 0:
  39.5 43.4 all-gather.1

commit v3 on v2

v3 whole, which is shorter than its diff:
```python
import functools

import jax
import jax.numpy as jnp
from jax import lax
from jax.experimental import pallas as pl
from jax.experimental.pallas import tpu as pltpu
from jax.sharding import PartitionSpec as P

BASE_DILATION = 4
RANK = 8
SLOTS = 64
COLS = 256
GROUP_AXES = ("pos", "head")
HALO_IN = {2: 32, 1: 16, 0: 8, -1: 0}
HALO_SAVED = {2: 48, 1: 32, 0: 16}
EDGE_START = {1: 0, 0: 32, 2: 48}
F32 = jnp.float32
BF16 = jnp.bfloat16
NT = (((1,), (1,)), ((), ()))


def cost(flops, bytes_accessed, transcendentals=0):
    return pl.CostEstimate(
        flops=int(flops / 5), bytes_accessed=int(bytes_accessed / 5), transcendentals=0
    )


def params():
    return pltpu.CompilerParams(vmem_limit_bytes=28 * 2**20)


VMEM = pl.BlockSpec(memory_space=pltpu.VMEM)
HBM = pl.BlockSpec(memory_space=pltpu.HBM)
SMEM = pl.BlockSpec(memory_space=pltpu.SMEM)
ROOT_HALF = 0.7071067811865476
DENSITY = 0.3989422804014327


def in_hbm(value):
    return pltpu.with_memory_space_constraint(value, pltpu.HBM)


def fetch(pairs, sems):
    copies = [pltpu.make_async_copy(a, b, sems.at[k]) for k, (a, b) in enumerate(pairs)]
    for copy in copies:
        copy.start()
    return copies


def column_blocks(share):
    return [slice(start, start + COLS) for start in range(0, share, COLS)]


def gelu_parts(value):
    half = 0.5 * (1.0 + lax.erf(value * ROOT_HALF))
    return value * half, half + value * jnp.exp(-0.5 * value * value) * DENSITY


def vectors_kernel(place, weight, share, batch, left, right, out):
    projected = lax.dot_general(left[...], weight[...], NT, preferred_element_type=F32)
    column = lax.broadcasted_iota(jnp.int32, projected.shape, 0) // RANK
    kept = jnp.where(column == batch[...], projected, 0.0)
    removed = lax.dot_general(
        kept, right[...].astype(F32), (((0,), (0,)), ((), ())),
        precision=lax.Precision.HIGHEST, preferred_element_type=F32,
    )
    out[...] = (share[...].astype(F32) - removed).astype(BF16)


def head_vectors(place, head_weight, batch_of, erase_left, erase_right, share):
    count, channels = head_weight.shape
    factors = erase_left.shape[1]
    whole = lambda i, place: (0, 0)
    mine = lambda i, place: (0, place[0])
    return pl.pallas_call(
        vectors_kernel,
        grid_spec=pltpu.PrefetchScalarGridSpec(
            num_scalar_prefetch=1,
            grid=(1,),
            in_specs=[
                pl.BlockSpec((count, channels), whole),
                pl.BlockSpec((count, share), mine),
                pl.BlockSpec((1, count), whole),
                pl.BlockSpec((factors, channels), whole),
                pl.BlockSpec((factors, share), mine),
            ],
            out_specs=pl.BlockSpec((count, share), whole),
        ),
        out_shape=jax.ShapeDtypeStruct((count, share), BF16),
        cost_estimate=cost(1e9, 1e6),
        compiler_params=params(),
        name="head_vectors",
    )(place, head_weight, head_weight, batch_of[None, :], erase_left.T, erase_right.T)


def bucket_kernel(rows, place_of, bins, grads, out):
    cover, experts = bins.shape
    together = 128 // experts
    lanes = together * experts
    chunks = cover // together
    members = out.shape[0]
    before = jnp.where(
        lax.broadcasted_iota(jnp.int32, (lanes, lanes), 0)
        < lax.broadcasted_iota(jnp.int32, (lanes, lanes), 1),
        1.0, 0.0,
    ).astype(BF16)
    index = lax.broadcasted_iota(jnp.int32, (members, lanes), 0)
    slot = lax.broadcasted_iota(jnp.int32, (COLS, lanes), 0) - place_of[0] * SLOTS
    expert = lax.broadcasted_iota(jnp.int32, (1, lanes), 1) % experts
    side = lambda ref, chunk: jnp.concatenate(
        [ref[chunk * together + k : chunk * together + k + 1, :] for k in range(together)], axis=1
    )
    base = jnp.zeros((members, 1), F32)
    total = jnp.zeros(out.shape, F32)
    grads = grads[...].astype(F32)
    for chunk in range(chunks):
        place = side(bins, chunk)
        target = place // rows
        offset = place - target * rows
        mine = jnp.where(target == index, 1.0, 0.0)
        mine_low = mine.astype(BF16)
        earlier = jnp.dot(mine_low, before, preferred_element_type=F32) + base
        rank = jnp.sum(mine * earlier, axis=0, keepdims=True).astype(jnp.int32)
        base = base + jnp.sum(mine, axis=1, keepdims=True)
        high = offset // 256
        low = (offset - high * 256).astype(F32)
        code = (expert + high * SLOTS).astype(F32)
        hit = rank == slot
        spread = jnp.concatenate(
            [jnp.where(hit, v, 0.0) for v in (low, code, side(grads, chunk))], axis=0
        ).astype(BF16)
        total = total + lax.dot_general(mine_low, spread, NT, preferred_element_type=F32)
    out[...] = total.astype(BF16)


def bucket(place, cover_bins, bin_gradient, members, rows):
    return pl.pallas_call(
        functools.partial(bucket_kernel, rows),
        in_specs=[SMEM, VMEM, VMEM],
        out_shape=jax.ShapeDtypeStruct((members, 3 * COLS), BF16),
        cost_estimate=cost(1e8, 1e5),
        compiler_params=params(),
        name="bucket_entries",
    )(place, cover_bins.T, bin_gradient.T)


def spread_kernel(rows, arrived, out, fields):
    group = pl.program_id(0)
    together = COLS // SLOTS

    @pl.when(group == 0)
    def _():
        members = arrived.shape[0]
        shape = (members // together, members)
        same = (
            lax.broadcasted_iota(jnp.int32, shape, 1) // together
            == lax.broadcasted_iota(jnp.int32, shape, 0)
        )
        fields[...] = jnp.dot(
            jnp.where(same, 1.0, 0.0).astype(BF16), arrived[...], preferred_element_type=F32
        )

    row = fields[pl.ds(group, 1), :]
    low = row[:, :COLS]
    code = row[:, COLS : 2 * COLS]
    value = row[:, 2 * COLS :]
    high = code >= SLOTS
    offset = (low + jnp.where(high, 256.0, 0.0)).astype(jnp.int32)
    slot = lax.broadcasted_iota(jnp.int32, code.shape, 1)
    column = (code - jnp.where(high, 1.0 * SLOTS, 0.0)).astype(jnp.int32) + slot // SLOTS * SLOTS
    width = out.shape[1]
    at_row = jnp.where(
        lax.broadcasted_iota(jnp.int32, (rows, width), 0) == offset, 1.0, 0.0
    ).astype(BF16)
    at_column = jnp.where(
        lax.broadcasted_iota(jnp.int32, (width, width), 0) == column, value, 0.0
    ).astype(BF16)
    reach = (out.shape[0] - rows) // 2
    out[reach : reach + rows, :] = lax.dot_general(
        at_row, at_column, NT, preferred_element_type=F32
    ).astype(BF16)
    out[:reach, :] = jnp.zeros((reach, width), BF16)
    out[reach + rows :, :] = jnp.zeros((reach, width), BF16)


def spread_entries(arrived, rows, reach):
    groups = arrived.shape[0] * SLOTS // COLS
    return pl.pallas_call(
        functools.partial(spread_kernel, rows),
        grid=(groups,),
        in_specs=[pl.BlockSpec(arrived.shape, lambda i: (0, 0))],
        scratch_shapes=[pltpu.VMEM((groups, arrived.shape[1]), F32)],
        out_specs=pl.BlockSpec((rows + 2 * reach, COLS), lambda i: (0, i)),
        out_shape=pltpu.HBM((rows + 2 * reach, groups * COLS), BF16),
        cost_estimate=cost(6e9, 8e6),
        compiler_params=params(),
        name="spread_entries",
    )(arrived)


def fill_edges(spread, low, high):
    reach = low.shape[0]
    rows = spread.shape[0]

    def body(old, low, high, out, sems):
        pairs = [
            (low, out.at[pl.ds(0, reach), :]),
            (high, out.at[pl.ds(rows - reach, reach), :]),
        ]
        for copy in fetch(pairs, sems):
            copy.wait()

    return pl.pallas_call(
        body,
        in_specs=[HBM, VMEM, VMEM],
        out_specs=HBM,
        out_shape=pltpu.HBM(spread.shape, spread.dtype),
        scratch_shapes=[pltpu.SemaphoreType.DMA((2,))],
        input_output_aliases={0: 0},
        cost_estimate=cost(1e6, 1e6),
        compiler_params=params(),
        name="fill_edges",
    )(in_hbm(spread), low, high)


def cut_edges(saved):
    _, rows, share = saved.shape
    count = sum(HALO_SAVED.values())

    def body(saved, first, last, sems):
        pairs = []
        for level, start in EDGE_START.items():
            size = HALO_SAVED[level]
            to = pl.ds(start, size)
            pairs.append((saved.at[level, pl.ds(0, size), :], first.at[to, :]))
            pairs.append((saved.at[level, pl.ds(rows - size, size), :], last.at[to, :]))
        for copy in fetch(pairs, sems):
            copy.wait()

    return pl.pallas_call(
        body,
        in_specs=[HBM],
        out_specs=[VMEM, VMEM],
        out_shape=[jax.ShapeDtypeStruct((count, share), BF16)] * 2,
        scratch_shapes=[pltpu.SemaphoreType.DMA((2 * len(EDGE_START),))],
        cost_estimate=cost(1e6, 6e5),
        compiler_params=params(),
        name="cut_edges",
    )(in_hbm(saved))


def pre_kernel(level, saved, low, high, weight, send, slope, value, act, shifted, kernel, sems):
    dilation = BASE_DILATION * 2**level
    halo, inner = HALO_SAVED[level], HALO_IN[level - 1]
    rows = value.shape[0]
    edge = slice(EDGE_START[level], EDGE_START[level] + halo)
    count = send.shape[0]
    taps = shifted.shape[0]
    columns = column_blocks(send.shape[1])
    pairs = [(saved.at[level], value)]
    for k, cols in enumerate(columns):
        pairs.append((weight.at[level, :, :, cols], kernel.at[k]))
    copies = fetch(pairs, sems)
    for side, start in ((low, 0), (high, halo + rows)):
        act[start : start + halo, :], outside = gelu_parts(side[edge, :].astype(F32))
        if inner and start:
            slope[inner + rows :, :] = outside[:inner].astype(BF16)
        elif inner:
            slope[:inner, :] = outside[halo - inner :].astype(BF16)
    copies[0].wait()
    step = 64

    def part_of(k, _):
        start = pl.multiple_of(k * step, step)
        one, two = gelu_parts(value[pl.ds(start, step), :].astype(F32))
        act[pl.ds(pl.multiple_of(start + halo, 16), step), :] = one
        value[pl.ds(start, step), :] = two.astype(BF16)
        return 0

    lax.fori_loop(0, rows // step, part_of, 0)
    slope[inner : inner + rows, :] = value[...]
    for tap in range(taps):
        start = halo - HALO_IN[level] + (tap - 1) * dilation
        shifted[tap] = act[start : start + count, :].astype(BF16)
    for k, cols in enumerate(columns):
        copies[1 + k].wait()
        total = None
        for tap in range(taps):
            part = jnp.dot(shifted[tap], kernel[k, tap], preferred_element_type=F32)
            total = part if total is None else total + part
        send[:, cols] = total.astype(BF16)


def pre_partial(level, saved, low, high, weights):
    rows, share = saved.shape[1:]
    count = rows + 2 * HALO_IN[level]
    halo = HALO_SAVED[level]
    _, taps, _, width = weights.shape
    blocks = width // COLS
    return pl.pallas_call(
        functools.partial(pre_kernel, level),
        in_specs=[HBM, VMEM, VMEM, HBM],
        out_specs=[VMEM, VMEM],
        out_shape=[
            jax.ShapeDtypeStruct((count, width), BF16),
            jax.ShapeDtypeStruct((rows + 2 * HALO_IN[level - 1], share), BF16),
        ],
        scratch_shapes=[
            pltpu.VMEM((rows, share), BF16),
            pltpu.VMEM((rows + 2 * halo, share), F32),
            pltpu.VMEM((taps, count, share), BF16),
            pltpu.VMEM((blocks, taps, share, COLS), BF16),
            pltpu.SemaphoreType.DMA((1 + blocks,)),
        ],
        cost_estimate=cost(5e9, 8e6),
        compiler_params=params(),
        name=f"pre_partial_{level}",
    )(in_hbm(saved), low, high, in_hbm(weights))


def pre_slope(level, flags, own, other, rows):
    count, width = own.shape
    blocks = pl.BlockSpec((count, COLS), lambda i, flags: (0, i))
    halo = HALO_IN[level]

    def body(flags, own, other, out):
        slope = gelu_parts(own[...].astype(F32) + other[...].astype(F32))[1]
        at = lax.broadcasted_iota(jnp.int32, slope.shape, 0)
        outside = ((at < halo) & (flags[0] != 0)) | ((at >= halo + rows) & (flags[1] != 0))
        out[...] = jnp.where(outside, 0.0, slope).astype(BF16)

    return pl.pallas_call(
        body,
        grid_spec=pltpu.PrefetchScalarGridSpec(
            num_scalar_prefetch=1, grid=(width // COLS,), in_specs=[blocks, blocks], out_specs=blocks
        ),
        out_shape=jax.ShapeDtypeStruct((count, width), BF16),
        cost_estimate=cost(4e9, 5e6),
        compiler_params=params(),
        name=f"pre_slope_{level}",
    )(flags, own, other)


def top_kernel(spread, vectors, expand, grad, send, matrix, held, kernel, sems):
    columns = column_blocks(grad.shape[1])
    level = expand.shape[0] - 1
    part = spread.shape[1] // 4
    quarters = [pl.ds(k * part, part) for k in range(4)]
    first, rest = [], []
    for rows in quarters:
        first.append((spread.at[:, rows], matrix.at[:, rows]))
        first.append((vectors.at[rows, columns[0]], held.at[0, rows, :]))
    for k, cols in enumerate(columns):
        rest.append((expand.at[level, :, cols], kernel.at[k]))
        if k:
            rest.append((vectors.at[:, cols], held.at[k]))
    copies = fetch(first + rest, sems)
    ready = iter(copies)
    middle = None
    for k, cols in enumerate(columns):
        if k == 0:
            top = None
            for rows in quarters:
                next(ready).wait()
                next(ready).wait()
                piece = jnp.dot(matrix[:, rows], held[0, rows, :], preferred_element_type=F32)
                top = piece if top is None else top + piece
            next(ready).wait()
        else:
            next(ready).wait()
            next(ready).wait()
            top = jnp.dot(matrix[...], held[k], preferred_element_type=F32)
        grad[:, cols] = top
        piece = lax.dot_general(top.astype(BF16), kernel[k], NT, preferred_element_type=F32)
        middle = piece if middle is None else middle + piece
    send[...] = middle.astype(BF16)


def top_gradient(spread, vectors, expand):
    count, depth = spread.shape
    share = vectors.shape[1]
    width = expand.shape[1]
    blocks = share // COLS
    return pl.pallas_call(
        top_kernel,
        in_specs=[HBM, HBM, HBM],
        out_specs=[VMEM, VMEM],
        out_shape=[
            jax.ShapeDtypeStruct((count, share), F32),
            jax.ShapeDtypeStruct((count, width), BF16),
        ],
        scratch_shapes=[
            pltpu.VMEM((count, depth), BF16),
            pltpu.VMEM((blocks, depth, COLS), BF16),
            pltpu.VMEM((blocks, width, COLS), BF16),
            pltpu.SemaphoreType.DMA((8 + 2 * blocks - 1,)),
        ],
        cost_estimate=cost(5e9, 14e6),
        compiler_params=params(),
        name="top_gradient",
    )(in_hbm(spread), in_hbm(vectors), in_hbm(expand))


def block_kernel(level, own, other, slope, weight, grad, outer, expand, out, *rest):
    last = level == 0
    pre, shifted, kernel, expander, sems = rest[-5:]
    dilation = BASE_DILATION * 2**level
    count, share = out.shape
    trim = HALO_IN[level] - HALO_IN[level - 1]
    taps = weight.shape[1]
    columns = column_blocks(share)
    pairs = [(weight.at[level, :, cols, :], kernel.at[k]) for k, cols in enumerate(columns)]
    if not last:
        pairs.append((expand.at[level - 1], expander))
    copies = fetch(pairs, sems)
    pre[...] = (own[...].astype(F32) + other[...].astype(F32)) * slope[...].astype(F32)
    for tap in range(taps):
        start = trim - (tap - 1) * dilation
        shifted[tap] = pre[start : start + count, :].astype(BF16)
    middle = None
    for k, cols in enumerate(columns):
        copies[k].wait()
        total = None
        for tap in range(taps):
            part = lax.dot_general(shifted[tap], kernel[k, tap], NT, preferred_element_type=F32)
            total = part if total is None else total + part
        new = grad[trim : trim + count, cols] + total * outer[:, cols].astype(F32)
        if last:
            out[:, cols] = new.astype(BF16)
            continue
        out[:, cols] = new
        if k == 0:
            copies[-1].wait()
        part = lax.dot_general(
            new.astype(BF16), expander[:, cols], NT, preferred_element_type=F32
        )
        middle = part if middle is None else middle + part
    if not last:
        rest[0][...] = middle.astype(BF16)


def block_step(level, own, other, slope, weight, grad, outer, expand):
    count_in, width = own.shape
    count, share = outer.shape
    taps = weight.shape[1]
    blocks = share // COLS
    last = level == 0
    out_shape = [jax.ShapeDtypeStruct((count, share), BF16 if last else F32)]
    if not last:
        out_shape.append(jax.ShapeDtypeStruct((count, width), BF16))
    return pl.pallas_call(
        functools.partial(block_kernel, level),
        in_specs=[VMEM, VMEM, VMEM, HBM, VMEM, VMEM, HBM],
        out_specs=[VMEM] * len(out_shape),
        out_shape=out_shape,
        scratch_shapes=[
            pltpu.VMEM((count_in, width), F32),
            pltpu.VMEM((taps, count, width), BF16),
            pltpu.VMEM((blocks, taps, COLS, width), BF16),
            pltpu.VMEM((width, share), BF16),
            pltpu.SemaphoreType.DMA((blocks + 1,)),
        ],
        cost_estimate=cost(5e9, 14e6),
        compiler_params=params(),
        name=f"block_step_{level}",
    )(own, other, slope, in_hbm(weight), grad, outer, in_hbm(expand))


def after(value, *earlier):
    return lax.optimization_barrier((value, *earlier))[0]


def gather_vectors(vectors, meanwhile, later):
    count = vectors.shape[0]
    place = lax.axis_index("head")
    along, turn = place // 4, place % 4
    same = lambda steps: [(a * 4 + z, a * 4 + (z - steps) % 4) for a in range(2) for z in range(4)]
    parts = [lax.ppermute(vectors, "head", same(k)) for k in (1, 2, 3)]
    parts = [after(vectors, *meanwhile)] + parts
    twice = jnp.concatenate(parts + parts, axis=0)
    ring = lax.dynamic_slice_in_dim(twice, (4 - turn) % 4 * count, 4 * count, 0)
    other = lax.ppermute(ring, "head", [(k, (k + 4) % 8) for k in range(8)])
    ring = after(ring, *later)
    both = jnp.where(
        along == 0,
        jnp.concatenate([ring, other], axis=0),
        jnp.concatenate([other, ring], axis=0),
    )
    return lax.all_gather(both, "pos", tiled=True)


def per_device(
    inputs_saved,
    conv_weight,
    expand_weight,
    head_weight,
    batch_of,
    erase_left,
    erase_right,
    bin_gradient,
    cover_bins,
):
    members = lax.axis_size(GROUP_AXES)
    layers, rows, share = inputs_saved.shape
    member = lax.axis_index(GROUP_AXES)
    chan_place = lax.axis_index("chan")
    up = [(k, k + 1) for k in range(members - 1)]
    down = [(k + 1, k) for k in range(members - 1)]
    swap = [(0, 1), (1, 0)]
    levels = list(reversed(range(layers)))

    vectors = head_vectors(
        chan_place[None].astype(jnp.int32), head_weight, batch_of, erase_left, erase_right, share
    )
    first, final = cut_edges(after(inputs_saved, vectors))
    low = lax.ppermute(final, GROUP_AXES, up)
    high = lax.ppermute(first, GROUP_AXES, down)
    flags = jnp.stack([member == 0, member == members - 1]).astype(jnp.int32)
    sends, outers, others = {}, {}, {}
    for n in levels:
        sends[n], outers[n] = pre_partial(n, inputs_saved, low, high, conv_weight)
        others[n] = lax.ppermute(sends[n], "chan", swap)

    payload = bucket(
        (member % (COLS // SLOTS))[None].astype(jnp.int32), cover_bins, bin_gradient, members, rows
    )
    arrived = lax.all_to_all(
        after(payload, sends[levels[0]]), GROUP_AXES, split_axis=0, concat_axis=0, tiled=True
    )
    gathered = gather_vectors(vectors, (payload, low, high), (sends[levels[0]],))
    reach = HALO_IN[layers - 1]
    spread = spread_entries(after(arrived, *sends.values()), rows, reach)
    spread_low = lax.ppermute(spread[rows : rows + reach], GROUP_AXES, up)
    spread_high = lax.ppermute(spread[reach : 2 * reach], GROUP_AXES, down)
    spread = fill_edges(spread, spread_low, spread_high)
    slopes = {n: pre_slope(n, flags, sends[n], others[n], rows) for n in levels}
    spread = after(spread, others[levels[1]], slopes[levels[0]])

    grad, send = top_gradient(spread, gathered, expand_weight)
    for n in levels:
        other = lax.ppermute(send, "chan", swap)
        outs = block_step(
            n, send, other, slopes[n], conv_weight, grad, outers[n], expand_weight
        )
        if n:
            grad, send = outs
    return outs[0]


def solution(mesh):
    return jax.shard_map(
        per_device,
        mesh=mesh,
        in_specs=(
            P(None, ("pos", "head"), "chan"),
            P(None, None, "chan", None),
            P(None, None, "chan"),
            P(("pos", "head"), None),
            P(("pos", "head")),
            P(),
            P(),
            P(("pos", "head"), None),
            P(("pos", "head"), None),
        ),
        out_specs=P(("pos", "head"), "chan"),
        check_vma=False,
    )
```

time: 220 us -> 208 us (0.945)
  the two profiles are of different devices: /device:TPU:8 before, /device:TPU:4 now
where the time goes in v3:
time: 208 us; the launch traced here: 207 us
  waiting for transfers between devices  72.4 us (35%)
  Pallas kernels  70.1 us (34%)
  starting transfers between devices  41.8 us (20%)
  between operations  13.7 us (7%)
  local copies, waits for them, and re-layouts  7.52 us (4%)
    ppermute x3, waiting for transfers between devices, per_device(): other = lax.ppermute(send, 'chan', swap)  53 us
    pallas_call x3, Pallas kernels, pre_partial(): pl.pallas_call(functools.partial(pre_kernel, level), in_specs=[HBM, VMEM,...  19.7 us
    pallas_call x3, Pallas kernels, block_step(): pl.pallas_call(functools.partial(block_kernel, level), in_specs=[VMEM, VM...  18 us
    pallas_call x1, Pallas kernels, top_gradient(): pl.pallas_call(top_kernel, in_specs=[HBM, HBM, HBM], out_specs=[VMEM, VME...  9.81 us
    ppermute x3, waiting for transfers between devices, per_device(): others[n] = lax.ppermute(sends[n], 'chan', swap)  9.72 us
    all_to_all x1, starting transfers between devices, per_device(): lax.all_to_all(after(payload, sends[levels[0]]), GROUP_AXES, split_axis=0...  9.17 us
    pallas_call x1, Pallas kernels, spread_entries(): pl.pallas_call(functools.partial(spread_kernel, rows), grid=(groups,), in...  8.62 us
    pallas_call x3, Pallas kernels, pre_slope(): pl.pallas_call(body, grid_spec=pltpu.PrefetchScalarGridSpec(num_scalar_pr...  8.02 us
  transfers between devices with their start and end apart: 16, of which 10 were waited for; matrix products, arithmetic and copies ran while one was open for 2% of the time, Pallas kernels for 22%

profile of v3, /device:TPU:4, one launch (start us, length us, event | category | flops | bytes accessed | tf_op | source)
XLA Modules:
  0.0 207.4 jit_solution(17757208749591474095)
XLA Ops:
  6.5 0.0 all-gather.2.cloned.1.call-start
  6.5 0.9 copy-done
  7.5 0.9 copy-done.1
  8.4 0.9 copy-done.2
  9.3 0.7 copy-done.5
  10.0 0.7 head_vectors.1
  10.6 1.1 cut_edges.1
  11.7 3.8 %collective-permute-start = (bf16[96,768]{1,0:T(8,128)(2,1)S(1)}, bf16[96,768]{1,0:T(8,128)(2,1)S(1)}, u32[]{:S(2)}, u32[]{:S(2)}) collective-permute-start(bf16[96,768]{1,0:T(8,128)(2,1)S(1)} %get-tuple-element.26), channel_id=1, source_target_pairs={{0,2},{2,4},{4,6},{6,8},{8,10},{10,12},{12,14},{14,16},{16,18},{18... | collective-permute-start | bytes 442376 | tf_op jit(solution)/shard_map/ppermute | solution.py:517
  15.6 4.7 %collective-permute-start.1 = (bf16[96,768]{1,0:T(8,128)(2,1)S(1)}, bf16[96,768]{1,0:T(8,128)(2,1)S(1)}, u32[]{:S(2)}, u32[]{:S(2)}) collective-permute-start(bf16[96,768]{1,0:T(8,128)(2,1)S(1)} %get-tuple-element.27), channel_id=1, source_target_pairs={{2,0},{4,2},{6,4},{8,6},{10,8},{12,10},{14,12},{16,14},{18,16},{20... | collective-permute-start | bytes 442376 | tf_op jit(solution)/shard_map/ppermute | solution.py:518
  20.3 1.4 collective-permute-start.6
  21.7 0.0 collective-permute-start.7
  21.7 1.2 collective-permute-start.8
  23.0 0.0 copy-done.4
  23.0 0.0 copy-done.3
  23.0 3.4 %bucket_entries.1 = bf16[64,768]{1,0:T(8,128)(2,1)S(1)} custom-call(s32[1]{0:T(128)} %bitcast.place_of, s32[32,64]{1,0:T(8,128)S(1)} %bitcast.17, bf16[32,64]{1,0:T(8,128)(2,1)S(1)} %bitcast.18), custom_call_target="tpu_custom_call" | custom-call | flops 20000000 | bytes 20000 | tf_op jit(solution)/shard_map/bucket_entries/pallas_call | solution.py:138
  26.3 0.0 collective-permute-done.low
  26.3 0.0 collective-permute-done.1.high
  26.4 1.5 collective-permute-done.6
  27.8 0.9 collective-permute-done.7
  28.7 0.5 collective-permute-done.8
  29.3 1.2 collective-permute-start.9
  30.5 7.0 %pre_partial_2.1 = (bf16[576,768]{1,0:T(8,128)(2,1)}, bf16[544,768]{1,0:T(8,128)(2,1)S(1)}) custom-call(bf16[3,512,768]{2,1,0:T(8,128)(2,1)} %saved.6, bf16[96,768]{1,0:T(8,128)(2,1)S(1)} %collective-permute-done.low, bf16[96,768]{1,0:T(8,128)(2,1)S(1)} %collective-permute-done.1.high, bf16[3,3,768,768]{3,2,1,0:T(8,128)(2,1)} %weight.13), custom_call_target="tpu_custom_call" | custom-call | flops 1000000000 | bytes 1600000 | tf_op jit(solution)/shard_map/pre_partial_2/pallas_call | solution.py:301
  37.5 2.5 %collective-permute-done.9 = bf16[256,768]{1,0:T(8,128)(2,1)S(1)} collective-permute-done((bf16[256,768]{1,0:T(8,128)(2,1)S(1)}, bf16[256,768]{1,0:T(8,128)(2,1)S(1)}, u32[]{:S(2)}, u32[]{:S(2)}) %collective-permute-start.9) | collective-permute-done | bytes 393248 | tf_op jit(solution)/shard_map/ppermute | solution.py:483
  39.9 1.2 maximum_select_fusion
  41.1 0.0 all-gather.2.cloned.1.call-update
  41.2 2.5 %collective-permute-start.5 = (bf16[576,768]{1,0:T(8,128)(2,1)}, bf16[576,768]{1,0:T(8,128)(2,1)}, u32[]{:S(2)}, u32[]{:S(2)}) collective-permute-start(bf16[576,768]{1,0:T(8,128)(2,1)} %get-tuple-element.28.own), channel_id=1, source_target_pairs={{0,1},{1,0},{2,3},{3,2},{4,5},{5,4},{6,7},{7,6},{8,9},{9,8},{10,11... | collective-permute-start | bytes 2654216 | tf_op jit(solution)/shard_map/ppermute | solution.py:523
  43.7 0.5 broadcast.4
  44.2 0.6 reduce
  44.8 0.7 reshape.2
  45.5 9.2 %all-to-all-start = ((bf16[64,2,384]{2,1,0:T(2,128)(2,1)}), bf16[64,2,384]{2,1,0:T(2,128)(2,1)S(1)}, u32[]{:S(2)}, u32[]{:S(2)}) async-start(bf16[64,2,384]{2,1,0:T(2,128)(2,1)} %reshape.2), calls=%async_computation | async-start | bytes 196608 | tf_op jit(solution)/shard_map/all_to_all | solution.py:528
  54.6 6.8 %pre_partial_1.1 = (bf16[544,768]{1,0:T(8,128)(2,1)}, bf16[528,768]{1,0:T(8,128)(2,1)S(1)}) custom-call(bf16[3,512,768]{2,1,0:T(8,128)(2,1)} %saved.6, bf16[96,768]{1,0:T(8,128)(2,1)S(1)} %collective-permute-done.low, bf16[96,768]{1,0:T(8,128)(2,1)S(1)} %collective-permute-done.1.high, bf16[3,3,768,768]{3,2,1,0:T(8,128)(2,1)} %weight.13), custom_call_target="tpu_custom_call" | custom-call | flops 1000000000 | bytes 1600000 | tf_op jit(solution)/shard_map/pre_partial_1/pallas_call | solution.py:301
  61.4 2.3 %collective-permute-start.4 = (bf16[544,768]{1,0:T(8,128)(2,1)}, bf16[544,768]{1,0:T(8,128)(2,1)}, u32[]{:S(2)}, u32[]{:S(2)}) collective-permute-start(bf16[544,768]{1,0:T(8,128)(2,1)} %get-tuple-element.30.own), channel_id=1, source_target_pairs={{0,1},{1,0},{2,3},{3,2},{4,5},{5,4},{6,7},{7,6},{8,9},{9,8},{10,11... | collective-permute-start | bytes 2506760 | tf_op jit(solution)/shard_map/ppermute | solution.py:523
  63.7 6.0 %pre_partial_0.1 = (bf16[528,768]{1,0:T(8,128)(2,1)S(1)}, bf16[512,768]{1,0:T(8,128)(2,1)S(1)}) custom-call(bf16[3,512,768]{2,1,0:T(8,128)(2,1)} %saved.6, bf16[96,768]{1,0:T(8,128)(2,1)S(1)} %collective-permute-done.low, bf16[96,768]{1,0:T(8,128)(2,1)S(1)} %collective-permute-done.1.high, bf16[3,3,768,768]{3,2,1,0:T(8,128)(2,1)} %weight.13), custom_call_target="tpu_custom_call" | custom-call | flops 1000000000 | bytes 1600000 | tf_op jit(solution)/shard_map/pre_partial_0/pallas_call | solution.py:301
  69.7 0.0 copy-start.6
  69.7 0.9 copy-done.6
  70.6 0.0 all-to-all-done
  70.6 0.1 reshape.3
  70.7 8.6 %spread_entries.1.old = bf16[576,4096]{1,0:T(8,128)(2,1)} custom-call(bf16[64,768]{1,0:T(8,128)(2,1)S(1)} %bitcast.14), custom_call_target="tpu_custom_call" | custom-call | flops 1200000000 | bytes 1600000 | tf_op jit(solution)/shard_map/spread_entries/pallas_call | solution.py:189
  79.3 1.8 fusion
  81.1 3.3 %collective-permute-start.2 = (bf16[32,4096]{1,0:T(8,128)(2,1)}, bf16[32,4096]{1,0:T(8,128)(2,1)S(1)}, u32[]{:S(2)}, u32[]{:S(2)}) collective-permute-start(bf16[32,4096]{1,0:T(8,128)(2,1)} %get-tuple-element.46), channel_id=1, source_target_pairs={{0,2},{2,4},{4,6},{6,8},{8,10},{10,12},{12,14},{14,16},{16,18},{18... | collective-permute-start | bytes 786440 | tf_op jit(solution)/shard_map/ppermute | solution.py:534
  84.4 5.3 %collective-permute-start.3 = (bf16[32,4096]{1,0:T(8,128)(2,1)S(1)}, bf16[32,4096]{1,0:T(8,128)(2,1)S(1)}, u32[]{:S(2)}, u32[]{:S(2)}) collective-permute-start(bf16[32,4096]{1,0:T(8,128)(2,1)S(1)} %get-tuple-element.45), channel_id=1, source_target_pairs={{2,0},{4,2},{6,4},{8,6},{10,8},{12,10},{14,12},{16,14},{18,16},{20... | collective-permute-start | bytes 786440 | tf_op jit(solution)/shard_map/ppermute | solution.py:535
  89.7 0.1 add_convert_fusion.flags
  89.8 2.3 %collective-permute-done.2.low = bf16[32,4096]{1,0:T(8,128)(2,1)S(1)} collective-permute-done((bf16[32,4096]{1,0:T(8,128)(2,1)}, bf16[32,4096]{1,0:T(8,128)(2,1)S(1)}, u32[]{:S(2)}, u32[]{:S(2)}) %collective-permute-start.2) | collective-permute-done | bytes 262176 | tf_op jit(solution)/shard_map/ppermute | solution.py:534
  92.1 2.0 collective-permute-done.3.high
  94.1 0.8 fill_edges.1.spread
  95.0 0.0 collective-permute-done.5.other
  95.0 3.3 %pre_slope_2.1.slope = bf16[576,768]{1,0:T(8,128)(2,1)S(1)} custom-call(s32[2]{0:T(128)S(1)} %add_convert_fusion.flags, bf16[576,768]{1,0:T(8,128)(2,1)} %get-tuple-element.28.own, bf16[576,768]{1,0:T(8,128)(2,1)} %collective-permute-done.5.other), custom_call_target="tpu_custom_call" | custom-call | flops 800000000 | bytes 1000000 | tf_op jit(solution)/shard_map/pre_slope_2/pallas_call | solution.py:333
  98.3 0.0 collective-permute-done.4.other
  98.3 0.0 all-gather.2.cloned.1.call-done.vectors
  98.3 9.8 %top_gradient.1 = (f32[576,768]{1,0:T(8,128)S(1)}, bf16[576,768]{1,0:T(8,128)(2,1)S(1)}) custom-call(bf16[576,4096]{1,0:T(8,128)(2,1)} %fill_edges.1.spread, bf16[4096,768]{1,0:T(8,128)(2,1)} %all-gather.2.cloned.1.call-done.vectors, bf16[3,768,768]{2,1,0:T(8,128)(2,1)} %expand.7), custom_call_target="tpu_custom_call" | custom-call | flops 1000000000 | bytes 2800000 | tf_op jit(solution)/shard_map/top_gradient/pallas_call | solution.py:385
  108.1 1.6 collective-permute-start.10
  109.7 22.2 %collective-permute-done.10.other = bf16[576,768]{1,0:T(8,128)(2,1)S(1)} collective-permute-done((bf16[576,768]{1,0:T(8,128)(2,1)S(1)}, bf16[576,768]{1,0:T(8,128)(2,1)S(1)}, u32[]{:S(2)}, u32[]{:S(2)}) %collective-permute-start.10) | collective-permute-done | bytes 884768 | tf_op jit(solution)/shard_map/ppermute | solution.py:542
  131.9 6.2 %block_step_2.1 = (f32[544,768]{1,0:T(8,128)S(1)}, bf16[544,768]{1,0:T(8,128)(2,1)S(1)}) custom-call(bf16[576,768]{1,0:T(8,128)(2,1)S(1)} %get-tuple-element.36.own, bf16[576,768]{1,0:T(8,128)(2,1)S(1)} %collective-permute-done.10.other, bf16[576,768]{1,0:T(8,128)(2,1)S(1)} %pre_slope_2.1.slope, bf16[3,3,768,768]{3,2,1,0:T(8,128)(2,1)} %weight.13, ...), custom_call_target="tpu_custom_call" | custom-call | flops 1000000000 | bytes 2800000 | tf_op jit(solution)/shard_map/block_step_2/pallas_call | solution.py:452
  138.1 1.7 collective-permute-start.11
  139.8 0.0 copy-done.7
  139.8 1.9 collective-permute-start.13
  141.7 3.2 %pre_slope_1.1.slope = bf16[544,768]{1,0:T(8,128)(2,1)S(1)} custom-call(s32[2]{0:T(128)S(1)} %add_convert_fusion.flags, bf16[544,768]{1,0:T(8,128)(2,1)} %get-tuple-element.30.own, bf16[544,768]{1,0:T(8,128)(2,1)} %collective-permute-done.4.other), custom_call_target="tpu_custom_call" | custom-call | flops 800000000 | bytes 1000000 | tf_op jit(solution)/shard_map/pre_slope_1/pallas_call | solution.py:333
  145.0 16.2 %collective-permute-done.11.other = bf16[544,768]{1,0:T(8,128)(2,1)S(1)} collective-permute-done((bf16[544,768]{1,0:T(8,128)(2,1)S(1)}, bf16[544,768]{1,0:T(8,128)(2,1)S(1)}, u32[]{:S(2)}, u32[]{:S(2)}) %collective-permute-start.11) | collective-permute-done | bytes 835616 | tf_op jit(solution)/shard_map/ppermute | solution.py:542
  161.2 6.0 %block_step_1.1 = (f32[528,768]{1,0:T(8,128)S(1)}, bf16[528,768]{1,0:T(8,128)(2,1)S(1)}) custom-call(bf16[544,768]{1,0:T(8,128)(2,1)S(1)} %get-tuple-element.39.own, bf16[544,768]{1,0:T(8,128)(2,1)S(1)} %collective-permute-done.11.other, bf16[544,768]{1,0:T(8,128)(2,1)S(1)} %pre_slope_1.1.slope, bf16[3,3,768,768]{3,2,1,0:T(8,128)(2,1)} %weight.13, ...), custom_call_target="tpu_custom_call" | custom-call | flops 1000000000 | bytes 2800000 | tf_op jit(solution)/shard_map/block_step_1/pallas_call | solution.py:452
  167.2 1.6 collective-permute-start.12
  168.9 9.7 %collective-permute-done.13.other = bf16[528,768]{1,0:T(8,128)(2,1)S(1)} collective-permute-done((bf16[528,768]{1,0:T(8,128)(2,1)S(1)}, bf16[528,768]{1,0:T(8,128)(2,1)S(1)}, u32[]{:S(2)}, u32[]{:S(2)}) %collective-permute-start.13) | collective-permute-done | bytes 811040 | tf_op jit(solution)/shard_map/ppermute | solution.py:523
  178.6 1.5 pre_slope_0.1.slope
  180.1 14.6 %collective-permute-done.12.other = bf16[528,768]{1,0:T(8,128)(2,1)S(1)} collective-permute-done((bf16[528,768]{1,0:T(8,128)(2,1)S(1)}, bf16[528,768]{1,0:T(8,128)(2,1)S(1)}, u32[]{:S(2)}, u32[]{:S(2)}) %collective-permute-start.12) | collective-permute-done | bytes 811040 | tf_op jit(solution)/shard_map/ppermute | solution.py:542
  194.7 5.8 %block_step_0.1 = bf16[512,768]{1,0:T(8,128)(2,1)} custom-call(bf16[528,768]{1,0:T(8,128)(2,1)S(1)} %get-tuple-element.42.own, bf16[528,768]{1,0:T(8,128)(2,1)S(1)} %collective-permute-done.12.other, bf16[528,768]{1,0:T(8,128)(2,1)S(1)} %pre_slope_0.1.slope, bf16[3,3,768,768]{3,2,1,0:T(8,128)(2,1)} %weight.13, f32[528,768]{1,0:T(8,128)S(1)} %get-tuple-element.43.grad, ...), custom_call_target="tpu_custom_call" | custom-call | flops 1000000000 | bytes 2800000 | tf_op jit(solution)/shard_map/block_step_0/pallas_call | solution.py:452
  (17 shorter events, 0.1 us)
Async XLA Ops:
  6.5 16.4 %copy-start.4 = (bf16[64,32]{0,1:T(8,128)(2,1)S(1)}, bf16[64,32]{0,1:T(8,128)(2,1)}, u32[]{:S(2)}) copy-start(bf16[64,32]{0,1:T(8,128)(2,1)} %param.16) | copy-start | bytes 12292
  6.5 91.8 %all-gather.2.cloned.1.call-start = ((), (), s32[]{:S(2)}) async-start(), calls=%async_computation.1 | async-start | bytes 7077888 | tf_op jit(solution)/shard_map/all_gather | solution.py:490
  6.5 0.9 copy-start
  7.5 0.9 copy-start.1
  8.4 0.9 copy-start.2
  9.3 0.7 copy-start.5
  10.0 13.0 %copy-start.3 = (s32[64,32]{0,1:T(8,128)S(1)}, s32[64,32]{0,1:T(8,128)}, u32[]{:S(2)}) copy-start(s32[64,32]{0,1:T(8,128)} %param.17) | copy-start | bytes 24580
  11.7 14.6 %collective-permute-start = (bf16[96,768]{1,0:T(8,128)(2,1)S(1)}, bf16[96,768]{1,0:T(8,128)(2,1)S(1)}, u32[]{:S(2)}, u32[]{:S(2)}) collective-permute-start(bf16[96,768]{1,0:T(8,128)(2,1)S(1)} %get-tuple-element.26), channel_id=1, source_target_pairs={{0,2},{2,4},{4,6},{6,8},{8,10},{10,12},{12,14},{14,16},{16,18},{18... | collective-permute-start | bytes 442376 | tf_op jit(solution)/shard_map/ppermute | solution.py:517
  15.6 10.8 %collective-permute-start.1 = (bf16[96,768]{1,0:T(8,128)(2,1)S(1)}, bf16[96,768]{1,0:T(8,128)(2,1)S(1)}, u32[]{:S(2)}, u32[]{:S(2)}) collective-permute-start(bf16[96,768]{1,0:T(8,128)(2,1)S(1)} %get-tuple-element.27), channel_id=1, source_target_pairs={{2,0},{4,2},{6,4},{8,6},{10,8},{12,10},{14,12},{16,14},{18,16},{20... | collective-permute-start | bytes 442376 | tf_op jit(solution)/shard_map/ppermute | solution.py:518
  20.3 7.5 %collective-permute-start.6 = (bf16[64,768]{1,0:T(8,128)(2,1)S(1)}, bf16[64,768]{1,0:T(8,128)(2,1)S(1)}, u32[]{:S(2)}, u32[]{:S(2)}) collective-permute-start(bf16[64,768]{1,0:T(8,128)(2,1)S(1)} %head_vectors.1), channel_id=1, source_target_pairs={{0,6},{2,0},{4,2},{6,4},{8,14},{10,8},{12,10},{14,12},{1,7},{3,1},... | collective-permute-start | bytes 294920 | tf_op jit(solution)/shard_map/ppermute | solution.py:479
  21.7 7.0 %collective-permute-start.7 = (bf16[64,768]{1,0:T(8,128)(2,1)S(1)}, bf16[64,768]{1,0:T(8,128)(2,1)S(1)}, u32[]{:S(2)}, u32[]{:S(2)}) collective-permute-start(bf16[64,768]{1,0:T(8,128)(2,1)S(1)} %head_vectors.1), channel_id=1, source_target_pairs={{0,4},{2,6},{4,0},{6,2},{8,12},{10,14},{12,8},{14,10},{1,5},{3,7},... | collective-permute-start | bytes 294920 | tf_op jit(solution)/shard_map/ppermute | solution.py:479
  21.7 7.5 %collective-permute-start.8 = (bf16[64,768]{1,0:T(8,128)(2,1)S(1)}, bf16[64,768]{1,0:T(8,128)(2,1)S(1)}, u32[]{:S(2)}, u32[]{:S(2)}) collective-permute-start(bf16[64,768]{1,0:T(8,128)(2,1)S(1)} %head_vectors.1), channel_id=1, source_target_pairs={{0,2},{2,4},{4,6},{6,0},{8,10},{10,12},{12,14},{14,8},{1,3},{3,5},... | collective-permute-start | bytes 294920 | tf_op jit(solution)/shard_map/ppermute | solution.py:479
  29.3 10.6 %collective-permute-start.9 = (bf16[256,768]{1,0:T(8,128)(2,1)S(1)}, bf16[256,768]{1,0:T(8,128)(2,1)S(1)}, u32[]{:S(2)}, u32[]{:S(2)}) collective-permute-start(bf16[256,768]{1,0:T(8,128)(2,1)S(1)} %constant_dynamic-slice_fusion), channel_id=1, source_target_pairs={{0,8},{2,10},{4,12},{6,14},{8,0},{10,2},{12,4},{14,6},{1,9},{3,11}... | collective-permute-start | bytes 1179656 | tf_op jit(solution)/shard_map/ppermute | solution.py:483
  41.2 53.8 %collective-permute-start.5 = (bf16[576,768]{1,0:T(8,128)(2,1)}, bf16[576,768]{1,0:T(8,128)(2,1)}, u32[]{:S(2)}, u32[]{:S(2)}) collective-permute-start(bf16[576,768]{1,0:T(8,128)(2,1)} %get-tuple-element.28.own), channel_id=1, source_target_pairs={{0,1},{1,0},{2,3},{3,2},{4,5},{5,4},{6,7},{7,6},{8,9},{9,8},{10,11... | collective-permute-start | bytes 2654216 | tf_op jit(solution)/shard_map/ppermute | solution.py:523
  45.5 25.2 %all-to-all-start = ((bf16[64,2,384]{2,1,0:T(2,128)(2,1)}), bf16[64,2,384]{2,1,0:T(2,128)(2,1)S(1)}, u32[]{:S(2)}, u32[]{:S(2)}) async-start(bf16[64,2,384]{2,1,0:T(2,128)(2,1)} %reshape.2), calls=%async_computation | async-start | bytes 196608 | tf_op jit(solution)/shard_map/all_to_all | solution.py:528
  61.4 36.9 %collective-permute-start.4 = (bf16[544,768]{1,0:T(8,128)(2,1)}, bf16[544,768]{1,0:T(8,128)(2,1)}, u32[]{:S(2)}, u32[]{:S(2)}) collective-permute-start(bf16[544,768]{1,0:T(8,128)(2,1)} %get-tuple-element.30.own), channel_id=1, source_target_pairs={{0,1},{1,0},{2,3},{3,2},{4,5},{5,4},{6,7},{7,6},{8,9},{9,8},{10,11... | collective-permute-start | bytes 2506760 | tf_op jit(solution)/shard_map/ppermute | solution.py:523
  69.7 0.9 copy-start.6
  81.1 11.0 %collective-permute-start.2 = (bf16[32,4096]{1,0:T(8,128)(2,1)}, bf16[32,4096]{1,0:T(8,128)(2,1)S(1)}, u32[]{:S(2)}, u32[]{:S(2)}) collective-permute-start(bf16[32,4096]{1,0:T(8,128)(2,1)} %get-tuple-element.46), channel_id=1, source_target_pairs={{0,2},{2,4},{4,6},{6,8},{8,10},{10,12},{12,14},{14,16},{16,18},{18... | collective-permute-start | bytes 786440 | tf_op jit(solution)/shard_map/ppermute | solution.py:534
  84.4 9.7 %collective-permute-start.3 = (bf16[32,4096]{1,0:T(8,128)(2,1)S(1)}, bf16[32,4096]{1,0:T(8,128)(2,1)S(1)}, u32[]{:S(2)}, u32[]{:S(2)}) collective-permute-start(bf16[32,4096]{1,0:T(8,128)(2,1)S(1)} %get-tuple-element.45), channel_id=1, source_target_pairs={{2,0},{4,2},{6,4},{8,6},{10,8},{12,10},{14,12},{16,14},{18,16},{20... | collective-permute-start | bytes 786440 | tf_op jit(solution)/shard_map/ppermute | solution.py:535
  108.1 23.8 %collective-permute-start.10 = (bf16[576,768]{1,0:T(8,128)(2,1)S(1)}, bf16[576,768]{1,0:T(8,128)(2,1)S(1)}, u32[]{:S(2)}, u32[]{:S(2)}) collective-permute-start(bf16[576,768]{1,0:T(8,128)(2,1)S(1)} %get-tuple-element.36.own), channel_id=1, source_target_pairs={{0,1},{1,0},{2,3},{3,2},{4,5},{5,4},{6,7},{7,6},{8,9},{9,8},{10,11... | collective-permute-start | bytes 2654216 | tf_op jit(solution)/shard_map/ppermute | solution.py:542
  131.9 7.9 %copy-start.7 = (bf16[528,768]{1,0:T(8,128)(2,1)S(1)}, bf16[528,768]{1,0:T(8,128)(2,1)}, u32[]{:S(2)}) copy-start(bf16[528,768]{1,0:T(8,128)(2,1)} %copy-done.6) | copy-start | bytes 2433028
  138.1 23.1 %collective-permute-start.11 = (bf16[544,768]{1,0:T(8,128)(2,1)S(1)}, bf16[544,768]{1,0:T(8,128)(2,1)S(1)}, u32[]{:S(2)}, u32[]{:S(2)}) collective-permute-start(bf16[544,768]{1,0:T(8,128)(2,1)S(1)} %get-tuple-element.39.own), channel_id=1, source_target_pairs={{0,1},{1,0},{2,3},{3,2},{4,5},{5,4},{6,7},{7,6},{8,9},{9,8},{10,11... | collective-permute-start | bytes 2506760 | tf_op jit(solution)/shard_map/ppermute | solution.py:542
  139.8 38.8 %collective-permute-start.13 = (bf16[528,768]{1,0:T(8,128)(2,1)S(1)}, bf16[528,768]{1,0:T(8,128)(2,1)S(1)}, u32[]{:S(2)}, u32[]{:S(2)}) collective-permute-start(bf16[528,768]{1,0:T(8,128)(2,1)S(1)} %copy-done.7), channel_id=1, source_target_pairs={{0,1},{1,0},{2,3},{3,2},{4,5},{5,4},{6,7},{7,6},{8,9},{9,8},{10,11... | collective-permute-start | bytes 2433032 | tf_op jit(solution)/shard_map/ppermute | solution.py:523
  167.2 27.5 %collective-permute-start.12 = (bf16[528,768]{1,0:T(8,128)(2,1)S(1)}, bf16[528,768]{1,0:T(8,128)(2,1)S(1)}, u32[]{:S(2)}, u32[]{:S(2)}) collective-permute-start(bf16[528,768]{1,0:T(8,128)(2,1)S(1)} %get-tuple-element.42.own), channel_id=1, source_target_pairs={{0,1},{1,0},{2,3},{3,2},{4,5},{5,4},{6,7},{7,6},{8,9},{9,8},{10,11... | collective-permute-start | bytes 2433032 | tf_op jit(solution)/shard_map/ppermute | solution.py:542
Sparse Core Ops, SparseCore 0:
  41.3 42.2 all-gather.1

commit v4 on v3

--- a/solution.py
+++ b/solution.py
@@ -91,10 +91,11 @@
         cost_estimate=cost(1e9, 1e6),
         compiler_params=params(),
         name="head_vectors",
-    )(place, head_weight, head_weight, batch_of[None, :], erase_left.T, erase_right.T)
-
-
-def bucket_kernel(rows, place_of, bins, grads, out):
+    )(place, *[in_hbm(a) for a in (head_weight, head_weight)], batch_of[None, :],
+      in_hbm(erase_left.T), in_hbm(erase_right.T))
+
+
+def bucket_kernel(rows, bins, grads, out):
     cover, experts = bins.shape
     together = 128 // experts
     lanes = together * experts
@@ -106,7 +107,7 @@
         1.0, 0.0,
     ).astype(BF16)
     index = lax.broadcasted_iota(jnp.int32, (members, lanes), 0)
-    slot = lax.broadcasted_iota(jnp.int32, (COLS, lanes), 0) - place_of[0] * SLOTS
+    slot = lax.broadcasted_iota(jnp.int32, (SLOTS, lanes), 0)
     expert = lax.broadcasted_iota(jnp.int32, (1, lanes), 1) % experts
     side = lambda ref, chunk: jnp.concatenate(
         [ref[chunk * together + k : chunk * together + k + 1, :] for k in range(together)], axis=1
@@ -128,40 +129,57 @@
         code = (expert + high * SLOTS).astype(F32)
         hit = rank == slot
         spread = jnp.concatenate(
-            [jnp.where(hit, v, 0.0) for v in (low, code, side(grads, chunk))], axis=0
+            [jnp.where(hit, v, 0.0) for v in (low, code, side(grads, chunk))]
+            + [jnp.zeros(hit.shape, F32)],
+            axis=0,
         ).astype(BF16)
         total = total + lax.dot_general(mine_low, spread, NT, preferred_element_type=F32)
     out[...] = total.astype(BF16)
 
 
-def bucket(place, cover_bins, bin_gradient, members, rows):
+def bucket(cover_bins, bin_gradient, members, rows):
     return pl.pallas_call(
         functools.partial(bucket_kernel, rows),
-        in_specs=[SMEM, VMEM, VMEM],
-        out_shape=jax.ShapeDtypeStruct((members, 3 * COLS), BF16),
+        in_specs=[VMEM, VMEM],
+        out_shape=jax.ShapeDtypeStruct((members, 4 * SLOTS), BF16),
         cost_estimate=cost(1e8, 1e5),
         compiler_params=params(),
         name="bucket_entries",
-    )(place, cover_bins.T, bin_gradient.T)
-
-
-def spread_kernel(rows, arrived, out, fields):
-    group = pl.program_id(0)
+    )(cover_bins.T, bin_gradient.T)
+
+
+def spread_kernel(rows, along, arrived, out, fields):
+    half, group = pl.program_id(0), pl.program_id(1)
     together = COLS // SLOTS
 
-    @pl.when(group == 0)
+    @pl.when((half == 0) & (group == 0))
     def _():
         members = arrived.shape[0]
+        repeat = jnp.where(
+            lax.broadcasted_iota(jnp.int32, (SLOTS, COLS), 1) % SLOTS
+            == lax.broadcasted_iota(jnp.int32, (SLOTS, COLS), 0),
+            1.0, 0.0,
+        ).astype(BF16)
+        own = (
+            lax.broadcasted_iota(jnp.int32, (members, COLS), 1) // SLOTS
+            == lax.broadcasted_iota(jnp.int32, (members, COLS), 0) % together
+        )
         shape = (members // together, members)
-        same = (
+        same = jnp.where(
             lax.broadcasted_iota(jnp.int32, shape, 1) // together
-            == lax.broadcasted_iota(jnp.int32, shape, 0)
-        )
-        fields[...] = jnp.dot(
-            jnp.where(same, 1.0, 0.0).astype(BF16), arrived[...], preferred_element_type=F32
-        )
-
-    row = fields[pl.ds(group, 1), :]
+            == lax.broadcasted_iota(jnp.int32, shape, 0),
+            1.0, 0.0,
+        ).astype(BF16)
+        for k in range(3):
+            wide = jnp.dot(
+                arrived[:, k * SLOTS : (k + 1) * SLOTS], repeat, preferred_element_type=F32
+            )
+            wide = jnp.where(own, wide, 0.0).astype(BF16)
+            fields[:, k * COLS : (k + 1) * COLS] = jnp.dot(
+                same, wide, preferred_element_type=F32
+            )
+
+    row = fields[pl.ds(group * 2 + (half + along[0]) % 2, 1), :]
     low = row[:, :COLS]
     code = row[:, COLS : 2 * COLS]
     value = row[:, 2 * COLS :]
@@ -176,52 +194,49 @@
     at_column = jnp.where(
         lax.broadcasted_iota(jnp.int32, (width, width), 0) == column, value, 0.0
     ).astype(BF16)
-    reach = (out.shape[0] - rows) // 2
-    out[reach : reach + rows, :] = lax.dot_general(
+    out[...] = lax.dot_general(
         at_row, at_column, NT, preferred_element_type=F32
     ).astype(BF16)
-    out[:reach, :] = jnp.zeros((reach, width), BF16)
-    out[reach + rows :, :] = jnp.zeros((reach, width), BF16)
-
-
-def spread_entries(arrived, rows, reach):
-    groups = arrived.shape[0] * SLOTS // COLS
+
+
+def spread_entries(along, arrived, rows):
+    groups = arrived.shape[0] * SLOTS // COLS // 2
     return pl.pallas_call(
         functools.partial(spread_kernel, rows),
-        grid=(groups,),
-        in_specs=[pl.BlockSpec(arrived.shape, lambda i: (0, 0))],
-        scratch_shapes=[pltpu.VMEM((groups, arrived.shape[1]), F32)],
-        out_specs=pl.BlockSpec((rows + 2 * reach, COLS), lambda i: (0, i)),
-        out_shape=pltpu.HBM((rows + 2 * reach, groups * COLS), BF16),
+        grid_spec=pltpu.PrefetchScalarGridSpec(
+            num_scalar_prefetch=1,
+            grid=(2, groups),
+            in_specs=[pl.BlockSpec(arrived.shape, lambda h, i, along: (0, 0))],
+            scratch_shapes=[pltpu.VMEM((2 * groups, 3 * COLS), F32)],
+            out_specs=pl.BlockSpec((None, rows, COLS), lambda h, i, along: (h, 0, i)),
+        ),
+        out_shape=jax.ShapeDtypeStruct((2, rows, groups * COLS), BF16),
         cost_estimate=cost(6e9, 8e6),
         compiler_params=params(),
         name="spread_entries",
-    )(arrived)
-
-
-def fill_edges(spread, low, high):
-    reach = low.shape[0]
-    rows = spread.shape[0]
-
-    def body(old, low, high, out, sems):
-        pairs = [
-            (low, out.at[pl.ds(0, reach), :]),
-            (high, out.at[pl.ds(rows - reach, reach), :]),
-        ]
+    )(along, arrived)
+
+
+def stage_weights(level, weight, expand):
+    last = level == 0
+    parts = [(weight, level)] + ([] if last else [(expand, level - 1)])
+
+    def body(*refs):
+        sems = refs[-1]
+        pairs = [(refs[k].at[n], refs[len(parts) + k]) for k, (_, n) in enumerate(parts)]
         for copy in fetch(pairs, sems):
             copy.wait()
 
     return pl.pallas_call(
         body,
-        in_specs=[HBM, VMEM, VMEM],
-        out_specs=HBM,
-        out_shape=pltpu.HBM(spread.shape, spread.dtype),
-        scratch_shapes=[pltpu.SemaphoreType.DMA((2,))],
-        input_output_aliases={0: 0},
-        cost_estimate=cost(1e6, 1e6),
-        compiler_params=params(),
-        name="fill_edges",
-    )(in_hbm(spread), low, high)
+        in_specs=[HBM] * len(parts),
+        out_specs=[VMEM] * len(parts),
+        out_shape=[jax.ShapeDtypeStruct(a.shape[1:], a.dtype) for a, _ in parts],
+        scratch_shapes=[pltpu.SemaphoreType.DMA((len(parts),))],
+        cost_estimate=cost(1e9, 1e6),
+        compiler_params=params(),
+        name=f"stage_weights_{level}",
+    )(*[in_hbm(a) for a, _ in parts])
 
 
 def cut_edges(saved):
@@ -342,152 +357,142 @@
     )(flags, own, other)
 
 
-def top_kernel(spread, vectors, expand, grad, send, matrix, held, kernel, sems):
+def top_kernel(half, turned, spread, low, high, vectors, *rest):
+    matrix, held, sems = rest[-3:]
+    last = half == 1
+    if last:
+        before, expand, grad, send, kernel = rest[:-3]
+    else:
+        (grad,) = rest[:-3]
+    rows, reach = spread.shape[1], low.shape[1]
     columns = column_blocks(grad.shape[1])
-    level = expand.shape[0] - 1
-    part = spread.shape[1] // 4
-    quarters = [pl.ds(k * part, part) for k in range(4)]
-    first, rest = [], []
-    for rows in quarters:
-        first.append((spread.at[:, rows], matrix.at[:, rows]))
-        first.append((vectors.at[rows, columns[0]], held.at[0, rows, :]))
-    for k, cols in enumerate(columns):
-        rest.append((expand.at[level, :, cols], kernel.at[k]))
-        if k:
-            rest.append((vectors.at[:, cols], held.at[k]))
-    copies = fetch(first + rest, sems)
-    ready = iter(copies)
+    pairs = [
+        (spread.at[half], matrix.at[pl.ds(reach, rows), :]),
+        (low.at[(half + turned[0]) % 2], matrix.at[pl.ds(0, reach), :]),
+        (high.at[(half + turned[1]) % 2], matrix.at[pl.ds(reach + rows, reach), :]),
+    ]
+    pairs += [(vectors.at[:, cols], held.at[k]) for k, cols in enumerate(columns)]
+    if last:
+        pairs.append((expand.at[expand.shape[0] - 1], kernel))
+    copies = fetch(pairs, sems)
+    for copy in copies[:3]:
+        copy.wait()
     middle = None
     for k, cols in enumerate(columns):
+        copies[3 + k].wait()
+        top = jnp.dot(matrix[...], held[k], preferred_element_type=F32)
+        if not last:
+            grad[:, cols] = top
+            continue
+        top = top + before[:, cols]
+        grad[:, cols] = top
         if k == 0:
-            top = None
-            for rows in quarters:
-                next(ready).wait()
-                next(ready).wait()
-                piece = jnp.dot(matrix[:, rows], held[0, rows, :], preferred_element_type=F32)
-                top = piece if top is None else top + piece
-            next(ready).wait()
-        else:
-            next(ready).wait()
-            next(ready).wait()
-            top = jnp.dot(matrix[...], held[k], preferred_element_type=F32)
-        grad[:, cols] = top
-        piece = lax.dot_general(top.astype(BF16), kernel[k], NT, preferred_element_type=F32)
+            copies[-1].wait()
+        piece = lax.dot_general(
+            top.astype(BF16), kernel[:, cols], NT, preferred_element_type=F32
+        )
         middle = piece if middle is None else middle + piece
-    send[...] = middle.astype(BF16)
-
-
-def top_gradient(spread, vectors, expand):
-    count, depth = spread.shape
+    if last:
+        send[...] = middle.astype(BF16)
+
+
+def top_gradient(half, turned, spread, low, high, vectors, *more):
+    _, rows, depth = spread.shape
+    count = rows + 2 * low.shape[1]
     share = vectors.shape[1]
-    width = expand.shape[1]
     blocks = share // COLS
-    return pl.pallas_call(
-        top_kernel,
-        in_specs=[HBM, HBM, HBM],
-        out_specs=[VMEM, VMEM],
-        out_shape=[
-            jax.ShapeDtypeStruct((count, share), F32),
-            jax.ShapeDtypeStruct((count, width), BF16),
-        ],
-        scratch_shapes=[
-            pltpu.VMEM((count, depth), BF16),
-            pltpu.VMEM((blocks, depth, COLS), BF16),
-            pltpu.VMEM((blocks, width, COLS), BF16),
-            pltpu.SemaphoreType.DMA((8 + 2 * blocks - 1,)),
-        ],
+    out_shape = [jax.ShapeDtypeStruct((count, share), F32)]
+    scratch = [pltpu.VMEM((count, depth), BF16), pltpu.VMEM((blocks, depth, COLS), BF16)]
+    args = [in_hbm(a) for a in (spread, low, high, vectors)]
+    if more:
+        before, expand = more
+        width = expand.shape[1]
+        out_shape.append(jax.ShapeDtypeStruct((count, width), BF16))
+        scratch.insert(0, pltpu.VMEM((width, share), BF16))
+        args += [before, in_hbm(expand)]
+    return pl.pallas_call(
+        functools.partial(top_kernel, half),
+        in_specs=[SMEM] + [HBM] * 4 + [VMEM, HBM][: len(more)],
+        out_specs=[VMEM] * len(out_shape),
+        out_shape=out_shape,
+        scratch_shapes=scratch + [pltpu.SemaphoreType.DMA((3 + blocks + bool(more),))],
         cost_estimate=cost(5e9, 14e6),
         compiler_params=params(),
-        name="top_gradient",
-    )(in_hbm(spread), in_hbm(vectors), in_hbm(expand))
-
-
-def block_kernel(level, own, other, slope, weight, grad, outer, expand, out, *rest):
+        name=f"top_gradient_{half}",
+    )(turned, *args)
+
+
+def block_kernel(level, own, other, slope, weight, grad, outer, *rest):
     last = level == 0
-    pre, shifted, kernel, expander, sems = rest[-5:]
+    if last:
+        out, pre, shifted = rest
+    else:
+        expand, out, send, pre, shifted = rest
     dilation = BASE_DILATION * 2**level
     count, share = out.shape
     trim = HALO_IN[level] - HALO_IN[level - 1]
-    taps = weight.shape[1]
-    columns = column_blocks(share)
-    pairs = [(weight.at[level, :, cols, :], kernel.at[k]) for k, cols in enumerate(columns)]
-    if not last:
-        pairs.append((expand.at[level - 1], expander))
-    copies = fetch(pairs, sems)
+    taps = weight.shape[0]
     pre[...] = (own[...].astype(F32) + other[...].astype(F32)) * slope[...].astype(F32)
     for tap in range(taps):
         start = trim - (tap - 1) * dilation
         shifted[tap] = pre[start : start + count, :].astype(BF16)
     middle = None
-    for k, cols in enumerate(columns):
-        copies[k].wait()
+    for cols in column_blocks(share):
         total = None
         for tap in range(taps):
-            part = lax.dot_general(shifted[tap], kernel[k, tap], NT, preferred_element_type=F32)
+            part = lax.dot_general(
+                shifted[tap], weight[tap, cols, :], NT, preferred_element_type=F32
+            )
             total = part if total is None else total + part
         new = grad[trim : trim + count, cols] + total * outer[:, cols].astype(F32)
         if last:
             out[:, cols] = new.astype(BF16)
             continue
         out[:, cols] = new
-        if k == 0:
-            copies[-1].wait()
-        part = lax.dot_general(
-            new.astype(BF16), expander[:, cols], NT, preferred_element_type=F32
-        )
+        part = lax.dot_general(new.astype(BF16), expand[:, cols], NT, preferred_element_type=F32)
         middle = part if middle is None else middle + part
     if not last:
-        rest[0][...] = middle.astype(BF16)
-
-
-def block_step(level, own, other, slope, weight, grad, outer, expand):
+        send[...] = middle.astype(BF16)
+
+
+def block_step(level, own, other, slope, weight, grad, outer, *expand):
     count_in, width = own.shape
     count, share = outer.shape
-    taps = weight.shape[1]
-    blocks = share // COLS
+    taps = weight.shape[0]
     last = level == 0
     out_shape = [jax.ShapeDtypeStruct((count, share), BF16 if last else F32)]
     if not last:
         out_shape.append(jax.ShapeDtypeStruct((count, width), BF16))
     return pl.pallas_call(
         functools.partial(block_kernel, level),
-        in_specs=[VMEM, VMEM, VMEM, HBM, VMEM, VMEM, HBM],
+        in_specs=[VMEM] * (6 + len(expand)),
         out_specs=[VMEM] * len(out_shape),
         out_shape=out_shape,
         scratch_shapes=[
             pltpu.VMEM((count_in, width), F32),
             pltpu.VMEM((taps, count, width), BF16),
-            pltpu.VMEM((blocks, taps, COLS, width), BF16),
-            pltpu.VMEM((width, share), BF16),
-            pltpu.SemaphoreType.DMA((blocks + 1,)),
         ],
         cost_estimate=cost(5e9, 14e6),
         compiler_params=params(),
         name=f"block_step_{level}",
-    )(own, other, slope, in_hbm(weight), grad, outer, in_hbm(expand))
+    )(own, other, slope, weight, grad, outer, *expand)
 
 
 def after(value, *earlier):
     return lax.optimization_barrier((value, *earlier))[0]
 
 
-def gather_vectors(vectors, meanwhile, later):
+def gather_vectors(vectors, place, meanwhile, later):
     count = vectors.shape[0]
-    place = lax.axis_index("head")
-    along, turn = place // 4, place % 4
+    turn = place % 4
     same = lambda steps: [(a * 4 + z, a * 4 + (z - steps) % 4) for a in range(2) for z in range(4)]
     parts = [lax.ppermute(vectors, "head", same(k)) for k in (1, 2, 3)]
     parts = [after(vectors, *meanwhile)] + parts
     twice = jnp.concatenate(parts + parts, axis=0)
     ring = lax.dynamic_slice_in_dim(twice, (4 - turn) % 4 * count, 4 * count, 0)
     other = lax.ppermute(ring, "head", [(k, (k + 4) % 8) for k in range(8)])
-    ring = after(ring, *later)
-    both = jnp.where(
-        along == 0,
-        jnp.concatenate([ring, other], axis=0),
-        jnp.concatenate([other, ring], axis=0),
-    )
-    return lax.all_gather(both, "pos", tiled=True)
+    near = lax.all_gather(ring, "pos", tiled=True)
+    return near, lax.all_gather(after(other, *later), "pos", tiled=True)
 
 
 def per_device(
@@ -510,39 +515,45 @@
     swap = [(0, 1), (1, 0)]
     levels = list(reversed(range(layers)))
 
+    place = lax.axis_index("head")
+    along, turn = place // 4, place % 4
     vectors = head_vectors(
         chan_place[None].astype(jnp.int32), head_weight, batch_of, erase_left, erase_right, share
     )
     first, final = cut_edges(after(inputs_saved, vectors))
     low = lax.ppermute(final, GROUP_AXES, up)
     high = lax.ppermute(first, GROUP_AXES, down)
+    payload = bucket(cover_bins, bin_gradient, members, rows)
     flags = jnp.stack([member == 0, member == members - 1]).astype(jnp.int32)
     sends, outers, others = {}, {}, {}
-    for n in levels:
-        sends[n], outers[n] = pre_partial(n, inputs_saved, low, high, conv_weight)
+
+    def begin(n, *earlier):
+        sends[n], outers[n] = pre_partial(
+            n, inputs_saved, after(low, *earlier), high, conv_weight
+        )
         others[n] = lax.ppermute(sends[n], "chan", swap)
 
-    payload = bucket(
-        (member % (COLS // SLOTS))[None].astype(jnp.int32), cover_bins, bin_gradient, members, rows
-    )
+    begin(levels[0])
+    near, far = gather_vectors(vectors, place, (payload, first), (sends[levels[0]],))
     arrived = lax.all_to_all(
         after(payload, sends[levels[0]]), GROUP_AXES, split_axis=0, concat_axis=0, tiled=True
     )
-    gathered = gather_vectors(vectors, (payload, low, high), (sends[levels[0]],))
     reach = HALO_IN[layers - 1]
-    spread = spread_entries(after(arrived, *sends.values()), rows, reach)
-    spread_low = lax.ppermute(spread[rows : rows + reach], GROUP_AXES, up)
-    spread_high = lax.ppermute(spread[reach : 2 * reach], GROUP_AXES, down)
-    spread = fill_edges(spread, spread_low, spread_high)
+    spread = spread_entries(along[None].astype(jnp.int32), arrived, rows)
+    spread_low = lax.ppermute(spread[:, rows - reach :], GROUP_AXES, up)
+    spread_high = lax.ppermute(spread[:, :reach], GROUP_AXES, down)
+    begin(levels[1], spread)
+    begin(levels[2], spread, sends[levels[1]])
+    turned = jnp.stack([turn == 0, turn == 3]).astype(jnp.int32)
     slopes = {n: pre_slope(n, flags, sends[n], others[n], rows) for n in levels}
-    spread = after(spread, others[levels[1]], slopes[levels[0]])
-
-    grad, send = top_gradient(spread, gathered, expand_weight)
+    entries = (turned, spread, spread_low, spread_high)
+    (half,) = top_gradient(0, *entries, after(near, sends[levels[2]]))
+    far = after(far, half, others[levels[1]])
+    grad, send = top_gradient(1, *entries, far, half, expand_weight)
     for n in levels:
         other = lax.ppermute(send, "chan", swap)
-        outs = block_step(
-            n, send, other, slopes[n], conv_weight, grad, outers[n], expand_weight
-        )
+        weights = stage_weights(n, after(conv_weight, send), expand_weight)
+        outs = block_step(n, send, other, slopes[n], weights[0], grad, outers[n], *weights[1:])
         if n:
             grad, send = outs
     return outs[0]

time: 208 us -> 215 us (1.034)
  the two profiles are of different devices: /device:TPU:4 before, /device:TPU:8 now
where the time goes in v4:
time: 215 us; the launch traced here: 212 us
  waiting for transfers between devices  78.1 us (36%)
  Pallas kernels  69.3 us (32%)
  starting transfers between devices  41.9 us (19%)
  between operations  13.8 us (6%)
  local copies, waits for them, and re-layouts  7.87 us (4%)
    ppermute x3, waiting for transfers between devices, per_device(): other = lax.ppermute(send, 'chan', swap)  39 us
    pallas_call x3, Pallas kernels, pre_partial(): pl.pallas_call(functools.partial(pre_kernel, level), in_specs=[HBM, VMEM,...  19.7 us
    pallas_call x2, Pallas kernels, top_gradient(): pl.pallas_call(functools.partial(top_kernel, half), in_specs=[SMEM] + [HB...  14.1 us
    ppermute x3, waiting for transfers between devices, begin(): others[n] = lax.ppermute(sends[n], 'chan', swap)  13 us
    pallas_call x3, Pallas kernels, block_step(): pl.pallas_call(functools.partial(block_kernel, level), in_specs=[VMEM] *...  11.8 us
    all_to_all x1, starting transfers between devices, per_device(): lax.all_to_all(after(payload, sends[levels[0]]), GROUP_AXES, split_axis=0...  11.5 us
    ppermute x1, waiting for transfers between devices, per_device(): spread_low = lax.ppermute(spread[:, rows - reach:], GROUP_AXES, up)  10.5 us
    all_to_all x1, waiting for transfers between devices, per_device(): lax.all_to_all(after(payload, sends[levels[0]]), GROUP_AXES, split_axis=0...  7.06 us
  transfers between devices with their start and end apart: 17, of which 10 were waited for; matrix products, arithmetic and copies ran while one was open for 1% of the time, Pallas kernels for 28%

profile of v4, /device:TPU:8, one launch (start us, length us, event | category | flops | bytes accessed | tf_op | source)
XLA Modules:
  0.0 211.8 jit_solution(5669053311923852093)
XLA Ops:
  6.5 0.7 copy-done.7
  7.2 1.8 head_vectors.1
  9.0 4.1 %collective-permute-start.4 = (bf16[64,768]{1,0:T(8,128)(2,1)S(1)}, bf16[64,768]{1,0:T(8,128)(2,1)S(1)}, u32[]{:S(2)}, u32[]{:S(2)}) collective-permute-start(bf16[64,768]{1,0:T(8,128)(2,1)S(1)} %head_vectors.1), channel_id=1, source_target_pairs={{0,6},{2,0},{4,2},{6,4},{8,14},{10,8},{12,10},{14,12},{1,7},{3,1},... | collective-permute-start | bytes 294920 | tf_op jit(solution)/shard_map/ppermute | solution.py:489
  13.1 0.0 collective-permute-start.5
  13.1 1.3 collective-permute-start.6
  14.4 1.1 cut_edges.1
  15.5 1.9 bucket_entries.1
  17.5 2.5 %collective-permute-done.5 = bf16[64,768]{1,0:T(8,128)(2,1)S(1)} collective-permute-done((bf16[64,768]{1,0:T(8,128)(2,1)S(1)}, bf16[64,768]{1,0:T(8,128)(2,1)S(1)}, u32[]{:S(2)}, u32[]{:S(2)}) %collective-permute-start.5) | collective-permute-done | bytes 98336 | tf_op jit(solution)/shard_map/ppermute | solution.py:489
  20.0 0.7 collective-permute-done.6
  20.8 0.8 constant_dynamic-slice_fusion
  21.6 0.0 all-gather.5.cloned.1.call-update
  21.6 0.0 all-gather.3.cloned.1.call-start
  21.6 0.5 collective-permute-start.7
  22.2 1.9 collective-permute-start
  24.1 6.0 %collective-permute-start.1 = (bf16[96,768]{1,0:T(8,128)(2,1)S(1)}, bf16[96,768]{1,0:T(8,128)(2,1)S(1)}, u32[]{:S(2)}, u32[]{:S(2)}) collective-permute-start(bf16[96,768]{1,0:T(8,128)(2,1)S(1)} %get-tuple-element.36), channel_id=1, source_target_pairs={{2,0},{4,2},{6,4},{8,6},{10,8},{12,10},{14,12},{16,14},{18,16},{20... | collective-permute-start | bytes 442376 | tf_op jit(solution)/shard_map/ppermute | solution.py:525
  30.1 5.3 %collective-permute-done.low = bf16[96,768]{1,0:T(8,128)(2,1)S(1)} collective-permute-done((bf16[96,768]{1,0:T(8,128)(2,1)S(1)}, bf16[96,768]{1,0:T(8,128)(2,1)S(1)}, u32[]{:S(2)}, u32[]{:S(2)}) %collective-permute-start) | collective-permute-done | bytes 147488 | tf_op jit(solution)/shard_map/ppermute | solution.py:524
  35.4 0.0 collective-permute-done.1.high
  35.4 7.0 %pre_partial_2.1 = (bf16[576,768]{1,0:T(8,128)(2,1)}, bf16[544,768]{1,0:T(8,128)(2,1)S(1)}) custom-call(bf16[3,512,768]{2,1,0:T(8,128)(2,1)} %saved.6, bf16[96,768]{1,0:T(8,128)(2,1)S(1)} %collective-permute-done.low, bf16[96,768]{1,0:T(8,128)(2,1)S(1)} %collective-permute-done.1.high, bf16[3,3,768,768]{3,2,1,0:T(8,128)(2,1)} %refs_0_.2), custom_call_target="tpu_custom_call" | custom-call | flops 1000000000 | bytes 1600000 | tf_op jit(solution)/shard_map/pre_partial_2/pallas_call | solution.py:316
  42.4 1.0 copy-done.1
  43.4 0.0 collective-permute-done.7
  43.4 0.7 copy-done.17
  44.1 0.0 all-gather.3.cloned.1.call-update
  44.2 0.5 broadcast.3
  44.7 0.7 reduce
  45.3 0.6 reshape.2
  46.0 11.5 %all-to-all-start = ((bf16[64,2,128]{2,1,0:T(2,128)(2,1)}), bf16[64,2,128]{2,1,0:T(2,128)(2,1)S(1)}, u32[]{:S(2)}, u32[]{:S(2)}) async-start(bf16[64,2,128]{2,1,0:T(2,128)(2,1)} %reshape.2), calls=%async_computation | async-start | bytes 65536 | tf_op jit(solution)/shard_map/all_to_all | solution.py:538
  57.4 7.1 %all-to-all-done = bf16[64,2,128]{2,1,0:T(2,128)(2,1)S(1)} async-done(((bf16[64,2,128]{2,1,0:T(2,128)(2,1)}), bf16[64,2,128]{2,1,0:T(2,128)(2,1)S(1)}, u32[]{:S(2)}, u32[]{:S(2)}) %all-to-all-start) | async-done | bytes 32800 | tf_op jit(solution)/shard_map/all_to_all | solution.py:538
  64.5 5.6 %spread_entries.1.spread = bf16[2,512,2048]{2,1,0:T(8,128)(2,1)S(1)} custom-call(s32[1]{0:T(128)} %bitcast.2.along, bf16[64,256]{1,0:T(8,128)(2,1)S(1)} %bitcast.15), custom_call_target="tpu_custom_call" | custom-call | flops 1200000000 | bytes 1600000 | tf_op jit(solution)/shard_map/spread_entries/pallas_call | solution.py:204
  70.1 6.8 %pre_partial_1.1 = (bf16[544,768]{1,0:T(8,128)(2,1)S(1)}, bf16[528,768]{1,0:T(8,128)(2,1)S(1)}) custom-call(bf16[3,512,768]{2,1,0:T(8,128)(2,1)} %saved.6, bf16[96,768]{1,0:T(8,128)(2,1)S(1)} %collective-permute-done.low, bf16[96,768]{1,0:T(8,128)(2,1)S(1)} %collective-permute-done.1.high, bf16[3,3,768,768]{3,2,1,0:T(8,128)(2,1)} %refs_0_.2), custom_call_target="tpu_custom_call" | custom-call | flops 1000000000 | bytes 1600000 | tf_op jit(solution)/shard_map/pre_partial_1/pallas_call | solution.py:316
  76.9 2.3 %collective-permute-start.8 = (bf16[544,768]{1,0:T(8,128)(2,1)S(1)}, bf16[544,768]{1,0:T(8,128)(2,1)S(1)}, u32[]{:S(2)}, u32[]{:S(2)}) collective-permute-start(bf16[544,768]{1,0:T(8,128)(2,1)S(1)} %get-tuple-element.42.own), channel_id=1, source_target_pairs={{0,1},{1,0},{2,3},{3,2},{4,5},{5,4},{6,7},{7,6},{8,9},{9,8},{10,11... | collective-permute-start | bytes 2506760 | tf_op jit(solution)/shard_map/ppermute | solution.py:534
  79.3 2.5 %collective-permute-start.2 = (bf16[2,32,2048]{2,1,0:T(8,128)(2,1)S(1)}, bf16[2,32,2048]{2,1,0:T(8,128)(2,1)S(1)}, u32[]{:S(2)}, u32[]{:S(2)}) collective-permute-start(bf16[2,32,2048]{2,1,0:T(8,128)(2,1)S(1)} %get-tuple-element.64), channel_id=1, source_target_pairs={{0,2},{2,4},{4,6},{6,8},{8,10},{10,12},{12,14},{14,16},{16,18},{18... | collective-permute-start | bytes 786440 | tf_op jit(solution)/shard_map/ppermute | solution.py:543
  81.8 5.5 %collective-permute-start.3 = (bf16[2,32,2048]{2,1,0:T(8,128)(2,1)S(1)}, bf16[2,32,2048]{2,1,0:T(8,128)(2,1)}, u32[]{:S(2)}, u32[]{:S(2)}) collective-permute-start(bf16[2,32,2048]{2,1,0:T(8,128)(2,1)S(1)} %get-tuple-element.63), channel_id=1, source_target_pairs={{2,0},{4,2},{6,4},{8,6},{10,8},{12,10},{14,12},{16,14},{18,16},{20... | collective-permute-start | bytes 786440 | tf_op jit(solution)/shard_map/ppermute | solution.py:544
  87.3 0.1 add_convert_fusion.turned
  87.4 1.5 collective-permute-start.10
  88.8 5.9 %pre_partial_0.1 = (bf16[528,768]{1,0:T(8,128)(2,1)S(1)}, bf16[512,768]{1,0:T(8,128)(2,1)S(1)}) custom-call(bf16[3,512,768]{2,1,0:T(8,128)(2,1)} %saved.6, bf16[96,768]{1,0:T(8,128)(2,1)S(1)} %collective-permute-done.low, bf16[96,768]{1,0:T(8,128)(2,1)S(1)} %collective-permute-done.1.high, bf16[3,3,768,768]{3,2,1,0:T(8,128)(2,1)} %refs_0_.2), custom_call_target="tpu_custom_call" | custom-call | flops 1000000000 | bytes 1600000 | tf_op jit(solution)/shard_map/pre_partial_0/pallas_call | solution.py:316
  94.8 0.0 copy-start.5
  94.8 0.9 copy-done.5
  95.7 0.9 copy-done.12
  96.6 10.5 %collective-permute-done.2.low = bf16[2,32,2048]{2,1,0:T(8,128)(2,1)S(1)} collective-permute-done((bf16[2,32,2048]{2,1,0:T(8,128)(2,1)S(1)}, bf16[2,32,2048]{2,1,0:T(8,128)(2,1)S(1)}, u32[]{:S(2)}, u32[]{:S(2)}) %collective-permute-start.2) | collective-permute-done | bytes 262176 | tf_op jit(solution)/shard_map/ppermute | solution.py:543
  107.0 0.7 copy-done.16
  107.7 6.0 %top_gradient_0.1.rest_0_ = f32[576,768]{1,0:T(8,128)S(1)} custom-call(s32[2]{0:T(128)S(1)} %add_convert_fusion.turned, bf16[2,512,2048]{2,1,0:T(8,128)(2,1)} %copy-done, bf16[2,32,2048]{2,1,0:T(8,128)(2,1)} %copy-done.16, bf16[2,32,2048]{2,1,0:T(8,128)(2,1)} %collective-permute-done.3.high, bf16[2048,768]{1,0:T(8,128)(2,1)} %all-gather.5.cloned.1.call-done.vectors), custom_call_target="tpu_custom_call" | custom-call | flops 1000000000 | bytes 2800000 | tf_op jit(solution)/shard_map/top_gradient_0/pallas_call | solution.py:413
  113.8 0.0 collective-permute-done.8.other
  113.8 0.9 copy-done.10
  114.7 8.1 %top_gradient_1.1 = (f32[576,768]{1,0:T(8,128)S(1)}, bf16[576,768]{1,0:T(8,128)(2,1)}) custom-call(s32[2]{0:T(128)S(1)} %add_convert_fusion.turned, bf16[2,512,2048]{2,1,0:T(8,128)(2,1)} %copy-done, bf16[2,32,2048]{2,1,0:T(8,128)(2,1)} %copy-done.16, bf16[2,32,2048]{2,1,0:T(8,128)(2,1)} %collective-permute-done.3.high, ...), custom_call_target="tpu_custom_call" | custom-call | flops 1000000000 | bytes 2800000 | tf_op jit(solution)/shard_map/top_gradient_1/pallas_call | solution.py:413
  122.8 0.1 collective-permute-start.9
  123.0 0.1 add_convert_fusion.1.flags
  123.1 0.4 collective-permute-done.10.other
  123.4 3.3 %pre_slope_2.1.slope = bf16[576,768]{1,0:T(8,128)(2,1)S(1)} custom-call(s32[2]{0:T(128)S(1)} %add_convert_fusion.1.flags, bf16[576,768]{1,0:T(8,128)(2,1)} %get-tuple-element.37.own, bf16[576,768]{1,0:T(8,128)(2,1)} %collective-permute-done.10.other), custom_call_target="tpu_custom_call" | custom-call | flops 800000000 | bytes 1000000 | tf_op jit(solution)/shard_map/pre_slope_2/pallas_call | solution.py:348
  126.7 2.4 %stage_weights_2.1 = (bf16[3,768,768]{2,1,0:T(8,128)(2,1)S(1)}, bf16[768,768]{1,0:T(8,128)(2,1)S(1)}) custom-call(bf16[3,3,768,768]{3,2,1,0:T(8,128)(2,1)} %refs_0_.2, bf16[3,768,768]{2,1,0:T(8,128)(2,1)} %refs_1_.3), custom_call_target="tpu_custom_call" | custom-call | flops 200000000 | bytes 200000 | tf_op jit(solution)/shard_map/stage_weights_2/pallas_call | solution.py:230
  129.2 14.4 %collective-permute-done.9.other = bf16[576,768]{1,0:T(8,128)(2,1)S(1)} collective-permute-done((bf16[576,768]{1,0:T(8,128)(2,1)}, bf16[576,768]{1,0:T(8,128)(2,1)S(1)}, u32[]{:S(2)}, u32[]{:S(2)}) %collective-permute-start.9) | collective-permute-done | bytes 884768 | tf_op jit(solution)/shard_map/ppermute | solution.py:554
  143.6 5.1 %block_step_2.1 = (f32[544,768]{1,0:T(8,128)S(1)}, bf16[544,768]{1,0:T(8,128)(2,1)S(1)}) custom-call(bf16[576,768]{1,0:T(8,128)(2,1)} %get-tuple-element.47.own, bf16[576,768]{1,0:T(8,128)(2,1)S(1)} %collective-permute-done.9.other, bf16[576,768]{1,0:T(8,128)(2,1)S(1)} %pre_slope_2.1.slope, bf16[3,768,768]{2,1,0:T(8,128)(2,1)S(1)} %get-tuple-element.49.weight, ...), custom_call_target="tpu_custom_call" | custom-call | flops 1000000000 | bytes 2800000 | tf_op jit(solution)/shard_map/block_step_2/pallas_call | solution.py:466
  148.6 1.1 collective-permute-start.11
  149.7 2.5 %collective-permute-start.13 = (bf16[528,768]{1,0:T(8,128)(2,1)S(1)}, bf16[528,768]{1,0:T(8,128)(2,1)S(1)}, u32[]{:S(2)}, u32[]{:S(2)}) collective-permute-start(bf16[528,768]{1,0:T(8,128)(2,1)S(1)} %copy-done.13), channel_id=1, source_target_pairs={{0,1},{1,0},{2,3},{3,2},{4,5},{5,4},{6,7},{7,6},{8,9},{9,8},{10,11... | collective-permute-start | bytes 2433032 | tf_op jit(solution)/shard_map/ppermute | solution.py:534
  152.3 1.6 pre_slope_1.1.slope
  153.8 2.4 %stage_weights_1.1 = (bf16[3,768,768]{2,1,0:T(8,128)(2,1)S(1)}, bf16[768,768]{1,0:T(8,128)(2,1)S(1)}) custom-call(bf16[3,3,768,768]{3,2,1,0:T(8,128)(2,1)} %refs_0_.2, bf16[3,768,768]{2,1,0:T(8,128)(2,1)} %refs_1_.3), custom_call_target="tpu_custom_call" | custom-call | flops 200000000 | bytes 200000 | tf_op jit(solution)/shard_map/stage_weights_1/pallas_call | solution.py:230
  156.3 15.5 %collective-permute-done.11.other = bf16[544,768]{1,0:T(8,128)(2,1)S(1)} collective-permute-done((bf16[544,768]{1,0:T(8,128)(2,1)S(1)}, bf16[544,768]{1,0:T(8,128)(2,1)S(1)}, u32[]{:S(2)}, u32[]{:S(2)}) %collective-permute-start.11) | collective-permute-done | bytes 835616 | tf_op jit(solution)/shard_map/ppermute | solution.py:554
  171.8 3.7 %block_step_1.1 = (f32[528,768]{1,0:T(8,128)S(1)}, bf16[528,768]{1,0:T(8,128)(2,1)S(1)}) custom-call(bf16[544,768]{1,0:T(8,128)(2,1)S(1)} %get-tuple-element.53.own, bf16[544,768]{1,0:T(8,128)(2,1)S(1)} %collective-permute-done.11.other, bf16[544,768]{1,0:T(8,128)(2,1)S(1)} %pre_slope_1.1.slope, bf16[3,768,768]{2,1,0:T(8,128)(2,1)S(1)} %get-tuple-element.55.weight, ...), custom_call_target="tpu_custom_call" | custom-call | flops 1000000000 | bytes 2800000 | tf_op jit(solution)/shard_map/block_step_1/pallas_call | solution.py:466
  175.4 1.1 collective-permute-start.12
  176.5 12.6 %collective-permute-done.13.other = bf16[528,768]{1,0:T(8,128)(2,1)S(1)} collective-permute-done((bf16[528,768]{1,0:T(8,128)(2,1)S(1)}, bf16[528,768]{1,0:T(8,128)(2,1)S(1)}, u32[]{:S(2)}, u32[]{:S(2)}) %collective-permute-start.13) | collective-permute-done | bytes 811040 | tf_op jit(solution)/shard_map/ppermute | solution.py:534
  189.1 1.5 pre_slope_0.1.slope
  190.7 0.0 copy-start.6
  190.7 2.1 stage_weights_0.1.weight
  192.8 9.1 %collective-permute-done.12.other = bf16[528,768]{1,0:T(8,128)(2,1)S(1)} collective-permute-done((bf16[528,768]{1,0:T(8,128)(2,1)S(1)}, bf16[528,768]{1,0:T(8,128)(2,1)S(1)}, u32[]{:S(2)}, u32[]{:S(2)}) %collective-permute-start.12) | collective-permute-done | bytes 811040 | tf_op jit(solution)/shard_map/ppermute | solution.py:554
  201.9 3.1 %block_step_0.1 = bf16[512,768]{1,0:T(8,128)(2,1)} custom-call(bf16[528,768]{1,0:T(8,128)(2,1)S(1)} %get-tuple-element.59.own, bf16[528,768]{1,0:T(8,128)(2,1)S(1)} %collective-permute-done.12.other, bf16[528,768]{1,0:T(8,128)(2,1)S(1)} %pre_slope_0.1.slope, bf16[3,768,768]{2,1,0:T(8,128)(2,1)S(1)} %stage_weights_0.1.weight, ...), custom_call_target="tpu_custom_call" | custom-call | flops 1000000000 | bytes 2800000 | tf_op jit(solution)/shard_map/block_step_0/pallas_call | solution.py:466
  (43 shorter events, 0.2 us)
Async XLA Ops:
  6.5 8.9 %copy-start.15 = (bf16[64,32]{0,1:T(8,128)(2,1)S(1)}, bf16[64,32]{0,1:T(8,128)(2,1)}, u32[]{:S(2)}) copy-start(bf16[64,32]{0,1:T(8,128)(2,1)} %param.16) | copy-start | bytes 12292
  6.5 90.0 %all-gather.5.cloned.1.call-start = ((), (), s32[]{:S(2)}) async-start(), calls=%async_computation.2 | async-start | bytes 3538944 | tf_op jit(solution)/shard_map/all_gather | solution.py:494
  6.5 0.7 copy-start.7
  7.2 8.3 %copy-start.14 = (s32[64,32]{0,1:T(8,128)S(1)}, s32[64,32]{0,1:T(8,128)}, u32[]{:S(2)}) copy-start(s32[64,32]{0,1:T(8,128)} %param.17) | copy-start | bytes 24580
  9.0 8.4 %collective-permute-start.4 = (bf16[64,768]{1,0:T(8,128)(2,1)S(1)}, bf16[64,768]{1,0:T(8,128)(2,1)S(1)}, u32[]{:S(2)}, u32[]{:S(2)}) collective-permute-start(bf16[64,768]{1,0:T(8,128)(2,1)S(1)} %head_vectors.1), channel_id=1, source_target_pairs={{0,6},{2,0},{4,2},{6,4},{8,14},{10,8},{12,10},{14,12},{1,7},{3,1},... | collective-permute-start | bytes 294920 | tf_op jit(solution)/shard_map/ppermute | solution.py:489
  13.1 6.9 %collective-permute-start.5 = (bf16[64,768]{1,0:T(8,128)(2,1)S(1)}, bf16[64,768]{1,0:T(8,128)(2,1)S(1)}, u32[]{:S(2)}, u32[]{:S(2)}) collective-permute-start(bf16[64,768]{1,0:T(8,128)(2,1)S(1)} %head_vectors.1), channel_id=1, source_target_pairs={{0,4},{2,6},{4,0},{6,2},{8,12},{10,14},{12,8},{14,10},{1,5},{3,7},... | collective-permute-start | bytes 294920 | tf_op jit(solution)/shard_map/ppermute | solution.py:489
  13.1 7.6 %collective-permute-start.6 = (bf16[64,768]{1,0:T(8,128)(2,1)S(1)}, bf16[64,768]{1,0:T(8,128)(2,1)S(1)}, u32[]{:S(2)}, u32[]{:S(2)}) collective-permute-start(bf16[64,768]{1,0:T(8,128)(2,1)S(1)} %head_vectors.1), channel_id=1, source_target_pairs={{0,2},{2,4},{4,6},{6,0},{8,10},{10,12},{12,14},{14,8},{1,3},{3,5},... | collective-permute-start | bytes 294920 | tf_op jit(solution)/shard_map/ppermute | solution.py:489
  21.6 93.1 %all-gather.3.cloned.1.call-start = ((), (), s32[]{:S(2)}) async-start(), calls=%async_computation.1 | async-start | bytes 3538944 | tf_op jit(solution)/shard_map/all_gather | solution.py:495
  21.6 21.8 %collective-permute-start.7 = (bf16[256,768]{1,0:T(8,128)(2,1)}, bf16[256,768]{1,0:T(8,128)(2,1)S(1)}, u32[]{:S(2)}, u32[]{:S(2)}) collective-permute-start(bf16[256,768]{1,0:T(8,128)(2,1)} %constant_dynamic-slice_fusion), channel_id=1, source_target_pairs={{0,8},{2,10},{4,12},{6,14},{8,0},{10,2},{12,4},{14,6},{1,9},{3,11}... | collective-permute-start | bytes 1179656 | tf_op jit(solution)/shard_map/ppermute | solution.py:493
  22.2 13.3 %collective-permute-start = (bf16[96,768]{1,0:T(8,128)(2,1)S(1)}, bf16[96,768]{1,0:T(8,128)(2,1)S(1)}, u32[]{:S(2)}, u32[]{:S(2)}) collective-permute-start(bf16[96,768]{1,0:T(8,128)(2,1)S(1)} %get-tuple-element.35), channel_id=1, source_target_pairs={{0,2},{2,4},{4,6},{6,8},{8,10},{10,12},{12,14},{14,16},{16,18},{18... | collective-permute-start | bytes 442376 | tf_op jit(solution)/shard_map/ppermute | solution.py:524
  24.1 11.4 %collective-permute-start.1 = (bf16[96,768]{1,0:T(8,128)(2,1)S(1)}, bf16[96,768]{1,0:T(8,128)(2,1)S(1)}, u32[]{:S(2)}, u32[]{:S(2)}) collective-permute-start(bf16[96,768]{1,0:T(8,128)(2,1)S(1)} %get-tuple-element.36), channel_id=1, source_target_pairs={{2,0},{4,2},{6,4},{8,6},{10,8},{12,10},{14,12},{16,14},{18,16},{20... | collective-permute-start | bytes 442376 | tf_op jit(solution)/shard_map/ppermute | solution.py:525
  42.4 1.0 copy-start.1
  43.4 0.7 copy-start.17
  46.0 18.5 %all-to-all-start = ((bf16[64,2,128]{2,1,0:T(2,128)(2,1)}), bf16[64,2,128]{2,1,0:T(2,128)(2,1)S(1)}, u32[]{:S(2)}, u32[]{:S(2)}) async-start(bf16[64,2,128]{2,1,0:T(2,128)(2,1)} %reshape.2), calls=%async_computation | async-start | bytes 65536 | tf_op jit(solution)/shard_map/all_to_all | solution.py:538
  70.1 9.2 %copy-start = (bf16[2,512,2048]{2,1,0:T(8,128)(2,1)}, bf16[2,512,2048]{2,1,0:T(8,128)(2,1)S(1)}, u32[]{:S(2)}) copy-start(bf16[2,512,2048]{2,1,0:T(8,128)(2,1)S(1)} %spread_entries.1.spread) | copy-start | bytes 12582916
  76.9 2.4 %copy-start.3 = (bf16[528,768]{1,0:T(8,128)(2,1)}, bf16[528,768]{1,0:T(8,128)(2,1)S(1)}, u32[]{:S(2)}) copy-start(bf16[528,768]{1,0:T(8,128)(2,1)S(1)} %get-tuple-element.57.outer) | copy-start | bytes 2433028
  76.9 17.9 %copy-start.8 = (bf16[544,768]{1,0:T(8,128)(2,1)}, bf16[544,768]{1,0:T(8,128)(2,1)S(1)}, u32[]{:S(2)}) copy-start(bf16[544,768]{1,0:T(8,128)(2,1)S(1)} %get-tuple-element.42.own) | copy-start | bytes 2506756
  76.9 36.9 %collective-permute-start.8 = (bf16[544,768]{1,0:T(8,128)(2,1)S(1)}, bf16[544,768]{1,0:T(8,128)(2,1)S(1)}, u32[]{:S(2)}, u32[]{:S(2)}) collective-permute-start(bf16[544,768]{1,0:T(8,128)(2,1)S(1)} %get-tuple-element.42.own), channel_id=1, source_target_pairs={{0,1},{1,0},{2,3},{3,2},{4,5},{5,4},{6,7},{7,6},{8,9},{9,8},{10,11... | collective-permute-start | bytes 2506760 | tf_op jit(solution)/shard_map/ppermute | solution.py:534
  79.3 27.7 %collective-permute-start.2 = (bf16[2,32,2048]{2,1,0:T(8,128)(2,1)S(1)}, bf16[2,32,2048]{2,1,0:T(8,128)(2,1)S(1)}, u32[]{:S(2)}, u32[]{:S(2)}) collective-permute-start(bf16[2,32,2048]{2,1,0:T(8,128)(2,1)S(1)} %get-tuple-element.64), channel_id=1, source_target_pairs={{0,2},{2,4},{4,6},{6,8},{8,10},{10,12},{12,14},{14,16},{16,18},{18... | collective-permute-start | bytes 786440 | tf_op jit(solution)/shard_map/ppermute | solution.py:543
  81.8 25.9 %collective-permute-start.3 = (bf16[2,32,2048]{2,1,0:T(8,128)(2,1)S(1)}, bf16[2,32,2048]{2,1,0:T(8,128)(2,1)}, u32[]{:S(2)}, u32[]{:S(2)}) collective-permute-start(bf16[2,32,2048]{2,1,0:T(8,128)(2,1)S(1)} %get-tuple-element.63), channel_id=1, source_target_pairs={{2,0},{4,2},{6,4},{8,6},{10,8},{12,10},{14,12},{16,14},{18,16},{20... | collective-permute-start | bytes 786440 | tf_op jit(solution)/shard_map/ppermute | solution.py:544
  87.4 36.1 %collective-permute-start.10 = (bf16[576,768]{1,0:T(8,128)(2,1)}, bf16[576,768]{1,0:T(8,128)(2,1)}, u32[]{:S(2)}, u32[]{:S(2)}) collective-permute-start(bf16[576,768]{1,0:T(8,128)(2,1)} %get-tuple-element.37.own), channel_id=1, source_target_pairs={{0,1},{1,0},{2,3},{3,2},{4,5},{5,4},{6,7},{7,6},{8,9},{9,8},{10,11... | collective-permute-start | bytes 2654216 | tf_op jit(solution)/shard_map/ppermute | solution.py:534
  94.8 0.9 copy-start.5
  95.7 0.9 copy-start.12
  107.0 0.7 copy-start.16
  113.8 0.9 copy-start.10
  122.8 20.7 %collective-permute-start.9 = (bf16[576,768]{1,0:T(8,128)(2,1)}, bf16[576,768]{1,0:T(8,128)(2,1)S(1)}, u32[]{:S(2)}, u32[]{:S(2)}) collective-permute-start(bf16[576,768]{1,0:T(8,128)(2,1)} %get-tuple-element.47.own), channel_id=1, source_target_pairs={{0,1},{1,0},{2,3},{3,2},{4,5},{5,4},{6,7},{7,6},{8,9},{9,8},{10,11... | collective-permute-start | bytes 2654216 | tf_op jit(solution)/shard_map/ppermute | solution.py:554
  126.7 16.8 %copy-start.2 = (bf16[544,768]{1,0:T(8,128)(2,1)S(1)}, bf16[544,768]{1,0:T(8,128)(2,1)}, u32[]{:S(2)}) copy-start(bf16[544,768]{1,0:T(8,128)(2,1)} %copy-done.1) | copy-start | bytes 2506756
  143.5 6.2 %copy-start.13 = (bf16[528,768]{1,0:T(8,128)(2,1)S(1)}, bf16[528,768]{1,0:T(8,128)(2,1)}, u32[]{:S(2)}) copy-start(bf16[528,768]{1,0:T(8,128)(2,1)} %copy-done.12) | copy-start | bytes 2433028
  143.6 8.7 %copy-start.9 = (bf16[544,768]{1,0:T(8,128)(2,1)S(1)}, bf16[544,768]{1,0:T(8,128)(2,1)}, u32[]{:S(2)}) copy-start(bf16[544,768]{1,0:T(8,128)(2,1)} %copy-done.8) | copy-start | bytes 2506756
  143.6 8.7 %copy-start.11 = (bf16[544,768]{1,0:T(8,128)(2,1)S(1)}, bf16[544,768]{1,0:T(8,128)(2,1)}, u32[]{:S(2)}) copy-start(bf16[544,768]{1,0:T(8,128)(2,1)} %copy-done.10) | copy-start | bytes 2506756
  148.6 23.1 %collective-permute-start.11 = (bf16[544,768]{1,0:T(8,128)(2,1)S(1)}, bf16[544,768]{1,0:T(8,128)(2,1)S(1)}, u32[]{:S(2)}, u32[]{:S(2)}) collective-permute-start(bf16[544,768]{1,0:T(8,128)(2,1)S(1)} %get-tuple-element.53.own), channel_id=1, source_target_pairs={{0,1},{1,0},{2,3},{3,2},{4,5},{5,4},{6,7},{7,6},{8,9},{9,8},{10,11... | collective-permute-start | bytes 2506760 | tf_op jit(solution)/shard_map/ppermute | solution.py:554
  149.7 39.4 %collective-permute-start.13 = (bf16[528,768]{1,0:T(8,128)(2,1)S(1)}, bf16[528,768]{1,0:T(8,128)(2,1)S(1)}, u32[]{:S(2)}, u32[]{:S(2)}) collective-permute-start(bf16[528,768]{1,0:T(8,128)(2,1)S(1)} %copy-done.13), channel_id=1, source_target_pairs={{0,1},{1,0},{2,3},{3,2},{4,5},{5,4},{6,7},{7,6},{8,9},{9,8},{10,11... | collective-permute-start | bytes 2433032 | tf_op jit(solution)/shard_map/ppermute | solution.py:534
  153.8 17.9 %copy-start.4 = (bf16[528,768]{1,0:T(8,128)(2,1)S(1)}, bf16[528,768]{1,0:T(8,128)(2,1)}, u32[]{:S(2)}) copy-start(bf16[528,768]{1,0:T(8,128)(2,1)} %copy-done.3) | copy-start | bytes 2433028
  175.4 26.5 %collective-permute-start.12 = (bf16[528,768]{1,0:T(8,128)(2,1)S(1)}, bf16[528,768]{1,0:T(8,128)(2,1)S(1)}, u32[]{:S(2)}, u32[]{:S(2)}) collective-permute-start(bf16[528,768]{1,0:T(8,128)(2,1)S(1)} %get-tuple-element.59.own), channel_id=1, source_target_pairs={{0,1},{1,0},{2,3},{3,2},{4,5},{5,4},{6,7},{7,6},{8,9},{9,8},{10,11... | collective-permute-start | bytes 2433032 | tf_op jit(solution)/shard_map/ppermute | solution.py:554
  190.7 11.2 %copy-start.6 = (bf16[512,768]{1,0:T(8,128)(2,1)S(1)}, bf16[512,768]{1,0:T(8,128)(2,1)}, u32[]{:S(2)}) copy-start(bf16[512,768]{1,0:T(8,128)(2,1)} %copy-done.5) | copy-start | bytes 2359300
Sparse Core Ops, SparseCore 0:
  21.7 26.8 all-gather.4
  50.3 27.7 all-gather.2

commit v5 on v4

--- a/solution.py
+++ b/solution.py
@@ -22,7 +22,7 @@
 
 def cost(flops, bytes_accessed, transcendentals=0):
     return pl.CostEstimate(
-        flops=int(flops / 5), bytes_accessed=int(bytes_accessed / 5), transcendentals=0
+        flops=int(flops / 100), bytes_accessed=int(bytes_accessed / 100), transcendentals=0
     )
 
 
@@ -357,69 +357,65 @@
     )(flags, own, other)
 
 
-def top_kernel(half, turned, spread, low, high, vectors, *rest):
-    matrix, held, sems = rest[-3:]
-    last = half == 1
-    if last:
-        before, expand, grad, send, kernel = rest[:-3]
-    else:
-        (grad,) = rest[:-3]
+def top_kernel(turned, spread, low, high, vectors, expand, grad, send, matrix, held, kernel, sems):
     rows, reach = spread.shape[1], low.shape[1]
     columns = column_blocks(grad.shape[1])
-    pairs = [
-        (spread.at[half], matrix.at[pl.ds(reach, rows), :]),
-        (low.at[(half + turned[0]) % 2], matrix.at[pl.ds(0, reach), :]),
-        (high.at[(half + turned[1]) % 2], matrix.at[pl.ds(reach + rows, reach), :]),
-    ]
-    pairs += [(vectors.at[:, cols], held.at[k]) for k, cols in enumerate(columns)]
-    if last:
-        pairs.append((expand.at[expand.shape[0] - 1], kernel))
-    copies = fetch(pairs, sems)
-    for copy in copies[:3]:
-        copy.wait()
+    pairs = []
+    for k, cols in enumerate(columns):
+        for half in range(2):
+            if k == 0:
+                pairs += [
+                    (spread.at[half], matrix.at[half, pl.ds(reach, rows), :]),
+                    (low.at[(half + turned[0]) % 2], matrix.at[half, pl.ds(0, reach), :]),
+                    (
+                        high.at[(half + turned[1]) % 2],
+                        matrix.at[half, pl.ds(reach + rows, reach), :],
+                    ),
+                ]
+            pairs.append((vectors.at[:, half, :, cols], held.at[k, half]))
+        pairs.append((expand.at[expand.shape[0] - 1, :, cols], kernel.at[k]))
+    copies = iter(fetch(pairs, sems))
     middle = None
     for k, cols in enumerate(columns):
-        copies[3 + k].wait()
-        top = jnp.dot(matrix[...], held[k], preferred_element_type=F32)
-        if not last:
-            grad[:, cols] = top
-            continue
-        top = top + before[:, cols]
+        top = None
+        for half in range(2):
+            for _ in range(1 if k else 4):
+                next(copies).wait()
+            these = held[k, half].reshape(matrix.shape[2], COLS)
+            piece = jnp.dot(matrix[half], these, preferred_element_type=F32)
+            top = piece if top is None else top + piece
         grad[:, cols] = top
-        if k == 0:
-            copies[-1].wait()
-        piece = lax.dot_general(
-            top.astype(BF16), kernel[:, cols], NT, preferred_element_type=F32
-        )
+        next(copies).wait()
+        piece = lax.dot_general(top.astype(BF16), kernel[k], NT, preferred_element_type=F32)
         middle = piece if middle is None else middle + piece
-    if last:
-        send[...] = middle.astype(BF16)
-
-
-def top_gradient(half, turned, spread, low, high, vectors, *more):
+    send[...] = middle.astype(BF16)
+
+
+def top_gradient(turned, spread, low, high, vectors, expand):
     _, rows, depth = spread.shape
     count = rows + 2 * low.shape[1]
     share = vectors.shape[1]
+    width = expand.shape[1]
     blocks = share // COLS
-    out_shape = [jax.ShapeDtypeStruct((count, share), F32)]
-    scratch = [pltpu.VMEM((count, depth), BF16), pltpu.VMEM((blocks, depth, COLS), BF16)]
-    args = [in_hbm(a) for a in (spread, low, high, vectors)]
-    if more:
-        before, expand = more
-        width = expand.shape[1]
-        out_shape.append(jax.ShapeDtypeStruct((count, width), BF16))
-        scratch.insert(0, pltpu.VMEM((width, share), BF16))
-        args += [before, in_hbm(expand)]
-    return pl.pallas_call(
-        functools.partial(top_kernel, half),
-        in_specs=[SMEM] + [HBM] * 4 + [VMEM, HBM][: len(more)],
-        out_specs=[VMEM] * len(out_shape),
-        out_shape=out_shape,
-        scratch_shapes=scratch + [pltpu.SemaphoreType.DMA((3 + blocks + bool(more),))],
+    vectors = vectors.reshape(depth // SLOTS, 2, SLOTS, share)
+    return pl.pallas_call(
+        top_kernel,
+        in_specs=[SMEM] + [HBM] * 5,
+        out_specs=[VMEM, VMEM],
+        out_shape=[
+            jax.ShapeDtypeStruct((count, share), F32),
+            jax.ShapeDtypeStruct((count, width), BF16),
+        ],
+        scratch_shapes=[
+            pltpu.VMEM((2, count, depth), BF16),
+            pltpu.VMEM((blocks, 2, depth // SLOTS, SLOTS, COLS), BF16),
+            pltpu.VMEM((blocks, width, COLS), BF16),
+            pltpu.SemaphoreType.DMA((6 + 3 * blocks,)),
+        ],
         cost_estimate=cost(5e9, 14e6),
         compiler_params=params(),
-        name=f"top_gradient_{half}",
-    )(turned, *args)
+        name="top_gradient",
+    )(turned, *[in_hbm(a) for a in (spread, low, high, vectors, expand)])
 
 
 def block_kernel(level, own, other, slope, weight, grad, outer, *rest):
@@ -482,17 +478,16 @@
     return lax.optimization_barrier((value, *earlier))[0]
 
 
-def gather_vectors(vectors, place, meanwhile, later):
+def along_head(vectors, place, first, second):
     count = vectors.shape[0]
     turn = place % 4
     same = lambda steps: [(a * 4 + z, a * 4 + (z - steps) % 4) for a in range(2) for z in range(4)]
-    parts = [lax.ppermute(vectors, "head", same(k)) for k in (1, 2, 3)]
-    parts = [after(vectors, *meanwhile)] + parts
+    other = lax.ppermute(vectors, "head", [(k, (k + 4) % 8) for k in range(8)])
+    both = jnp.concatenate([after(vectors, *first), other], axis=0)
+    parts = [lax.ppermute(both, "head", same(k)) for k in (1, 2, 3)]
+    parts = [after(both, *second)] + parts
     twice = jnp.concatenate(parts + parts, axis=0)
-    ring = lax.dynamic_slice_in_dim(twice, (4 - turn) % 4 * count, 4 * count, 0)
-    other = lax.ppermute(ring, "head", [(k, (k + 4) % 8) for k in range(8)])
-    near = lax.all_gather(ring, "pos", tiled=True)
-    return near, lax.all_gather(after(other, *later), "pos", tiled=True)
+    return lax.dynamic_slice_in_dim(twice, (4 - turn) % 4 * 2 * count, 8 * count, 0)
 
 
 def per_device(
@@ -531,29 +526,38 @@
         sends[n], outers[n] = pre_partial(
             n, inputs_saved, after(low, *earlier), high, conv_weight
         )
-        others[n] = lax.ppermute(sends[n], "chan", swap)
+
+    def exchange(n, *earlier):
+        others[n] = lax.ppermute(after(sends[n], *earlier), "chan", swap)
 
     begin(levels[0])
-    near, far = gather_vectors(vectors, place, (payload, first), (sends[levels[0]],))
+    exchange(levels[0])
+    ring = along_head(vectors, place, (payload, first), (sends[levels[0]],))
+    gathered = lax.all_gather(ring, "pos", tiled=True)
     arrived = lax.all_to_all(
-        after(payload, sends[levels[0]]), GROUP_AXES, split_axis=0, concat_axis=0, tiled=True
-    )
+        after(payload, ring), GROUP_AXES, split_axis=0, concat_axis=0, tiled=True
+    )
+    begin(levels[1], ring)
+    exchange(levels[1])
     reach = HALO_IN[layers - 1]
-    spread = spread_entries(along[None].astype(jnp.int32), arrived, rows)
+    spread = spread_entries(
+        along[None].astype(jnp.int32), after(arrived, sends[levels[1]]), rows
+    )
     spread_low = lax.ppermute(spread[:, rows - reach :], GROUP_AXES, up)
     spread_high = lax.ppermute(spread[:, :reach], GROUP_AXES, down)
-    begin(levels[1], spread)
-    begin(levels[2], spread, sends[levels[1]])
+    begin(levels[2], spread, others[levels[0]])
     turned = jnp.stack([turn == 0, turn == 3]).astype(jnp.int32)
-    slopes = {n: pre_slope(n, flags, sends[n], others[n], rows) for n in levels}
-    entries = (turned, spread, spread_low, spread_high)
-    (half,) = top_gradient(0, *entries, after(near, sends[levels[2]]))
-    far = after(far, half, others[levels[1]])
-    grad, send = top_gradient(1, *entries, far, half, expand_weight)
+    gathered = after(gathered, sends[levels[2]], others[levels[1]])
+    grad, send = top_gradient(
+        turned, spread, spread_low, spread_high, gathered, expand_weight
+    )
     for n in levels:
         other = lax.ppermute(send, "chan", swap)
-        weights = stage_weights(n, after(conv_weight, send), expand_weight)
-        outs = block_step(n, send, other, slopes[n], weights[0], grad, outers[n], *weights[1:])
+        if n == levels[0]:
+            exchange(levels[2], other)
+        slope = pre_slope(n, flags, sends[n], after(others[n], send), rows)
+        weights = stage_weights(n, after(conv_weight, slope), expand_weight)
+        outs = block_step(n, send, other, slope, weights[0], grad, outers[n], *weights[1:])
         if n:
             grad, send = outs
     return outs[0]

time: 215 us -> 208 us (0.967)
  starting transfers between devices: 41.9 us -> 35.9 us
  Pallas kernels: 69.3 us -> 64.6 us
  local copies, waits for them, and re-layouts: 7.87 us -> 11.6 us
    all_to_all x1, waiting for transfers between devices: 7.06 us -> 22.6 us  [per_device(): lax.all_to_all(after(payload, ring), GROUP_AXES, split_axis=0, concat_axi...]
    ppermute x1, waiting for transfers between devices: 10.5 us -> 0.88 us  [per_device(): spread_low = lax.ppermute(spread[:, rows - reach:], GROUP_AXES, up)]
    ppermute x1, waiting for transfers between devices: 5.33 us -> 0.01 us  [per_device(): low = lax.ppermute(final, GROUP_AXES, up)]
    all_to_all x1, starting transfers between devices: 11.5 us -> 7.43 us  [per_device(): lax.all_to_all(after(payload, ring), GROUP_AXES, split_axis=0, concat_axi...]
    ppermute x7, starting transfers between devices: 12.2 us -> 9.09 us  [the longest x3 5.72 us: exchange(): others[n] = lax.ppermute(after(sends[n], *earlier), 'chan', swap)]
    ppermute x1, starting transfers between devices: 5.48 us -> 2.78 us  [per_device(): spread_high = lax.ppermute(spread[:, :reach], GROUP_AXES, down)]
    unnamed x46 -> x51, local copies, waits for them, and re-layouts: 6.52 us -> 9.2 us
    pallas_call x2 -> x1, Pallas kernels: 14.1 us -> 12.4 us  [top_gradient(): pl.pallas_call(top_kernel, in_specs=[SMEM] + [HBM] * 5, out_specs=[VMEM,...]
  transfers between devices with their start and end apart: 17 -> 16, of which waited for: 10 -> 9; matrix products, arithmetic and copies ran while one was open for 1% -> 1% of each run, Pallas kernels for 28% -> 21%
where the time goes in v5:
time: 208 us; the launch traced here: 205 us
  waiting for transfers between devices  77.9 us (37%)
  Pallas kernels  64.6 us (31%)
  starting transfers between devices  35.9 us (17%)
  between operations  13.8 us (7%)
  local copies, waits for them, and re-layouts  11.6 us (6%)
    ppermute x3, waiting for transfers between devices, per_device(): other = lax.ppermute(send, 'chan', swap)  39 us
    all_to_all x1, waiting for transfers between devices, per_device(): lax.all_to_all(after(payload, ring), GROUP_AXES, split_axis=0, concat_axi...  22.6 us
    pallas_call x3, Pallas kernels, pre_partial(): pl.pallas_call(functools.partial(pre_kernel, level), in_specs=[HBM, VMEM,...  18.2 us
    pallas_call x1, Pallas kernels, top_gradient(): pl.pallas_call(top_kernel, in_specs=[SMEM] + [HBM] * 5, out_specs=[VMEM,...  12.4 us
    ppermute x3, waiting for transfers between devices, exchange(): others[n] = lax.ppermute(after(sends[n], *earlier), 'chan', swap)  12.2 us
    pallas_call x3, Pallas kernels, block_step(): pl.pallas_call(functools.partial(block_kernel, level), in_specs=[VMEM] *...  10.5 us
    unnamed x51, local copies, waits for them, and re-layouts  9.2 us
    all_to_all x1, starting transfers between devices, per_device(): lax.all_to_all(after(payload, ring), GROUP_AXES, split_axis=0, concat_axi...  7.43 us
  transfers between devices with their start and end apart: 16, of which 9 were waited for; matrix products, arithmetic and copies ran while one was open for 1% of the time, Pallas kernels for 21%

profile of v5, /device:TPU:8, one launch (start us, length us, event | category | flops | bytes accessed | tf_op | source)
XLA Modules:
  0.0 204.6 jit_solution(3389162974246787588)
XLA Ops:
  6.5 0.7 copy-done.17
  7.2 1.8 head_vectors.1
  9.0 0.4 collective-permute-start
  9.4 1.1 cut_edges.1
  10.5 3.9 %collective-permute-start.1 = (bf16[96,768]{1,0:T(8,128)(2,1)S(1)}, bf16[96,768]{1,0:T(8,128)(2,1)S(1)}, u32[]{:S(2)}, u32[]{:S(2)}) collective-permute-start(bf16[96,768]{1,0:T(8,128)(2,1)S(1)} %get-tuple-element.41), channel_id=1, source_target_pairs={{0,2},{2,4},{4,6},{6,8},{8,10},{10,12},{12,14},{14,16},{16,18},{18... | collective-permute-start | bytes 442376 | tf_op jit(solution)/shard_map/ppermute | solution.py:519
  14.4 5.1 %collective-permute-start.2 = (bf16[96,768]{1,0:T(8,128)(2,1)S(1)}, bf16[96,768]{1,0:T(8,128)(2,1)S(1)}, u32[]{:S(2)}, u32[]{:S(2)}) collective-permute-start(bf16[96,768]{1,0:T(8,128)(2,1)S(1)} %get-tuple-element.39), channel_id=1, source_target_pairs={{2,0},{4,2},{6,4},{8,6},{10,8},{12,10},{14,12},{16,14},{18,16},{20... | collective-permute-start | bytes 442376 | tf_op jit(solution)/shard_map/ppermute | solution.py:520
  19.5 1.9 bucket_entries.1
  21.5 0.0 collective-permute-done
  21.5 1.1 collective-permute-start.3
  22.6 1.0 collective-permute-start.5
  23.6 0.8 collective-permute-start.4
  24.4 0.0 collective-permute-done.1.low
  24.5 0.0 collective-permute-done.2.high
  24.5 6.1 %pre_partial_2.1 = (bf16[576,768]{1,0:T(8,128)(2,1)S(1)}, bf16[544,768]{1,0:T(8,128)(2,1)S(1)}) custom-call(bf16[3,512,768]{2,1,0:T(8,128)(2,1)} %saved.6, bf16[96,768]{1,0:T(8,128)(2,1)S(1)} %collective-permute-done.1.low, bf16[96,768]{1,0:T(8,128)(2,1)S(1)} %collective-permute-done.2.high, bf16[3,3,768,768]{3,2,1,0:T(8,128)(2,1)} %refs_0_.2), custom_call_target="tpu_custom_call" | custom-call | flops 50000000 | bytes 80000 | tf_op jit(solution)/shard_map/pre_partial_2/pallas_call | solution.py:316
  30.6 1.4 collective-permute-done.3
  32.0 0.5 collective-permute-done.4
  32.5 1.2 collective-permute-done.5
  33.9 0.0 copy-done.5
  33.9 0.9 constant_dynamic-slice_fusion
  34.8 0.0 all-gather.2.cloned.1.call-update
  34.9 2.4 %collective-permute-start.8 = (bf16[576,768]{1,0:T(8,128)(2,1)S(1)}, bf16[576,768]{1,0:T(8,128)(2,1)S(1)}, u32[]{:S(2)}, u32[]{:S(2)}) collective-permute-start(bf16[576,768]{1,0:T(8,128)(2,1)S(1)} %get-tuple-element.42.own), channel_id=1, source_target_pairs={{0,1},{1,0},{2,3},{3,2},{4,5},{5,4},{6,7},{7,6},{8,9},{9,8},{10,11... | collective-permute-start | bytes 2654216 | tf_op jit(solution)/shard_map/ppermute | solution.py:531
  37.3 5.9 %pre_partial_1.1 = (bf16[544,768]{1,0:T(8,128)(2,1)S(1)}, bf16[528,768]{1,0:T(8,128)(2,1)S(1)}) custom-call(bf16[3,512,768]{2,1,0:T(8,128)(2,1)} %saved.6, bf16[96,768]{1,0:T(8,128)(2,1)S(1)} %collective-permute-done.1.low, bf16[96,768]{1,0:T(8,128)(2,1)S(1)} %collective-permute-done.2.high, bf16[3,3,768,768]{3,2,1,0:T(8,128)(2,1)} %refs_0_.2), custom_call_target="tpu_custom_call" | custom-call | flops 50000000 | bytes 80000 | tf_op jit(solution)/shard_map/pre_partial_1/pallas_call | solution.py:316
  43.2 0.9 copy-done.9
  44.1 1.2 collective-permute-start.9
  45.3 0.5 broadcast.3
  45.8 0.6 reduce
  46.4 0.6 reshape.6
  47.1 7.4 %all-to-all-start = ((bf16[64,2,128]{2,1,0:T(2,128)(2,1)}), bf16[64,2,128]{2,1,0:T(2,128)(2,1)S(1)}, u32[]{:S(2)}, u32[]{:S(2)}) async-start(bf16[64,2,128]{2,1,0:T(2,128)(2,1)} %reshape.6), calls=%async_computation | async-start | bytes 65536 | tf_op jit(solution)/shard_map/all_to_all | solution.py:537
  54.5 22.6 %all-to-all-done = bf16[64,2,128]{2,1,0:T(2,128)(2,1)S(1)} async-done(((bf16[64,2,128]{2,1,0:T(2,128)(2,1)}), bf16[64,2,128]{2,1,0:T(2,128)(2,1)S(1)}, u32[]{:S(2)}, u32[]{:S(2)}) %all-to-all-start) | async-done | bytes 32800 | tf_op jit(solution)/shard_map/all_to_all | solution.py:537
  77.2 5.5 %spread_entries.1.spread = bf16[2,512,2048]{2,1,0:T(8,128)(2,1)S(1)} custom-call(s32[1]{0:T(128)} %bitcast.2.along, bf16[64,256]{1,0:T(8,128)(2,1)S(1)} %bitcast.16), custom_call_target="tpu_custom_call" | custom-call | flops 60000000 | bytes 80000 | tf_op jit(solution)/shard_map/spread_entries/pallas_call | solution.py:204
  82.8 2.1 %copy-done = bf16[2,512,2048]{2,1,0:T(8,128)(2,1)} copy-done((bf16[2,512,2048]{2,1,0:T(8,128)(2,1)}, bf16[2,512,2048]{2,1,0:T(8,128)(2,1)S(1)}, u32[]{:S(2)}) %copy-start) | copy-done | bytes 4194328
  84.8 0.8 fusion
  85.7 2.8 %collective-permute-start.7 = (bf16[2,32,2048]{2,1,0:T(8,128)(2,1)}, bf16[2,32,2048]{2,1,0:T(8,128)(2,1)S(1)}, u32[]{:S(2)}, u32[]{:S(2)}) collective-permute-start(bf16[2,32,2048]{2,1,0:T(8,128)(2,1)} %get-tuple-element.71), channel_id=1, source_target_pairs={{2,0},{4,2},{6,4},{8,6},{10,8},{12,10},{14,12},{16,14},{18,16},{20... | collective-permute-start | bytes 786440 | tf_op jit(solution)/shard_map/ppermute | solution.py:547
  88.5 3.2 %collective-permute-start.6 = (bf16[2,32,2048]{2,1,0:T(8,128)(2,1)}, bf16[2,32,2048]{2,1,0:T(8,128)(2,1)S(1)}, u32[]{:S(2)}, u32[]{:S(2)}) collective-permute-start(bf16[2,32,2048]{2,1,0:T(8,128)(2,1)} %get-tuple-element.72), channel_id=1, source_target_pairs={{0,2},{2,4},{4,6},{6,8},{8,10},{10,12},{12,14},{14,16},{16,18},{18... | collective-permute-start | bytes 786440 | tf_op jit(solution)/shard_map/ppermute | solution.py:546
  91.7 0.1 add_convert_fusion.turned
  91.8 0.0 collective-permute-done.8.other
  91.8 6.3 %pre_partial_0.1 = (bf16[528,768]{1,0:T(8,128)(2,1)S(1)}, bf16[512,768]{1,0:T(8,128)(2,1)S(1)}) custom-call(bf16[3,512,768]{2,1,0:T(8,128)(2,1)} %saved.6, bf16[96,768]{1,0:T(8,128)(2,1)S(1)} %collective-permute-done.1.low, bf16[96,768]{1,0:T(8,128)(2,1)S(1)} %collective-permute-done.2.high, bf16[3,3,768,768]{3,2,1,0:T(8,128)(2,1)} %refs_0_.2), custom_call_target="tpu_custom_call" | custom-call | flops 50000000 | bytes 80000 | tf_op jit(solution)/shard_map/pre_partial_0/pallas_call | solution.py:316
  98.1 0.9 copy-done.11
  99.0 0.9 copy-done.13
  99.9 0.0 collective-permute-done.9.other
  99.9 0.0 collective-permute-done.7.high
  99.9 0.9 collective-permute-done.6.low
  100.8 0.7 copy-done.19
  101.5 12.4 %top_gradient.1 = (f32[576,768]{1,0:T(8,128)S(1)}, bf16[576,768]{1,0:T(8,128)(2,1)S(1)}) custom-call(s32[2]{0:T(128)S(1)} %add_convert_fusion.turned, bf16[2,512,2048]{2,1,0:T(8,128)(2,1)} %copy-done, bf16[2,32,2048]{2,1,0:T(8,128)(2,1)} %copy-done.19, bf16[2,32,2048]{2,1,0:T(8,128)(2,1)} %copy-done.18, bf16[32,2,64,768]{3,2,1,0:T(8,128)(2,1)} %bitcast.21, ...), custom_call_target="tpu_custom_call" | custom-call | flops 50000000 | bytes 140000 | tf_op jit(solution)/shard_map/top_gradient/pallas_call | solution.py:401
  113.9 1.4 collective-permute-start.10
  115.3 0.1 add_convert_fusion.1.flags
  115.3 1.2 copy-done.2
  116.5 1.2 copy-done.4
  117.7 1.6 pre_slope_2.1.slope
  119.3 2.4 %stage_weights_2.1 = (bf16[3,768,768]{2,1,0:T(8,128)(2,1)S(1)}, bf16[768,768]{1,0:T(8,128)(2,1)S(1)}) custom-call(bf16[3,3,768,768]{3,2,1,0:T(8,128)(2,1)} %refs_0_.2, bf16[3,768,768]{2,1,0:T(8,128)(2,1)} %refs_1_.3), custom_call_target="tpu_custom_call" | custom-call | flops 10000000 | bytes 10000 | tf_op jit(solution)/shard_map/stage_weights_2/pallas_call | solution.py:230
  121.8 14.2 %collective-permute-done.10.other = bf16[576,768]{1,0:T(8,128)(2,1)S(1)} collective-permute-done((bf16[576,768]{1,0:T(8,128)(2,1)S(1)}, bf16[576,768]{1,0:T(8,128)(2,1)S(1)}, u32[]{:S(2)}, u32[]{:S(2)}) %collective-permute-start.10) | collective-permute-done | bytes 884768 | tf_op jit(solution)/shard_map/ppermute | solution.py:555
  136.0 3.8 %block_step_2.1 = (f32[544,768]{1,0:T(8,128)S(1)}, bf16[544,768]{1,0:T(8,128)(2,1)S(1)}) custom-call(bf16[576,768]{1,0:T(8,128)(2,1)S(1)} %get-tuple-element.51.own, bf16[576,768]{1,0:T(8,128)(2,1)S(1)} %collective-permute-done.10.other, bf16[576,768]{1,0:T(8,128)(2,1)S(1)} %pre_slope_2.1.slope, bf16[3,768,768]{2,1,0:T(8,128)(2,1)S(1)} %get-tuple-element.54.weight, ...), custom_call_target="tpu_custom_call" | custom-call | flops 50000000 | bytes 140000 | tf_op jit(solution)/shard_map/block_step_2/pallas_call | solution.py:462
  139.8 1.5 collective-permute-start.11
  141.3 2.1 %collective-permute-start.13 = (bf16[528,768]{1,0:T(8,128)(2,1)S(1)}, bf16[528,768]{1,0:T(8,128)(2,1)S(1)}, u32[]{:S(2)}, u32[]{:S(2)}) collective-permute-start(bf16[528,768]{1,0:T(8,128)(2,1)S(1)} %copy-done.12), channel_id=1, source_target_pairs={{0,1},{1,0},{2,3},{3,2},{4,5},{5,4},{6,7},{7,6},{8,9},{9,8},{10,11... | collective-permute-start | bytes 2433032 | tf_op jit(solution)/shard_map/ppermute | solution.py:531
  143.4 3.1 %pre_slope_1.1.slope = bf16[544,768]{1,0:T(8,128)(2,1)S(1)} custom-call(s32[2]{0:T(128)S(1)} %add_convert_fusion.1.flags, bf16[544,768]{1,0:T(8,128)(2,1)S(1)} %copy-done.8, bf16[544,768]{1,0:T(8,128)(2,1)} %collective-permute-done.9.other), custom_call_target="tpu_custom_call" | custom-call | flops 40000000 | bytes 50000 | tf_op jit(solution)/shard_map/pre_slope_1/pallas_call | solution.py:348
  146.5 2.4 %stage_weights_1.1 = (bf16[3,768,768]{2,1,0:T(8,128)(2,1)S(1)}, bf16[768,768]{1,0:T(8,128)(2,1)S(1)}) custom-call(bf16[3,3,768,768]{3,2,1,0:T(8,128)(2,1)} %refs_0_.2, bf16[3,768,768]{2,1,0:T(8,128)(2,1)} %refs_1_.3), custom_call_target="tpu_custom_call" | custom-call | flops 10000000 | bytes 10000 | tf_op jit(solution)/shard_map/stage_weights_1/pallas_call | solution.py:230
  148.9 14.0 %collective-permute-done.11.other = bf16[544,768]{1,0:T(8,128)(2,1)S(1)} collective-permute-done((bf16[544,768]{1,0:T(8,128)(2,1)S(1)}, bf16[544,768]{1,0:T(8,128)(2,1)S(1)}, u32[]{:S(2)}, u32[]{:S(2)}) %collective-permute-start.11) | collective-permute-done | bytes 835616 | tf_op jit(solution)/shard_map/ppermute | solution.py:555
  162.9 3.7 %block_step_1.1 = (f32[528,768]{1,0:T(8,128)S(1)}, bf16[528,768]{1,0:T(8,128)(2,1)S(1)}) custom-call(bf16[544,768]{1,0:T(8,128)(2,1)S(1)} %get-tuple-element.58.own, bf16[544,768]{1,0:T(8,128)(2,1)S(1)} %collective-permute-done.11.other, bf16[544,768]{1,0:T(8,128)(2,1)S(1)} %pre_slope_1.1.slope, bf16[3,768,768]{2,1,0:T(8,128)(2,1)S(1)} %get-tuple-element.61.weight, ...), custom_call_target="tpu_custom_call" | custom-call | flops 50000000 | bytes 140000 | tf_op jit(solution)/shard_map/block_step_1/pallas_call | solution.py:462
  166.5 1.5 collective-permute-start.12
  168.1 12.2 %collective-permute-done.13.other = bf16[528,768]{1,0:T(8,128)(2,1)S(1)} collective-permute-done((bf16[528,768]{1,0:T(8,128)(2,1)S(1)}, bf16[528,768]{1,0:T(8,128)(2,1)S(1)}, u32[]{:S(2)}, u32[]{:S(2)}) %collective-permute-start.13) | collective-permute-done | bytes 811040 | tf_op jit(solution)/shard_map/ppermute | solution.py:531
  180.3 1.5 pre_slope_0.1.slope
  181.8 2.1 %stage_weights_0.1.weight = bf16[3,768,768]{2,1,0:T(8,128)(2,1)S(1)} custom-call(bf16[3,3,768,768]{3,2,1,0:T(8,128)(2,1)} %refs_0_.2), custom_call_target="tpu_custom_call" | custom-call | flops 10000000 | bytes 10000 | tf_op jit(solution)/shard_map/stage_weights_0/pallas_call | solution.py:230
  183.9 10.8 %collective-permute-done.12.other = bf16[528,768]{1,0:T(8,128)(2,1)S(1)} collective-permute-done((bf16[528,768]{1,0:T(8,128)(2,1)S(1)}, bf16[528,768]{1,0:T(8,128)(2,1)S(1)}, u32[]{:S(2)}, u32[]{:S(2)}) %collective-permute-start.12) | collective-permute-done | bytes 811040 | tf_op jit(solution)/shard_map/ppermute | solution.py:555
  194.7 3.0 %block_step_0.1 = bf16[512,768]{1,0:T(8,128)(2,1)} custom-call(bf16[528,768]{1,0:T(8,128)(2,1)S(1)} %get-tuple-element.65.own, bf16[528,768]{1,0:T(8,128)(2,1)S(1)} %collective-permute-done.12.other, bf16[528,768]{1,0:T(8,128)(2,1)S(1)} %pre_slope_0.1.slope, bf16[3,768,768]{2,1,0:T(8,128)(2,1)S(1)} %stage_weights_0.1.weight, ...), custom_call_target="tpu_custom_call" | custom-call | flops 50000000 | bytes 140000 | tf_op jit(solution)/shard_map/block_step_0/pallas_call | solution.py:462
  (45 shorter events, 0.2 us)
Async XLA Ops:
  6.5 93.3 %all-gather.2.cloned.1.call-start = ((), (), s32[]{:S(2)}) async-start(), calls=%async_computation.1 | async-start | bytes 7077888 | tf_op jit(solution)/shard_map/all_gather | solution.py:536
  6.5 0.7 copy-start.17
  7.2 12.3 %copy-start.15 = (s32[64,32]{0,1:T(8,128)S(1)}, s32[64,32]{0,1:T(8,128)}, u32[]{:S(2)}) copy-start(s32[64,32]{0,1:T(8,128)} %param.17) | copy-start | bytes 24580
  7.2 12.3 %copy-start.16 = (bf16[64,32]{0,1:T(8,128)(2,1)S(1)}, bf16[64,32]{0,1:T(8,128)(2,1)}, u32[]{:S(2)}) copy-start(bf16[64,32]{0,1:T(8,128)(2,1)} %param.16) | copy-start | bytes 12292
  9.0 12.5 %collective-permute-start = (bf16[64,768]{1,0:T(8,128)(2,1)S(1)}, bf16[64,768]{1,0:T(8,128)(2,1)S(1)}, u32[]{:S(2)}, u32[]{:S(2)}) collective-permute-start(bf16[64,768]{1,0:T(8,128)(2,1)S(1)} %head_vectors.1), channel_id=1, source_target_pairs={{0,8},{2,10},{4,12},{6,14},{8,0},{10,2},{12,4},{14,6},{1,9},{3,11}... | collective-permute-start | bytes 294920 | tf_op jit(solution)/shard_map/ppermute | solution.py:485
  10.5 13.9 %collective-permute-start.1 = (bf16[96,768]{1,0:T(8,128)(2,1)S(1)}, bf16[96,768]{1,0:T(8,128)(2,1)S(1)}, u32[]{:S(2)}, u32[]{:S(2)}) collective-permute-start(bf16[96,768]{1,0:T(8,128)(2,1)S(1)} %get-tuple-element.41), channel_id=1, source_target_pairs={{0,2},{2,4},{4,6},{6,8},{8,10},{10,12},{12,14},{14,16},{16,18},{18... | collective-permute-start | bytes 442376 | tf_op jit(solution)/shard_map/ppermute | solution.py:519
  14.4 10.0 %collective-permute-start.2 = (bf16[96,768]{1,0:T(8,128)(2,1)S(1)}, bf16[96,768]{1,0:T(8,128)(2,1)S(1)}, u32[]{:S(2)}, u32[]{:S(2)}) collective-permute-start(bf16[96,768]{1,0:T(8,128)(2,1)S(1)} %get-tuple-element.39), channel_id=1, source_target_pairs={{2,0},{4,2},{6,4},{8,6},{10,8},{12,10},{14,12},{16,14},{18,16},{20... | collective-permute-start | bytes 442376 | tf_op jit(solution)/shard_map/ppermute | solution.py:520
  21.5 10.5 %collective-permute-start.3 = (bf16[128,768]{1,0:T(8,128)(2,1)S(1)}, bf16[128,768]{1,0:T(8,128)(2,1)S(1)}, u32[]{:S(2)}, u32[]{:S(2)}) collective-permute-start(bf16[128,768]{1,0:T(8,128)(2,1)S(1)} %constant_dynamic-update-slice_fusion), channel_id=1, source_target_pairs={{0,6},{2,0},{4,2},{6,4},{8,14},{10,8},{12,10},{14,12},{1,7},{3,1},... | collective-permute-start | bytes 589832 | tf_op jit(solution)/shard_map/ppermute | solution.py:487
  22.6 11.2 %collective-permute-start.5 = (bf16[128,768]{1,0:T(8,128)(2,1)S(1)}, bf16[128,768]{1,0:T(8,128)(2,1)S(1)}, u32[]{:S(2)}, u32[]{:S(2)}) collective-permute-start(bf16[128,768]{1,0:T(8,128)(2,1)S(1)} %constant_dynamic-update-slice_fusion), channel_id=1, source_target_pairs={{0,2},{2,4},{4,6},{6,0},{8,10},{10,12},{12,14},{14,8},{1,3},{3,5},... | collective-permute-start | bytes 589832 | tf_op jit(solution)/shard_map/ppermute | solution.py:487
  23.6 8.9 %collective-permute-start.4 = (bf16[128,768]{1,0:T(8,128)(2,1)S(1)}, bf16[128,768]{1,0:T(8,128)(2,1)S(1)}, u32[]{:S(2)}, u32[]{:S(2)}) collective-permute-start(bf16[128,768]{1,0:T(8,128)(2,1)S(1)} %constant_dynamic-update-slice_fusion), channel_id=1, source_target_pairs={{0,4},{2,6},{4,0},{6,2},{8,12},{10,14},{12,8},{14,10},{1,5},{3,7},... | collective-permute-start | bytes 589832 | tf_op jit(solution)/shard_map/ppermute | solution.py:487
  30.5 3.4 %copy-start.5 = (bf16[544,768]{1,0:T(8,128)(2,1)}, bf16[544,768]{1,0:T(8,128)(2,1)S(1)}, u32[]{:S(2)}) copy-start(bf16[544,768]{1,0:T(8,128)(2,1)S(1)} %get-tuple-element.56.outer) | copy-start | bytes 2506756
  30.5 4.3 %copy-start.1 = (bf16[576,768]{1,0:T(8,128)(2,1)}, bf16[576,768]{1,0:T(8,128)(2,1)S(1)}, u32[]{:S(2)}) copy-start(bf16[576,768]{1,0:T(8,128)(2,1)S(1)} %get-tuple-element.42.own) | copy-start | bytes 2654212
  34.9 56.9 %collective-permute-start.8 = (bf16[576,768]{1,0:T(8,128)(2,1)S(1)}, bf16[576,768]{1,0:T(8,128)(2,1)S(1)}, u32[]{:S(2)}, u32[]{:S(2)}) collective-permute-start(bf16[576,768]{1,0:T(8,128)(2,1)S(1)} %get-tuple-element.42.own), channel_id=1, source_target_pairs={{0,1},{1,0},{2,3},{3,2},{4,5},{5,4},{6,7},{7,6},{8,9},{9,8},{10,11... | collective-permute-start | bytes 2654216 | tf_op jit(solution)/shard_map/ppermute | solution.py:531
  43.2 0.9 copy-start.9
  44.1 38.7 %copy-start.7 = (bf16[544,768]{1,0:T(8,128)(2,1)}, bf16[544,768]{1,0:T(8,128)(2,1)S(1)}, u32[]{:S(2)}) copy-start(bf16[544,768]{1,0:T(8,128)(2,1)S(1)} %get-tuple-element.46.own) | copy-start | bytes 2506756
  44.1 55.8 %collective-permute-start.9 = (bf16[544,768]{1,0:T(8,128)(2,1)S(1)}, bf16[544,768]{1,0:T(8,128)(2,1)}, u32[]{:S(2)}, u32[]{:S(2)}) collective-permute-start(bf16[544,768]{1,0:T(8,128)(2,1)S(1)} %get-tuple-element.46.own), channel_id=1, source_target_pairs={{0,1},{1,0},{2,3},{3,2},{4,5},{5,4},{6,7},{7,6},{8,9},{9,8},{10,11... | collective-permute-start | bytes 2506760 | tf_op jit(solution)/shard_map/ppermute | solution.py:531
  47.1 30.1 %all-to-all-start = ((bf16[64,2,128]{2,1,0:T(2,128)(2,1)}), bf16[64,2,128]{2,1,0:T(2,128)(2,1)S(1)}, u32[]{:S(2)}, u32[]{:S(2)}) async-start(bf16[64,2,128]{2,1,0:T(2,128)(2,1)} %reshape.6), calls=%async_computation | async-start | bytes 65536 | tf_op jit(solution)/shard_map/all_to_all | solution.py:537
  82.8 2.1 %copy-start = (bf16[2,512,2048]{2,1,0:T(8,128)(2,1)}, bf16[2,512,2048]{2,1,0:T(8,128)(2,1)S(1)}, u32[]{:S(2)}) copy-start(bf16[2,512,2048]{2,1,0:T(8,128)(2,1)S(1)} %spread_entries.1.spread) | copy-start | bytes 12582916
  85.7 14.2 %collective-permute-start.7 = (bf16[2,32,2048]{2,1,0:T(8,128)(2,1)}, bf16[2,32,2048]{2,1,0:T(8,128)(2,1)S(1)}, u32[]{:S(2)}, u32[]{:S(2)}) collective-permute-start(bf16[2,32,2048]{2,1,0:T(8,128)(2,1)} %get-tuple-element.71), channel_id=1, source_target_pairs={{2,0},{4,2},{6,4},{8,6},{10,8},{12,10},{14,12},{16,14},{18,16},{20... | collective-permute-start | bytes 786440 | tf_op jit(solution)/shard_map/ppermute | solution.py:547
  88.5 12.3 %collective-permute-start.6 = (bf16[2,32,2048]{2,1,0:T(8,128)(2,1)}, bf16[2,32,2048]{2,1,0:T(8,128)(2,1)S(1)}, u32[]{:S(2)}, u32[]{:S(2)}) collective-permute-start(bf16[2,32,2048]{2,1,0:T(8,128)(2,1)} %get-tuple-element.72), channel_id=1, source_target_pairs={{0,2},{2,4},{4,6},{6,8},{8,10},{10,12},{12,14},{14,16},{16,18},{18... | collective-permute-start | bytes 786440 | tf_op jit(solution)/shard_map/ppermute | solution.py:546
  91.8 6.3 %copy-start.3 = (bf16[576,768]{1,0:T(8,128)(2,1)}, bf16[576,768]{1,0:T(8,128)(2,1)S(1)}, u32[]{:S(2)}) copy-start(bf16[576,768]{1,0:T(8,128)(2,1)S(1)} %collective-permute-done.8.other) | copy-start | bytes 2654212
  98.1 0.9 copy-start.11
  99.0 0.9 copy-start.13
  99.9 0.9 copy-start.18
  100.8 0.7 copy-start.19
  113.9 22.1 %collective-permute-start.10 = (bf16[576,768]{1,0:T(8,128)(2,1)S(1)}, bf16[576,768]{1,0:T(8,128)(2,1)S(1)}, u32[]{:S(2)}, u32[]{:S(2)}) collective-permute-start(bf16[576,768]{1,0:T(8,128)(2,1)S(1)} %get-tuple-element.51.own), channel_id=1, source_target_pairs={{0,1},{1,0},{2,3},{3,2},{4,5},{5,4},{6,7},{7,6},{8,9},{9,8},{10,11... | collective-permute-start | bytes 2654216 | tf_op jit(solution)/shard_map/ppermute | solution.py:555
  115.3 1.2 copy-start.2
  116.5 1.2 copy-start.4
  119.3 16.7 %copy-start.6 = (bf16[544,768]{1,0:T(8,128)(2,1)S(1)}, bf16[544,768]{1,0:T(8,128)(2,1)}, u32[]{:S(2)}) copy-start(bf16[544,768]{1,0:T(8,128)(2,1)} %copy-done.5) | copy-start | bytes 2506756
  136.0 5.3 %copy-start.12 = (bf16[528,768]{1,0:T(8,128)(2,1)S(1)}, bf16[528,768]{1,0:T(8,128)(2,1)}, u32[]{:S(2)}) copy-start(bf16[528,768]{1,0:T(8,128)(2,1)} %copy-done.11) | copy-start | bytes 2433028
  136.0 7.4 %copy-start.8 = (bf16[544,768]{1,0:T(8,128)(2,1)S(1)}, bf16[544,768]{1,0:T(8,128)(2,1)}, u32[]{:S(2)}) copy-start(bf16[544,768]{1,0:T(8,128)(2,1)} %copy-done.7) | copy-start | bytes 2506756
  139.8 23.1 %collective-permute-start.11 = (bf16[544,768]{1,0:T(8,128)(2,1)S(1)}, bf16[544,768]{1,0:T(8,128)(2,1)S(1)}, u32[]{:S(2)}, u32[]{:S(2)}) collective-permute-start(bf16[544,768]{1,0:T(8,128)(2,1)S(1)} %get-tuple-element.58.own), channel_id=1, source_target_pairs={{0,1},{1,0},{2,3},{3,2},{4,5},{5,4},{6,7},{7,6},{8,9},{9,8},{10,11... | collective-permute-start | bytes 2506760 | tf_op jit(solution)/shard_map/ppermute | solution.py:555
  141.3 39.0 %collective-permute-start.13 = (bf16[528,768]{1,0:T(8,128)(2,1)S(1)}, bf16[528,768]{1,0:T(8,128)(2,1)S(1)}, u32[]{:S(2)}, u32[]{:S(2)}) collective-permute-start(bf16[528,768]{1,0:T(8,128)(2,1)S(1)} %copy-done.12), channel_id=1, source_target_pairs={{0,1},{1,0},{2,3},{3,2},{4,5},{5,4},{6,7},{7,6},{8,9},{9,8},{10,11... | collective-permute-start | bytes 2433032 | tf_op jit(solution)/shard_map/ppermute | solution.py:531
  146.5 16.4 %copy-start.10 = (bf16[528,768]{1,0:T(8,128)(2,1)S(1)}, bf16[528,768]{1,0:T(8,128)(2,1)}, u32[]{:S(2)}) copy-start(bf16[528,768]{1,0:T(8,128)(2,1)} %copy-done.9) | copy-start | bytes 2433028
  166.5 28.1 %collective-permute-start.12 = (bf16[528,768]{1,0:T(8,128)(2,1)S(1)}, bf16[528,768]{1,0:T(8,128)(2,1)S(1)}, u32[]{:S(2)}, u32[]{:S(2)}) collective-permute-start(bf16[528,768]{1,0:T(8,128)(2,1)S(1)} %get-tuple-element.65.own), channel_id=1, source_target_pairs={{0,1},{1,0},{2,3},{3,2},{4,5},{5,4},{6,7},{7,6},{8,9},{9,8},{10,11... | collective-permute-start | bytes 2433032 | tf_op jit(solution)/shard_map/ppermute | solution.py:555
  181.8 12.9 %copy-start.14 = (bf16[512,768]{1,0:T(8,128)(2,1)S(1)}, bf16[512,768]{1,0:T(8,128)(2,1)}, u32[]{:S(2)}) copy-start(bf16[512,768]{1,0:T(8,128)(2,1)} %copy-done.13) | copy-start | bytes 2359300
Sparse Core Ops, SparseCore 0:
  35.0 41.6 all-gather.1

commit v6 on v5

--- a/solution.py
+++ b/solution.py
@@ -46,6 +46,29 @@
     for copy in copies:
         copy.start()
     return copies
+
+
+def staged(batches, sems):
+    made, k = [], 0
+    for batch in batches:
+        made.append([pltpu.make_async_copy(a, b, sems.at[k + i]) for i, (a, b) in enumerate(batch)])
+        k += len(batch)
+    ahead = iter(made)
+
+    def begin():
+        for copy in next(ahead, ()):
+            copy.start()
+
+    behind = iter(made)
+
+    def arrive():
+        for copy in next(behind):
+            copy.wait()
+        begin()
+
+    begin()
+    begin()
+    return arrive
 
 
 def column_blocks(share):
@@ -273,17 +296,18 @@
     count = send.shape[0]
     taps = shifted.shape[0]
     columns = column_blocks(send.shape[1])
-    pairs = [(saved.at[level], value)]
+    batches = [[(saved.at[level], value)], []]
     for k, cols in enumerate(columns):
-        pairs.append((weight.at[level, :, :, cols], kernel.at[k]))
-    copies = fetch(pairs, sems)
+        batches.append([(weight.at[level, :, :, cols], kernel.at[k])])
+    arrive = staged(batches, sems)
     for side, start in ((low, 0), (high, halo + rows)):
         act[start : start + halo, :], outside = gelu_parts(side[edge, :].astype(F32))
         if inner and start:
             slope[inner + rows :, :] = outside[:inner].astype(BF16)
         elif inner:
             slope[:inner, :] = outside[halo - inner :].astype(BF16)
-    copies[0].wait()
+    arrive()
+    arrive()
     step = 64
 
     def part_of(k, _):
@@ -299,7 +323,7 @@
         start = halo - HALO_IN[level] + (tap - 1) * dilation
         shifted[tap] = act[start : start + count, :].astype(BF16)
     for k, cols in enumerate(columns):
-        copies[1 + k].wait()
+        arrive()
         total = None
         for tap in range(taps):
             part = jnp.dot(shifted[tap], kernel[k, tap], preferred_element_type=F32)
@@ -357,38 +381,41 @@
     )(flags, own, other)
 
 
-def top_kernel(turned, spread, low, high, vectors, expand, grad, send, matrix, held, kernel, sems):
+def top_kernel(
+    turned, spread, low, high, vectors, expand, grad, send, matrix, held, kernel, rounded, sems
+):
     rows, reach = spread.shape[1], low.shape[1]
     columns = column_blocks(grad.shape[1])
-    pairs = []
-    for k, cols in enumerate(columns):
-        for half in range(2):
-            if k == 0:
-                pairs += [
-                    (spread.at[half], matrix.at[half, pl.ds(reach, rows), :]),
-                    (low.at[(half + turned[0]) % 2], matrix.at[half, pl.ds(0, reach), :]),
-                    (
-                        high.at[(half + turned[1]) % 2],
-                        matrix.at[half, pl.ds(reach + rows, reach), :],
-                    ),
-                ]
-            pairs.append((vectors.at[:, half, :, cols], held.at[k, half]))
-        pairs.append((expand.at[expand.shape[0] - 1, :, cols], kernel.at[k]))
-    copies = iter(fetch(pairs, sems))
-    middle = None
+    to_held = lambda k, half: (
+        vectors.at[:, half, :, columns[k]],
+        held.at[k, half].reshape(vectors.shape[0], vectors.shape[2], COLS),
+    )
+    batches = []
+    for half in range(2):
+        batches.append([
+            (spread.at[half], matrix.at[half, pl.ds(reach, rows), :]),
+            (low.at[(half + turned[0]) % 2], matrix.at[half, pl.ds(0, reach), :]),
+            (high.at[(half + turned[1]) % 2], matrix.at[half, pl.ds(reach + rows, reach), :]),
+            to_held(0, half),
+        ])
+    for k in range(1, len(columns)):
+        batches.append([to_held(k, half) for half in range(2)])
+    batches.append([(expand.at[expand.shape[0] - 1], kernel)])
+    arrive = staged(batches, sems)
     for k, cols in enumerate(columns):
         top = None
         for half in range(2):
-            for _ in range(1 if k else 4):
-                next(copies).wait()
-            these = held[k, half].reshape(matrix.shape[2], COLS)
-            piece = jnp.dot(matrix[half], these, preferred_element_type=F32)
+            if k == 0 or half == 0:
+                arrive()
+            piece = jnp.dot(matrix[half], held[k, half], preferred_element_type=F32)
             top = piece if top is None else top + piece
         grad[:, cols] = top
-        next(copies).wait()
-        piece = lax.dot_general(top.astype(BF16), kernel[k], NT, preferred_element_type=F32)
-        middle = piece if middle is None else middle + piece
-    send[...] = middle.astype(BF16)
+        rounded[:, cols] = top.astype(BF16)
+    arrive()
+    for cols in column_blocks(send.shape[1]):
+        send[:, cols] = lax.dot_general(
+            rounded[...], kernel[cols, :], NT, preferred_element_type=F32
+        ).astype(BF16)
 
 
 def top_gradient(turned, spread, low, high, vectors, expand):
@@ -408,9 +435,10 @@
         ],
         scratch_shapes=[
             pltpu.VMEM((2, count, depth), BF16),
-            pltpu.VMEM((blocks, 2, depth // SLOTS, SLOTS, COLS), BF16),
-            pltpu.VMEM((blocks, width, COLS), BF16),
-            pltpu.SemaphoreType.DMA((6 + 3 * blocks,)),
+            pltpu.VMEM((blocks, 2, depth, COLS), BF16),
+            pltpu.VMEM((width, share), BF16),
+            pltpu.VMEM((count, share), BF16),
+            pltpu.SemaphoreType.DMA((7 + 2 * blocks,)),
         ],
         cost_estimate=cost(5e9, 14e6),
         compiler_params=params(),
@@ -532,11 +560,9 @@
 
     begin(levels[0])
     exchange(levels[0])
-    ring = along_head(vectors, place, (payload, first), (sends[levels[0]],))
+    arrived = lax.all_to_all(payload, GROUP_AXES, split_axis=0, concat_axis=0, tiled=True)
+    ring = along_head(vectors, place, (payload, first), (sends[levels[0]], arrived))
     gathered = lax.all_gather(ring, "pos", tiled=True)
-    arrived = lax.all_to_all(
-        after(payload, ring), GROUP_AXES, split_axis=0, concat_axis=0, tiled=True
-    )
     begin(levels[1], ring)
     exchange(levels[1])
     reach = HALO_IN[layers - 1]

time: 208 us -> 202 us (0.971)
  the two profiles are of different devices: /device:TPU:8 before, /device:TPU:0 now
where the time goes in v6:
time: 202 us; the launch traced here: 201 us
  waiting for transfers between devices  72.6 us (36%)
  Pallas kernels  65.3 us (32%)
  starting transfers between devices  37.2 us (18%)
  between operations  13.8 us (7%)
  local copies, waits for them, and re-layouts  11.6 us (6%)
    ppermute x3, waiting for transfers between devices, per_device(): other = lax.ppermute(send, 'chan', swap)  37.4 us
    ppermute x3, waiting for transfers between devices, exchange(): others[n] = lax.ppermute(after(sends[n], *earlier), 'chan', swap)  24.5 us
    pallas_call x3, Pallas kernels, pre_partial(): pl.pallas_call(functools.partial(pre_kernel, level), in_specs=[HBM, VMEM,...  18.9 us
    pallas_call x1, Pallas kernels, top_gradient(): pl.pallas_call(top_kernel, in_specs=[SMEM] + [HBM] * 5, out_specs=[VMEM,...  12.4 us
    pallas_call x3, Pallas kernels, block_step(): pl.pallas_call(functools.partial(block_kernel, level), in_specs=[VMEM] *...  10.5 us
    unnamed x51, local copies, waits for them, and re-layouts  9.28 us
    all_to_all x1, waiting for transfers between devices, per_device(): lax.all_to_all(payload, GROUP_AXES, split_axis=0, concat_axis=0, tiled=True)  7.84 us
    ppermute x3, starting transfers between devices, along_head(): parts = [lax.ppermute(both, 'head', same(k)) for k in (1, 2, 3)]  7.68 us
  transfers between devices with their start and end apart: 16, of which 8 were waited for; matrix products, arithmetic and copies ran while one was open for 1% of the time, Pallas kernels for 22%

profile of v6, /device:TPU:0, one launch (start us, length us, event | category | flops | bytes accessed | tf_op | source)
XLA Modules:
  0.0 201.3 jit_solution(11890771155349727357)
XLA Ops:
  6.5 0.7 copy-done.17
  7.2 1.8 head_vectors.1
  9.0 1.7 collective-permute-start.1
  10.7 1.1 cut_edges.1
  11.8 3.8 %collective-permute-start = (bf16[96,768]{1,0:T(8,128)(2,1)S(1)}, bf16[96,768]{1,0:T(8,128)(2,1)S(1)}, u32[]{:S(2)}, u32[]{:S(2)}) collective-permute-start(bf16[96,768]{1,0:T(8,128)(2,1)S(1)} %get-tuple-element.38), channel_id=1, source_target_pairs={{0,2},{2,4},{4,6},{6,8},{8,10},{10,12},{12,14},{14,16},{16,18},{18... | collective-permute-start | bytes 442376 | tf_op jit(solution)/shard_map/ppermute | solution.py:547
  15.6 1.3 collective-permute-start.2
  17.0 1.9 bucket_entries.1
  18.9 0.0 collective-permute-done.1
  19.0 4.8 %collective-permute-start.3 = (bf16[128,768]{1,0:T(8,128)(2,1)S(1)}, bf16[128,768]{1,0:T(8,128)(2,1)S(1)}, u32[]{:S(2)}, u32[]{:S(2)}) collective-permute-start(bf16[128,768]{1,0:T(8,128)(2,1)S(1)} %constant_dynamic-update-slice_fusion), channel_id=1, source_target_pairs={{0,6},{2,0},{4,2},{6,4},{8,14},{10,8},{12,10},{14,12},{1,7},{3,1},... | collective-permute-start | bytes 589832 | tf_op jit(solution)/shard_map/ppermute | solution.py:515
  23.8 0.5 broadcast.3
  24.3 0.7 reduce
  25.0 0.6 reshape.6
  25.6 5.7 %all-to-all-start = ((bf16[64,2,128]{2,1,0:T(2,128)(2,1)}), bf16[64,2,128]{2,1,0:T(2,128)(2,1)S(1)}, u32[]{:S(2)}, u32[]{:S(2)}) async-start(bf16[64,2,128]{2,1,0:T(2,128)(2,1)} %reshape.6), calls=%async_computation | async-start | bytes 65536 | tf_op jit(solution)/shard_map/all_to_all | solution.py:563
  31.3 0.0 all-gather.2.cloned.1.call-start
  31.3 7.8 %all-to-all-done = bf16[64,2,128]{2,1,0:T(2,128)(2,1)S(1)} async-done(((bf16[64,2,128]{2,1,0:T(2,128)(2,1)}), bf16[64,2,128]{2,1,0:T(2,128)(2,1)S(1)}, u32[]{:S(2)}, u32[]{:S(2)}) %all-to-all-start) | async-done | bytes 32800 | tf_op jit(solution)/shard_map/all_to_all | solution.py:563
  39.2 0.6 collective-permute-start.5
  39.9 2.2 %collective-permute-start.4 = (bf16[128,768]{1,0:T(8,128)(2,1)S(1)}, bf16[128,768]{1,0:T(8,128)(2,1)S(1)}, u32[]{:S(2)}, u32[]{:S(2)}) collective-permute-start(bf16[128,768]{1,0:T(8,128)(2,1)S(1)} %constant_dynamic-update-slice_fusion), channel_id=1, source_target_pairs={{0,4},{2,6},{4,0},{6,2},{8,12},{10,14},{12,8},{14,10},{1,5},{3,7},... | collective-permute-start | bytes 589832 | tf_op jit(solution)/shard_map/ppermute | solution.py:515
  42.1 0.0 collective-permute-done.low
  42.1 0.0 collective-permute-done.2.high
  42.1 6.3 %pre_partial_2.1 = (bf16[576,768]{1,0:T(8,128)(2,1)S(1)}, bf16[544,768]{1,0:T(8,128)(2,1)S(1)}) custom-call(bf16[3,512,768]{2,1,0:T(8,128)(2,1)} %saved.6, bf16[96,768]{1,0:T(8,128)(2,1)S(1)} %collective-permute-done.low, bf16[96,768]{1,0:T(8,128)(2,1)S(1)} %collective-permute-done.2.high, bf16[3,3,768,768]{3,2,1,0:T(8,128)(2,1)} %refs_0_.2), custom_call_target="tpu_custom_call" | custom-call | flops 50000000 | bytes 80000 | tf_op jit(solution)/shard_map/pre_partial_2/pallas_call | solution.py:340
  48.4 0.0 collective-permute-done.3
  48.5 2.3 %collective-permute-done.4 = bf16[128,768]{1,0:T(8,128)(2,1)S(1)} collective-permute-done((bf16[128,768]{1,0:T(8,128)(2,1)S(1)}, bf16[128,768]{1,0:T(8,128)(2,1)S(1)}, u32[]{:S(2)}, u32[]{:S(2)}) %collective-permute-start.4) | collective-permute-done | bytes 196640 | tf_op jit(solution)/shard_map/ppermute | solution.py:515
  50.8 0.5 collective-permute-done.5
  51.5 0.9 constant_dynamic-slice_fusion
  52.4 0.0 all-gather.2.cloned.1.call-update
  52.4 3.0 %collective-permute-start.8 = (bf16[576,768]{1,0:T(8,128)(2,1)S(1)}, bf16[576,768]{1,0:T(8,128)(2,1)S(1)}, u32[]{:S(2)}, u32[]{:S(2)}) collective-permute-start(bf16[576,768]{1,0:T(8,128)(2,1)S(1)} %get-tuple-element.41.own), channel_id=1, source_target_pairs={{0,1},{1,0},{2,3},{3,2},{4,5},{5,4},{6,7},{7,6},{8,9},{9,8},{10,11... | collective-permute-start | bytes 2654216 | tf_op jit(solution)/shard_map/ppermute | solution.py:559
  55.4 6.1 %pre_partial_1.1 = (bf16[544,768]{1,0:T(8,128)(2,1)S(1)}, bf16[528,768]{1,0:T(8,128)(2,1)S(1)}) custom-call(bf16[3,512,768]{2,1,0:T(8,128)(2,1)} %saved.6, bf16[96,768]{1,0:T(8,128)(2,1)S(1)} %collective-permute-done.low, bf16[96,768]{1,0:T(8,128)(2,1)S(1)} %collective-permute-done.2.high, bf16[3,3,768,768]{3,2,1,0:T(8,128)(2,1)} %refs_0_.2), custom_call_target="tpu_custom_call" | custom-call | flops 50000000 | bytes 80000 | tf_op jit(solution)/shard_map/pre_partial_1/pallas_call | solution.py:340
  61.6 0.9 copy-done.9
  62.4 0.6 collective-permute-start.9
  63.1 5.5 %spread_entries.1.spread = bf16[2,512,2048]{2,1,0:T(8,128)(2,1)S(1)} custom-call(s32[1]{0:T(128)} %bitcast.2.along, bf16[64,256]{1,0:T(8,128)(2,1)S(1)} %bitcast.16), custom_call_target="tpu_custom_call" | custom-call | flops 60000000 | bytes 80000 | tf_op jit(solution)/shard_map/spread_entries/pallas_call | solution.py:227
  68.6 2.1 %copy-done = bf16[2,512,2048]{2,1,0:T(8,128)(2,1)} copy-done((bf16[2,512,2048]{2,1,0:T(8,128)(2,1)}, bf16[2,512,2048]{2,1,0:T(8,128)(2,1)S(1)}, u32[]{:S(2)}) %copy-start) | copy-done | bytes 4194328
  70.7 0.8 fusion
  71.5 1.3 collective-permute-start.7
  72.8 4.7 %collective-permute-start.6 = (bf16[2,32,2048]{2,1,0:T(8,128)(2,1)}, bf16[2,32,2048]{2,1,0:T(8,128)(2,1)S(1)}, u32[]{:S(2)}, u32[]{:S(2)}) collective-permute-start(bf16[2,32,2048]{2,1,0:T(8,128)(2,1)} %get-tuple-element.70), channel_id=1, source_target_pairs={{0,2},{2,4},{4,6},{6,8},{8,10},{10,12},{12,14},{14,16},{16,18},{18... | collective-permute-start | bytes 786440 | tf_op jit(solution)/shard_map/ppermute | solution.py:572
  77.6 0.1 add_convert_fusion.turned
  77.6 0.0 collective-permute-done.8.other
  77.6 6.4 %pre_partial_0.1 = (bf16[528,768]{1,0:T(8,128)(2,1)S(1)}, bf16[512,768]{1,0:T(8,128)(2,1)S(1)}) custom-call(bf16[3,512,768]{2,1,0:T(8,128)(2,1)} %saved.6, bf16[96,768]{1,0:T(8,128)(2,1)S(1)} %collective-permute-done.low, bf16[96,768]{1,0:T(8,128)(2,1)S(1)} %collective-permute-done.2.high, bf16[3,3,768,768]{3,2,1,0:T(8,128)(2,1)} %refs_0_.2), custom_call_target="tpu_custom_call" | custom-call | flops 50000000 | bytes 80000 | tf_op jit(solution)/shard_map/pre_partial_0/pallas_call | solution.py:340
  84.1 0.9 copy-done.11
  85.0 0.9 copy-done.13
  85.9 11.5 %collective-permute-done.9.other = bf16[544,768]{1,0:T(8,128)(2,1)} collective-permute-done((bf16[544,768]{1,0:T(8,128)(2,1)S(1)}, bf16[544,768]{1,0:T(8,128)(2,1)}, u32[]{:S(2)}, u32[]{:S(2)}) %collective-permute-start.9) | collective-permute-done | bytes 835616 | tf_op jit(solution)/shard_map/ppermute | solution.py:559
  97.4 0.0 copy-start.19
  97.4 0.7 copy-done.18
  98.1 0.1 copy-done.19
  98.2 12.4 %top_gradient.1 = (f32[576,768]{1,0:T(8,128)S(1)}, bf16[576,768]{1,0:T(8,128)(2,1)S(1)}) custom-call(s32[2]{0:T(128)S(1)} %add_convert_fusion.turned, bf16[2,512,2048]{2,1,0:T(8,128)(2,1)} %copy-done, bf16[2,32,2048]{2,1,0:T(8,128)(2,1)} %copy-done.19, bf16[2,32,2048]{2,1,0:T(8,128)(2,1)} %copy-done.18, bf16[32,2,64,768]{3,2,1,0:T(8,128)(2,1)} %bitcast.21, ...), custom_call_target="tpu_custom_call" | custom-call | flops 50000000 | bytes 140000 | tf_op jit(solution)/shard_map/top_gradient/pallas_call | solution.py:428
  110.6 3.0 %collective-permute-start.10 = (bf16[576,768]{1,0:T(8,128)(2,1)S(1)}, bf16[576,768]{1,0:T(8,128)(2,1)S(1)}, u32[]{:S(2)}, u32[]{:S(2)}) collective-permute-start(bf16[576,768]{1,0:T(8,128)(2,1)S(1)} %get-tuple-element.49.own), channel_id=1, source_target_pairs={{0,1},{1,0},{2,3},{3,2},{4,5},{5,4},{6,7},{7,6},{8,9},{9,8},{10,11... | collective-permute-start | bytes 2654216 | tf_op jit(solution)/shard_map/ppermute | solution.py:581
  113.6 0.1 add_convert_fusion.1.flags
  113.7 1.2 copy-done.2
  114.8 1.2 copy-done.4
  116.0 1.6 pre_slope_2.1.slope
  117.6 2.4 %stage_weights_2.1 = (bf16[3,768,768]{2,1,0:T(8,128)(2,1)S(1)}, bf16[768,768]{1,0:T(8,128)(2,1)S(1)}) custom-call(bf16[3,3,768,768]{3,2,1,0:T(8,128)(2,1)} %refs_0_.2, bf16[3,768,768]{2,1,0:T(8,128)(2,1)} %refs_1_.3), custom_call_target="tpu_custom_call" | custom-call | flops 10000000 | bytes 10000 | tf_op jit(solution)/shard_map/stage_weights_2/pallas_call | solution.py:253
  120.1 12.6 %collective-permute-done.10.other = bf16[576,768]{1,0:T(8,128)(2,1)S(1)} collective-permute-done((bf16[576,768]{1,0:T(8,128)(2,1)S(1)}, bf16[576,768]{1,0:T(8,128)(2,1)S(1)}, u32[]{:S(2)}, u32[]{:S(2)}) %collective-permute-start.10) | collective-permute-done | bytes 884768 | tf_op jit(solution)/shard_map/ppermute | solution.py:581
  132.7 3.8 %block_step_2.1 = (f32[544,768]{1,0:T(8,128)S(1)}, bf16[544,768]{1,0:T(8,128)(2,1)S(1)}) custom-call(bf16[576,768]{1,0:T(8,128)(2,1)S(1)} %get-tuple-element.49.own, bf16[576,768]{1,0:T(8,128)(2,1)S(1)} %collective-permute-done.10.other, bf16[576,768]{1,0:T(8,128)(2,1)S(1)} %pre_slope_2.1.slope, bf16[3,768,768]{2,1,0:T(8,128)(2,1)S(1)} %get-tuple-element.52.weight, ...), custom_call_target="tpu_custom_call" | custom-call | flops 50000000 | bytes 140000 | tf_op jit(solution)/shard_map/block_step_2/pallas_call | solution.py:490
  136.5 0.7 collective-permute-start.11
  137.2 2.9 %collective-permute-start.13 = (bf16[528,768]{1,0:T(8,128)(2,1)S(1)}, bf16[528,768]{1,0:T(8,128)(2,1)S(1)}, u32[]{:S(2)}, u32[]{:S(2)}) collective-permute-start(bf16[528,768]{1,0:T(8,128)(2,1)S(1)} %copy-done.12), channel_id=1, source_target_pairs={{0,1},{1,0},{2,3},{3,2},{4,5},{5,4},{6,7},{7,6},{8,9},{9,8},{10,11... | collective-permute-start | bytes 2433032 | tf_op jit(solution)/shard_map/ppermute | solution.py:559
  140.1 3.1 %pre_slope_1.1.slope = bf16[544,768]{1,0:T(8,128)(2,1)S(1)} custom-call(s32[2]{0:T(128)S(1)} %add_convert_fusion.1.flags, bf16[544,768]{1,0:T(8,128)(2,1)S(1)} %copy-done.8, bf16[544,768]{1,0:T(8,128)(2,1)} %collective-permute-done.9.other), custom_call_target="tpu_custom_call" | custom-call | flops 40000000 | bytes 50000 | tf_op jit(solution)/shard_map/pre_slope_1/pallas_call | solution.py:372
  143.2 2.4 %stage_weights_1.1 = (bf16[3,768,768]{2,1,0:T(8,128)(2,1)S(1)}, bf16[768,768]{1,0:T(8,128)(2,1)S(1)}) custom-call(bf16[3,3,768,768]{3,2,1,0:T(8,128)(2,1)} %refs_0_.2, bf16[3,768,768]{2,1,0:T(8,128)(2,1)} %refs_1_.3), custom_call_target="tpu_custom_call" | custom-call | flops 10000000 | bytes 10000 | tf_op jit(solution)/shard_map/stage_weights_1/pallas_call | solution.py:253
  145.6 14.0 %collective-permute-done.11.other = bf16[544,768]{1,0:T(8,128)(2,1)S(1)} collective-permute-done((bf16[544,768]{1,0:T(8,128)(2,1)S(1)}, bf16[544,768]{1,0:T(8,128)(2,1)S(1)}, u32[]{:S(2)}, u32[]{:S(2)}) %collective-permute-start.11) | collective-permute-done | bytes 835616 | tf_op jit(solution)/shard_map/ppermute | solution.py:581
  159.6 3.7 %block_step_1.1 = (f32[528,768]{1,0:T(8,128)S(1)}, bf16[528,768]{1,0:T(8,128)(2,1)S(1)}) custom-call(bf16[544,768]{1,0:T(8,128)(2,1)S(1)} %get-tuple-element.56.own, bf16[544,768]{1,0:T(8,128)(2,1)S(1)} %collective-permute-done.11.other, bf16[544,768]{1,0:T(8,128)(2,1)S(1)} %pre_slope_1.1.slope, bf16[3,768,768]{2,1,0:T(8,128)(2,1)S(1)} %get-tuple-element.59.weight, ...), custom_call_target="tpu_custom_call" | custom-call | flops 50000000 | bytes 140000 | tf_op jit(solution)/shard_map/block_step_1/pallas_call | solution.py:490
  163.3 0.7 collective-permute-start.12
  164.0 13.0 %collective-permute-done.13.other = bf16[528,768]{1,0:T(8,128)(2,1)S(1)} collective-permute-done((bf16[528,768]{1,0:T(8,128)(2,1)S(1)}, bf16[528,768]{1,0:T(8,128)(2,1)S(1)}, u32[]{:S(2)}, u32[]{:S(2)}) %collective-permute-start.13) | collective-permute-done | bytes 811040 | tf_op jit(solution)/shard_map/ppermute | solution.py:559
  177.0 1.5 pre_slope_0.1.slope
  178.5 2.1 %stage_weights_0.1.weight = bf16[3,768,768]{2,1,0:T(8,128)(2,1)S(1)} custom-call(bf16[3,3,768,768]{3,2,1,0:T(8,128)(2,1)} %refs_0_.2), custom_call_target="tpu_custom_call" | custom-call | flops 10000000 | bytes 10000 | tf_op jit(solution)/shard_map/stage_weights_0/pallas_call | solution.py:253
  180.6 10.8 %collective-permute-done.12.other = bf16[528,768]{1,0:T(8,128)(2,1)S(1)} collective-permute-done((bf16[528,768]{1,0:T(8,128)(2,1)S(1)}, bf16[528,768]{1,0:T(8,128)(2,1)S(1)}, u32[]{:S(2)}, u32[]{:S(2)}) %collective-permute-start.12) | collective-permute-done | bytes 811040 | tf_op jit(solution)/shard_map/ppermute | solution.py:581
  191.4 3.0 %block_step_0.1 = bf16[512,768]{1,0:T(8,128)(2,1)} custom-call(bf16[528,768]{1,0:T(8,128)(2,1)S(1)} %get-tuple-element.63.own, bf16[528,768]{1,0:T(8,128)(2,1)S(1)} %collective-permute-done.12.other, bf16[528,768]{1,0:T(8,128)(2,1)S(1)} %pre_slope_0.1.slope, bf16[3,768,768]{2,1,0:T(8,128)(2,1)S(1)} %stage_weights_0.1.weight, ...), custom_call_target="tpu_custom_call" | custom-call | flops 50000000 | bytes 140000 | tf_op jit(solution)/shard_map/block_step_0/pallas_call | solution.py:490
  (45 shorter events, 0.2 us)
Async XLA Ops:
  6.5 0.7 copy-start.17
  7.2 9.8 %copy-start.15 = (s32[64,32]{0,1:T(8,128)S(1)}, s32[64,32]{0,1:T(8,128)}, u32[]{:S(2)}) copy-start(s32[64,32]{0,1:T(8,128)} %param.17) | copy-start | bytes 24580
  7.2 9.8 %copy-start.16 = (bf16[64,32]{0,1:T(8,128)(2,1)S(1)}, bf16[64,32]{0,1:T(8,128)(2,1)}, u32[]{:S(2)}) copy-start(bf16[64,32]{0,1:T(8,128)(2,1)} %param.16) | copy-start | bytes 12292
  9.0 9.9 %collective-permute-start.1 = (bf16[64,768]{1,0:T(8,128)(2,1)S(1)}, bf16[64,768]{1,0:T(8,128)(2,1)S(1)}, u32[]{:S(2)}, u32[]{:S(2)}) collective-permute-start(bf16[64,768]{1,0:T(8,128)(2,1)S(1)} %head_vectors.1), channel_id=1, source_target_pairs={{0,8},{2,10},{4,12},{6,14},{8,0},{10,2},{12,4},{14,6},{1,9},{3,11}... | collective-permute-start | bytes 294920 | tf_op jit(solution)/shard_map/ppermute | solution.py:513
  11.8 30.3 %collective-permute-start = (bf16[96,768]{1,0:T(8,128)(2,1)S(1)}, bf16[96,768]{1,0:T(8,128)(2,1)S(1)}, u32[]{:S(2)}, u32[]{:S(2)}) collective-permute-start(bf16[96,768]{1,0:T(8,128)(2,1)S(1)} %get-tuple-element.38), channel_id=1, source_target_pairs={{0,2},{2,4},{4,6},{6,8},{8,10},{10,12},{12,14},{14,16},{16,18},{18... | collective-permute-start | bytes 442376 | tf_op jit(solution)/shard_map/ppermute | solution.py:547
  15.6 26.4 %collective-permute-start.2 = (bf16[96,768]{1,0:T(8,128)(2,1)S(1)}, bf16[96,768]{1,0:T(8,128)(2,1)S(1)}, u32[]{:S(2)}, u32[]{:S(2)}) collective-permute-start(bf16[96,768]{1,0:T(8,128)(2,1)S(1)} %get-tuple-element.39), channel_id=1, source_target_pairs={{2,0},{4,2},{6,4},{8,6},{10,8},{12,10},{14,12},{16,14},{18,16},{20... | collective-permute-start | bytes 442376 | tf_op jit(solution)/shard_map/ppermute | solution.py:548
  19.0 29.5 %collective-permute-start.3 = (bf16[128,768]{1,0:T(8,128)(2,1)S(1)}, bf16[128,768]{1,0:T(8,128)(2,1)S(1)}, u32[]{:S(2)}, u32[]{:S(2)}) collective-permute-start(bf16[128,768]{1,0:T(8,128)(2,1)S(1)} %constant_dynamic-update-slice_fusion), channel_id=1, source_target_pairs={{0,6},{2,0},{4,2},{6,4},{8,14},{10,8},{12,10},{14,12},{1,7},{3,1},... | collective-permute-start | bytes 589832 | tf_op jit(solution)/shard_map/ppermute | solution.py:515
  25.6 13.6 %all-to-all-start = ((bf16[64,2,128]{2,1,0:T(2,128)(2,1)}), bf16[64,2,128]{2,1,0:T(2,128)(2,1)S(1)}, u32[]{:S(2)}, u32[]{:S(2)}) async-start(bf16[64,2,128]{2,1,0:T(2,128)(2,1)} %reshape.6), calls=%async_computation | async-start | bytes 65536 | tf_op jit(solution)/shard_map/all_to_all | solution.py:563
  31.3 66.1 %all-gather.2.cloned.1.call-start = ((), (), s32[]{:S(2)}) async-start(), calls=%async_computation.1 | async-start | bytes 7077888 | tf_op jit(solution)/shard_map/all_gather | solution.py:565
  39.2 12.1 %collective-permute-start.5 = (bf16[128,768]{1,0:T(8,128)(2,1)S(1)}, bf16[128,768]{1,0:T(8,128)(2,1)S(1)}, u32[]{:S(2)}, u32[]{:S(2)}) collective-permute-start(bf16[128,768]{1,0:T(8,128)(2,1)S(1)} %constant_dynamic-update-slice_fusion), channel_id=1, source_target_pairs={{0,2},{2,4},{4,6},{6,0},{8,10},{10,12},{12,14},{14,8},{1,3},{3,5},... | collective-permute-start | bytes 589832 | tf_op jit(solution)/shard_map/ppermute | solution.py:515
  39.9 10.9 %collective-permute-start.4 = (bf16[128,768]{1,0:T(8,128)(2,1)S(1)}, bf16[128,768]{1,0:T(8,128)(2,1)S(1)}, u32[]{:S(2)}, u32[]{:S(2)}) collective-permute-start(bf16[128,768]{1,0:T(8,128)(2,1)S(1)} %constant_dynamic-update-slice_fusion), channel_id=1, source_target_pairs={{0,4},{2,6},{4,0},{6,2},{8,12},{10,14},{12,8},{14,10},{1,5},{3,7},... | collective-permute-start | bytes 589832 | tf_op jit(solution)/shard_map/ppermute | solution.py:515
  48.4 3.0 %copy-start.5 = (bf16[544,768]{1,0:T(8,128)(2,1)}, bf16[544,768]{1,0:T(8,128)(2,1)S(1)}, u32[]{:S(2)}) copy-start(bf16[544,768]{1,0:T(8,128)(2,1)S(1)} %get-tuple-element.54.outer) | copy-start | bytes 2506756
  48.4 4.0 %copy-start.1 = (bf16[576,768]{1,0:T(8,128)(2,1)}, bf16[576,768]{1,0:T(8,128)(2,1)S(1)}, u32[]{:S(2)}) copy-start(bf16[576,768]{1,0:T(8,128)(2,1)S(1)} %get-tuple-element.41.own) | copy-start | bytes 2654212
  52.4 25.2 %collective-permute-start.8 = (bf16[576,768]{1,0:T(8,128)(2,1)S(1)}, bf16[576,768]{1,0:T(8,128)(2,1)S(1)}, u32[]{:S(2)}, u32[]{:S(2)}) collective-permute-start(bf16[576,768]{1,0:T(8,128)(2,1)S(1)} %get-tuple-element.41.own), channel_id=1, source_target_pairs={{0,1},{1,0},{2,3},{3,2},{4,5},{5,4},{6,7},{7,6},{8,9},{9,8},{10,11... | collective-permute-start | bytes 2654216 | tf_op jit(solution)/shard_map/ppermute | solution.py:559
  61.5 0.9 copy-start.9
  62.4 6.2 %copy-start.7 = (bf16[544,768]{1,0:T(8,128)(2,1)}, bf16[544,768]{1,0:T(8,128)(2,1)S(1)}, u32[]{:S(2)}) copy-start(bf16[544,768]{1,0:T(8,128)(2,1)S(1)} %get-tuple-element.44.own) | copy-start | bytes 2506756
  62.4 34.9 %collective-permute-start.9 = (bf16[544,768]{1,0:T(8,128)(2,1)S(1)}, bf16[544,768]{1,0:T(8,128)(2,1)}, u32[]{:S(2)}, u32[]{:S(2)}) collective-permute-start(bf16[544,768]{1,0:T(8,128)(2,1)S(1)} %get-tuple-element.44.own), channel_id=1, source_target_pairs={{0,1},{1,0},{2,3},{3,2},{4,5},{5,4},{6,7},{7,6},{8,9},{9,8},{10,11... | collective-permute-start | bytes 2506760 | tf_op jit(solution)/shard_map/ppermute | solution.py:559
  68.6 2.1 %copy-start = (bf16[2,512,2048]{2,1,0:T(8,128)(2,1)}, bf16[2,512,2048]{2,1,0:T(8,128)(2,1)S(1)}, u32[]{:S(2)}) copy-start(bf16[2,512,2048]{2,1,0:T(8,128)(2,1)S(1)} %spread_entries.1.spread) | copy-start | bytes 12582916
  71.5 25.9 %collective-permute-start.7 = (bf16[2,32,2048]{2,1,0:T(8,128)(2,1)}, bf16[2,32,2048]{2,1,0:T(8,128)(2,1)S(1)}, u32[]{:S(2)}, u32[]{:S(2)}) collective-permute-start(bf16[2,32,2048]{2,1,0:T(8,128)(2,1)} %get-tuple-element.69), channel_id=1, source_target_pairs={{2,0},{4,2},{6,4},{8,6},{10,8},{12,10},{14,12},{16,14},{18,16},{20... | collective-permute-start | bytes 786440 | tf_op jit(solution)/shard_map/ppermute | solution.py:573
  72.8 24.6 %collective-permute-start.6 = (bf16[2,32,2048]{2,1,0:T(8,128)(2,1)}, bf16[2,32,2048]{2,1,0:T(8,128)(2,1)S(1)}, u32[]{:S(2)}, u32[]{:S(2)}) collective-permute-start(bf16[2,32,2048]{2,1,0:T(8,128)(2,1)} %get-tuple-element.70), channel_id=1, source_target_pairs={{0,2},{2,4},{4,6},{6,8},{8,10},{10,12},{12,14},{14,16},{16,18},{18... | collective-permute-start | bytes 786440 | tf_op jit(solution)/shard_map/ppermute | solution.py:572
  77.6 6.4 %copy-start.3 = (bf16[576,768]{1,0:T(8,128)(2,1)}, bf16[576,768]{1,0:T(8,128)(2,1)S(1)}, u32[]{:S(2)}) copy-start(bf16[576,768]{1,0:T(8,128)(2,1)S(1)} %collective-permute-done.8.other) | copy-start | bytes 2654212
  84.1 0.9 copy-start.11
  85.0 0.9 copy-start.13
  97.4 0.7 copy-start.18
  97.4 0.8 copy-start.19
  110.6 22.1 %collective-permute-start.10 = (bf16[576,768]{1,0:T(8,128)(2,1)S(1)}, bf16[576,768]{1,0:T(8,128)(2,1)S(1)}, u32[]{:S(2)}, u32[]{:S(2)}) collective-permute-start(bf16[576,768]{1,0:T(8,128)(2,1)S(1)} %get-tuple-element.49.own), channel_id=1, source_target_pairs={{0,1},{1,0},{2,3},{3,2},{4,5},{5,4},{6,7},{7,6},{8,9},{9,8},{10,11... | collective-permute-start | bytes 2654216 | tf_op jit(solution)/shard_map/ppermute | solution.py:581
  113.6 1.2 copy-start.2
  114.8 1.2 copy-start.4
  117.6 15.1 %copy-start.6 = (bf16[544,768]{1,0:T(8,128)(2,1)S(1)}, bf16[544,768]{1,0:T(8,128)(2,1)}, u32[]{:S(2)}) copy-start(bf16[544,768]{1,0:T(8,128)(2,1)} %copy-done.5) | copy-start | bytes 2506756
  132.7 4.5 %copy-start.12 = (bf16[528,768]{1,0:T(8,128)(2,1)S(1)}, bf16[528,768]{1,0:T(8,128)(2,1)}, u32[]{:S(2)}) copy-start(bf16[528,768]{1,0:T(8,128)(2,1)} %copy-done.11) | copy-start | bytes 2433028
  132.7 7.4 %copy-start.8 = (bf16[544,768]{1,0:T(8,128)(2,1)S(1)}, bf16[544,768]{1,0:T(8,128)(2,1)}, u32[]{:S(2)}) copy-start(bf16[544,768]{1,0:T(8,128)(2,1)} %copy-done.7) | copy-start | bytes 2506756
  136.5 23.1 %collective-permute-start.11 = (bf16[544,768]{1,0:T(8,128)(2,1)S(1)}, bf16[544,768]{1,0:T(8,128)(2,1)S(1)}, u32[]{:S(2)}, u32[]{:S(2)}) collective-permute-start(bf16[544,768]{1,0:T(8,128)(2,1)S(1)} %get-tuple-element.56.own), channel_id=1, source_target_pairs={{0,1},{1,0},{2,3},{3,2},{4,5},{5,4},{6,7},{7,6},{8,9},{9,8},{10,11... | collective-permute-start | bytes 2506760 | tf_op jit(solution)/shard_map/ppermute | solution.py:581
  137.2 39.8 %collective-permute-start.13 = (bf16[528,768]{1,0:T(8,128)(2,1)S(1)}, bf16[528,768]{1,0:T(8,128)(2,1)S(1)}, u32[]{:S(2)}, u32[]{:S(2)}) collective-permute-start(bf16[528,768]{1,0:T(8,128)(2,1)S(1)} %copy-done.12), channel_id=1, source_target_pairs={{0,1},{1,0},{2,3},{3,2},{4,5},{5,4},{6,7},{7,6},{8,9},{9,8},{10,11... | collective-permute-start | bytes 2433032 | tf_op jit(solution)/shard_map/ppermute | solution.py:559
  143.2 16.4 %copy-start.10 = (bf16[528,768]{1,0:T(8,128)(2,1)S(1)}, bf16[528,768]{1,0:T(8,128)(2,1)}, u32[]{:S(2)}) copy-start(bf16[528,768]{1,0:T(8,128)(2,1)} %copy-done.9) | copy-start | bytes 2433028
  163.3 28.1 %collective-permute-start.12 = (bf16[528,768]{1,0:T(8,128)(2,1)S(1)}, bf16[528,768]{1,0:T(8,128)(2,1)S(1)}, u32[]{:S(2)}, u32[]{:S(2)}) collective-permute-start(bf16[528,768]{1,0:T(8,128)(2,1)S(1)} %get-tuple-element.63.own), channel_id=1, source_target_pairs={{0,1},{1,0},{2,3},{3,2},{4,5},{5,4},{6,7},{7,6},{8,9},{9,8},{10,11... | collective-permute-start | bytes 2433032 | tf_op jit(solution)/shard_map/ppermute | solution.py:581
  178.5 12.9 %copy-start.14 = (bf16[512,768]{1,0:T(8,128)(2,1)S(1)}, bf16[512,768]{1,0:T(8,128)(2,1)}, u32[]{:S(2)}) copy-start(bf16[512,768]{1,0:T(8,128)(2,1)} %copy-done.13) | copy-start | bytes 2359300
Sparse Core Ops, SparseCore 0:
  52.5 39.9 all-gather.1

commit v7 on v6

--- a/solution.py
+++ b/solution.py
@@ -543,10 +543,13 @@
     vectors = head_vectors(
         chan_place[None].astype(jnp.int32), head_weight, batch_of, erase_left, erase_right, share
     )
-    first, final = cut_edges(after(inputs_saved, vectors))
+    payload = bucket(cover_bins, bin_gradient, members, rows)
+    arrived = lax.all_to_all(
+        after(payload, vectors), GROUP_AXES, split_axis=0, concat_axis=0, tiled=True
+    )
+    first, final = cut_edges(after(inputs_saved, payload))
     low = lax.ppermute(final, GROUP_AXES, up)
     high = lax.ppermute(first, GROUP_AXES, down)
-    payload = bucket(cover_bins, bin_gradient, members, rows)
     flags = jnp.stack([member == 0, member == members - 1]).astype(jnp.int32)
     sends, outers, others = {}, {}, {}
 
@@ -560,8 +563,7 @@
 
     begin(levels[0])
     exchange(levels[0])
-    arrived = lax.all_to_all(payload, GROUP_AXES, split_axis=0, concat_axis=0, tiled=True)
-    ring = along_head(vectors, place, (payload, first), (sends[levels[0]], arrived))
+    ring = along_head(vectors, place, (arrived, first), (sends[levels[0]],))
     gathered = lax.all_gather(ring, "pos", tiled=True)
     begin(levels[1], ring)
     exchange(levels[1])

time: 202 us -> 202 us (level)
  the two profiles are of different devices: /device:TPU:0 before, /device:TPU:8 now
where the time goes in v7:
time: 202 us; the launch traced here: 201 us
  waiting for transfers between devices  72.3 us (36%)
  Pallas kernels  65.2 us (32%)
  starting transfers between devices  35.7 us (18%)
  between operations  13.8 us (7%)
  local copies, waits for them, and re-layouts  12.9 us (6%)
    ppermute x3, waiting for transfers between devices, per_device(): other = lax.ppermute(send, 'chan', swap)  40.6 us
    ppermute x3, waiting for transfers between devices, exchange(): others[n] = lax.ppermute(after(sends[n], *earlier), 'chan', swap)  21.6 us
    pallas_call x3, Pallas kernels, pre_partial(): pl.pallas_call(functools.partial(pre_kernel, level), in_specs=[HBM, VMEM,...  18.8 us
    pallas_call x1, Pallas kernels, top_gradient(): pl.pallas_call(top_kernel, in_specs=[SMEM] + [HBM] * 5, out_specs=[VMEM,...  12.4 us
    unnamed x51, local copies, waits for them, and re-layouts  10.6 us
    pallas_call x3, Pallas kernels, block_step(): pl.pallas_call(functools.partial(block_kernel, level), in_specs=[VMEM] *...  10.5 us
    all_to_all x1, starting transfers between devices, per_device(): lax.all_to_all(after(payload, vectors), GROUP_AXES, split_axis=0, concat_...  9.79 us
    pallas_call x3, Pallas kernels, stage_weights(): pl.pallas_call(body, in_specs=[HBM] * len(parts), out_specs=[VMEM] * len(...  6.94 us
  transfers between devices with their start and end apart: 16, of which 10 were waited for; matrix products, arithmetic and copies ran while one was open for 1% of the time, Pallas kernels for 21%

profile of v7, /device:TPU:8, one launch (start us, length us, event | category | flops | bytes accessed | tf_op | source)
XLA Modules:
  0.0 200.7 jit_solution(4225596684148135294)
XLA Ops:
  6.5 0.7 copy-done.15
  7.3 0.7 copy-done.16
  8.0 1.9 bucket_entries.1
  9.9 0.0 copy-start.17
  9.9 0.6 copy-done.17
  10.6 1.8 head_vectors.1
  12.3 0.5 broadcast.3
  12.8 0.7 reduce
  13.5 0.6 reshape.6
  14.1 9.8 %all-to-all-start = ((bf16[64,2,128]{2,1,0:T(2,128)(2,1)}), bf16[64,2,128]{2,1,0:T(2,128)(2,1)S(1)}, u32[]{:S(2)}, u32[]{:S(2)}) async-start(bf16[64,2,128]{2,1,0:T(2,128)(2,1)} %reshape.6), calls=%async_computation | async-start | bytes 65536 | tf_op jit(solution)/shard_map/all_to_all | solution.py:547
  23.9 0.0 all-gather.2.cloned.1.call-start
  24.0 0.5 collective-permute-start.1
  24.5 1.1 cut_edges.1
  25.6 3.5 %collective-permute-start = (bf16[96,768]{1,0:T(8,128)(2,1)S(1)}, bf16[96,768]{1,0:T(8,128)(2,1)S(1)}, u32[]{:S(2)}, u32[]{:S(2)}) collective-permute-start(bf16[96,768]{1,0:T(8,128)(2,1)S(1)} %get-tuple-element.40), channel_id=1, source_target_pairs={{0,2},{2,4},{4,6},{6,8},{8,10},{10,12},{12,14},{14,16},{16,18},{18... | collective-permute-start | bytes 442376 | tf_op jit(solution)/shard_map/ppermute | solution.py:551
  29.1 4.5 %collective-permute-start.2 = (bf16[96,768]{1,0:T(8,128)(2,1)S(1)}, bf16[96,768]{1,0:T(8,128)(2,1)S(1)}, u32[]{:S(2)}, u32[]{:S(2)}) collective-permute-start(bf16[96,768]{1,0:T(8,128)(2,1)S(1)} %get-tuple-element.41), channel_id=1, source_target_pairs={{2,0},{4,2},{6,4},{8,6},{10,8},{12,10},{14,12},{16,14},{18,16},{20... | collective-permute-start | bytes 442376 | tf_op jit(solution)/shard_map/ppermute | solution.py:552
  33.6 0.0 all-to-all-done
  33.7 0.7 collective-permute-start.3
  34.4 1.4 collective-permute-start.5
  35.8 1.0 collective-permute-start.4
  36.7 0.4 collective-permute-done.2.high
  37.1 6.3 %pre_partial_2.1 = (bf16[576,768]{1,0:T(8,128)(2,1)S(1)}, bf16[544,768]{1,0:T(8,128)(2,1)S(1)}) custom-call(bf16[3,512,768]{2,1,0:T(8,128)(2,1)} %saved.6, bf16[96,768]{1,0:T(8,128)(2,1)S(1)} %collective-permute-done.low, bf16[96,768]{1,0:T(8,128)(2,1)S(1)} %collective-permute-done.2.high, bf16[3,3,768,768]{3,2,1,0:T(8,128)(2,1)} %refs_0_.2), custom_call_target="tpu_custom_call" | custom-call | flops 50000000 | bytes 80000 | tf_op jit(solution)/shard_map/pre_partial_2/pallas_call | solution.py:340
  43.5 2.7 %collective-permute-done.3 = bf16[128,768]{1,0:T(8,128)(2,1)S(1)} collective-permute-done((bf16[128,768]{1,0:T(8,128)(2,1)S(1)}, bf16[128,768]{1,0:T(8,128)(2,1)S(1)}, u32[]{:S(2)}, u32[]{:S(2)}) %collective-permute-start.3) | collective-permute-done | bytes 196640 | tf_op jit(solution)/shard_map/ppermute | solution.py:515
  46.2 0.6 collective-permute-done.5
  46.9 0.9 constant_dynamic-slice_fusion
  47.9 0.0 all-gather.2.cloned.1.call-update
  47.9 2.4 %collective-permute-start.8 = (bf16[576,768]{1,0:T(8,128)(2,1)S(1)}, bf16[576,768]{1,0:T(8,128)(2,1)S(1)}, u32[]{:S(2)}, u32[]{:S(2)}) collective-permute-start(bf16[576,768]{1,0:T(8,128)(2,1)S(1)} %get-tuple-element.43.own), channel_id=1, source_target_pairs={{0,1},{1,0},{2,3},{3,2},{4,5},{5,4},{6,7},{7,6},{8,9},{9,8},{10,11... | collective-permute-start | bytes 2654216 | tf_op jit(solution)/shard_map/ppermute | solution.py:562
  50.3 6.1 %pre_partial_1.1 = (bf16[544,768]{1,0:T(8,128)(2,1)S(1)}, bf16[528,768]{1,0:T(8,128)(2,1)S(1)}) custom-call(bf16[3,512,768]{2,1,0:T(8,128)(2,1)} %saved.6, bf16[96,768]{1,0:T(8,128)(2,1)S(1)} %collective-permute-done.low, bf16[96,768]{1,0:T(8,128)(2,1)S(1)} %collective-permute-done.2.high, bf16[3,3,768,768]{3,2,1,0:T(8,128)(2,1)} %refs_0_.2), custom_call_target="tpu_custom_call" | custom-call | flops 50000000 | bytes 80000 | tf_op jit(solution)/shard_map/pre_partial_1/pallas_call | solution.py:340
  56.4 0.9 copy-done.9
  57.3 1.2 collective-permute-start.9
  58.6 5.5 %spread_entries.1.spread = bf16[2,512,2048]{2,1,0:T(8,128)(2,1)S(1)} custom-call(s32[1]{0:T(128)} %bitcast.2.along, bf16[64,256]{1,0:T(8,128)(2,1)S(1)} %bitcast.16), custom_call_target="tpu_custom_call" | custom-call | flops 60000000 | bytes 80000 | tf_op jit(solution)/shard_map/spread_entries/pallas_call | solution.py:227
  64.1 2.1 %copy-done = bf16[2,512,2048]{2,1,0:T(8,128)(2,1)} copy-done((bf16[2,512,2048]{2,1,0:T(8,128)(2,1)}, bf16[2,512,2048]{2,1,0:T(8,128)(2,1)S(1)}, u32[]{:S(2)}) %copy-start) | copy-done | bytes 4194328
  66.2 0.8 fusion
  67.0 4.5 %collective-permute-start.7 = (bf16[2,32,2048]{2,1,0:T(8,128)(2,1)}, bf16[2,32,2048]{2,1,0:T(8,128)(2,1)S(1)}, u32[]{:S(2)}, u32[]{:S(2)}) collective-permute-start(bf16[2,32,2048]{2,1,0:T(8,128)(2,1)} %get-tuple-element.71), channel_id=1, source_target_pairs={{2,0},{4,2},{6,4},{8,6},{10,8},{12,10},{14,12},{16,14},{18,16},{20... | collective-permute-start | bytes 786440 | tf_op jit(solution)/shard_map/ppermute | solution.py:575
  71.5 2.1 %collective-permute-start.6 = (bf16[2,32,2048]{2,1,0:T(8,128)(2,1)}, bf16[2,32,2048]{2,1,0:T(8,128)(2,1)S(1)}, u32[]{:S(2)}, u32[]{:S(2)}) collective-permute-start(bf16[2,32,2048]{2,1,0:T(8,128)(2,1)} %get-tuple-element.72), channel_id=1, source_target_pairs={{0,2},{2,4},{4,6},{6,8},{8,10},{10,12},{12,14},{14,16},{16,18},{18... | collective-permute-start | bytes 786440 | tf_op jit(solution)/shard_map/ppermute | solution.py:574
  73.6 0.1 add_convert_fusion.turned
  73.7 6.4 %pre_partial_0.1 = (bf16[528,768]{1,0:T(8,128)(2,1)S(1)}, bf16[512,768]{1,0:T(8,128)(2,1)S(1)}) custom-call(bf16[3,512,768]{2,1,0:T(8,128)(2,1)} %saved.6, bf16[96,768]{1,0:T(8,128)(2,1)S(1)} %collective-permute-done.low, bf16[96,768]{1,0:T(8,128)(2,1)S(1)} %collective-permute-done.2.high, bf16[3,3,768,768]{3,2,1,0:T(8,128)(2,1)} %refs_0_.2), custom_call_target="tpu_custom_call" | custom-call | flops 50000000 | bytes 80000 | tf_op jit(solution)/shard_map/pre_partial_0/pallas_call | solution.py:340
  80.1 0.9 copy-done.11
  81.0 0.9 copy-done.13
  81.9 8.2 %collective-permute-done.9.other = bf16[544,768]{1,0:T(8,128)(2,1)} collective-permute-done((bf16[544,768]{1,0:T(8,128)(2,1)S(1)}, bf16[544,768]{1,0:T(8,128)(2,1)}, u32[]{:S(2)}, u32[]{:S(2)}) %collective-permute-start.9) | collective-permute-done | bytes 835616 | tf_op jit(solution)/shard_map/ppermute | solution.py:562
  90.1 0.0 all-gather.2.cloned.1.call-done
  90.1 2.3 %collective-permute-done.7.high = bf16[2,32,2048]{2,1,0:T(8,128)(2,1)S(1)} collective-permute-done((bf16[2,32,2048]{2,1,0:T(8,128)(2,1)}, bf16[2,32,2048]{2,1,0:T(8,128)(2,1)S(1)}, u32[]{:S(2)}, u32[]{:S(2)}) %collective-permute-start.7) | collective-permute-done | bytes 262176 | tf_op jit(solution)/shard_map/ppermute | solution.py:575
  92.4 4.1 %collective-permute-done.6.low = bf16[2,32,2048]{2,1,0:T(8,128)(2,1)S(1)} collective-permute-done((bf16[2,32,2048]{2,1,0:T(8,128)(2,1)}, bf16[2,32,2048]{2,1,0:T(8,128)(2,1)S(1)}, u32[]{:S(2)}, u32[]{:S(2)}) %collective-permute-start.6) | collective-permute-done | bytes 262176 | tf_op jit(solution)/shard_map/ppermute | solution.py:574
  96.5 0.7 copy-done.19
  97.2 12.4 %top_gradient.1 = (f32[576,768]{1,0:T(8,128)S(1)}, bf16[576,768]{1,0:T(8,128)(2,1)S(1)}) custom-call(s32[2]{0:T(128)S(1)} %add_convert_fusion.turned, bf16[2,512,2048]{2,1,0:T(8,128)(2,1)} %copy-done, bf16[2,32,2048]{2,1,0:T(8,128)(2,1)} %copy-done.19, bf16[2,32,2048]{2,1,0:T(8,128)(2,1)} %copy-done.18, bf16[32,2,64,768]{3,2,1,0:T(8,128)(2,1)} %bitcast.21, ...), custom_call_target="tpu_custom_call" | custom-call | flops 50000000 | bytes 140000 | tf_op jit(solution)/shard_map/top_gradient/pallas_call | solution.py:428
  109.7 0.1 collective-permute-start.10
  109.8 0.1 add_convert_fusion.1.flags
  109.8 1.2 copy-done.2
  111.0 1.2 copy-done.4
  112.2 1.6 pre_slope_2.1.slope
  113.8 2.4 %stage_weights_2.1 = (bf16[3,768,768]{2,1,0:T(8,128)(2,1)S(1)}, bf16[768,768]{1,0:T(8,128)(2,1)S(1)}) custom-call(bf16[3,3,768,768]{3,2,1,0:T(8,128)(2,1)} %refs_0_.2, bf16[3,768,768]{2,1,0:T(8,128)(2,1)} %refs_1_.3), custom_call_target="tpu_custom_call" | custom-call | flops 10000000 | bytes 10000 | tf_op jit(solution)/shard_map/stage_weights_2/pallas_call | solution.py:253
  116.3 15.7 %collective-permute-done.10.other = bf16[576,768]{1,0:T(8,128)(2,1)S(1)} collective-permute-done((bf16[576,768]{1,0:T(8,128)(2,1)S(1)}, bf16[576,768]{1,0:T(8,128)(2,1)S(1)}, u32[]{:S(2)}, u32[]{:S(2)}) %collective-permute-start.10) | collective-permute-done | bytes 884768 | tf_op jit(solution)/shard_map/ppermute | solution.py:583
  132.0 3.7 %block_step_2.1 = (f32[544,768]{1,0:T(8,128)S(1)}, bf16[544,768]{1,0:T(8,128)(2,1)S(1)}) custom-call(bf16[576,768]{1,0:T(8,128)(2,1)S(1)} %get-tuple-element.51.own, bf16[576,768]{1,0:T(8,128)(2,1)S(1)} %collective-permute-done.10.other, bf16[576,768]{1,0:T(8,128)(2,1)S(1)} %pre_slope_2.1.slope, bf16[3,768,768]{2,1,0:T(8,128)(2,1)S(1)} %get-tuple-element.54.weight, ...), custom_call_target="tpu_custom_call" | custom-call | flops 50000000 | bytes 140000 | tf_op jit(solution)/shard_map/block_step_2/pallas_call | solution.py:490
  135.7 0.4 collective-permute-start.11
  136.1 3.2 %collective-permute-start.13 = (bf16[528,768]{1,0:T(8,128)(2,1)S(1)}, bf16[528,768]{1,0:T(8,128)(2,1)S(1)}, u32[]{:S(2)}, u32[]{:S(2)}) collective-permute-start(bf16[528,768]{1,0:T(8,128)(2,1)S(1)} %copy-done.12), channel_id=1, source_target_pairs={{0,1},{1,0},{2,3},{3,2},{4,5},{5,4},{6,7},{7,6},{8,9},{9,8},{10,11... | collective-permute-start | bytes 2433032 | tf_op jit(solution)/shard_map/ppermute | solution.py:562
  139.3 3.1 %pre_slope_1.1.slope = bf16[544,768]{1,0:T(8,128)(2,1)S(1)} custom-call(s32[2]{0:T(128)S(1)} %add_convert_fusion.1.flags, bf16[544,768]{1,0:T(8,128)(2,1)S(1)} %copy-done.8, bf16[544,768]{1,0:T(8,128)(2,1)} %collective-permute-done.9.other), custom_call_target="tpu_custom_call" | custom-call | flops 40000000 | bytes 50000 | tf_op jit(solution)/shard_map/pre_slope_1/pallas_call | solution.py:372
  142.4 2.4 %stage_weights_1.1 = (bf16[3,768,768]{2,1,0:T(8,128)(2,1)S(1)}, bf16[768,768]{1,0:T(8,128)(2,1)S(1)}) custom-call(bf16[3,3,768,768]{3,2,1,0:T(8,128)(2,1)} %refs_0_.2, bf16[3,768,768]{2,1,0:T(8,128)(2,1)} %refs_1_.3), custom_call_target="tpu_custom_call" | custom-call | flops 10000000 | bytes 10000 | tf_op jit(solution)/shard_map/stage_weights_1/pallas_call | solution.py:253
  144.9 14.0 %collective-permute-done.11.other = bf16[544,768]{1,0:T(8,128)(2,1)S(1)} collective-permute-done((bf16[544,768]{1,0:T(8,128)(2,1)S(1)}, bf16[544,768]{1,0:T(8,128)(2,1)S(1)}, u32[]{:S(2)}, u32[]{:S(2)}) %collective-permute-start.11) | collective-permute-done | bytes 835616 | tf_op jit(solution)/shard_map/ppermute | solution.py:583
  158.8 3.7 %block_step_1.1 = (f32[528,768]{1,0:T(8,128)S(1)}, bf16[528,768]{1,0:T(8,128)(2,1)S(1)}) custom-call(bf16[544,768]{1,0:T(8,128)(2,1)S(1)} %get-tuple-element.58.own, bf16[544,768]{1,0:T(8,128)(2,1)S(1)} %collective-permute-done.11.other, bf16[544,768]{1,0:T(8,128)(2,1)S(1)} %pre_slope_1.1.slope, bf16[3,768,768]{2,1,0:T(8,128)(2,1)S(1)} %get-tuple-element.61.weight, ...), custom_call_target="tpu_custom_call" | custom-call | flops 50000000 | bytes 140000 | tf_op jit(solution)/shard_map/block_step_1/pallas_call | solution.py:490
  162.5 0.4 collective-permute-start.12
  162.9 13.3 %collective-permute-done.13.other = bf16[528,768]{1,0:T(8,128)(2,1)S(1)} collective-permute-done((bf16[528,768]{1,0:T(8,128)(2,1)S(1)}, bf16[528,768]{1,0:T(8,128)(2,1)S(1)}, u32[]{:S(2)}, u32[]{:S(2)}) %collective-permute-start.13) | collective-permute-done | bytes 811040 | tf_op jit(solution)/shard_map/ppermute | solution.py:562
  176.2 1.5 pre_slope_0.1.slope
  177.8 2.1 %stage_weights_0.1.weight = bf16[3,768,768]{2,1,0:T(8,128)(2,1)S(1)} custom-call(bf16[3,3,768,768]{3,2,1,0:T(8,128)(2,1)} %refs_0_.2), custom_call_target="tpu_custom_call" | custom-call | flops 10000000 | bytes 10000 | tf_op jit(solution)/shard_map/stage_weights_0/pallas_call | solution.py:253
  179.9 10.9 %collective-permute-done.12.other = bf16[528,768]{1,0:T(8,128)(2,1)S(1)} collective-permute-done((bf16[528,768]{1,0:T(8,128)(2,1)S(1)}, bf16[528,768]{1,0:T(8,128)(2,1)S(1)}, u32[]{:S(2)}, u32[]{:S(2)}) %collective-permute-start.12) | collective-permute-done | bytes 811040 | tf_op jit(solution)/shard_map/ppermute | solution.py:583
  190.8 3.0 %block_step_0.1 = bf16[512,768]{1,0:T(8,128)(2,1)} custom-call(bf16[528,768]{1,0:T(8,128)(2,1)S(1)} %get-tuple-element.65.own, bf16[528,768]{1,0:T(8,128)(2,1)S(1)} %collective-permute-done.12.other, bf16[528,768]{1,0:T(8,128)(2,1)S(1)} %pre_slope_0.1.slope, bf16[3,768,768]{2,1,0:T(8,128)(2,1)S(1)} %stage_weights_0.1.weight, ...), custom_call_target="tpu_custom_call" | custom-call | flops 50000000 | bytes 140000 | tf_op jit(solution)/shard_map/block_step_0/pallas_call | solution.py:490
  (45 shorter events, 0.2 us)
Async XLA Ops:
  6.5 0.7 copy-start.15
  7.3 0.7 copy-start.16
  9.9 0.7 copy-start.17
  14.1 19.4 %all-to-all-start = ((bf16[64,2,128]{2,1,0:T(2,128)(2,1)}), bf16[64,2,128]{2,1,0:T(2,128)(2,1)S(1)}, u32[]{:S(2)}, u32[]{:S(2)}) async-start(bf16[64,2,128]{2,1,0:T(2,128)(2,1)} %reshape.6), calls=%async_computation | async-start | bytes 65536 | tf_op jit(solution)/shard_map/all_to_all | solution.py:547
  23.9 66.2 %all-gather.2.cloned.1.call-start = ((), (), s32[]{:S(2)}) async-start(), calls=%async_computation.1 | async-start | bytes 7077888 | tf_op jit(solution)/shard_map/all_gather | solution.py:567
  24.0 9.6 %collective-permute-start.1 = (bf16[64,768]{1,0:T(8,128)(2,1)S(1)}, bf16[64,768]{1,0:T(8,128)(2,1)S(1)}, u32[]{:S(2)}, u32[]{:S(2)}) collective-permute-start(bf16[64,768]{1,0:T(8,128)(2,1)S(1)} %head_vectors.1), channel_id=1, source_target_pairs={{0,8},{2,10},{4,12},{6,14},{8,0},{10,2},{12,4},{14,6},{1,9},{3,11}... | collective-permute-start | bytes 294920 | tf_op jit(solution)/shard_map/ppermute | solution.py:513
  25.6 11.1 %collective-permute-start = (bf16[96,768]{1,0:T(8,128)(2,1)S(1)}, bf16[96,768]{1,0:T(8,128)(2,1)S(1)}, u32[]{:S(2)}, u32[]{:S(2)}) collective-permute-start(bf16[96,768]{1,0:T(8,128)(2,1)S(1)} %get-tuple-element.40), channel_id=1, source_target_pairs={{0,2},{2,4},{4,6},{6,8},{8,10},{10,12},{12,14},{14,16},{16,18},{18... | collective-permute-start | bytes 442376 | tf_op jit(solution)/shard_map/ppermute | solution.py:551
  29.1 8.0 %collective-permute-start.2 = (bf16[96,768]{1,0:T(8,128)(2,1)S(1)}, bf16[96,768]{1,0:T(8,128)(2,1)S(1)}, u32[]{:S(2)}, u32[]{:S(2)}) collective-permute-start(bf16[96,768]{1,0:T(8,128)(2,1)S(1)} %get-tuple-element.41), channel_id=1, source_target_pairs={{2,0},{4,2},{6,4},{8,6},{10,8},{12,10},{14,12},{16,14},{18,16},{20... | collective-permute-start | bytes 442376 | tf_op jit(solution)/shard_map/ppermute | solution.py:552
  33.7 12.5 %collective-permute-start.3 = (bf16[128,768]{1,0:T(8,128)(2,1)S(1)}, bf16[128,768]{1,0:T(8,128)(2,1)S(1)}, u32[]{:S(2)}, u32[]{:S(2)}) collective-permute-start(bf16[128,768]{1,0:T(8,128)(2,1)S(1)} %constant_dynamic-update-slice_fusion), channel_id=1, source_target_pairs={{0,6},{2,0},{4,2},{6,4},{8,14},{10,8},{12,10},{14,12},{1,7},{3,1},... | collective-permute-start | bytes 589832 | tf_op jit(solution)/shard_map/ppermute | solution.py:515
  34.4 12.4 %collective-permute-start.5 = (bf16[128,768]{1,0:T(8,128)(2,1)S(1)}, bf16[128,768]{1,0:T(8,128)(2,1)S(1)}, u32[]{:S(2)}, u32[]{:S(2)}) collective-permute-start(bf16[128,768]{1,0:T(8,128)(2,1)S(1)} %constant_dynamic-update-slice_fusion), channel_id=1, source_target_pairs={{0,2},{2,4},{4,6},{6,0},{8,10},{10,12},{12,14},{14,8},{1,3},{3,5},... | collective-permute-start | bytes 589832 | tf_op jit(solution)/shard_map/ppermute | solution.py:515
  35.8 10.4 %collective-permute-start.4 = (bf16[128,768]{1,0:T(8,128)(2,1)S(1)}, bf16[128,768]{1,0:T(8,128)(2,1)S(1)}, u32[]{:S(2)}, u32[]{:S(2)}) collective-permute-start(bf16[128,768]{1,0:T(8,128)(2,1)S(1)} %constant_dynamic-update-slice_fusion), channel_id=1, source_target_pairs={{0,4},{2,6},{4,0},{6,2},{8,12},{10,14},{12,8},{14,10},{1,5},{3,7},... | collective-permute-start | bytes 589832 | tf_op jit(solution)/shard_map/ppermute | solution.py:515
  43.4 3.5 %copy-start.5 = (bf16[544,768]{1,0:T(8,128)(2,1)}, bf16[544,768]{1,0:T(8,128)(2,1)S(1)}, u32[]{:S(2)}) copy-start(bf16[544,768]{1,0:T(8,128)(2,1)S(1)} %get-tuple-element.56.outer) | copy-start | bytes 2506756
  43.4 4.5 %copy-start.1 = (bf16[576,768]{1,0:T(8,128)(2,1)}, bf16[576,768]{1,0:T(8,128)(2,1)S(1)}, u32[]{:S(2)}) copy-start(bf16[576,768]{1,0:T(8,128)(2,1)S(1)} %get-tuple-element.43.own) | copy-start | bytes 2654212
  47.9 25.8 %collective-permute-start.8 = (bf16[576,768]{1,0:T(8,128)(2,1)S(1)}, bf16[576,768]{1,0:T(8,128)(2,1)S(1)}, u32[]{:S(2)}, u32[]{:S(2)}) collective-permute-start(bf16[576,768]{1,0:T(8,128)(2,1)S(1)} %get-tuple-element.43.own), channel_id=1, source_target_pairs={{0,1},{1,0},{2,3},{3,2},{4,5},{5,4},{6,7},{7,6},{8,9},{9,8},{10,11... | collective-permute-start | bytes 2654216 | tf_op jit(solution)/shard_map/ppermute | solution.py:562
  56.4 0.9 copy-start.9
  57.3 6.8 %copy-start.7 = (bf16[544,768]{1,0:T(8,128)(2,1)}, bf16[544,768]{1,0:T(8,128)(2,1)S(1)}, u32[]{:S(2)}) copy-start(bf16[544,768]{1,0:T(8,128)(2,1)S(1)} %get-tuple-element.46.own) | copy-start | bytes 2506756
  57.3 32.8 %collective-permute-start.9 = (bf16[544,768]{1,0:T(8,128)(2,1)S(1)}, bf16[544,768]{1,0:T(8,128)(2,1)}, u32[]{:S(2)}, u32[]{:S(2)}) collective-permute-start(bf16[544,768]{1,0:T(8,128)(2,1)S(1)} %get-tuple-element.46.own), channel_id=1, source_target_pairs={{0,1},{1,0},{2,3},{3,2},{4,5},{5,4},{6,7},{7,6},{8,9},{9,8},{10,11... | collective-permute-start | bytes 2506760 | tf_op jit(solution)/shard_map/ppermute | solution.py:562
  64.1 2.1 %copy-start = (bf16[2,512,2048]{2,1,0:T(8,128)(2,1)}, bf16[2,512,2048]{2,1,0:T(8,128)(2,1)S(1)}, u32[]{:S(2)}) copy-start(bf16[2,512,2048]{2,1,0:T(8,128)(2,1)S(1)} %spread_entries.1.spread) | copy-start | bytes 12582916
  67.0 25.4 %collective-permute-start.7 = (bf16[2,32,2048]{2,1,0:T(8,128)(2,1)}, bf16[2,32,2048]{2,1,0:T(8,128)(2,1)S(1)}, u32[]{:S(2)}, u32[]{:S(2)}) collective-permute-start(bf16[2,32,2048]{2,1,0:T(8,128)(2,1)} %get-tuple-element.71), channel_id=1, source_target_pairs={{2,0},{4,2},{6,4},{8,6},{10,8},{12,10},{14,12},{16,14},{18,16},{20... | collective-permute-start | bytes 786440 | tf_op jit(solution)/shard_map/ppermute | solution.py:575
  71.5 25.0 %collective-permute-start.6 = (bf16[2,32,2048]{2,1,0:T(8,128)(2,1)}, bf16[2,32,2048]{2,1,0:T(8,128)(2,1)S(1)}, u32[]{:S(2)}, u32[]{:S(2)}) collective-permute-start(bf16[2,32,2048]{2,1,0:T(8,128)(2,1)} %get-tuple-element.72), channel_id=1, source_target_pairs={{0,2},{2,4},{4,6},{6,8},{8,10},{10,12},{12,14},{14,16},{16,18},{18... | collective-permute-start | bytes 786440 | tf_op jit(solution)/shard_map/ppermute | solution.py:574
  73.7 6.4 %copy-start.3 = (bf16[576,768]{1,0:T(8,128)(2,1)}, bf16[576,768]{1,0:T(8,128)(2,1)S(1)}, u32[]{:S(2)}) copy-start(bf16[576,768]{1,0:T(8,128)(2,1)S(1)} %collective-permute-done.8.other) | copy-start | bytes 2654212
  80.1 0.9 copy-start.11
  81.0 0.9 copy-start.13
  92.4 4.1 %copy-start.18 = (bf16[2,32,2048]{2,1,0:T(8,128)(2,1)}, bf16[2,32,2048]{2,1,0:T(8,128)(2,1)S(1)}, u32[]{:S(2)}) copy-start(bf16[2,32,2048]{2,1,0:T(8,128)(2,1)S(1)} %collective-permute-done.7.high) | copy-start | bytes 786436
  96.5 0.7 copy-start.19
  109.7 22.3 %collective-permute-start.10 = (bf16[576,768]{1,0:T(8,128)(2,1)S(1)}, bf16[576,768]{1,0:T(8,128)(2,1)S(1)}, u32[]{:S(2)}, u32[]{:S(2)}) collective-permute-start(bf16[576,768]{1,0:T(8,128)(2,1)S(1)} %get-tuple-element.51.own), channel_id=1, source_target_pairs={{0,1},{1,0},{2,3},{3,2},{4,5},{5,4},{6,7},{7,6},{8,9},{9,8},{10,11... | collective-permute-start | bytes 2654216 | tf_op jit(solution)/shard_map/ppermute | solution.py:583
  109.8 1.2 copy-start.2
  111.0 1.2 copy-start.4
  113.8 18.2 %copy-start.6 = (bf16[544,768]{1,0:T(8,128)(2,1)S(1)}, bf16[544,768]{1,0:T(8,128)(2,1)}, u32[]{:S(2)}) copy-start(bf16[544,768]{1,0:T(8,128)(2,1)} %copy-done.5) | copy-start | bytes 2506756
  132.0 4.1 %copy-start.12 = (bf16[528,768]{1,0:T(8,128)(2,1)S(1)}, bf16[528,768]{1,0:T(8,128)(2,1)}, u32[]{:S(2)}) copy-start(bf16[528,768]{1,0:T(8,128)(2,1)} %copy-done.11) | copy-start | bytes 2433028
  132.0 7.4 %copy-start.8 = (bf16[544,768]{1,0:T(8,128)(2,1)S(1)}, bf16[544,768]{1,0:T(8,128)(2,1)}, u32[]{:S(2)}) copy-start(bf16[544,768]{1,0:T(8,128)(2,1)} %copy-done.7) | copy-start | bytes 2506756
  135.7 23.1 %collective-permute-start.11 = (bf16[544,768]{1,0:T(8,128)(2,1)S(1)}, bf16[544,768]{1,0:T(8,128)(2,1)S(1)}, u32[]{:S(2)}, u32[]{:S(2)}) collective-permute-start(bf16[544,768]{1,0:T(8,128)(2,1)S(1)} %get-tuple-element.58.own), channel_id=1, source_target_pairs={{0,1},{1,0},{2,3},{3,2},{4,5},{5,4},{6,7},{7,6},{8,9},{9,8},{10,11... | collective-permute-start | bytes 2506760 | tf_op jit(solution)/shard_map/ppermute | solution.py:583
  136.1 40.1 %collective-permute-start.13 = (bf16[528,768]{1,0:T(8,128)(2,1)S(1)}, bf16[528,768]{1,0:T(8,128)(2,1)S(1)}, u32[]{:S(2)}, u32[]{:S(2)}) collective-permute-start(bf16[528,768]{1,0:T(8,128)(2,1)S(1)} %copy-done.12), channel_id=1, source_target_pairs={{0,1},{1,0},{2,3},{3,2},{4,5},{5,4},{6,7},{7,6},{8,9},{9,8},{10,11... | collective-permute-start | bytes 2433032 | tf_op jit(solution)/shard_map/ppermute | solution.py:562
  142.4 16.4 %copy-start.10 = (bf16[528,768]{1,0:T(8,128)(2,1)S(1)}, bf16[528,768]{1,0:T(8,128)(2,1)}, u32[]{:S(2)}) copy-start(bf16[528,768]{1,0:T(8,128)(2,1)} %copy-done.9) | copy-start | bytes 2433028
  162.5 28.3 %collective-permute-start.12 = (bf16[528,768]{1,0:T(8,128)(2,1)S(1)}, bf16[528,768]{1,0:T(8,128)(2,1)S(1)}, u32[]{:S(2)}, u32[]{:S(2)}) collective-permute-start(bf16[528,768]{1,0:T(8,128)(2,1)S(1)} %get-tuple-element.65.own), channel_id=1, source_target_pairs={{0,1},{1,0},{2,3},{3,2},{4,5},{5,4},{6,7},{7,6},{8,9},{9,8},{10,11... | collective-permute-start | bytes 2433032 | tf_op jit(solution)/shard_map/ppermute | solution.py:583
  177.8 13.1 %copy-start.14 = (bf16[512,768]{1,0:T(8,128)(2,1)S(1)}, bf16[512,768]{1,0:T(8,128)(2,1)}, u32[]{:S(2)}) copy-start(bf16[512,768]{1,0:T(8,128)(2,1)} %copy-done.13) | copy-start | bytes 2359300
Sparse Core Ops, SparseCore 0:
  48.0 42.0 all-gather.1

commit v8 on v6

--- a/solution.py
+++ b/solution.py
@@ -358,27 +358,35 @@
     )(in_hbm(saved), low, high, in_hbm(weights))
 
 
-def pre_slope(level, flags, own, other, rows):
+def pre_slope(level, flags, own, others, rows):
     count, width = own.shape
-    blocks = pl.BlockSpec((count, COLS), lambda i, flags: (0, i))
+    blocks = lambda size: pl.BlockSpec((size, COLS), lambda i, flags: (0, i))
     halo = HALO_IN[level]
 
-    def body(flags, own, other, out):
-        slope = gelu_parts(own[...].astype(F32) + other[...].astype(F32))[1]
-        at = lax.broadcasted_iota(jnp.int32, slope.shape, 0)
-        outside = ((at < halo) & (flags[0] != 0)) | ((at >= halo + rows) & (flags[1] != 0))
-        out[...] = jnp.where(outside, 0.0, slope).astype(BF16)
+    def body(flags, own, *refs):
+        out = refs[-1]
+        start = 0
+        for other in refs[:-1]:
+            end = start + other.shape[0]
+            slope = gelu_parts(own[start:end, :].astype(F32) + other[...].astype(F32))[1]
+            at = lax.broadcasted_iota(jnp.int32, slope.shape, 0) + start
+            outside = ((at < halo) & (flags[0] != 0)) | ((at >= halo + rows) & (flags[1] != 0))
+            out[start:end, :] = jnp.where(outside, 0.0, slope).astype(BF16)
+            start = end
 
     return pl.pallas_call(
         body,
         grid_spec=pltpu.PrefetchScalarGridSpec(
-            num_scalar_prefetch=1, grid=(width // COLS,), in_specs=[blocks, blocks], out_specs=blocks
+            num_scalar_prefetch=1,
+            grid=(width // COLS,),
+            in_specs=[blocks(count)] + [blocks(other.shape[0]) for other in others],
+            out_specs=blocks(count),
         ),
         out_shape=jax.ShapeDtypeStruct((count, width), BF16),
         cost_estimate=cost(4e9, 5e6),
         compiler_params=params(),
         name=f"pre_slope_{level}",
-    )(flags, own, other)
+    )(flags, own, *others)
 
 
 def top_kernel(
@@ -386,29 +394,24 @@
 ):
     rows, reach = spread.shape[1], low.shape[1]
     columns = column_blocks(grad.shape[1])
-    to_held = lambda k, half: (
-        vectors.at[:, half, :, columns[k]],
-        held.at[k, half].reshape(vectors.shape[0], vectors.shape[2], COLS),
-    )
     batches = []
     for half in range(2):
         batches.append([
             (spread.at[half], matrix.at[half, pl.ds(reach, rows), :]),
             (low.at[(half + turned[0]) % 2], matrix.at[half, pl.ds(0, reach), :]),
             (high.at[(half + turned[1]) % 2], matrix.at[half, pl.ds(reach + rows, reach), :]),
-            to_held(0, half),
+            (vectors.at[:, half], held.at[half].reshape(vectors.shape[0], *vectors.shape[2:])),
         ])
-    for k in range(1, len(columns)):
-        batches.append([to_held(k, half) for half in range(2)])
     batches.append([(expand.at[expand.shape[0] - 1], kernel)])
     arrive = staged(batches, sems)
-    for k, cols in enumerate(columns):
-        top = None
-        for half in range(2):
-            if k == 0 or half == 0:
-                arrive()
-            piece = jnp.dot(matrix[half], held[k, half], preferred_element_type=F32)
-            top = piece if top is None else top + piece
+    arrive()
+    for cols in columns:
+        grad[:, cols] = jnp.dot(matrix[0], held[0, :, cols], preferred_element_type=F32)
+    arrive()
+    for cols in columns:
+        top = grad[:, cols] + jnp.dot(
+            matrix[1], held[1, :, cols], preferred_element_type=F32
+        )
         grad[:, cols] = top
         rounded[:, cols] = top.astype(BF16)
     arrive()
@@ -423,7 +426,6 @@
     count = rows + 2 * low.shape[1]
     share = vectors.shape[1]
     width = expand.shape[1]
-    blocks = share // COLS
     vectors = vectors.reshape(depth // SLOTS, 2, SLOTS, share)
     return pl.pallas_call(
         top_kernel,
@@ -435,10 +437,10 @@
         ],
         scratch_shapes=[
             pltpu.VMEM((2, count, depth), BF16),
-            pltpu.VMEM((blocks, 2, depth, COLS), BF16),
+            pltpu.VMEM((2, depth, share), BF16),
             pltpu.VMEM((width, share), BF16),
             pltpu.VMEM((count, share), BF16),
-            pltpu.SemaphoreType.DMA((7 + 2 * blocks,)),
+            pltpu.SemaphoreType.DMA((9,)),
         ],
         cost_estimate=cost(5e9, 14e6),
         compiler_params=params(),
@@ -506,11 +508,10 @@
     return lax.optimization_barrier((value, *earlier))[0]
 
 
-def along_head(vectors, place, first, second):
+def along_head(vectors, other, place, first, second):
     count = vectors.shape[0]
     turn = place % 4
     same = lambda steps: [(a * 4 + z, a * 4 + (z - steps) % 4) for a in range(2) for z in range(4)]
-    other = lax.ppermute(vectors, "head", [(k, (k + 4) % 8) for k in range(8)])
     both = jnp.concatenate([after(vectors, *first), other], axis=0)
     parts = [lax.ppermute(both, "head", same(k)) for k in (1, 2, 3)]
     parts = [after(both, *second)] + parts
@@ -540,13 +541,17 @@
 
     place = lax.axis_index("head")
     along, turn = place // 4, place % 4
-    vectors = head_vectors(
-        chan_place[None].astype(jnp.int32), head_weight, batch_of, erase_left, erase_right, share
-    )
-    first, final = cut_edges(after(inputs_saved, vectors))
+    first, final = cut_edges(inputs_saved)
     low = lax.ppermute(final, GROUP_AXES, up)
     high = lax.ppermute(first, GROUP_AXES, down)
-    payload = bucket(cover_bins, bin_gradient, members, rows)
+    vectors = head_vectors(
+        chan_place[None].astype(jnp.int32), after(head_weight, first), batch_of, erase_left, erase_right, share
+    )
+    beside = lax.ppermute(vectors, "head", [(k, (k + 4) % 8) for k in range(8)])
+    payload = bucket(after(cover_bins, vectors), bin_gradient, members, rows)
+    arrived = lax.all_to_all(
+        after(payload, low, high, beside), GROUP_AXES, split_axis=0, concat_axis=0, tiled=True
+    )
     flags = jnp.stack([member == 0, member == members - 1]).astype(jnp.int32)
     sends, outers, others = {}, {}, {}
 
@@ -556,33 +561,39 @@
         )
 
     def exchange(n, *earlier):
-        others[n] = lax.ppermute(after(sends[n], *earlier), "chan", swap)
+        others[n] = (lax.ppermute(after(sends[n], *earlier), "chan", swap),)
 
     begin(levels[0])
     exchange(levels[0])
-    arrived = lax.all_to_all(payload, GROUP_AXES, split_axis=0, concat_axis=0, tiled=True)
-    ring = along_head(vectors, place, (payload, first), (sends[levels[0]], arrived))
+    begin(levels[1], arrived)
+    exchange(levels[1])
+    ring = along_head(
+        vectors, beside, place, (arrived, sends[levels[0]]), (sends[levels[1]],)
+    )
     gathered = lax.all_gather(ring, "pos", tiled=True)
-    begin(levels[1], ring)
-    exchange(levels[1])
     reach = HALO_IN[layers - 1]
     spread = spread_entries(
-        along[None].astype(jnp.int32), after(arrived, sends[levels[1]]), rows
+        along[None].astype(jnp.int32), after(arrived, ring), rows
     )
     spread_low = lax.ppermute(spread[:, rows - reach :], GROUP_AXES, up)
     spread_high = lax.ppermute(spread[:, :reach], GROUP_AXES, down)
-    begin(levels[2], spread, others[levels[0]])
+    begin(levels[2], spread, *others[levels[0]])
+    parts = sends[levels[2]].shape[0] // 32 * 16
+    early = lax.ppermute(sends[levels[2]][:parts], "chan", swap)
     turned = jnp.stack([turn == 0, turn == 3]).astype(jnp.int32)
-    gathered = after(gathered, sends[levels[2]], others[levels[1]])
+    gathered = after(gathered, early, *others[levels[1]])
     grad, send = top_gradient(
         turned, spread, spread_low, spread_high, gathered, expand_weight
     )
     for n in levels:
         other = lax.ppermute(send, "chan", swap)
         if n == levels[0]:
-            exchange(levels[2], other)
-        slope = pre_slope(n, flags, sends[n], after(others[n], send), rows)
-        weights = stage_weights(n, after(conv_weight, slope), expand_weight)
+            late = after(sends[levels[2]][parts:], other)
+            others[levels[2]] = (early, lax.ppermute(late, "chan", swap))
+        there = (after(others[n][0], send), *others[n][1:])
+        slope = pre_slope(n, flags, sends[n], there, rows)
+        ready = (slope, *others[levels[2]]) if n == levels[1] else (slope,)
+        weights = stage_weights(n, after(conv_weight, *ready), expand_weight)
         outs = block_step(n, send, other, slope, weights[0], grad, outers[n], *weights[1:])
         if n:
             grad, send = outs

time: 202 us -> 216 us (1.069)
  the two profiles are of different devices: /device:TPU:0 before, /device:TPU:6 now
where the time goes in v8:
time: 216 us; the launch traced here: 215 us
  waiting for transfers between devices  83.7 us (39%)
  Pallas kernels  63.5 us (29%)
  starting transfers between devices  44.3 us (21%)
  between operations  13.8 us (6%)
  local copies, waits for them, and re-layouts  8.74 us (4%)
    ppermute x3, waiting for transfers between devices, per_device(): other = lax.ppermute(send, 'chan', swap)  28.1 us
    ppermute x1, waiting for transfers between devices, per_device(): others[levels[2]] = (early, lax.ppermute(late, 'chan', swap))  24.8 us
    pallas_call x3, Pallas kernels, pre_partial(): pl.pallas_call(functools.partial(pre_kernel, level), in_specs=[HBM, VMEM,...  18.9 us
    ppermute x2, waiting for transfers between devices, exchange(): others[n] = (lax.ppermute(after(sends[n], *earlier), 'chan', swap),)  17.6 us
    pallas_call x3, Pallas kernels, block_step(): pl.pallas_call(functools.partial(block_kernel, level), in_specs=[VMEM] *...  11.8 us
    ppermute x3, starting transfers between devices, per_device(): other = lax.ppermute(send, 'chan', swap)  10.1 us
    pallas_call x1, Pallas kernels, top_gradient(): pl.pallas_call(top_kernel, in_specs=[SMEM] + [HBM] * 5, out_specs=[VMEM,...  9.45 us
    ppermute x1, waiting for transfers between devices, per_device(): early = lax.ppermute(sends[levels[2]][:parts], 'chan', swap)  8.27 us
  transfers between devices with their start and end apart: 17, of which 9 were waited for; matrix products, arithmetic and copies ran while one was open for 0% of the time, Pallas kernels for 19%

profile of v8, /device:TPU:6, one launch (start us, length us, event | category | flops | bytes accessed | tf_op | source)
XLA Modules:
  0.0 214.9 jit_solution(7378620958740986178)
XLA Ops:
  6.5 1.1 cut_edges.1
  7.6 3.8 %collective-permute-start = (bf16[96,768]{1,0:T(8,128)(2,1)S(1)}, bf16[96,768]{1,0:T(8,128)(2,1)S(1)}, u32[]{:S(2)}, u32[]{:S(2)}) collective-permute-start(bf16[96,768]{1,0:T(8,128)(2,1)S(1)} %get-tuple-element.42), channel_id=1, source_target_pairs={{0,2},{2,4},{4,6},{6,8},{8,10},{10,12},{12,14},{14,16},{16,18},{18... | collective-permute-start | bytes 442376 | tf_op jit(solution)/shard_map/ppermute | solution.py:545
  11.5 4.8 %collective-permute-start.1 = (bf16[96,768]{1,0:T(8,128)(2,1)S(1)}, bf16[96,768]{1,0:T(8,128)(2,1)S(1)}, u32[]{:S(2)}, u32[]{:S(2)}) collective-permute-start(bf16[96,768]{1,0:T(8,128)(2,1)S(1)} %get-tuple-element.39), channel_id=1, source_target_pairs={{2,0},{4,2},{6,4},{8,6},{10,8},{12,10},{14,12},{16,14},{18,16},{20... | collective-permute-start | bytes 442376 | tf_op jit(solution)/shard_map/ppermute | solution.py:546
  16.3 1.8 head_vectors.1
  18.0 1.0 collective-permute-start.2
  19.1 1.9 bucket_entries.1
  21.0 2.2 %collective-permute-done.2 = bf16[64,768]{1,0:T(8,128)(2,1)S(1)} collective-permute-done((bf16[64,768]{1,0:T(8,128)(2,1)S(1)}, bf16[64,768]{1,0:T(8,128)(2,1)S(1)}, u32[]{:S(2)}, u32[]{:S(2)}) %collective-permute-start.2) | collective-permute-done | bytes 98336 | tf_op jit(solution)/shard_map/ppermute | solution.py:550
  23.2 0.0 collective-permute-done.low
  23.3 0.0 collective-permute-done.1.high
  23.3 0.5 broadcast.3
  23.8 0.7 reduce
  24.4 0.6 reshape.6
  25.1 6.8 %all-to-all-start = ((bf16[64,2,128]{2,1,0:T(2,128)(2,1)}), bf16[64,2,128]{2,1,0:T(2,128)(2,1)S(1)}, u32[]{:S(2)}, u32[]{:S(2)}) async-start(bf16[64,2,128]{2,1,0:T(2,128)(2,1)} %reshape.6), calls=%async_computation | async-start | bytes 65536 | tf_op jit(solution)/shard_map/all_to_all | solution.py:552
  31.8 0.0 all-gather.2.cloned.1.call-start
  31.9 6.3 %pre_partial_2.1 = (bf16[576,768]{1,0:T(8,128)(2,1)S(1)}, bf16[544,768]{1,0:T(8,128)(2,1)S(1)}) custom-call(bf16[3,512,768]{2,1,0:T(8,128)(2,1)} %saved.7, bf16[96,768]{1,0:T(8,128)(2,1)S(1)} %collective-permute-done.low, bf16[96,768]{1,0:T(8,128)(2,1)S(1)} %collective-permute-done.1.high, bf16[3,3,768,768]{3,2,1,0:T(8,128)(2,1)} %refs_0_.2), custom_call_target="tpu_custom_call" | custom-call | flops 50000000 | bytes 80000 | tf_op jit(solution)/shard_map/pre_partial_2/pallas_call | solution.py:340
  38.2 1.0 copy-done.5
  39.2 0.0 all-to-all-done
  39.3 2.8 %collective-permute-start.3 = (bf16[128,768]{1,0:T(8,128)(2,1)S(1)}, bf16[128,768]{1,0:T(8,128)(2,1)S(1)}, u32[]{:S(2)}, u32[]{:S(2)}) collective-permute-start(bf16[128,768]{1,0:T(8,128)(2,1)S(1)} %constant_dynamic-update-slice_fusion), channel_id=1, source_target_pairs={{0,6},{2,0},{4,2},{6,4},{8,14},{10,8},{12,10},{14,12},{1,7},{3,1},... | collective-permute-start | bytes 589832 | tf_op jit(solution)/shard_map/ppermute | solution.py:516
  42.0 0.0 collective-permute-start.5
  42.0 2.3 %collective-permute-start.4 = (bf16[128,768]{1,0:T(8,128)(2,1)S(1)}, bf16[128,768]{1,0:T(8,128)(2,1)S(1)}, u32[]{:S(2)}, u32[]{:S(2)}) collective-permute-start(bf16[128,768]{1,0:T(8,128)(2,1)S(1)} %constant_dynamic-update-slice_fusion), channel_id=1, source_target_pairs={{0,4},{2,6},{4,0},{6,2},{8,12},{10,14},{12,8},{14,10},{1,5},{3,7},... | collective-permute-start | bytes 589832 | tf_op jit(solution)/shard_map/ppermute | solution.py:516
  44.4 6.1 %pre_partial_1.1 = (bf16[544,768]{1,0:T(8,128)(2,1)S(1)}, bf16[528,768]{1,0:T(8,128)(2,1)S(1)}) custom-call(bf16[3,512,768]{2,1,0:T(8,128)(2,1)} %saved.7, bf16[96,768]{1,0:T(8,128)(2,1)S(1)} %collective-permute-done.low, bf16[96,768]{1,0:T(8,128)(2,1)S(1)} %collective-permute-done.1.high, bf16[3,3,768,768]{3,2,1,0:T(8,128)(2,1)} %refs_0_.2), custom_call_target="tpu_custom_call" | custom-call | flops 50000000 | bytes 80000 | tf_op jit(solution)/shard_map/pre_partial_1/pallas_call | solution.py:340
  50.5 0.9 copy-done.7
  51.4 0.0 collective-permute-done.3
  51.5 1.9 collective-permute-done.4
  53.4 0.8 collective-permute-done.5
  54.3 0.9 constant_dynamic-slice_fusion
  55.2 0.0 all-gather.2.cloned.1.call-update
  55.3 3.0 %collective-permute-start.8 = (bf16[576,768]{1,0:T(8,128)(2,1)S(1)}, bf16[576,768]{1,0:T(8,128)(2,1)S(1)}, u32[]{:S(2)}, u32[]{:S(2)}) collective-permute-start(bf16[576,768]{1,0:T(8,128)(2,1)S(1)} %get-tuple-element.44.own), channel_id=1, source_target_pairs={{0,1},{1,0},{2,3},{3,2},{4,5},{5,4},{6,7},{7,6},{8,9},{9,8},{10,11... | collective-permute-start | bytes 2654216 | tf_op jit(solution)/shard_map/ppermute | solution.py:564
  58.2 0.6 collective-permute-start.10
  58.9 5.5 %spread_entries.1.spread = bf16[2,512,2048]{2,1,0:T(8,128)(2,1)S(1)} custom-call(s32[1]{0:T(128)} %bitcast.2.along, bf16[64,256]{1,0:T(8,128)(2,1)S(1)} %bitcast.16), custom_call_target="tpu_custom_call" | custom-call | flops 60000000 | bytes 80000 | tf_op jit(solution)/shard_map/spread_entries/pallas_call | solution.py:227
  64.4 15.0 %collective-permute-done.8.refs_0_ = bf16[576,768]{1,0:T(8,128)(2,1)S(1)} collective-permute-done((bf16[576,768]{1,0:T(8,128)(2,1)S(1)}, bf16[576,768]{1,0:T(8,128)(2,1)S(1)}, u32[]{:S(2)}, u32[]{:S(2)}) %collective-permute-start.8) | collective-permute-done | bytes 884768 | tf_op jit(solution)/shard_map/ppermute | solution.py:564
  79.4 6.4 %pre_partial_0.1 = (bf16[528,768]{1,0:T(8,128)(2,1)S(1)}, bf16[512,768]{1,0:T(8,128)(2,1)S(1)}) custom-call(bf16[3,512,768]{2,1,0:T(8,128)(2,1)} %saved.7, bf16[96,768]{1,0:T(8,128)(2,1)S(1)} %collective-permute-done.low, bf16[96,768]{1,0:T(8,128)(2,1)S(1)} %collective-permute-done.1.high, bf16[3,3,768,768]{3,2,1,0:T(8,128)(2,1)} %refs_0_.2), custom_call_target="tpu_custom_call" | custom-call | flops 50000000 | bytes 80000 | tf_op jit(solution)/shard_map/pre_partial_0/pallas_call | solution.py:340
  85.9 3.0 %collective-permute-start.9 = (bf16[256,768]{1,0:T(8,128)(2,1)S(1)}, bf16[256,768]{1,0:T(8,128)(2,1)S(1)}, u32[]{:S(2)}, u32[]{:S(2)}) collective-permute-start(bf16[256,768]{1,0:T(8,128)(2,1)S(1)} %slice.14), channel_id=1, source_target_pairs={{0,1},{1,0},{2,3},{3,2},{4,5},{5,4},{6,7},{7,6},{8,9},{9,8},{10,11... | collective-permute-start | bytes 1179656 | tf_op jit(solution)/shard_map/ppermute | solution.py:582
  88.9 1.9 collective-permute-start.7
  90.8 3.9 %collective-permute-start.6 = (bf16[2,32,2048]{2,1,0:T(8,128)(2,1)S(1)}, bf16[2,32,2048]{2,1,0:T(8,128)(2,1)S(1)}, u32[]{:S(2)}, u32[]{:S(2)}) collective-permute-start(bf16[2,32,2048]{2,1,0:T(8,128)(2,1)S(1)} %get-tuple-element.74), channel_id=1, source_target_pairs={{0,2},{2,4},{4,6},{6,8},{8,10},{10,12},{12,14},{14,16},{16,18},{18... | collective-permute-start | bytes 786440 | tf_op jit(solution)/shard_map/ppermute | solution.py:578
  94.8 0.1 add_convert_fusion.turned
  94.8 2.6 %collective-permute-done.10.refs_0_ = bf16[544,768]{1,0:T(8,128)(2,1)} collective-permute-done((bf16[544,768]{1,0:T(8,128)(2,1)}, bf16[544,768]{1,0:T(8,128)(2,1)}, u32[]{:S(2)}, u32[]{:S(2)}) %collective-permute-start.10) | collective-permute-done | bytes 835616 | tf_op jit(solution)/shard_map/ppermute | solution.py:564
  97.4 8.3 %collective-permute-done.9.refs_0_ = bf16[256,768]{1,0:T(8,128)(2,1)S(1)} collective-permute-done((bf16[256,768]{1,0:T(8,128)(2,1)S(1)}, bf16[256,768]{1,0:T(8,128)(2,1)S(1)}, u32[]{:S(2)}, u32[]{:S(2)}) %collective-permute-start.9) | collective-permute-done | bytes 393248 | tf_op jit(solution)/shard_map/ppermute | solution.py:582
  105.7 0.7 copy-done.13
  106.5 0.0 collective-permute-done.7.high
  106.5 0.0 collective-permute-done.6.low
  106.5 0.7 copy-done.18
  107.2 0.7 copy-done.19
  107.9 9.5 %top_gradient.1 = (f32[576,768]{1,0:T(8,128)S(1)}, bf16[576,768]{1,0:T(8,128)(2,1)S(1)}) custom-call(s32[2]{0:T(128)S(1)} %add_convert_fusion.turned, bf16[2,512,2048]{2,1,0:T(8,128)(2,1)} %copy-done, bf16[2,32,2048]{2,1,0:T(8,128)(2,1)} %copy-done.19, bf16[2,32,2048]{2,1,0:T(8,128)(2,1)} %copy-done.18, bf16[32,2,64,768]{3,2,1,0:T(8,128)(2,1)} %bitcast.21, ...), custom_call_target="tpu_custom_call" | custom-call | flops 50000000 | bytes 140000 | tf_op jit(solution)/shard_map/top_gradient/pallas_call | solution.py:430
  117.4 3.0 %collective-permute-start.11 = (bf16[576,768]{1,0:T(8,128)(2,1)S(1)}, bf16[576,768]{1,0:T(8,128)(2,1)}, u32[]{:S(2)}, u32[]{:S(2)}) collective-permute-start(bf16[576,768]{1,0:T(8,128)(2,1)S(1)} %get-tuple-element.53.own), channel_id=1, source_target_pairs={{0,1},{1,0},{2,3},{3,2},{4,5},{5,4},{6,7},{7,6},{8,9},{9,8},{10,11... | collective-permute-start | bytes 2654216 | tf_op jit(solution)/shard_map/ppermute | solution.py:589
  120.3 0.1 add_convert_fusion.1.flags
  120.4 1.2 copy-done.2
  121.6 1.2 copy-done.4
  122.8 1.6 pre_slope_2.1.slope
  124.4 2.4 %stage_weights_2.1 = (bf16[3,768,768]{2,1,0:T(8,128)(2,1)S(1)}, bf16[768,768]{1,0:T(8,128)(2,1)S(1)}) custom-call(bf16[3,3,768,768]{3,2,1,0:T(8,128)(2,1)} %refs_0_.2, bf16[3,768,768]{2,1,0:T(8,128)(2,1)} %refs_1_.3), custom_call_target="tpu_custom_call" | custom-call | flops 10000000 | bytes 10000 | tf_op jit(solution)/shard_map/stage_weights_2/pallas_call | solution.py:253
  126.8 13.3 %collective-permute-done.11.other = bf16[576,768]{1,0:T(8,128)(2,1)} collective-permute-done((bf16[576,768]{1,0:T(8,128)(2,1)S(1)}, bf16[576,768]{1,0:T(8,128)(2,1)}, u32[]{:S(2)}, u32[]{:S(2)}) %collective-permute-start.11) | collective-permute-done | bytes 884768 | tf_op jit(solution)/shard_map/ppermute | solution.py:589
  140.1 5.0 %block_step_2.1 = (f32[544,768]{1,0:T(8,128)S(1)}, bf16[544,768]{1,0:T(8,128)(2,1)S(1)}) custom-call(bf16[576,768]{1,0:T(8,128)(2,1)S(1)} %get-tuple-element.53.own, bf16[576,768]{1,0:T(8,128)(2,1)} %collective-permute-done.11.other, bf16[576,768]{1,0:T(8,128)(2,1)S(1)} %pre_slope_2.1.slope, bf16[3,768,768]{2,1,0:T(8,128)(2,1)S(1)} %get-tuple-element.56.weight, ...), custom_call_target="tpu_custom_call" | custom-call | flops 50000000 | bytes 140000 | tf_op jit(solution)/shard_map/block_step_2/pallas_call | solution.py:492
  145.2 4.1 %collective-permute-start.12 = (bf16[544,768]{1,0:T(8,128)(2,1)S(1)}, bf16[544,768]{1,0:T(8,128)(2,1)S(1)}, u32[]{:S(2)}, u32[]{:S(2)}) collective-permute-start(bf16[544,768]{1,0:T(8,128)(2,1)S(1)} %get-tuple-element.60.own), channel_id=1, source_target_pairs={{0,1},{1,0},{2,3},{3,2},{4,5},{5,4},{6,7},{7,6},{8,9},{9,8},{10,11... | collective-permute-start | bytes 2506760 | tf_op jit(solution)/shard_map/ppermute | solution.py:589
  149.3 0.3 collective-permute-start.13
  149.6 3.1 %pre_slope_1.1.slope = bf16[544,768]{1,0:T(8,128)(2,1)S(1)} custom-call(s32[2]{0:T(128)S(1)} %add_convert_fusion.1.flags, bf16[544,768]{1,0:T(8,128)(2,1)S(1)} %copy-done.8, bf16[544,768]{1,0:T(8,128)(2,1)} %collective-permute-done.10.refs_0_), custom_call_target="tpu_custom_call" | custom-call | flops 40000000 | bytes 50000 | tf_op jit(solution)/shard_map/pre_slope_1/pallas_call | solution.py:377
  152.7 24.8 %collective-permute-done.13.refs_1_ = bf16[272,768]{1,0:T(8,128)(2,1)S(1)} collective-permute-done((bf16[272,768]{1,0:T(8,128)(2,1)S(1)}, bf16[272,768]{1,0:T(8,128)(2,1)S(1)}, u32[]{:S(2)}, u32[]{:S(2)}) %collective-permute-start.13) | collective-permute-done | bytes 417824 | tf_op jit(solution)/shard_map/ppermute | solution.py:592
  177.5 2.4 %stage_weights_1.1 = (bf16[3,768,768]{2,1,0:T(8,128)(2,1)S(1)}, bf16[768,768]{1,0:T(8,128)(2,1)S(1)}) custom-call(bf16[3,3,768,768]{3,2,1,0:T(8,128)(2,1)} %refs_0_.2, bf16[3,768,768]{2,1,0:T(8,128)(2,1)} %refs_1_.3), custom_call_target="tpu_custom_call" | custom-call | flops 10000000 | bytes 10000 | tf_op jit(solution)/shard_map/stage_weights_1/pallas_call | solution.py:253
  179.8 0.0 collective-permute-done.12.other
  179.9 3.7 %block_step_1.1 = (f32[528,768]{1,0:T(8,128)S(1)}, bf16[528,768]{1,0:T(8,128)(2,1)S(1)}) custom-call(bf16[544,768]{1,0:T(8,128)(2,1)S(1)} %get-tuple-element.60.own, bf16[544,768]{1,0:T(8,128)(2,1)S(1)} %collective-permute-done.12.other, bf16[544,768]{1,0:T(8,128)(2,1)S(1)} %pre_slope_1.1.slope, bf16[3,768,768]{2,1,0:T(8,128)(2,1)S(1)} %get-tuple-element.64.weight, ...), custom_call_target="tpu_custom_call" | custom-call | flops 50000000 | bytes 140000 | tf_op jit(solution)/shard_map/block_step_1/pallas_call | solution.py:492
  183.5 3.0 %collective-permute-start.14 = (bf16[528,768]{1,0:T(8,128)(2,1)S(1)}, bf16[528,768]{1,0:T(8,128)(2,1)S(1)}, u32[]{:S(2)}, u32[]{:S(2)}) collective-permute-start(bf16[528,768]{1,0:T(8,128)(2,1)S(1)} %get-tuple-element.68.own), channel_id=1, source_target_pairs={{0,1},{1,0},{2,3},{3,2},{4,5},{5,4},{6,7},{7,6},{8,9},{9,8},{10,11... | collective-permute-start | bytes 2433032 | tf_op jit(solution)/shard_map/ppermute | solution.py:589
  186.5 1.5 pre_slope_0.1.slope
  188.1 2.1 stage_weights_0.1.weight
  190.2 14.8 %collective-permute-done.14.other = bf16[528,768]{1,0:T(8,128)(2,1)S(1)} collective-permute-done((bf16[528,768]{1,0:T(8,128)(2,1)S(1)}, bf16[528,768]{1,0:T(8,128)(2,1)S(1)}, u32[]{:S(2)}, u32[]{:S(2)}) %collective-permute-start.14) | collective-permute-done | bytes 811040 | tf_op jit(solution)/shard_map/ppermute | solution.py:589
  205.0 3.1 %block_step_0.1 = bf16[512,768]{1,0:T(8,128)(2,1)} custom-call(bf16[528,768]{1,0:T(8,128)(2,1)S(1)} %get-tuple-element.68.own, bf16[528,768]{1,0:T(8,128)(2,1)S(1)} %collective-permute-done.14.other, bf16[528,768]{1,0:T(8,128)(2,1)S(1)} %pre_slope_0.1.slope, bf16[3,768,768]{2,1,0:T(8,128)(2,1)S(1)} %stage_weights_0.1.weight, ...), custom_call_target="tpu_custom_call" | custom-call | flops 50000000 | bytes 140000 | tf_op jit(solution)/shard_map/block_step_0/pallas_call | solution.py:492
  (49 shorter events, 0.3 us)
Async XLA Ops:
  6.5 9.7 %copy-start.17 = (s32[64]{0:T(128)S(1)}, s32[64]{0:T(128)}, u32[]{:S(2)}) copy-start(s32[64]{0:T(128)} %param.13) | copy-start | bytes 772
  6.5 12.5 %copy-start.15 = (s32[64,32]{0,1:T(8,128)S(1)}, s32[64,32]{0,1:T(8,128)}, u32[]{:S(2)}) copy-start(s32[64,32]{0,1:T(8,128)} %param.17) | copy-start | bytes 24580
  6.5 12.5 %copy-start.16 = (bf16[64,32]{0,1:T(8,128)(2,1)S(1)}, bf16[64,32]{0,1:T(8,128)(2,1)}, u32[]{:S(2)}) copy-start(bf16[64,32]{0,1:T(8,128)(2,1)} %param.16) | copy-start | bytes 12292
  7.6 15.6 %collective-permute-start = (bf16[96,768]{1,0:T(8,128)(2,1)S(1)}, bf16[96,768]{1,0:T(8,128)(2,1)S(1)}, u32[]{:S(2)}, u32[]{:S(2)}) collective-permute-start(bf16[96,768]{1,0:T(8,128)(2,1)S(1)} %get-tuple-element.42), channel_id=1, source_target_pairs={{0,2},{2,4},{4,6},{6,8},{8,10},{10,12},{12,14},{14,16},{16,18},{18... | collective-permute-start | bytes 442376 | tf_op jit(solution)/shard_map/ppermute | solution.py:545
  11.5 11.8 %collective-permute-start.1 = (bf16[96,768]{1,0:T(8,128)(2,1)S(1)}, bf16[96,768]{1,0:T(8,128)(2,1)S(1)}, u32[]{:S(2)}, u32[]{:S(2)}) collective-permute-start(bf16[96,768]{1,0:T(8,128)(2,1)S(1)} %get-tuple-element.39), channel_id=1, source_target_pairs={{2,0},{4,2},{6,4},{8,6},{10,8},{12,10},{14,12},{16,14},{18,16},{20... | collective-permute-start | bytes 442376 | tf_op jit(solution)/shard_map/ppermute | solution.py:546
  18.0 5.2 %collective-permute-start.2 = (bf16[64,768]{1,0:T(8,128)(2,1)S(1)}, bf16[64,768]{1,0:T(8,128)(2,1)S(1)}, u32[]{:S(2)}, u32[]{:S(2)}) collective-permute-start(bf16[64,768]{1,0:T(8,128)(2,1)S(1)} %head_vectors.1), channel_id=1, source_target_pairs={{0,8},{2,10},{4,12},{6,14},{8,0},{10,2},{12,4},{14,6},{1,9},{3,11}... | collective-permute-start | bytes 294920 | tf_op jit(solution)/shard_map/ppermute | solution.py:550
  25.1 14.1 %all-to-all-start = ((bf16[64,2,128]{2,1,0:T(2,128)(2,1)}), bf16[64,2,128]{2,1,0:T(2,128)(2,1)S(1)}, u32[]{:S(2)}, u32[]{:S(2)}) async-start(bf16[64,2,128]{2,1,0:T(2,128)(2,1)} %reshape.6), calls=%async_computation | async-start | bytes 65536 | tf_op jit(solution)/shard_map/all_to_all | solution.py:552
  31.8 74.6 %all-gather.2.cloned.1.call-start = ((), (), s32[]{:S(2)}) async-start(), calls=%async_computation.1 | async-start | bytes 7077888 | tf_op jit(solution)/shard_map/all_gather | solution.py:573
  38.2 1.0 copy-start.5
  39.2 16.0 %copy-start.1 = (bf16[576,768]{1,0:T(8,128)(2,1)}, bf16[576,768]{1,0:T(8,128)(2,1)S(1)}, u32[]{:S(2)}) copy-start(bf16[576,768]{1,0:T(8,128)(2,1)S(1)} %get-tuple-element.44.own) | copy-start | bytes 2654212
  39.3 12.1 %collective-permute-start.3 = (bf16[128,768]{1,0:T(8,128)(2,1)S(1)}, bf16[128,768]{1,0:T(8,128)(2,1)S(1)}, u32[]{:S(2)}, u32[]{:S(2)}) collective-permute-start(bf16[128,768]{1,0:T(8,128)(2,1)S(1)} %constant_dynamic-update-slice_fusion), channel_id=1, source_target_pairs={{0,6},{2,0},{4,2},{6,4},{8,14},{10,8},{12,10},{14,12},{1,7},{3,1},... | collective-permute-start | bytes 589832 | tf_op jit(solution)/shard_map/ppermute | solution.py:516
  42.0 12.1 %collective-permute-start.5 = (bf16[128,768]{1,0:T(8,128)(2,1)S(1)}, bf16[128,768]{1,0:T(8,128)(2,1)S(1)}, u32[]{:S(2)}, u32[]{:S(2)}) collective-permute-start(bf16[128,768]{1,0:T(8,128)(2,1)S(1)} %constant_dynamic-update-slice_fusion), channel_id=1, source_target_pairs={{0,2},{2,4},{4,6},{6,0},{8,10},{10,12},{12,14},{14,8},{1,3},{3,5},... | collective-permute-start | bytes 589832 | tf_op jit(solution)/shard_map/ppermute | solution.py:516
  42.0 11.3 %collective-permute-start.4 = (bf16[128,768]{1,0:T(8,128)(2,1)S(1)}, bf16[128,768]{1,0:T(8,128)(2,1)S(1)}, u32[]{:S(2)}, u32[]{:S(2)}) collective-permute-start(bf16[128,768]{1,0:T(8,128)(2,1)S(1)} %constant_dynamic-update-slice_fusion), channel_id=1, source_target_pairs={{0,4},{2,6},{4,0},{6,2},{8,12},{10,14},{12,8},{14,10},{1,5},{3,7},... | collective-permute-start | bytes 589832 | tf_op jit(solution)/shard_map/ppermute | solution.py:516
  50.5 0.9 copy-start.7
  51.4 2.9 %copy-start.9 = (bf16[528,768]{1,0:T(8,128)(2,1)}, bf16[528,768]{1,0:T(8,128)(2,1)S(1)}, u32[]{:S(2)}) copy-start(bf16[528,768]{1,0:T(8,128)(2,1)S(1)} %get-tuple-element.66.outer) | copy-start | bytes 2433028
  55.3 24.2 %collective-permute-start.8 = (bf16[576,768]{1,0:T(8,128)(2,1)S(1)}, bf16[576,768]{1,0:T(8,128)(2,1)S(1)}, u32[]{:S(2)}, u32[]{:S(2)}) collective-permute-start(bf16[576,768]{1,0:T(8,128)(2,1)S(1)} %get-tuple-element.44.own), channel_id=1, source_target_pairs={{0,1},{1,0},{2,3},{3,2},{4,5},{5,4},{6,7},{7,6},{8,9},{9,8},{10,11... | collective-permute-start | bytes 2654216 | tf_op jit(solution)/shard_map/ppermute | solution.py:564
  58.2 39.2 %collective-permute-start.10 = (bf16[544,768]{1,0:T(8,128)(2,1)}, bf16[544,768]{1,0:T(8,128)(2,1)}, u32[]{:S(2)}, u32[]{:S(2)}) collective-permute-start(bf16[544,768]{1,0:T(8,128)(2,1)} %copy-done.7), channel_id=1, source_target_pairs={{0,1},{1,0},{2,3},{3,2},{4,5},{5,4},{6,7},{7,6},{8,9},{9,8},{10,11... | collective-permute-start | bytes 2506760 | tf_op jit(solution)/shard_map/ppermute | solution.py:564
  64.4 24.5 %copy-start = (bf16[2,512,2048]{2,1,0:T(8,128)(2,1)}, bf16[2,512,2048]{2,1,0:T(8,128)(2,1)S(1)}, u32[]{:S(2)}) copy-start(bf16[2,512,2048]{2,1,0:T(8,128)(2,1)S(1)} %spread_entries.1.spread) | copy-start | bytes 12582916
  79.4 6.4 %copy-start.3 = (bf16[576,768]{1,0:T(8,128)(2,1)}, bf16[576,768]{1,0:T(8,128)(2,1)S(1)}, u32[]{:S(2)}) copy-start(bf16[576,768]{1,0:T(8,128)(2,1)S(1)} %collective-permute-done.8.refs_0_) | copy-start | bytes 2654212
  85.8 20.6 %copy-start.11 = (bf16[512,768]{1,0:T(8,128)(2,1)}, bf16[512,768]{1,0:T(8,128)(2,1)S(1)}, u32[]{:S(2)}) copy-start(bf16[512,768]{1,0:T(8,128)(2,1)S(1)} %get-tuple-element.72.outer) | copy-start | bytes 2359300
  85.9 19.8 %collective-permute-start.9 = (bf16[256,768]{1,0:T(8,128)(2,1)S(1)}, bf16[256,768]{1,0:T(8,128)(2,1)S(1)}, u32[]{:S(2)}, u32[]{:S(2)}) collective-permute-start(bf16[256,768]{1,0:T(8,128)(2,1)S(1)} %slice.14), channel_id=1, source_target_pairs={{0,1},{1,0},{2,3},{3,2},{4,5},{5,4},{6,7},{7,6},{8,9},{9,8},{10,11... | collective-permute-start | bytes 1179656 | tf_op jit(solution)/shard_map/ppermute | solution.py:582
  88.9 17.6 %collective-permute-start.7 = (bf16[2,32,2048]{2,1,0:T(8,128)(2,1)S(1)}, bf16[2,32,2048]{2,1,0:T(8,128)(2,1)S(1)}, u32[]{:S(2)}, u32[]{:S(2)}) collective-permute-start(bf16[2,32,2048]{2,1,0:T(8,128)(2,1)S(1)} %get-tuple-element.73), channel_id=1, source_target_pairs={{2,0},{4,2},{6,4},{8,6},{10,8},{12,10},{14,12},{16,14},{18,16},{20... | collective-permute-start | bytes 786440 | tf_op jit(solution)/shard_map/ppermute | solution.py:579
  90.8 15.6 %collective-permute-start.6 = (bf16[2,32,2048]{2,1,0:T(8,128)(2,1)S(1)}, bf16[2,32,2048]{2,1,0:T(8,128)(2,1)S(1)}, u32[]{:S(2)}, u32[]{:S(2)}) collective-permute-start(bf16[2,32,2048]{2,1,0:T(8,128)(2,1)S(1)} %get-tuple-element.74), channel_id=1, source_target_pairs={{0,2},{2,4},{4,6},{6,8},{8,10},{10,12},{12,14},{14,16},{16,18},{18... | collective-permute-start | bytes 786440 | tf_op jit(solution)/shard_map/ppermute | solution.py:578
  105.7 0.8 copy-start.13
  106.5 0.7 copy-start.18
  107.2 0.7 copy-start.19
  117.4 22.8 %collective-permute-start.11 = (bf16[576,768]{1,0:T(8,128)(2,1)S(1)}, bf16[576,768]{1,0:T(8,128)(2,1)}, u32[]{:S(2)}, u32[]{:S(2)}) collective-permute-start(bf16[576,768]{1,0:T(8,128)(2,1)S(1)} %get-tuple-element.53.own), channel_id=1, source_target_pairs={{0,1},{1,0},{2,3},{3,2},{4,5},{5,4},{6,7},{7,6},{8,9},{9,8},{10,11... | collective-permute-start | bytes 2654216 | tf_op jit(solution)/shard_map/ppermute | solution.py:589
  120.4 1.2 copy-start.2
  121.6 1.2 copy-start.4
  124.4 15.7 %copy-start.6 = (bf16[544,768]{1,0:T(8,128)(2,1)S(1)}, bf16[544,768]{1,0:T(8,128)(2,1)}, u32[]{:S(2)}) copy-start(bf16[544,768]{1,0:T(8,128)(2,1)} %copy-done.5) | copy-start | bytes 2506756
  140.1 9.5 %copy-start.8 = (bf16[544,768]{1,0:T(8,128)(2,1)S(1)}, bf16[544,768]{1,0:T(8,128)(2,1)}, u32[]{:S(2)}) copy-start(bf16[544,768]{1,0:T(8,128)(2,1)} %copy-done.7) | copy-start | bytes 2506756
  145.2 34.7 %collective-permute-start.12 = (bf16[544,768]{1,0:T(8,128)(2,1)S(1)}, bf16[544,768]{1,0:T(8,128)(2,1)S(1)}, u32[]{:S(2)}, u32[]{:S(2)}) collective-permute-start(bf16[544,768]{1,0:T(8,128)(2,1)S(1)} %get-tuple-element.60.own), channel_id=1, source_target_pairs={{0,1},{1,0},{2,3},{3,2},{4,5},{5,4},{6,7},{7,6},{8,9},{9,8},{10,11... | collective-permute-start | bytes 2506760 | tf_op jit(solution)/shard_map/ppermute | solution.py:589
  149.3 28.2 %collective-permute-start.13 = (bf16[272,768]{1,0:T(8,128)(2,1)S(1)}, bf16[272,768]{1,0:T(8,128)(2,1)S(1)}, u32[]{:S(2)}, u32[]{:S(2)}) collective-permute-start(bf16[272,768]{1,0:T(8,128)(2,1)S(1)} %slice.15), channel_id=1, source_target_pairs={{0,1},{1,0},{2,3},{3,2},{4,5},{5,4},{6,7},{7,6},{8,9},{9,8},{10,11... | collective-permute-start | bytes 1253384 | tf_op jit(solution)/shard_map/ppermute | solution.py:592
  152.7 27.1 %copy-start.10 = (bf16[528,768]{1,0:T(8,128)(2,1)S(1)}, bf16[528,768]{1,0:T(8,128)(2,1)}, u32[]{:S(2)}) copy-start(bf16[528,768]{1,0:T(8,128)(2,1)} %copy-done.9) | copy-start | bytes 2433028
  179.8 6.7 %copy-start.14 = (bf16[256,768]{1,0:T(8,128)(2,1)S(1)}, bf16[256,768]{1,0:T(8,128)(2,1)}, u32[]{:S(2)}) copy-start(bf16[256,768]{1,0:T(8,128)(2,1)} %copy-done.13) | copy-start | bytes 1179652
  183.5 21.5 %collective-permute-start.14 = (bf16[528,768]{1,0:T(8,128)(2,1)S(1)}, bf16[528,768]{1,0:T(8,128)(2,1)S(1)}, u32[]{:S(2)}, u32[]{:S(2)}) collective-permute-start(bf16[528,768]{1,0:T(8,128)(2,1)S(1)} %get-tuple-element.68.own), channel_id=1, source_target_pairs={{0,1},{1,0},{2,3},{3,2},{4,5},{5,4},{6,7},{7,6},{8,9},{9,8},{10,11... | collective-permute-start | bytes 2433032 | tf_op jit(solution)/shard_map/ppermute | solution.py:589
  188.1 16.9 %copy-start.12 = (bf16[512,768]{1,0:T(8,128)(2,1)S(1)}, bf16[512,768]{1,0:T(8,128)(2,1)}, u32[]{:S(2)}) copy-start(bf16[512,768]{1,0:T(8,128)(2,1)} %copy-done.11) | copy-start | bytes 2359300
Sparse Core Ops, SparseCore 0:
  55.4 37.5 all-gather.1

commit v9 on v7

--- a/solution.py
+++ b/solution.py
@@ -386,29 +386,24 @@
 ):
     rows, reach = spread.shape[1], low.shape[1]
     columns = column_blocks(grad.shape[1])
-    to_held = lambda k, half: (
-        vectors.at[:, half, :, columns[k]],
-        held.at[k, half].reshape(vectors.shape[0], vectors.shape[2], COLS),
-    )
     batches = []
     for half in range(2):
         batches.append([
             (spread.at[half], matrix.at[half, pl.ds(reach, rows), :]),
             (low.at[(half + turned[0]) % 2], matrix.at[half, pl.ds(0, reach), :]),
             (high.at[(half + turned[1]) % 2], matrix.at[half, pl.ds(reach + rows, reach), :]),
-            to_held(0, half),
+            (vectors.at[:, half], held.at[half].reshape(vectors.shape[0], *vectors.shape[2:])),
         ])
-    for k in range(1, len(columns)):
-        batches.append([to_held(k, half) for half in range(2)])
     batches.append([(expand.at[expand.shape[0] - 1], kernel)])
     arrive = staged(batches, sems)
-    for k, cols in enumerate(columns):
-        top = None
-        for half in range(2):
-            if k == 0 or half == 0:
-                arrive()
-            piece = jnp.dot(matrix[half], held[k, half], preferred_element_type=F32)
-            top = piece if top is None else top + piece
+    arrive()
+    for cols in columns:
+        grad[:, cols] = jnp.dot(matrix[0], held[0, :, cols], preferred_element_type=F32)
+    arrive()
+    for cols in columns:
+        top = grad[:, cols] + jnp.dot(
+            matrix[1], held[1, :, cols], preferred_element_type=F32
+        )
         grad[:, cols] = top
         rounded[:, cols] = top.astype(BF16)
     arrive()
@@ -423,7 +418,6 @@
     count = rows + 2 * low.shape[1]
     share = vectors.shape[1]
     width = expand.shape[1]
-    blocks = share // COLS
     vectors = vectors.reshape(depth // SLOTS, 2, SLOTS, share)
     return pl.pallas_call(
         top_kernel,
@@ -435,10 +429,10 @@
         ],
         scratch_shapes=[
             pltpu.VMEM((2, count, depth), BF16),
-            pltpu.VMEM((blocks, 2, depth, COLS), BF16),
+            pltpu.VMEM((2, depth, share), BF16),
             pltpu.VMEM((width, share), BF16),
             pltpu.VMEM((count, share), BF16),
-            pltpu.SemaphoreType.DMA((7 + 2 * blocks,)),
+            pltpu.SemaphoreType.DMA((9,)),
         ],
         cost_estimate=cost(5e9, 14e6),
         compiler_params=params(),
@@ -579,10 +573,10 @@
     grad, send = top_gradient(
         turned, spread, spread_low, spread_high, gathered, expand_weight
     )
+    exchange(levels[2])
+    send = after(send, others[levels[2]])
     for n in levels:
         other = lax.ppermute(send, "chan", swap)
-        if n == levels[0]:
-            exchange(levels[2], other)
         slope = pre_slope(n, flags, sends[n], after(others[n], send), rows)
         weights = stage_weights(n, after(conv_weight, slope), expand_weight)
         outs = block_step(n, send, other, slope, weights[0], grad, outers[n], *weights[1:])

time: 202 us -> 204 us (level)
  waiting for transfers between devices: 72.3 us -> 79.8 us
  local copies, waits for them, and re-layouts: 12.9 us -> 8.32 us
    ppermute x1, waiting for transfers between devices: 2.27 us -> 19.5 us  [per_device(): spread_high = lax.ppermute(spread[:, :reach], GROUP_AXES, down)]
    ppermute x3, waiting for transfers between devices: 21.6 us -> 9.22 us  [exchange(): others[n] = lax.ppermute(after(sends[n], *earlier), 'chan', swap)]
    unnamed x51 -> x47, local copies, waits for them, and re-layouts: 10.6 us -> 6.81 us
    pallas_call x1, Pallas kernels: 12.4 us -> 9.44 us  [top_gradient(): pl.pallas_call(top_kernel, in_specs=[SMEM] + [HBM] * 5, out_specs=[VMEM,...]
    ppermute x3, waiting for transfers between devices: 40.6 us -> 43.1 us  [per_device(): other = lax.ppermute(send, 'chan', swap)]
  transfers between devices with their start and end apart: 16 -> 16, of which waited for: 10 -> 11; matrix products, arithmetic and copies ran while one was open for 1% -> 0% of each run, Pallas kernels for 21% -> 25%
where the time goes in v9:
time: 204 us; the launch traced here: 203 us
  waiting for transfers between devices  79.8 us (39%)
  Pallas kernels  64.8 us (32%)
  starting transfers between devices  35.6 us (17%)
  between operations  13.8 us (7%)
  local copies, waits for them, and re-layouts  8.32 us (4%)
    ppermute x3, waiting for transfers between devices, per_device(): other = lax.ppermute(send, 'chan', swap)  43.1 us
    pallas_call x3, Pallas kernels, pre_partial(): pl.pallas_call(functools.partial(pre_kernel, level), in_specs=[HBM, VMEM,...  19.7 us
    ppermute x1, waiting for transfers between devices, per_device(): spread_high = lax.ppermute(spread[:, :reach], GROUP_AXES, down)  19.5 us
    pallas_call x3, Pallas kernels, block_step(): pl.pallas_call(functools.partial(block_kernel, level), in_specs=[VMEM] *...  10.5 us
    all_to_all x1, starting transfers between devices, per_device(): lax.all_to_all(after(payload, vectors), GROUP_AXES, split_axis=0, concat_...  9.79 us
    pallas_call x1, Pallas kernels, top_gradient(): pl.pallas_call(top_kernel, in_specs=[SMEM] + [HBM] * 5, out_specs=[VMEM,...  9.44 us
    ppermute x3, waiting for transfers between devices, exchange(): others[n] = lax.ppermute(after(sends[n], *earlier), 'chan', swap)  9.22 us
    pallas_call x3, Pallas kernels, pre_slope(): pl.pallas_call(body, grid_spec=pltpu.PrefetchScalarGridSpec(num_scalar_pr...  7.89 us
  transfers between devices with their start and end apart: 16, of which 11 were waited for; matrix products, arithmetic and copies ran while one was open for 0% of the time, Pallas kernels for 25%

profile of v9, /device:TPU:8, one launch (start us, length us, event | category | flops | bytes accessed | tf_op | source)
XLA Modules:
  0.0 203.1 jit_solution(7115364178335346792)
XLA Ops:
  6.5 0.7 copy-done.13
  7.3 0.7 copy-done.14
  8.0 1.9 bucket_entries.1
  9.9 0.0 copy-start.15
  9.9 0.6 copy-done.15
  10.6 1.8 head_vectors.1
  12.3 0.5 broadcast.3
  12.8 0.7 reduce
  13.5 0.6 reshape.6
  14.1 9.8 %all-to-all-start = ((bf16[64,2,128]{2,1,0:T(2,128)(2,1)}), bf16[64,2,128]{2,1,0:T(2,128)(2,1)S(1)}, u32[]{:S(2)}, u32[]{:S(2)}) async-start(bf16[64,2,128]{2,1,0:T(2,128)(2,1)} %reshape.6), calls=%async_computation | async-start | bytes 65536 | tf_op jit(solution)/shard_map/all_to_all | solution.py:541
  23.9 0.0 all-gather.2.cloned.1.call-start
  24.0 0.5 collective-permute-start.1
  24.5 1.1 cut_edges.1
  25.6 3.5 %collective-permute-start = (bf16[96,768]{1,0:T(8,128)(2,1)S(1)}, bf16[96,768]{1,0:T(8,128)(2,1)S(1)}, u32[]{:S(2)}, u32[]{:S(2)}) collective-permute-start(bf16[96,768]{1,0:T(8,128)(2,1)S(1)} %get-tuple-element.40), channel_id=1, source_target_pairs={{0,2},{2,4},{4,6},{6,8},{8,10},{10,12},{12,14},{14,16},{16,18},{18... | collective-permute-start | bytes 442376 | tf_op jit(solution)/shard_map/ppermute | solution.py:545
  29.1 4.5 %collective-permute-start.2 = (bf16[96,768]{1,0:T(8,128)(2,1)S(1)}, bf16[96,768]{1,0:T(8,128)(2,1)S(1)}, u32[]{:S(2)}, u32[]{:S(2)}) collective-permute-start(bf16[96,768]{1,0:T(8,128)(2,1)S(1)} %get-tuple-element.41), channel_id=1, source_target_pairs={{2,0},{4,2},{6,4},{8,6},{10,8},{12,10},{14,12},{16,14},{18,16},{20... | collective-permute-start | bytes 442376 | tf_op jit(solution)/shard_map/ppermute | solution.py:546
  33.6 0.0 all-to-all-done
  33.6 0.0 collective-permute-done.1
  33.7 0.7 collective-permute-start.3
  34.4 1.4 collective-permute-start.5
  35.8 1.0 collective-permute-start.4
  36.7 0.0 collective-permute-done.low
  36.7 0.4 collective-permute-done.2.high
  37.1 6.3 %pre_partial_2.1 = (bf16[576,768]{1,0:T(8,128)(2,1)S(1)}, bf16[544,768]{1,0:T(8,128)(2,1)S(1)}) custom-call(bf16[3,512,768]{2,1,0:T(8,128)(2,1)} %saved.6, bf16[96,768]{1,0:T(8,128)(2,1)S(1)} %collective-permute-done.low, bf16[96,768]{1,0:T(8,128)(2,1)S(1)} %collective-permute-done.2.high, bf16[3,3,768,768]{3,2,1,0:T(8,128)(2,1)} %refs_0_.2), custom_call_target="tpu_custom_call" | custom-call | flops 50000000 | bytes 80000 | tf_op jit(solution)/shard_map/pre_partial_2/pallas_call | solution.py:340
  43.5 2.7 %collective-permute-done.3 = bf16[128,768]{1,0:T(8,128)(2,1)S(1)} collective-permute-done((bf16[128,768]{1,0:T(8,128)(2,1)S(1)}, bf16[128,768]{1,0:T(8,128)(2,1)S(1)}, u32[]{:S(2)}, u32[]{:S(2)}) %collective-permute-start.3) | collective-permute-done | bytes 196640 | tf_op jit(solution)/shard_map/ppermute | solution.py:509
  46.2 0.0 collective-permute-done.4
  46.2 0.6 collective-permute-done.5
  46.9 0.9 constant_dynamic-slice_fusion
  47.9 0.0 all-gather.2.cloned.1.call-update
  47.9 2.4 %collective-permute-start.8 = (bf16[576,768]{1,0:T(8,128)(2,1)S(1)}, bf16[576,768]{1,0:T(8,128)(2,1)S(1)}, u32[]{:S(2)}, u32[]{:S(2)}) collective-permute-start(bf16[576,768]{1,0:T(8,128)(2,1)S(1)} %get-tuple-element.43.own), channel_id=1, source_target_pairs={{0,1},{1,0},{2,3},{3,2},{4,5},{5,4},{6,7},{7,6},{8,9},{9,8},{10,11... | collective-permute-start | bytes 2654216 | tf_op jit(solution)/shard_map/ppermute | solution.py:556
  50.3 6.1 %pre_partial_1.1 = (bf16[544,768]{1,0:T(8,128)(2,1)S(1)}, bf16[528,768]{1,0:T(8,128)(2,1)S(1)}) custom-call(bf16[3,512,768]{2,1,0:T(8,128)(2,1)} %saved.6, bf16[96,768]{1,0:T(8,128)(2,1)S(1)} %collective-permute-done.low, bf16[96,768]{1,0:T(8,128)(2,1)S(1)} %collective-permute-done.2.high, bf16[3,3,768,768]{3,2,1,0:T(8,128)(2,1)} %refs_0_.2), custom_call_target="tpu_custom_call" | custom-call | flops 50000000 | bytes 80000 | tf_op jit(solution)/shard_map/pre_partial_1/pallas_call | solution.py:340
  56.4 0.9 copy-done.9
  57.3 1.2 collective-permute-start.9
  58.6 5.5 %spread_entries.1.spread = bf16[2,512,2048]{2,1,0:T(8,128)(2,1)S(1)} custom-call(s32[1]{0:T(128)} %bitcast.2.along, bf16[64,256]{1,0:T(8,128)(2,1)S(1)} %bitcast.16), custom_call_target="tpu_custom_call" | custom-call | flops 60000000 | bytes 80000 | tf_op jit(solution)/shard_map/spread_entries/pallas_call | solution.py:227
  64.1 8.0 %collective-permute-done.8.other = bf16[576,768]{1,0:T(8,128)(2,1)S(1)} collective-permute-done((bf16[576,768]{1,0:T(8,128)(2,1)S(1)}, bf16[576,768]{1,0:T(8,128)(2,1)S(1)}, u32[]{:S(2)}, u32[]{:S(2)}) %collective-permute-start.8) | collective-permute-done | bytes 884768 | tf_op jit(solution)/shard_map/ppermute | solution.py:556
  72.1 7.3 %pre_partial_0.1 = (bf16[528,768]{1,0:T(8,128)(2,1)}, bf16[512,768]{1,0:T(8,128)(2,1)S(1)}) custom-call(bf16[3,512,768]{2,1,0:T(8,128)(2,1)} %saved.6, bf16[96,768]{1,0:T(8,128)(2,1)S(1)} %collective-permute-done.low, bf16[96,768]{1,0:T(8,128)(2,1)S(1)} %collective-permute-done.2.high, bf16[3,3,768,768]{3,2,1,0:T(8,128)(2,1)} %refs_0_.2), custom_call_target="tpu_custom_call" | custom-call | flops 50000000 | bytes 80000 | tf_op jit(solution)/shard_map/pre_partial_0/pallas_call | solution.py:340
  79.4 2.4 %collective-permute-start.10 = (bf16[528,768]{1,0:T(8,128)(2,1)}, bf16[528,768]{1,0:T(8,128)(2,1)}, u32[]{:S(2)}, u32[]{:S(2)}) collective-permute-start(bf16[528,768]{1,0:T(8,128)(2,1)} %get-tuple-element.49.own), channel_id=1, source_target_pairs={{0,1},{1,0},{2,3},{3,2},{4,5},{5,4},{6,7},{7,6},{8,9},{9,8},{10,11... | collective-permute-start | bytes 2433032 | tf_op jit(solution)/shard_map/ppermute | solution.py:556
  81.8 5.0 %collective-permute-start.7 = (bf16[2,32,2048]{2,1,0:T(8,128)(2,1)S(1)}, bf16[2,32,2048]{2,1,0:T(8,128)(2,1)S(1)}, u32[]{:S(2)}, u32[]{:S(2)}) collective-permute-start(bf16[2,32,2048]{2,1,0:T(8,128)(2,1)S(1)} %get-tuple-element.71), channel_id=1, source_target_pairs={{2,0},{4,2},{6,4},{8,6},{10,8},{12,10},{14,12},{16,14},{18,16},{20... | collective-permute-start | bytes 786440 | tf_op jit(solution)/shard_map/ppermute | solution.py:569
  86.8 1.9 collective-permute-start.6
  88.8 0.1 add_convert_fusion.turned
  88.8 1.3 collective-permute-done.9.other
  90.1 0.1 all-gather.2.cloned.1.call-done
  90.2 19.5 %collective-permute-done.7.high = bf16[2,32,2048]{2,1,0:T(8,128)(2,1)S(1)} collective-permute-done((bf16[2,32,2048]{2,1,0:T(8,128)(2,1)S(1)}, bf16[2,32,2048]{2,1,0:T(8,128)(2,1)S(1)}, u32[]{:S(2)}, u32[]{:S(2)}) %collective-permute-start.7) | collective-permute-done | bytes 262176 | tf_op jit(solution)/shard_map/ppermute | solution.py:569
  109.7 4.2 %collective-permute-done.6.low = bf16[2,32,2048]{2,1,0:T(8,128)(2,1)S(1)} collective-permute-done((bf16[2,32,2048]{2,1,0:T(8,128)(2,1)S(1)}, bf16[2,32,2048]{2,1,0:T(8,128)(2,1)S(1)}, u32[]{:S(2)}, u32[]{:S(2)}) %collective-permute-start.6) | collective-permute-done | bytes 262176 | tf_op jit(solution)/shard_map/ppermute | solution.py:568
  113.9 0.7 copy-done.17
  114.6 9.4 %top_gradient.1 = (f32[576,768]{1,0:T(8,128)S(1)}, bf16[576,768]{1,0:T(8,128)(2,1)S(1)}) custom-call(s32[2]{0:T(128)S(1)} %add_convert_fusion.turned, bf16[2,512,2048]{2,1,0:T(8,128)(2,1)} %copy-done, bf16[2,32,2048]{2,1,0:T(8,128)(2,1)} %copy-done.17, bf16[2,32,2048]{2,1,0:T(8,128)(2,1)} %copy-done.16, bf16[32,2,64,768]{3,2,1,0:T(8,128)(2,1)} %bitcast.21, ...), custom_call_target="tpu_custom_call" | custom-call | flops 50000000 | bytes 140000 | tf_op jit(solution)/shard_map/top_gradient/pallas_call | solution.py:422
  124.1 0.0 collective-permute-done.10.other
  124.1 0.1 collective-permute-start.11
  124.2 0.1 add_convert_fusion.1.flags
  124.3 1.2 copy-done.2
  125.4 1.2 copy-done.4
  126.6 1.6 pre_slope_2.1.slope
  128.2 2.4 %stage_weights_2.1 = (bf16[3,768,768]{2,1,0:T(8,128)(2,1)S(1)}, bf16[768,768]{1,0:T(8,128)(2,1)S(1)}) custom-call(bf16[3,3,768,768]{3,2,1,0:T(8,128)(2,1)} %refs_0_.2, bf16[3,768,768]{2,1,0:T(8,128)(2,1)} %refs_1_.3), custom_call_target="tpu_custom_call" | custom-call | flops 10000000 | bytes 10000 | tf_op jit(solution)/shard_map/stage_weights_2/pallas_call | solution.py:253
  130.7 15.7 %collective-permute-done.11.other = bf16[576,768]{1,0:T(8,128)(2,1)S(1)} collective-permute-done((bf16[576,768]{1,0:T(8,128)(2,1)S(1)}, bf16[576,768]{1,0:T(8,128)(2,1)S(1)}, u32[]{:S(2)}, u32[]{:S(2)}) %collective-permute-start.11) | collective-permute-done | bytes 884768 | tf_op jit(solution)/shard_map/ppermute | solution.py:579
  146.4 3.7 %block_step_2.1 = (f32[544,768]{1,0:T(8,128)S(1)}, bf16[544,768]{1,0:T(8,128)(2,1)S(1)}) custom-call(bf16[576,768]{1,0:T(8,128)(2,1)S(1)} %get-tuple-element.52.own, bf16[576,768]{1,0:T(8,128)(2,1)S(1)} %collective-permute-done.11.other, bf16[576,768]{1,0:T(8,128)(2,1)S(1)} %pre_slope_2.1.slope, bf16[3,768,768]{2,1,0:T(8,128)(2,1)S(1)} %get-tuple-element.55.weight, ...), custom_call_target="tpu_custom_call" | custom-call | flops 50000000 | bytes 140000 | tf_op jit(solution)/shard_map/block_step_2/pallas_call | solution.py:484
  150.1 0.6 collective-permute-start.12
  150.7 3.1 %pre_slope_1.1.slope = bf16[544,768]{1,0:T(8,128)(2,1)S(1)} custom-call(s32[2]{0:T(128)S(1)} %add_convert_fusion.1.flags, bf16[544,768]{1,0:T(8,128)(2,1)S(1)} %copy-done.8, bf16[544,768]{1,0:T(8,128)(2,1)} %collective-permute-done.9.other), custom_call_target="tpu_custom_call" | custom-call | flops 40000000 | bytes 50000 | tf_op jit(solution)/shard_map/pre_slope_1/pallas_call | solution.py:372
  153.8 2.4 %stage_weights_1.1 = (bf16[3,768,768]{2,1,0:T(8,128)(2,1)S(1)}, bf16[768,768]{1,0:T(8,128)(2,1)S(1)}) custom-call(bf16[3,3,768,768]{3,2,1,0:T(8,128)(2,1)} %refs_0_.2, bf16[3,768,768]{2,1,0:T(8,128)(2,1)} %refs_1_.3), custom_call_target="tpu_custom_call" | custom-call | flops 10000000 | bytes 10000 | tf_op jit(solution)/shard_map/stage_weights_1/pallas_call | solution.py:253
  156.3 14.4 %collective-permute-done.12.other = bf16[544,768]{1,0:T(8,128)(2,1)S(1)} collective-permute-done((bf16[544,768]{1,0:T(8,128)(2,1)S(1)}, bf16[544,768]{1,0:T(8,128)(2,1)S(1)}, u32[]{:S(2)}, u32[]{:S(2)}) %collective-permute-start.12) | collective-permute-done | bytes 835616 | tf_op jit(solution)/shard_map/ppermute | solution.py:579
  170.7 3.7 %block_step_1.1 = (f32[528,768]{1,0:T(8,128)S(1)}, bf16[528,768]{1,0:T(8,128)(2,1)S(1)}) custom-call(bf16[544,768]{1,0:T(8,128)(2,1)S(1)} %get-tuple-element.59.own, bf16[544,768]{1,0:T(8,128)(2,1)S(1)} %collective-permute-done.12.other, bf16[544,768]{1,0:T(8,128)(2,1)S(1)} %pre_slope_1.1.slope, bf16[3,768,768]{2,1,0:T(8,128)(2,1)S(1)} %get-tuple-element.62.weight, ...), custom_call_target="tpu_custom_call" | custom-call | flops 50000000 | bytes 140000 | tf_op jit(solution)/shard_map/block_step_1/pallas_call | solution.py:484
  174.4 0.6 collective-permute-start.13
  175.0 3.2 %pre_slope_0.1.slope = bf16[528,768]{1,0:T(8,128)(2,1)S(1)} custom-call(s32[2]{0:T(128)S(1)} %add_convert_fusion.1.flags, bf16[528,768]{1,0:T(8,128)(2,1)} %get-tuple-element.49.own, bf16[528,768]{1,0:T(8,128)(2,1)} %collective-permute-done.10.other), custom_call_target="tpu_custom_call" | custom-call | flops 40000000 | bytes 50000 | tf_op jit(solution)/shard_map/pre_slope_0/pallas_call | solution.py:372
  178.2 2.1 %stage_weights_0.1.weight = bf16[3,768,768]{2,1,0:T(8,128)(2,1)S(1)} custom-call(bf16[3,3,768,768]{3,2,1,0:T(8,128)(2,1)} %refs_0_.2), custom_call_target="tpu_custom_call" | custom-call | flops 10000000 | bytes 10000 | tf_op jit(solution)/shard_map/stage_weights_0/pallas_call | solution.py:253
  180.3 13.0 %collective-permute-done.13.other = bf16[528,768]{1,0:T(8,128)(2,1)S(1)} collective-permute-done((bf16[528,768]{1,0:T(8,128)(2,1)S(1)}, bf16[528,768]{1,0:T(8,128)(2,1)S(1)}, u32[]{:S(2)}, u32[]{:S(2)}) %collective-permute-start.13) | collective-permute-done | bytes 811040 | tf_op jit(solution)/shard_map/ppermute | solution.py:579
  193.2 3.1 %block_step_0.1 = bf16[512,768]{1,0:T(8,128)(2,1)} custom-call(bf16[528,768]{1,0:T(8,128)(2,1)S(1)} %get-tuple-element.66.own, bf16[528,768]{1,0:T(8,128)(2,1)S(1)} %collective-permute-done.13.other, bf16[528,768]{1,0:T(8,128)(2,1)S(1)} %pre_slope_0.1.slope, bf16[3,768,768]{2,1,0:T(8,128)(2,1)S(1)} %stage_weights_0.1.weight, ...), custom_call_target="tpu_custom_call" | custom-call | flops 50000000 | bytes 140000 | tf_op jit(solution)/shard_map/block_step_0/pallas_call | solution.py:484
  (41 shorter events, 0.2 us)
Async XLA Ops:
  6.5 0.7 copy-start.13
  7.3 0.7 copy-start.14
  9.9 0.7 copy-start.15
  14.1 19.4 %all-to-all-start = ((bf16[64,2,128]{2,1,0:T(2,128)(2,1)}), bf16[64,2,128]{2,1,0:T(2,128)(2,1)S(1)}, u32[]{:S(2)}, u32[]{:S(2)}) async-start(bf16[64,2,128]{2,1,0:T(2,128)(2,1)} %reshape.6), calls=%async_computation | async-start | bytes 65536 | tf_op jit(solution)/shard_map/all_to_all | solution.py:541
  23.9 66.2 %all-gather.2.cloned.1.call-start = ((), (), s32[]{:S(2)}) async-start(), calls=%async_computation.1 | async-start | bytes 7077888 | tf_op jit(solution)/shard_map/all_gather | solution.py:561
  24.0 9.6 %collective-permute-start.1 = (bf16[64,768]{1,0:T(8,128)(2,1)S(1)}, bf16[64,768]{1,0:T(8,128)(2,1)S(1)}, u32[]{:S(2)}, u32[]{:S(2)}) collective-permute-start(bf16[64,768]{1,0:T(8,128)(2,1)S(1)} %head_vectors.1), channel_id=1, source_target_pairs={{0,8},{2,10},{4,12},{6,14},{8,0},{10,2},{12,4},{14,6},{1,9},{3,11}... | collective-permute-start | bytes 294920 | tf_op jit(solution)/shard_map/ppermute | solution.py:507
  25.6 11.1 %collective-permute-start = (bf16[96,768]{1,0:T(8,128)(2,1)S(1)}, bf16[96,768]{1,0:T(8,128)(2,1)S(1)}, u32[]{:S(2)}, u32[]{:S(2)}) collective-permute-start(bf16[96,768]{1,0:T(8,128)(2,1)S(1)} %get-tuple-element.40), channel_id=1, source_target_pairs={{0,2},{2,4},{4,6},{6,8},{8,10},{10,12},{12,14},{14,16},{16,18},{18... | collective-permute-start | bytes 442376 | tf_op jit(solution)/shard_map/ppermute | solution.py:545
  29.1 8.0 %collective-permute-start.2 = (bf16[96,768]{1,0:T(8,128)(2,1)S(1)}, bf16[96,768]{1,0:T(8,128)(2,1)S(1)}, u32[]{:S(2)}, u32[]{:S(2)}) collective-permute-start(bf16[96,768]{1,0:T(8,128)(2,1)S(1)} %get-tuple-element.41), channel_id=1, source_target_pairs={{2,0},{4,2},{6,4},{8,6},{10,8},{12,10},{14,12},{16,14},{18,16},{20... | collective-permute-start | bytes 442376 | tf_op jit(solution)/shard_map/ppermute | solution.py:546
  33.7 12.5 %collective-permute-start.3 = (bf16[128,768]{1,0:T(8,128)(2,1)S(1)}, bf16[128,768]{1,0:T(8,128)(2,1)S(1)}, u32[]{:S(2)}, u32[]{:S(2)}) collective-permute-start(bf16[128,768]{1,0:T(8,128)(2,1)S(1)} %constant_dynamic-update-slice_fusion), channel_id=1, source_target_pairs={{0,6},{2,0},{4,2},{6,4},{8,14},{10,8},{12,10},{14,12},{1,7},{3,1},... | collective-permute-start | bytes 589832 | tf_op jit(solution)/shard_map/ppermute | solution.py:509
  34.4 12.4 %collective-permute-start.5 = (bf16[128,768]{1,0:T(8,128)(2,1)S(1)}, bf16[128,768]{1,0:T(8,128)(2,1)S(1)}, u32[]{:S(2)}, u32[]{:S(2)}) collective-permute-start(bf16[128,768]{1,0:T(8,128)(2,1)S(1)} %constant_dynamic-update-slice_fusion), channel_id=1, source_target_pairs={{0,2},{2,4},{4,6},{6,0},{8,10},{10,12},{12,14},{14,8},{1,3},{3,5},... | collective-permute-start | bytes 589832 | tf_op jit(solution)/shard_map/ppermute | solution.py:509
  35.8 10.4 %collective-permute-start.4 = (bf16[128,768]{1,0:T(8,128)(2,1)S(1)}, bf16[128,768]{1,0:T(8,128)(2,1)S(1)}, u32[]{:S(2)}, u32[]{:S(2)}) collective-permute-start(bf16[128,768]{1,0:T(8,128)(2,1)S(1)} %constant_dynamic-update-slice_fusion), channel_id=1, source_target_pairs={{0,4},{2,6},{4,0},{6,2},{8,12},{10,14},{12,8},{14,10},{1,5},{3,7},... | collective-permute-start | bytes 589832 | tf_op jit(solution)/shard_map/ppermute | solution.py:509
  43.4 3.5 %copy-start.5 = (bf16[544,768]{1,0:T(8,128)(2,1)}, bf16[544,768]{1,0:T(8,128)(2,1)S(1)}, u32[]{:S(2)}) copy-start(bf16[544,768]{1,0:T(8,128)(2,1)S(1)} %get-tuple-element.57.outer) | copy-start | bytes 2506756
  43.4 4.5 %copy-start.1 = (bf16[576,768]{1,0:T(8,128)(2,1)}, bf16[576,768]{1,0:T(8,128)(2,1)S(1)}, u32[]{:S(2)}) copy-start(bf16[576,768]{1,0:T(8,128)(2,1)S(1)} %get-tuple-element.43.own) | copy-start | bytes 2654212
  47.9 24.2 %collective-permute-start.8 = (bf16[576,768]{1,0:T(8,128)(2,1)S(1)}, bf16[576,768]{1,0:T(8,128)(2,1)S(1)}, u32[]{:S(2)}, u32[]{:S(2)}) collective-permute-start(bf16[576,768]{1,0:T(8,128)(2,1)S(1)} %get-tuple-element.43.own), channel_id=1, source_target_pairs={{0,1},{1,0},{2,3},{3,2},{4,5},{5,4},{6,7},{7,6},{8,9},{9,8},{10,11... | collective-permute-start | bytes 2654216 | tf_op jit(solution)/shard_map/ppermute | solution.py:556
  56.4 0.9 copy-start.9
  57.3 6.8 %copy-start.7 = (bf16[544,768]{1,0:T(8,128)(2,1)}, bf16[544,768]{1,0:T(8,128)(2,1)S(1)}, u32[]{:S(2)}) copy-start(bf16[544,768]{1,0:T(8,128)(2,1)S(1)} %get-tuple-element.46.own) | copy-start | bytes 2506756
  57.3 32.8 %collective-permute-start.9 = (bf16[544,768]{1,0:T(8,128)(2,1)S(1)}, bf16[544,768]{1,0:T(8,128)(2,1)}, u32[]{:S(2)}, u32[]{:S(2)}) collective-permute-start(bf16[544,768]{1,0:T(8,128)(2,1)S(1)} %get-tuple-element.46.own), channel_id=1, source_target_pairs={{0,1},{1,0},{2,3},{3,2},{4,5},{5,4},{6,7},{7,6},{8,9},{9,8},{10,11... | collective-permute-start | bytes 2506760 | tf_op jit(solution)/shard_map/ppermute | solution.py:556
  64.1 17.7 %copy-start = (bf16[2,512,2048]{2,1,0:T(8,128)(2,1)}, bf16[2,512,2048]{2,1,0:T(8,128)(2,1)S(1)}, u32[]{:S(2)}) copy-start(bf16[2,512,2048]{2,1,0:T(8,128)(2,1)S(1)} %spread_entries.1.spread) | copy-start | bytes 12582916
  72.1 7.3 %copy-start.3 = (bf16[576,768]{1,0:T(8,128)(2,1)}, bf16[576,768]{1,0:T(8,128)(2,1)S(1)}, u32[]{:S(2)}) copy-start(bf16[576,768]{1,0:T(8,128)(2,1)S(1)} %collective-permute-done.8.other) | copy-start | bytes 2654212
  79.4 2.4 %copy-start.11 = (bf16[512,768]{1,0:T(8,128)(2,1)}, bf16[512,768]{1,0:T(8,128)(2,1)S(1)}, u32[]{:S(2)}) copy-start(bf16[512,768]{1,0:T(8,128)(2,1)S(1)} %get-tuple-element.70.outer) | copy-start | bytes 2359300
  79.4 44.7 %collective-permute-start.10 = (bf16[528,768]{1,0:T(8,128)(2,1)}, bf16[528,768]{1,0:T(8,128)(2,1)}, u32[]{:S(2)}, u32[]{:S(2)}) collective-permute-start(bf16[528,768]{1,0:T(8,128)(2,1)} %get-tuple-element.49.own), channel_id=1, source_target_pairs={{0,1},{1,0},{2,3},{3,2},{4,5},{5,4},{6,7},{7,6},{8,9},{9,8},{10,11... | collective-permute-start | bytes 2433032 | tf_op jit(solution)/shard_map/ppermute | solution.py:556
  81.8 27.9 %collective-permute-start.7 = (bf16[2,32,2048]{2,1,0:T(8,128)(2,1)S(1)}, bf16[2,32,2048]{2,1,0:T(8,128)(2,1)S(1)}, u32[]{:S(2)}, u32[]{:S(2)}) collective-permute-start(bf16[2,32,2048]{2,1,0:T(8,128)(2,1)S(1)} %get-tuple-element.71), channel_id=1, source_target_pairs={{2,0},{4,2},{6,4},{8,6},{10,8},{12,10},{14,12},{16,14},{18,16},{20... | collective-permute-start | bytes 786440 | tf_op jit(solution)/shard_map/ppermute | solution.py:569
  86.8 27.1 %collective-permute-start.6 = (bf16[2,32,2048]{2,1,0:T(8,128)(2,1)S(1)}, bf16[2,32,2048]{2,1,0:T(8,128)(2,1)S(1)}, u32[]{:S(2)}, u32[]{:S(2)}) collective-permute-start(bf16[2,32,2048]{2,1,0:T(8,128)(2,1)S(1)} %get-tuple-element.72), channel_id=1, source_target_pairs={{0,2},{2,4},{4,6},{6,8},{8,10},{10,12},{12,14},{14,16},{16,18},{18... | collective-permute-start | bytes 786440 | tf_op jit(solution)/shard_map/ppermute | solution.py:568
  109.7 4.2 %copy-start.16 = (bf16[2,32,2048]{2,1,0:T(8,128)(2,1)}, bf16[2,32,2048]{2,1,0:T(8,128)(2,1)S(1)}, u32[]{:S(2)}) copy-start(bf16[2,32,2048]{2,1,0:T(8,128)(2,1)S(1)} %collective-permute-done.7.high) | copy-start | bytes 786436
  113.9 0.7 copy-start.17
  124.1 22.3 %collective-permute-start.11 = (bf16[576,768]{1,0:T(8,128)(2,1)S(1)}, bf16[576,768]{1,0:T(8,128)(2,1)S(1)}, u32[]{:S(2)}, u32[]{:S(2)}) collective-permute-start(bf16[576,768]{1,0:T(8,128)(2,1)S(1)} %get-tuple-element.52.own), channel_id=1, source_target_pairs={{0,1},{1,0},{2,3},{3,2},{4,5},{5,4},{6,7},{7,6},{8,9},{9,8},{10,11... | collective-permute-start | bytes 2654216 | tf_op jit(solution)/shard_map/ppermute | solution.py:579
  124.3 1.2 copy-start.2
  125.4 1.2 copy-start.4
  128.2 18.2 %copy-start.6 = (bf16[544,768]{1,0:T(8,128)(2,1)S(1)}, bf16[544,768]{1,0:T(8,128)(2,1)}, u32[]{:S(2)}) copy-start(bf16[544,768]{1,0:T(8,128)(2,1)} %copy-done.5) | copy-start | bytes 2506756
  146.4 4.3 %copy-start.8 = (bf16[544,768]{1,0:T(8,128)(2,1)S(1)}, bf16[544,768]{1,0:T(8,128)(2,1)}, u32[]{:S(2)}) copy-start(bf16[544,768]{1,0:T(8,128)(2,1)} %copy-done.7) | copy-start | bytes 2506756
  150.1 20.5 %collective-permute-start.12 = (bf16[544,768]{1,0:T(8,128)(2,1)S(1)}, bf16[544,768]{1,0:T(8,128)(2,1)S(1)}, u32[]{:S(2)}, u32[]{:S(2)}) collective-permute-start(bf16[544,768]{1,0:T(8,128)(2,1)S(1)} %get-tuple-element.59.own), channel_id=1, source_target_pairs={{0,1},{1,0},{2,3},{3,2},{4,5},{5,4},{6,7},{7,6},{8,9},{9,8},{10,11... | collective-permute-start | bytes 2506760 | tf_op jit(solution)/shard_map/ppermute | solution.py:579
  153.8 16.9 %copy-start.10 = (bf16[528,768]{1,0:T(8,128)(2,1)S(1)}, bf16[528,768]{1,0:T(8,128)(2,1)}, u32[]{:S(2)}) copy-start(bf16[528,768]{1,0:T(8,128)(2,1)} %copy-done.9) | copy-start | bytes 2433028
  174.4 18.9 %collective-permute-start.13 = (bf16[528,768]{1,0:T(8,128)(2,1)S(1)}, bf16[528,768]{1,0:T(8,128)(2,1)S(1)}, u32[]{:S(2)}, u32[]{:S(2)}) collective-permute-start(bf16[528,768]{1,0:T(8,128)(2,1)S(1)} %get-tuple-element.66.own), channel_id=1, source_target_pairs={{0,1},{1,0},{2,3},{3,2},{4,5},{5,4},{6,7},{7,6},{8,9},{9,8},{10,11... | collective-permute-start | bytes 2433032 | tf_op jit(solution)/shard_map/ppermute | solution.py:579
  178.2 15.1 %copy-start.12 = (bf16[512,768]{1,0:T(8,128)(2,1)S(1)}, bf16[512,768]{1,0:T(8,128)(2,1)}, u32[]{:S(2)}) copy-start(bf16[512,768]{1,0:T(8,128)(2,1)} %copy-done.11) | copy-start | bytes 2359300
Sparse Core Ops, SparseCore 0:
  48.0 42.0 all-gather.1

commit v10 on v9

--- a/solution.py
+++ b/solution.py
@@ -171,13 +171,15 @@
     )(cover_bins.T, bin_gradient.T)
 
 
-def spread_kernel(rows, along, arrived, out, fields):
+def spread_kernel(rows, reach, along, *refs):
+    arrived, (out, fields) = refs[:3], refs[3:]
     half, group = pl.program_id(0), pl.program_id(1)
     together = COLS // SLOTS
+    groups = fields.shape[1]
 
     @pl.when((half == 0) & (group == 0))
     def _():
-        members = arrived.shape[0]
+        members = arrived[0].shape[0]
         repeat = jnp.where(
             lax.broadcasted_iota(jnp.int32, (SLOTS, COLS), 1) % SLOTS
             == lax.broadcasted_iota(jnp.int32, (SLOTS, COLS), 0),
@@ -187,57 +189,61 @@
             lax.broadcasted_iota(jnp.int32, (members, COLS), 1) // SLOTS
             == lax.broadcasted_iota(jnp.int32, (members, COLS), 0) % together
         )
-        shape = (members // together, members)
+        shape = (groups, members)
         same = jnp.where(
             lax.broadcasted_iota(jnp.int32, shape, 1) // together
             == lax.broadcasted_iota(jnp.int32, shape, 0),
             1.0, 0.0,
         ).astype(BF16)
-        for k in range(3):
-            wide = jnp.dot(
-                arrived[:, k * SLOTS : (k + 1) * SLOTS], repeat, preferred_element_type=F32
-            )
-            wide = jnp.where(own, wide, 0.0).astype(BF16)
-            fields[:, k * COLS : (k + 1) * COLS] = jnp.dot(
-                same, wide, preferred_element_type=F32
-            )
-
-    row = fields[pl.ds(group * 2 + (half + along[0]) % 2, 1), :]
-    low = row[:, :COLS]
-    code = row[:, COLS : 2 * COLS]
-    value = row[:, 2 * COLS :]
-    high = code >= SLOTS
-    offset = (low + jnp.where(high, 256.0, 0.0)).astype(jnp.int32)
-    slot = lax.broadcasted_iota(jnp.int32, code.shape, 1)
-    column = (code - jnp.where(high, 1.0 * SLOTS, 0.0)).astype(jnp.int32) + slot // SLOTS * SLOTS
+        for which, payload in enumerate(arrived):
+            for k in range(3):
+                wide = jnp.dot(
+                    payload[:, k * SLOTS : (k + 1) * SLOTS], repeat, preferred_element_type=F32
+                )
+                wide = jnp.where(own, wide, 0.0).astype(BF16)
+                fields[which, :, k * COLS : (k + 1) * COLS] = jnp.dot(
+                    same, wide, preferred_element_type=F32
+                )
+
     width = out.shape[1]
-    at_row = jnp.where(
-        lax.broadcasted_iota(jnp.int32, (rows, width), 0) == offset, 1.0, 0.0
-    ).astype(BF16)
-    at_column = jnp.where(
-        lax.broadcasted_iota(jnp.int32, (width, width), 0) == column, value, 0.0
-    ).astype(BF16)
-    out[...] = lax.dot_general(
-        at_row, at_column, NT, preferred_element_type=F32
-    ).astype(BF16)
-
-
-def spread_entries(along, arrived, rows):
-    groups = arrived.shape[0] * SLOTS // COLS // 2
-    return pl.pallas_call(
-        functools.partial(spread_kernel, rows),
+    square = lax.broadcasted_iota(jnp.int32, (width, width), 0)
+    parts = ((reach, rows, 0), (0, reach, rows - reach), (reach + rows, reach, 0))
+    for which, (start, count, first) in enumerate(parts):
+        row = fields[which, pl.ds(group * 2 + (half + along[0]) % 2, 1), :]
+        low = row[:, :COLS]
+        code = row[:, COLS : 2 * COLS]
+        value = row[:, 2 * COLS :]
+        high = code >= SLOTS
+        offset = (low + jnp.where(high, 256.0, 0.0)).astype(jnp.int32) - first
+        slot = lax.broadcasted_iota(jnp.int32, code.shape, 1)
+        column = (code - jnp.where(high, 1.0 * SLOTS, 0.0)).astype(jnp.int32)
+        column = column + slot // SLOTS * SLOTS
+        at_row = jnp.where(
+            lax.broadcasted_iota(jnp.int32, (count, width), 0) == offset, 1.0, 0.0
+        ).astype(BF16)
+        at_column = jnp.where(square == column, value, 0.0).astype(BF16)
+        out[start : start + count, :] = lax.dot_general(
+            at_row, at_column, NT, preferred_element_type=F32
+        ).astype(BF16)
+
+
+def spread_entries(along, arrived, below, above, rows, reach):
+    groups = arrived.shape[0] * SLOTS // COLS
+    whole = pl.BlockSpec(arrived.shape, lambda h, i, along: (0, 0))
+    return pl.pallas_call(
+        functools.partial(spread_kernel, rows, reach),
         grid_spec=pltpu.PrefetchScalarGridSpec(
             num_scalar_prefetch=1,
-            grid=(2, groups),
-            in_specs=[pl.BlockSpec(arrived.shape, lambda h, i, along: (0, 0))],
-            scratch_shapes=[pltpu.VMEM((2 * groups, 3 * COLS), F32)],
-            out_specs=pl.BlockSpec((None, rows, COLS), lambda h, i, along: (h, 0, i)),
+            grid=(2, groups // 2),
+            in_specs=[whole] * 3,
+            scratch_shapes=[pltpu.VMEM((3, groups, 3 * COLS), F32)],
+            out_specs=pl.BlockSpec((None, rows + 2 * reach, COLS), lambda h, i, along: (h, 0, i)),
         ),
-        out_shape=jax.ShapeDtypeStruct((2, rows, groups * COLS), BF16),
+        out_shape=jax.ShapeDtypeStruct((2, rows + 2 * reach, groups // 2 * COLS), BF16),
         cost_estimate=cost(6e9, 8e6),
         compiler_params=params(),
         name="spread_entries",
-    )(along, arrived)
+    )(along, arrived, below, above)
 
 
 def stage_weights(level, weight, expand):
@@ -381,17 +387,12 @@
     )(flags, own, other)
 
 
-def top_kernel(
-    turned, spread, low, high, vectors, expand, grad, send, matrix, held, kernel, rounded, sems
-):
-    rows, reach = spread.shape[1], low.shape[1]
+def top_kernel(spread, vectors, expand, grad, send, matrix, held, kernel, rounded, sems):
     columns = column_blocks(grad.shape[1])
     batches = []
     for half in range(2):
         batches.append([
-            (spread.at[half], matrix.at[half, pl.ds(reach, rows), :]),
-            (low.at[(half + turned[0]) % 2], matrix.at[half, pl.ds(0, reach), :]),
-            (high.at[(half + turned[1]) % 2], matrix.at[half, pl.ds(reach + rows, reach), :]),
+            (spread.at[half], matrix.at[half]),
             (vectors.at[:, half], held.at[half].reshape(vectors.shape[0], *vectors.shape[2:])),
         ])
     batches.append([(expand.at[expand.shape[0] - 1], kernel)])
@@ -413,15 +414,14 @@
         ).astype(BF16)
 
 
-def top_gradient(turned, spread, low, high, vectors, expand):
-    _, rows, depth = spread.shape
-    count = rows + 2 * low.shape[1]
+def top_gradient(spread, vectors, expand):
+    _, count, depth = spread.shape
     share = vectors.shape[1]
     width = expand.shape[1]
     vectors = vectors.reshape(depth // SLOTS, 2, SLOTS, share)
     return pl.pallas_call(
         top_kernel,
-        in_specs=[SMEM] + [HBM] * 5,
+        in_specs=[HBM] * 3,
         out_specs=[VMEM, VMEM],
         out_shape=[
             jax.ShapeDtypeStruct((count, share), F32),
@@ -432,12 +432,12 @@
             pltpu.VMEM((2, depth, share), BF16),
             pltpu.VMEM((width, share), BF16),
             pltpu.VMEM((count, share), BF16),
-            pltpu.SemaphoreType.DMA((9,)),
+            pltpu.SemaphoreType.DMA((5,)),
         ],
         cost_estimate=cost(5e9, 14e6),
         compiler_params=params(),
         name="top_gradient",
-    )(turned, *[in_hbm(a) for a in (spread, low, high, vectors, expand)])
+    )(*[in_hbm(a) for a in (spread, vectors, expand)])
 
 
 def block_kernel(level, own, other, slope, weight, grad, outer, *rest):
@@ -533,7 +533,7 @@
     levels = list(reversed(range(layers)))
 
     place = lax.axis_index("head")
-    along, turn = place // 4, place % 4
+    along = place // 4
     vectors = head_vectors(
         chan_place[None].astype(jnp.int32), head_weight, batch_of, erase_left, erase_right, share
     )
@@ -562,17 +562,15 @@
     begin(levels[1], ring)
     exchange(levels[1])
     reach = HALO_IN[layers - 1]
+    passed = after(arrived, ring)
+    below = lax.ppermute(passed, GROUP_AXES, up)
+    above = lax.ppermute(passed, GROUP_AXES, down)
     spread = spread_entries(
-        along[None].astype(jnp.int32), after(arrived, sends[levels[1]]), rows
+        along[None].astype(jnp.int32), after(arrived, sends[levels[1]]), below, above, rows, reach
     )
-    spread_low = lax.ppermute(spread[:, rows - reach :], GROUP_AXES, up)
-    spread_high = lax.ppermute(spread[:, :reach], GROUP_AXES, down)
     begin(levels[2], spread, others[levels[0]])
-    turned = jnp.stack([turn == 0, turn == 3]).astype(jnp.int32)
     gathered = after(gathered, sends[levels[2]], others[levels[1]])
-    grad, send = top_gradient(
-        turned, spread, spread_low, spread_high, gathered, expand_weight
-    )
+    grad, send = top_gradient(spread, gathered, expand_weight)
     exchange(levels[2])
     send = after(send, others[levels[2]])
     for n in levels:

time: 204 us -> 186 us (0.912)
  waiting for transfers between devices: 79.8 us -> 60.3 us
  starting transfers between devices: 35.6 us -> 33 us
  local copies, waits for them, and re-layouts: 8.32 us -> 10.7 us
    ppermute x2, waiting for transfers between devices: 23.7 us -> 10.1 us  [the longest x1 6.53 us: per_device(): above = lax.ppermute(passed, GROUP_AXES, down)]
    ppermute x3, waiting for transfers between devices: 43.1 us -> 35.7 us  [per_device(): other = lax.ppermute(send, 'chan', swap)]
    ppermute x3, starting transfers between devices: 5.98 us -> 2.4 us  [exchange(): others[n] = lax.ppermute(after(sends[n], *earlier), 'chan', swap)]
    unnamed x47 -> x43, local copies, waits for them, and re-layouts: 6.81 us -> 9.22 us
  transfers between devices with their start and end apart: 16 -> 16, of which waited for: 11 -> 9; matrix products, arithmetic and copies ran while one was open for 0% -> 0% of each run, Pallas kernels for 25% -> 28%
where the time goes in v10:
time: 186 us; the launch traced here: 185 us
  Pallas kernels  66.1 us (36%)
  waiting for transfers between devices  60.3 us (32%)
  starting transfers between devices  33 us (18%)
  between operations  13.8 us (7%)
  local copies, waits for them, and re-layouts  10.7 us (6%)
    ppermute x3, waiting for transfers between devices, per_device(): other = lax.ppermute(send, 'chan', swap)  35.7 us
    pallas_call x3, Pallas kernels, pre_partial(): pl.pallas_call(functools.partial(pre_kernel, level), in_specs=[HBM, VMEM,...  19.9 us
    ppermute x3, waiting for transfers between devices, exchange(): others[n] = lax.ppermute(after(sends[n], *earlier), 'chan', swap)  10.8 us
    pallas_call x3, Pallas kernels, block_step(): pl.pallas_call(functools.partial(block_kernel, level), in_specs=[VMEM] *...  10.5 us
    all_to_all x1, starting transfers between devices, per_device(): lax.all_to_all(after(payload, vectors), GROUP_AXES, split_axis=0, concat_...  9.79 us
    unnamed x43, local copies, waits for them, and re-layouts  9.22 us
    pallas_call x1, Pallas kernels, top_gradient(): pl.pallas_call(top_kernel, in_specs=[HBM] * 3, out_specs=[VMEM, VMEM], ou...  8.87 us
    pallas_call x3, Pallas kernels, pre_slope(): pl.pallas_call(body, grid_spec=pltpu.PrefetchScalarGridSpec(num_scalar_pr...  7.89 us
  transfers between devices with their start and end apart: 16, of which 9 were waited for; matrix products, arithmetic and copies ran while one was open for 0% of the time, Pallas kernels for 28%

profile of v10, /device:TPU:8, one launch (start us, length us, event | category | flops | bytes accessed | tf_op | source)
XLA Modules:
  0.0 184.6 jit_solution(5479058404084615517)
XLA Ops:
  6.5 0.7 copy-done.13
  7.3 0.7 copy-done.14
  8.0 1.9 %bucket_entries.1 = bf16[64,256]{1,0:T(8,128)(2,1)S(1)} custom-call(s32[32,64]{1,0:T(8,128)S(1)} %bitcast.18, bf16[32,64]{1,0:T(8,128)(2,1)S(1)} %bitcast.19), custom_call_target="tpu_custom_call" | custom-call | flops 1000000 | bytes 1000 | tf_op jit(solution)/shard_map/bucket_entries/pallas_call | solution.py:164
  9.9 0.0 copy-start.15
  9.9 0.6 copy-done.15
  10.6 1.8 head_vectors.1
  12.3 0.5 broadcast.3
  12.8 0.7 reduce
  13.5 0.6 reshape.6
  14.1 9.8 %all-to-all-start = ((bf16[64,2,128]{2,1,0:T(2,128)(2,1)}), bf16[64,2,128]{2,1,0:T(2,128)(2,1)S(1)}, u32[]{:S(2)}, u32[]{:S(2)}) async-start(bf16[64,2,128]{2,1,0:T(2,128)(2,1)} %reshape.6), calls=%async_computation | async-start | bytes 65536 | tf_op jit(solution)/shard_map/all_to_all | solution.py:541
  23.9 0.0 all-gather.2.cloned.1.call-start
  24.0 0.5 collective-permute-start.1
  24.5 1.1 cut_edges.1
  25.6 3.5 %collective-permute-start = (bf16[96,768]{1,0:T(8,128)(2,1)S(1)}, bf16[96,768]{1,0:T(8,128)(2,1)S(1)}, u32[]{:S(2)}, u32[]{:S(2)}) collective-permute-start(bf16[96,768]{1,0:T(8,128)(2,1)S(1)} %get-tuple-element.41), channel_id=1, source_target_pairs={{0,2},{2,4},{4,6},{6,8},{8,10},{10,12},{12,14},{14,16},{16,18},{18... | collective-permute-start | bytes 442376 | tf_op jit(solution)/shard_map/ppermute | solution.py:545
  29.1 4.5 %collective-permute-start.2 = (bf16[96,768]{1,0:T(8,128)(2,1)S(1)}, bf16[96,768]{1,0:T(8,128)(2,1)S(1)}, u32[]{:S(2)}, u32[]{:S(2)}) collective-permute-start(bf16[96,768]{1,0:T(8,128)(2,1)S(1)} %get-tuple-element.42), channel_id=1, source_target_pairs={{2,0},{4,2},{6,4},{8,6},{10,8},{12,10},{14,12},{16,14},{18,16},{20... | collective-permute-start | bytes 442376 | tf_op jit(solution)/shard_map/ppermute | solution.py:546
  33.6 0.0 all-to-all-done
  33.6 0.0 collective-permute-done.1
  33.7 0.7 collective-permute-start.3
  34.4 1.4 collective-permute-start.5
  35.8 1.0 collective-permute-start.4
  36.7 0.0 collective-permute-done.low
  36.7 0.4 collective-permute-done.2.high
  37.1 6.3 %pre_partial_2.1 = (bf16[576,768]{1,0:T(8,128)(2,1)S(1)}, bf16[544,768]{1,0:T(8,128)(2,1)S(1)}) custom-call(bf16[3,512,768]{2,1,0:T(8,128)(2,1)} %saved.6, bf16[96,768]{1,0:T(8,128)(2,1)S(1)} %collective-permute-done.low, bf16[96,768]{1,0:T(8,128)(2,1)S(1)} %collective-permute-done.2.high, bf16[3,3,768,768]{3,2,1,0:T(8,128)(2,1)} %refs_0_.2), custom_call_target="tpu_custom_call" | custom-call | flops 50000000 | bytes 80000 | tf_op jit(solution)/shard_map/pre_partial_2/pallas_call | solution.py:346
  43.5 2.7 %collective-permute-done.3 = bf16[128,768]{1,0:T(8,128)(2,1)S(1)} collective-permute-done((bf16[128,768]{1,0:T(8,128)(2,1)S(1)}, bf16[128,768]{1,0:T(8,128)(2,1)S(1)}, u32[]{:S(2)}, u32[]{:S(2)}) %collective-permute-start.3) | collective-permute-done | bytes 196640 | tf_op jit(solution)/shard_map/ppermute | solution.py:509
  46.2 0.0 collective-permute-done.4
  46.2 0.6 collective-permute-done.5
  46.9 0.0 copy-done.5
  46.9 0.9 constant_dynamic-slice_fusion
  47.9 0.0 all-gather.2.cloned.1.call-update
  47.9 2.4 %collective-permute-start.8 = (bf16[576,768]{1,0:T(8,128)(2,1)S(1)}, bf16[576,768]{1,0:T(8,128)(2,1)S(1)}, u32[]{:S(2)}, u32[]{:S(2)}) collective-permute-start(bf16[576,768]{1,0:T(8,128)(2,1)S(1)} %get-tuple-element.44.own), channel_id=1, source_target_pairs={{0,1},{1,0},{2,3},{3,2},{4,5},{5,4},{6,7},{7,6},{8,9},{9,8},{10,11... | collective-permute-start | bytes 2654216 | tf_op jit(solution)/shard_map/ppermute | solution.py:556
  50.3 5.1 %collective-permute-start.7 = (bf16[64,256]{1,0:T(8,128)(2,1)S(1)}, bf16[64,256]{1,0:T(8,128)(2,1)S(1)}, u32[]{:S(2)}, u32[]{:S(2)}) collective-permute-start(bf16[64,256]{1,0:T(8,128)(2,1)S(1)} %bitcast.14), channel_id=1, source_target_pairs={{2,0},{4,2},{6,4},{8,6},{10,8},{12,10},{14,12},{16,14},{18,16},{20... | collective-permute-start | bytes 98312 | tf_op jit(solution)/shard_map/ppermute | solution.py:567
  55.4 1.9 %collective-permute-start.6 = (bf16[64,256]{1,0:T(8,128)(2,1)S(1)}, bf16[64,256]{1,0:T(8,128)(2,1)S(1)}, u32[]{:S(2)}, u32[]{:S(2)}) collective-permute-start(bf16[64,256]{1,0:T(8,128)(2,1)S(1)} %bitcast.15), channel_id=1, source_target_pairs={{0,2},{2,4},{4,6},{6,8},{8,10},{10,12},{12,14},{14,16},{16,18},{18... | collective-permute-start | bytes 98312 | tf_op jit(solution)/shard_map/ppermute | solution.py:566
  57.3 6.3 %pre_partial_1.1 = (bf16[544,768]{1,0:T(8,128)(2,1)S(1)}, bf16[528,768]{1,0:T(8,128)(2,1)S(1)}) custom-call(bf16[3,512,768]{2,1,0:T(8,128)(2,1)} %saved.6, bf16[96,768]{1,0:T(8,128)(2,1)S(1)} %collective-permute-done.low, bf16[96,768]{1,0:T(8,128)(2,1)S(1)} %collective-permute-done.2.high, bf16[3,3,768,768]{3,2,1,0:T(8,128)(2,1)} %refs_0_.2), custom_call_target="tpu_custom_call" | custom-call | flops 50000000 | bytes 80000 | tf_op jit(solution)/shard_map/pre_partial_1/pallas_call | solution.py:346
  63.6 0.9 copy-done.9
  64.6 0.0 collective-permute-start.9
  64.6 6.5 %collective-permute-done.7.refs_2_ = bf16[64,256]{1,0:T(8,128)(2,1)S(1)} collective-permute-done((bf16[64,256]{1,0:T(8,128)(2,1)S(1)}, bf16[64,256]{1,0:T(8,128)(2,1)S(1)}, u32[]{:S(2)}, u32[]{:S(2)}) %collective-permute-start.7) | collective-permute-done | bytes 32800 | tf_op jit(solution)/shard_map/ppermute | solution.py:567
  71.1 3.6 %collective-permute-done.6.refs_1_ = bf16[64,256]{1,0:T(8,128)(2,1)S(1)} collective-permute-done((bf16[64,256]{1,0:T(8,128)(2,1)S(1)}, bf16[64,256]{1,0:T(8,128)(2,1)S(1)}, u32[]{:S(2)}, u32[]{:S(2)}) %collective-permute-start.6) | collective-permute-done | bytes 32800 | tf_op jit(solution)/shard_map/ppermute | solution.py:566
  74.6 7.2 %spread_entries.1.spread = bf16[2,576,2048]{2,1,0:T(8,128)(2,1)S(1)} custom-call(s32[1]{0:T(128)} %bitcast.along, bf16[64,256]{1,0:T(8,128)(2,1)S(1)} %bitcast.16, bf16[64,256]{1,0:T(8,128)(2,1)S(1)} %collective-permute-done.6.refs_1_, bf16[64,256]{1,0:T(8,128)(2,1)S(1)} %collective-permute-done.7.refs_2_), custom_call_target="tpu_custom_call" | custom-call | flops 60000000 | bytes 80000 | tf_op jit(solution)/shard_map/spread_entries/pallas_call | solution.py:233
  81.9 2.2 %copy-done = bf16[2,576,2048]{2,1,0:T(8,128)(2,1)} copy-done((bf16[2,576,2048]{2,1,0:T(8,128)(2,1)}, bf16[2,576,2048]{2,1,0:T(8,128)(2,1)S(1)}, u32[]{:S(2)}) %copy-start) | copy-done | bytes 4718616
  84.1 0.0 collective-permute-done.8.other
  84.1 7.3 %pre_partial_0.1 = (bf16[528,768]{1,0:T(8,128)(2,1)}, bf16[512,768]{1,0:T(8,128)(2,1)S(1)}) custom-call(bf16[3,512,768]{2,1,0:T(8,128)(2,1)} %saved.6, bf16[96,768]{1,0:T(8,128)(2,1)S(1)} %collective-permute-done.low, bf16[96,768]{1,0:T(8,128)(2,1)S(1)} %collective-permute-done.2.high, bf16[3,3,768,768]{3,2,1,0:T(8,128)(2,1)} %refs_0_.2), custom_call_target="tpu_custom_call" | custom-call | flops 50000000 | bytes 80000 | tf_op jit(solution)/shard_map/pre_partial_0/pallas_call | solution.py:346
  91.4 0.9 copy-done.11
  92.3 0.0 collective-permute-start.10
  92.3 0.0 collective-permute-done.9.other
  92.3 8.9 %top_gradient.1 = (f32[576,768]{1,0:T(8,128)S(1)}, bf16[576,768]{1,0:T(8,128)(2,1)S(1)}) custom-call(bf16[2,576,2048]{2,1,0:T(8,128)(2,1)} %copy-done, bf16[32,2,64,768]{3,2,1,0:T(8,128)(2,1)} %bitcast.21, bf16[3,768,768]{2,1,0:T(8,128)(2,1)} %refs_1_.3), custom_call_target="tpu_custom_call" | custom-call | flops 50000000 | bytes 140000 | tf_op jit(solution)/shard_map/top_gradient/pallas_call | solution.py:422
  101.2 10.8 %collective-permute-done.10.other = bf16[528,768]{1,0:T(8,128)(2,1)} collective-permute-done((bf16[528,768]{1,0:T(8,128)(2,1)}, bf16[528,768]{1,0:T(8,128)(2,1)}, u32[]{:S(2)}, u32[]{:S(2)}) %collective-permute-start.10) | collective-permute-done | bytes 811040 | tf_op jit(solution)/shard_map/ppermute | solution.py:556
  112.0 0.3 collective-permute-start.11
  112.4 0.1 add_convert_fusion.flags
  112.4 1.2 copy-done.2
  113.6 1.2 copy-done.4
  114.8 1.6 pre_slope_2.1.slope
  116.4 2.4 %stage_weights_2.1 = (bf16[3,768,768]{2,1,0:T(8,128)(2,1)S(1)}, bf16[768,768]{1,0:T(8,128)(2,1)S(1)}) custom-call(bf16[3,3,768,768]{3,2,1,0:T(8,128)(2,1)} %refs_0_.2, bf16[3,768,768]{2,1,0:T(8,128)(2,1)} %refs_1_.3), custom_call_target="tpu_custom_call" | custom-call | flops 10000000 | bytes 10000 | tf_op jit(solution)/shard_map/stage_weights_2/pallas_call | solution.py:259
  118.9 13.3 %collective-permute-done.11.other = bf16[576,768]{1,0:T(8,128)(2,1)S(1)} collective-permute-done((bf16[576,768]{1,0:T(8,128)(2,1)S(1)}, bf16[576,768]{1,0:T(8,128)(2,1)S(1)}, u32[]{:S(2)}, u32[]{:S(2)}) %collective-permute-start.11) | collective-permute-done | bytes 884768 | tf_op jit(solution)/shard_map/ppermute | solution.py:577
  132.1 3.7 %block_step_2.1 = (f32[544,768]{1,0:T(8,128)S(1)}, bf16[544,768]{1,0:T(8,128)(2,1)S(1)}) custom-call(bf16[576,768]{1,0:T(8,128)(2,1)S(1)} %get-tuple-element.54.own, bf16[576,768]{1,0:T(8,128)(2,1)S(1)} %collective-permute-done.11.other, bf16[576,768]{1,0:T(8,128)(2,1)S(1)} %pre_slope_2.1.slope, bf16[3,768,768]{2,1,0:T(8,128)(2,1)S(1)} %get-tuple-element.57.weight, ...), custom_call_target="tpu_custom_call" | custom-call | flops 50000000 | bytes 140000 | tf_op jit(solution)/shard_map/block_step_2/pallas_call | solution.py:484
  135.9 0.9 collective-permute-start.12
  136.8 3.1 %pre_slope_1.1.slope = bf16[544,768]{1,0:T(8,128)(2,1)S(1)} custom-call(s32[2]{0:T(128)S(1)} %add_convert_fusion.flags, bf16[544,768]{1,0:T(8,128)(2,1)S(1)} %copy-done.8, bf16[544,768]{1,0:T(8,128)(2,1)} %collective-permute-done.9.other), custom_call_target="tpu_custom_call" | custom-call | flops 40000000 | bytes 50000 | tf_op jit(solution)/shard_map/pre_slope_1/pallas_call | solution.py:378
  139.9 2.4 %stage_weights_1.1 = (bf16[3,768,768]{2,1,0:T(8,128)(2,1)S(1)}, bf16[768,768]{1,0:T(8,128)(2,1)S(1)}) custom-call(bf16[3,3,768,768]{3,2,1,0:T(8,128)(2,1)} %refs_0_.2, bf16[3,768,768]{2,1,0:T(8,128)(2,1)} %refs_1_.3), custom_call_target="tpu_custom_call" | custom-call | flops 10000000 | bytes 10000 | tf_op jit(solution)/shard_map/stage_weights_1/pallas_call | solution.py:259
  142.3 11.9 %collective-permute-done.12.other = bf16[544,768]{1,0:T(8,128)(2,1)S(1)} collective-permute-done((bf16[544,768]{1,0:T(8,128)(2,1)S(1)}, bf16[544,768]{1,0:T(8,128)(2,1)S(1)}, u32[]{:S(2)}, u32[]{:S(2)}) %collective-permute-start.12) | collective-permute-done | bytes 835616 | tf_op jit(solution)/shard_map/ppermute | solution.py:577
  154.3 3.7 %block_step_1.1 = (f32[528,768]{1,0:T(8,128)S(1)}, bf16[528,768]{1,0:T(8,128)(2,1)S(1)}) custom-call(bf16[544,768]{1,0:T(8,128)(2,1)S(1)} %get-tuple-element.61.own, bf16[544,768]{1,0:T(8,128)(2,1)S(1)} %collective-permute-done.12.other, bf16[544,768]{1,0:T(8,128)(2,1)S(1)} %pre_slope_1.1.slope, bf16[3,768,768]{2,1,0:T(8,128)(2,1)S(1)} %get-tuple-element.64.weight, ...), custom_call_target="tpu_custom_call" | custom-call | flops 50000000 | bytes 140000 | tf_op jit(solution)/shard_map/block_step_1/pallas_call | solution.py:484
  158.0 1.0 collective-permute-start.13
  159.0 3.2 %pre_slope_0.1.slope = bf16[528,768]{1,0:T(8,128)(2,1)S(1)} custom-call(s32[2]{0:T(128)S(1)} %add_convert_fusion.flags, bf16[528,768]{1,0:T(8,128)(2,1)} %get-tuple-element.51.own, bf16[528,768]{1,0:T(8,128)(2,1)} %collective-permute-done.10.other), custom_call_target="tpu_custom_call" | custom-call | flops 40000000 | bytes 50000 | tf_op jit(solution)/shard_map/pre_slope_0/pallas_call | solution.py:378
  162.2 2.1 %stage_weights_0.1.weight = bf16[3,768,768]{2,1,0:T(8,128)(2,1)S(1)} custom-call(bf16[3,3,768,768]{3,2,1,0:T(8,128)(2,1)} %refs_0_.2), custom_call_target="tpu_custom_call" | custom-call | flops 10000000 | bytes 10000 | tf_op jit(solution)/shard_map/stage_weights_0/pallas_call | solution.py:259
  164.3 10.4 %collective-permute-done.13.other = bf16[528,768]{1,0:T(8,128)(2,1)S(1)} collective-permute-done((bf16[528,768]{1,0:T(8,128)(2,1)S(1)}, bf16[528,768]{1,0:T(8,128)(2,1)S(1)}, u32[]{:S(2)}, u32[]{:S(2)}) %collective-permute-start.13) | collective-permute-done | bytes 811040 | tf_op jit(solution)/shard_map/ppermute | solution.py:577
  174.7 3.1 %block_step_0.1 = bf16[512,768]{1,0:T(8,128)(2,1)} custom-call(bf16[528,768]{1,0:T(8,128)(2,1)S(1)} %get-tuple-element.68.own, bf16[528,768]{1,0:T(8,128)(2,1)S(1)} %collective-permute-done.13.other, bf16[528,768]{1,0:T(8,128)(2,1)S(1)} %pre_slope_0.1.slope, bf16[3,768,768]{2,1,0:T(8,128)(2,1)S(1)} %stage_weights_0.1.weight, ...), custom_call_target="tpu_custom_call" | custom-call | flops 50000000 | bytes 140000 | tf_op jit(solution)/shard_map/block_step_0/pallas_call | solution.py:484
  (35 shorter events, 0.2 us)
Async XLA Ops:
  6.5 0.7 copy-start.13
  7.3 0.7 copy-start.14
  9.9 0.7 copy-start.15
  14.1 19.4 %all-to-all-start = ((bf16[64,2,128]{2,1,0:T(2,128)(2,1)}), bf16[64,2,128]{2,1,0:T(2,128)(2,1)S(1)}, u32[]{:S(2)}, u32[]{:S(2)}) async-start(bf16[64,2,128]{2,1,0:T(2,128)(2,1)} %reshape.6), calls=%async_computation | async-start | bytes 65536 | tf_op jit(solution)/shard_map/all_to_all | solution.py:541
  23.9 68.4 %all-gather.2.cloned.1.call-start = ((), (), s32[]{:S(2)}) async-start(), calls=%async_computation.1 | async-start | bytes 7077888 | tf_op jit(solution)/shard_map/all_gather | solution.py:561
  24.0 9.6 %collective-permute-start.1 = (bf16[64,768]{1,0:T(8,128)(2,1)S(1)}, bf16[64,768]{1,0:T(8,128)(2,1)S(1)}, u32[]{:S(2)}, u32[]{:S(2)}) collective-permute-start(bf16[64,768]{1,0:T(8,128)(2,1)S(1)} %head_vectors.1), channel_id=1, source_target_pairs={{0,8},{2,10},{4,12},{6,14},{8,0},{10,2},{12,4},{14,6},{1,9},{3,11}... | collective-permute-start | bytes 294920 | tf_op jit(solution)/shard_map/ppermute | solution.py:507
  25.6 11.1 %collective-permute-start = (bf16[96,768]{1,0:T(8,128)(2,1)S(1)}, bf16[96,768]{1,0:T(8,128)(2,1)S(1)}, u32[]{:S(2)}, u32[]{:S(2)}) collective-permute-start(bf16[96,768]{1,0:T(8,128)(2,1)S(1)} %get-tuple-element.41), channel_id=1, source_target_pairs={{0,2},{2,4},{4,6},{6,8},{8,10},{10,12},{12,14},{14,16},{16,18},{18... | collective-permute-start | bytes 442376 | tf_op jit(solution)/shard_map/ppermute | solution.py:545
  29.1 8.0 %collective-permute-start.2 = (bf16[96,768]{1,0:T(8,128)(2,1)S(1)}, bf16[96,768]{1,0:T(8,128)(2,1)S(1)}, u32[]{:S(2)}, u32[]{:S(2)}) collective-permute-start(bf16[96,768]{1,0:T(8,128)(2,1)S(1)} %get-tuple-element.42), channel_id=1, source_target_pairs={{2,0},{4,2},{6,4},{8,6},{10,8},{12,10},{14,12},{16,14},{18,16},{20... | collective-permute-start | bytes 442376 | tf_op jit(solution)/shard_map/ppermute | solution.py:546
  33.7 12.5 %collective-permute-start.3 = (bf16[128,768]{1,0:T(8,128)(2,1)S(1)}, bf16[128,768]{1,0:T(8,128)(2,1)S(1)}, u32[]{:S(2)}, u32[]{:S(2)}) collective-permute-start(bf16[128,768]{1,0:T(8,128)(2,1)S(1)} %constant_dynamic-update-slice_fusion), channel_id=1, source_target_pairs={{0,6},{2,0},{4,2},{6,4},{8,14},{10,8},{12,10},{14,12},{1,7},{3,1},... | collective-permute-start | bytes 589832 | tf_op jit(solution)/shard_map/ppermute | solution.py:509
  34.4 12.4 %collective-permute-start.5 = (bf16[128,768]{1,0:T(8,128)(2,1)S(1)}, bf16[128,768]{1,0:T(8,128)(2,1)S(1)}, u32[]{:S(2)}, u32[]{:S(2)}) collective-permute-start(bf16[128,768]{1,0:T(8,128)(2,1)S(1)} %constant_dynamic-update-slice_fusion), channel_id=1, source_target_pairs={{0,2},{2,4},{4,6},{6,0},{8,10},{10,12},{12,14},{14,8},{1,3},{3,5},... | collective-permute-start | bytes 589832 | tf_op jit(solution)/shard_map/ppermute | solution.py:509
  35.8 10.4 %collective-permute-start.4 = (bf16[128,768]{1,0:T(8,128)(2,1)S(1)}, bf16[128,768]{1,0:T(8,128)(2,1)S(1)}, u32[]{:S(2)}, u32[]{:S(2)}) collective-permute-start(bf16[128,768]{1,0:T(8,128)(2,1)S(1)} %constant_dynamic-update-slice_fusion), channel_id=1, source_target_pairs={{0,4},{2,6},{4,0},{6,2},{8,12},{10,14},{12,8},{14,10},{1,5},{3,7},... | collective-permute-start | bytes 589832 | tf_op jit(solution)/shard_map/ppermute | solution.py:509
  43.4 3.5 %copy-start.5 = (bf16[544,768]{1,0:T(8,128)(2,1)}, bf16[544,768]{1,0:T(8,128)(2,1)S(1)}, u32[]{:S(2)}) copy-start(bf16[544,768]{1,0:T(8,128)(2,1)S(1)} %get-tuple-element.59.outer) | copy-start | bytes 2506756
  43.4 4.5 %copy-start.1 = (bf16[576,768]{1,0:T(8,128)(2,1)}, bf16[576,768]{1,0:T(8,128)(2,1)S(1)}, u32[]{:S(2)}) copy-start(bf16[576,768]{1,0:T(8,128)(2,1)S(1)} %get-tuple-element.44.own) | copy-start | bytes 2654212
  47.9 36.2 %collective-permute-start.8 = (bf16[576,768]{1,0:T(8,128)(2,1)S(1)}, bf16[576,768]{1,0:T(8,128)(2,1)S(1)}, u32[]{:S(2)}, u32[]{:S(2)}) collective-permute-start(bf16[576,768]{1,0:T(8,128)(2,1)S(1)} %get-tuple-element.44.own), channel_id=1, source_target_pairs={{0,1},{1,0},{2,3},{3,2},{4,5},{5,4},{6,7},{7,6},{8,9},{9,8},{10,11... | collective-permute-start | bytes 2654216 | tf_op jit(solution)/shard_map/ppermute | solution.py:556
  50.3 20.8 %collective-permute-start.7 = (bf16[64,256]{1,0:T(8,128)(2,1)S(1)}, bf16[64,256]{1,0:T(8,128)(2,1)S(1)}, u32[]{:S(2)}, u32[]{:S(2)}) collective-permute-start(bf16[64,256]{1,0:T(8,128)(2,1)S(1)} %bitcast.14), channel_id=1, source_target_pairs={{2,0},{4,2},{6,4},{8,6},{10,8},{12,10},{14,12},{16,14},{18,16},{20... | collective-permute-start | bytes 98312 | tf_op jit(solution)/shard_map/ppermute | solution.py:567
  55.4 19.3 %collective-permute-start.6 = (bf16[64,256]{1,0:T(8,128)(2,1)S(1)}, bf16[64,256]{1,0:T(8,128)(2,1)S(1)}, u32[]{:S(2)}, u32[]{:S(2)}) collective-permute-start(bf16[64,256]{1,0:T(8,128)(2,1)S(1)} %bitcast.15), channel_id=1, source_target_pairs={{0,2},{2,4},{4,6},{6,8},{8,10},{10,12},{12,14},{14,16},{16,18},{18... | collective-permute-start | bytes 98312 | tf_op jit(solution)/shard_map/ppermute | solution.py:566
  63.6 0.9 copy-start.9
  64.6 17.3 %copy-start.7 = (bf16[544,768]{1,0:T(8,128)(2,1)}, bf16[544,768]{1,0:T(8,128)(2,1)S(1)}, u32[]{:S(2)}) copy-start(bf16[544,768]{1,0:T(8,128)(2,1)S(1)} %get-tuple-element.47.own) | copy-start | bytes 2506756
  64.6 27.8 %collective-permute-start.9 = (bf16[544,768]{1,0:T(8,128)(2,1)S(1)}, bf16[544,768]{1,0:T(8,128)(2,1)}, u32[]{:S(2)}, u32[]{:S(2)}) collective-permute-start(bf16[544,768]{1,0:T(8,128)(2,1)S(1)} %get-tuple-element.47.own), channel_id=1, source_target_pairs={{0,1},{1,0},{2,3},{3,2},{4,5},{5,4},{6,7},{7,6},{8,9},{9,8},{10,11... | collective-permute-start | bytes 2506760 | tf_op jit(solution)/shard_map/ppermute | solution.py:556
  81.9 2.2 %copy-start = (bf16[2,576,2048]{2,1,0:T(8,128)(2,1)}, bf16[2,576,2048]{2,1,0:T(8,128)(2,1)S(1)}, u32[]{:S(2)}) copy-start(bf16[2,576,2048]{2,1,0:T(8,128)(2,1)S(1)} %spread_entries.1.spread) | copy-start | bytes 14155780
  84.1 7.3 %copy-start.3 = (bf16[576,768]{1,0:T(8,128)(2,1)}, bf16[576,768]{1,0:T(8,128)(2,1)S(1)}, u32[]{:S(2)}) copy-start(bf16[576,768]{1,0:T(8,128)(2,1)S(1)} %collective-permute-done.8.other) | copy-start | bytes 2654212
  91.4 0.9 copy-start.11
  92.3 19.7 %collective-permute-start.10 = (bf16[528,768]{1,0:T(8,128)(2,1)}, bf16[528,768]{1,0:T(8,128)(2,1)}, u32[]{:S(2)}, u32[]{:S(2)}) collective-permute-start(bf16[528,768]{1,0:T(8,128)(2,1)} %get-tuple-element.51.own), channel_id=1, source_target_pairs={{0,1},{1,0},{2,3},{3,2},{4,5},{5,4},{6,7},{7,6},{8,9},{9,8},{10,11... | collective-permute-start | bytes 2433032 | tf_op jit(solution)/shard_map/ppermute | solution.py:556
  112.0 20.1 %collective-permute-start.11 = (bf16[576,768]{1,0:T(8,128)(2,1)S(1)}, bf16[576,768]{1,0:T(8,128)(2,1)S(1)}, u32[]{:S(2)}, u32[]{:S(2)}) collective-permute-start(bf16[576,768]{1,0:T(8,128)(2,1)S(1)} %get-tuple-element.54.own), channel_id=1, source_target_pairs={{0,1},{1,0},{2,3},{3,2},{4,5},{5,4},{6,7},{7,6},{8,9},{9,8},{10,11... | collective-permute-start | bytes 2654216 | tf_op jit(solution)/shard_map/ppermute | solution.py:577
  112.4 1.2 copy-start.2
  113.6 1.2 copy-start.4
  116.4 15.7 %copy-start.6 = (bf16[544,768]{1,0:T(8,128)(2,1)S(1)}, bf16[544,768]{1,0:T(8,128)(2,1)}, u32[]{:S(2)}) copy-start(bf16[544,768]{1,0:T(8,128)(2,1)} %copy-done.5) | copy-start | bytes 2506756
  132.1 4.7 %copy-start.8 = (bf16[544,768]{1,0:T(8,128)(2,1)S(1)}, bf16[544,768]{1,0:T(8,128)(2,1)}, u32[]{:S(2)}) copy-start(bf16[544,768]{1,0:T(8,128)(2,1)} %copy-done.7) | copy-start | bytes 2506756
  135.9 18.4 %collective-permute-start.12 = (bf16[544,768]{1,0:T(8,128)(2,1)S(1)}, bf16[544,768]{1,0:T(8,128)(2,1)S(1)}, u32[]{:S(2)}, u32[]{:S(2)}) collective-permute-start(bf16[544,768]{1,0:T(8,128)(2,1)S(1)} %get-tuple-element.61.own), channel_id=1, source_target_pairs={{0,1},{1,0},{2,3},{3,2},{4,5},{5,4},{6,7},{7,6},{8,9},{9,8},{10,11... | collective-permute-start | bytes 2506760 | tf_op jit(solution)/shard_map/ppermute | solution.py:577
  139.9 14.4 %copy-start.10 = (bf16[528,768]{1,0:T(8,128)(2,1)S(1)}, bf16[528,768]{1,0:T(8,128)(2,1)}, u32[]{:S(2)}) copy-start(bf16[528,768]{1,0:T(8,128)(2,1)} %copy-done.9) | copy-start | bytes 2433028
  158.0 16.7 %collective-permute-start.13 = (bf16[528,768]{1,0:T(8,128)(2,1)S(1)}, bf16[528,768]{1,0:T(8,128)(2,1)S(1)}, u32[]{:S(2)}, u32[]{:S(2)}) collective-permute-start(bf16[528,768]{1,0:T(8,128)(2,1)S(1)} %get-tuple-element.68.own), channel_id=1, source_target_pairs={{0,1},{1,0},{2,3},{3,2},{4,5},{5,4},{6,7},{7,6},{8,9},{9,8},{10,11... | collective-permute-start | bytes 2433032 | tf_op jit(solution)/shard_map/ppermute | solution.py:577
  162.2 12.5 %copy-start.12 = (bf16[512,768]{1,0:T(8,128)(2,1)S(1)}, bf16[512,768]{1,0:T(8,128)(2,1)}, u32[]{:S(2)}) copy-start(bf16[512,768]{1,0:T(8,128)(2,1)} %copy-done.11) | copy-start | bytes 2359300
Sparse Core Ops, SparseCore 0:
  48.0 42.0 all-gather.1

commit v11 on v10

--- a/solution.py
+++ b/solution.py
@@ -114,11 +114,13 @@
         cost_estimate=cost(1e9, 1e6),
         compiler_params=params(),
         name="head_vectors",
-    )(place, *[in_hbm(a) for a in (head_weight, head_weight)], batch_of[None, :],
+    )(place, *[in_hbm(a) for a in (head_weight, head_weight, batch_of[None, :])],
       in_hbm(erase_left.T), in_hbm(erase_right.T))
 
 
-def bucket_kernel(rows, bins, grads, out):
+def bucket_kernel(rows, bins_at, grads_at, out, bins, grads, sems):
+    for copy in fetch([(bins_at, bins), (grads_at, grads)], sems):
+        copy.wait()
     cover, experts = bins.shape
     together = 128 // experts
     lanes = together * experts
@@ -136,7 +138,7 @@
         [ref[chunk * together + k : chunk * together + k + 1, :] for k in range(together)], axis=1
     )
     base = jnp.zeros((members, 1), F32)
-    total = jnp.zeros(out.shape, F32)
+    total = jnp.zeros((members, 4 * SLOTS), F32)
     grads = grads[...].astype(F32)
     for chunk in range(chunks):
         place = side(bins, chunk)
@@ -157,18 +159,25 @@
             axis=0,
         ).astype(BF16)
         total = total + lax.dot_general(mine_low, spread, NT, preferred_element_type=F32)
-    out[...] = total.astype(BF16)
+    for k in range(out.shape[1]):
+        out[:, k, :] = total[:, k * 128 : (k + 1) * 128].astype(BF16)
 
 
 def bucket(cover_bins, bin_gradient, members, rows):
+    bins, grads = cover_bins.T, bin_gradient.T
     return pl.pallas_call(
         functools.partial(bucket_kernel, rows),
-        in_specs=[VMEM, VMEM],
-        out_shape=jax.ShapeDtypeStruct((members, 4 * SLOTS), BF16),
+        in_specs=[HBM, HBM],
+        out_shape=jax.ShapeDtypeStruct((members, 4 * SLOTS // 128, 128), BF16),
+        scratch_shapes=[
+            pltpu.VMEM(bins.shape, bins.dtype),
+            pltpu.VMEM(grads.shape, grads.dtype),
+            pltpu.SemaphoreType.DMA((2,)),
+        ],
         cost_estimate=cost(1e8, 1e5),
         compiler_params=params(),
         name="bucket_entries",
-    )(cover_bins.T, bin_gradient.T)
+    )(in_hbm(bins), in_hbm(grads))
 
 
 def spread_kernel(rows, reach, along, *refs):
@@ -197,9 +206,9 @@
         ).astype(BF16)
         for which, payload in enumerate(arrived):
             for k in range(3):
-                wide = jnp.dot(
-                    payload[:, k * SLOTS : (k + 1) * SLOTS], repeat, preferred_element_type=F32
-                )
+                first = k % 2 * SLOTS
+                these = payload[:, k // 2, first : first + SLOTS]
+                wide = jnp.dot(these, repeat, preferred_element_type=F32)
                 wide = jnp.where(own, wide, 0.0).astype(BF16)
                 fields[which, :, k * COLS : (k + 1) * COLS] = jnp.dot(
                     same, wide, preferred_element_type=F32
@@ -229,7 +238,7 @@
 
 def spread_entries(along, arrived, below, above, rows, reach):
     groups = arrived.shape[0] * SLOTS // COLS
-    whole = pl.BlockSpec(arrived.shape, lambda h, i, along: (0, 0))
+    whole = pl.BlockSpec(arrived.shape, lambda h, i, along: (0, 0, 0))
     return pl.pallas_call(
         functools.partial(spread_kernel, rows, reach),
         grid_spec=pltpu.PrefetchScalarGridSpec(

time: 186 us -> 183 us (0.984)
  local copies, waits for them, and re-layouts: 10.7 us -> 7.47 us
    unnamed x43 -> x34, local copies, waits for them, and re-layouts: 9.22 us -> 6.51 us
  transfers between devices with their start and end apart: 16 -> 16, of which waited for: 9 -> 9; matrix products, arithmetic and copies ran while one was open for 0% -> 0% of each run, Pallas kernels for 28% -> 29%
where the time goes in v11:
time: 183 us; the launch traced here: 182 us
  Pallas kernels  67.6 us (37%)
  waiting for transfers between devices  60.3 us (33%)
  starting transfers between devices  33.1 us (18%)
  between operations  13.8 us (8%)
  local copies, waits for them, and re-layouts  7.47 us (4%)
    ppermute x3, waiting for transfers between devices, per_device(): other = lax.ppermute(send, 'chan', swap)  35.6 us
    pallas_call x3, Pallas kernels, pre_partial(): pl.pallas_call(functools.partial(pre_kernel, level), in_specs=[HBM, VMEM,...  19.9 us
    ppermute x3, waiting for transfers between devices, exchange(): others[n] = lax.ppermute(after(sends[n], *earlier), 'chan', swap)  10.8 us
    pallas_call x3, Pallas kernels, block_step(): pl.pallas_call(functools.partial(block_kernel, level), in_specs=[VMEM] *...  10.5 us
    all_to_all x1, starting transfers between devices, per_device(): lax.all_to_all(after(payload, vectors), GROUP_AXES, split_axis=0, concat_...  9.81 us
    pallas_call x1, Pallas kernels, top_gradient(): pl.pallas_call(top_kernel, in_specs=[HBM] * 3, out_specs=[VMEM, VMEM], ou...  8.86 us
    pallas_call x3, Pallas kernels, pre_slope(): pl.pallas_call(body, grid_spec=pltpu.PrefetchScalarGridSpec(num_scalar_pr...  7.89 us
    pallas_call x1, Pallas kernels, spread_entries(): pl.pallas_call(functools.partial(spread_kernel, rows, reach), grid_spec=p...  7.26 us
  transfers between devices with their start and end apart: 16, of which 9 were waited for; matrix products, arithmetic and copies ran while one was open for 0% of the time, Pallas kernels for 29%

profile of v11, /device:TPU:8, one launch (start us, length us, event | category | flops | bytes accessed | tf_op | source)
XLA Modules:
  0.0 182.2 jit_solution(8971925060088104826)
XLA Ops:
  6.5 3.4 %bucket_entries.1 = bf16[64,2,128]{2,1,0:T(2,128)(2,1)} custom-call(s32[32,64]{1,0:T(8,128)} %bitcast.13, bf16[32,64]{1,0:T(8,128)(2,1)} %bitcast.14), custom_call_target="tpu_custom_call" | custom-call | flops 1000000 | bytes 1000 | tf_op jit(solution)/shard_map/bucket_entries/pallas_call | solution.py:168
  9.9 1.8 head_vectors.1
  11.7 9.8 %all-to-all-start = ((bf16[64,2,128]{2,1,0:T(2,128)(2,1)}), bf16[64,2,128]{2,1,0:T(2,128)(2,1)S(1)}, u32[]{:S(2)}, u32[]{:S(2)}) async-start(bf16[64,2,128]{2,1,0:T(2,128)(2,1)} %bucket_entries.1), calls=%async_computation | async-start | bytes 65536 | tf_op jit(solution)/shard_map/all_to_all | solution.py:550
  21.5 0.0 all-gather.2.cloned.1.call-start
  21.6 0.5 collective-permute-start.1
  22.1 1.1 cut_edges.1
  23.2 3.5 %collective-permute-start = (bf16[96,768]{1,0:T(8,128)(2,1)S(1)}, bf16[96,768]{1,0:T(8,128)(2,1)S(1)}, u32[]{:S(2)}, u32[]{:S(2)}) collective-permute-start(bf16[96,768]{1,0:T(8,128)(2,1)S(1)} %get-tuple-element.41), channel_id=1, source_target_pairs={{0,2},{2,4},{4,6},{6,8},{8,10},{10,12},{12,14},{14,16},{16,18},{18... | collective-permute-start | bytes 442376 | tf_op jit(solution)/shard_map/ppermute | solution.py:554
  26.7 4.5 %collective-permute-start.2 = (bf16[96,768]{1,0:T(8,128)(2,1)S(1)}, bf16[96,768]{1,0:T(8,128)(2,1)S(1)}, u32[]{:S(2)}, u32[]{:S(2)}) collective-permute-start(bf16[96,768]{1,0:T(8,128)(2,1)S(1)} %get-tuple-element.42), channel_id=1, source_target_pairs={{2,0},{4,2},{6,4},{8,6},{10,8},{12,10},{14,12},{16,14},{18,16},{20... | collective-permute-start | bytes 442376 | tf_op jit(solution)/shard_map/ppermute | solution.py:555
  31.1 0.0 all-to-all-done.refs_0_
  31.2 0.0 collective-permute-done.1
  31.2 0.7 collective-permute-start.3
  31.9 1.4 collective-permute-start.5
  33.3 1.0 collective-permute-start.4
  34.3 0.0 collective-permute-done.low
  34.3 0.5 collective-permute-done.2.high
  34.7 6.3 %pre_partial_2.1 = (bf16[576,768]{1,0:T(8,128)(2,1)S(1)}, bf16[544,768]{1,0:T(8,128)(2,1)S(1)}) custom-call(bf16[3,512,768]{2,1,0:T(8,128)(2,1)} %saved.6, bf16[96,768]{1,0:T(8,128)(2,1)S(1)} %collective-permute-done.low, bf16[96,768]{1,0:T(8,128)(2,1)S(1)} %collective-permute-done.2.high, bf16[3,3,768,768]{3,2,1,0:T(8,128)(2,1)} %refs_0_.2), custom_call_target="tpu_custom_call" | custom-call | flops 50000000 | bytes 80000 | tf_op jit(solution)/shard_map/pre_partial_2/pallas_call | solution.py:355
  41.1 0.0 copy-start.5
  41.1 0.0 copy-start.1
  41.1 2.6 %collective-permute-done.3 = bf16[128,768]{1,0:T(8,128)(2,1)S(1)} collective-permute-done((bf16[128,768]{1,0:T(8,128)(2,1)S(1)}, bf16[128,768]{1,0:T(8,128)(2,1)S(1)}, u32[]{:S(2)}, u32[]{:S(2)}) %collective-permute-start.3) | collective-permute-done | bytes 196640 | tf_op jit(solution)/shard_map/ppermute | solution.py:518
  43.7 0.0 collective-permute-done.4
  43.8 0.6 collective-permute-done.5
  44.5 0.0 copy-done.5
  44.5 0.9 constant_dynamic-slice_fusion
  45.4 0.0 all-gather.2.cloned.1.call-update
  45.5 0.0 copy-done.1
  45.5 2.4 %collective-permute-start.8 = (bf16[576,768]{1,0:T(8,128)(2,1)S(1)}, bf16[576,768]{1,0:T(8,128)(2,1)S(1)}, u32[]{:S(2)}, u32[]{:S(2)}) collective-permute-start(bf16[576,768]{1,0:T(8,128)(2,1)S(1)} %get-tuple-element.44.own), channel_id=1, source_target_pairs={{0,1},{1,0},{2,3},{3,2},{4,5},{5,4},{6,7},{7,6},{8,9},{9,8},{10,11... | collective-permute-start | bytes 2654216 | tf_op jit(solution)/shard_map/ppermute | solution.py:565
  47.8 5.1 %collective-permute-start.7 = (bf16[64,2,128]{2,1,0:T(2,128)(2,1)S(1)}, bf16[64,2,128]{2,1,0:T(2,128)(2,1)S(1)}, u32[]{:S(2)}, u32[]{:S(2)}) collective-permute-start(bf16[64,2,128]{2,1,0:T(2,128)(2,1)S(1)} %all-to-all-done.refs_0_), channel_id=1, source_target_pairs={{2,0},{4,2},{6,4},{8,6},{10,8},{12,10},{14,12},{16,14},{18,16},{20... | collective-permute-start | bytes 98312 | tf_op jit(solution)/shard_map/ppermute | solution.py:576
  53.0 1.9 %collective-permute-start.6 = (bf16[64,2,128]{2,1,0:T(2,128)(2,1)S(1)}, bf16[64,2,128]{2,1,0:T(2,128)(2,1)S(1)}, u32[]{:S(2)}, u32[]{:S(2)}) collective-permute-start(bf16[64,2,128]{2,1,0:T(2,128)(2,1)S(1)} %all-to-all-done.refs_0_), channel_id=1, source_target_pairs={{0,2},{2,4},{4,6},{6,8},{8,10},{10,12},{12,14},{14,16},{16,18},{18... | collective-permute-start | bytes 98312 | tf_op jit(solution)/shard_map/ppermute | solution.py:575
  54.9 6.3 %pre_partial_1.1 = (bf16[544,768]{1,0:T(8,128)(2,1)S(1)}, bf16[528,768]{1,0:T(8,128)(2,1)S(1)}) custom-call(bf16[3,512,768]{2,1,0:T(8,128)(2,1)} %saved.6, bf16[96,768]{1,0:T(8,128)(2,1)S(1)} %collective-permute-done.low, bf16[96,768]{1,0:T(8,128)(2,1)S(1)} %collective-permute-done.2.high, bf16[3,3,768,768]{3,2,1,0:T(8,128)(2,1)} %refs_0_.2), custom_call_target="tpu_custom_call" | custom-call | flops 50000000 | bytes 80000 | tf_op jit(solution)/shard_map/pre_partial_1/pallas_call | solution.py:355
  61.2 0.0 copy-start.9
  61.2 0.9 copy-done.9
  62.1 0.0 collective-permute-start.9
  62.2 6.5 %collective-permute-done.7.refs_2_ = bf16[64,2,128]{2,1,0:T(2,128)(2,1)S(1)} collective-permute-done((bf16[64,2,128]{2,1,0:T(2,128)(2,1)S(1)}, bf16[64,2,128]{2,1,0:T(2,128)(2,1)S(1)}, u32[]{:S(2)}, u32[]{:S(2)}) %collective-permute-start.7) | collective-permute-done | bytes 32800 | tf_op jit(solution)/shard_map/ppermute | solution.py:576
  68.6 3.6 %collective-permute-done.6.refs_1_ = bf16[64,2,128]{2,1,0:T(2,128)(2,1)S(1)} collective-permute-done((bf16[64,2,128]{2,1,0:T(2,128)(2,1)S(1)}, bf16[64,2,128]{2,1,0:T(2,128)(2,1)S(1)}, u32[]{:S(2)}, u32[]{:S(2)}) %collective-permute-start.6) | collective-permute-done | bytes 32800 | tf_op jit(solution)/shard_map/ppermute | solution.py:575
  72.2 7.3 %spread_entries.1.spread = bf16[2,576,2048]{2,1,0:T(8,128)(2,1)S(1)} custom-call(s32[1]{0:T(128)} %bitcast.along, bf16[64,2,128]{2,1,0:T(2,128)(2,1)S(1)} %all-to-all-done.refs_0_, bf16[64,2,128]{2,1,0:T(2,128)(2,1)S(1)} %collective-permute-done.6.refs_1_, bf16[64,2,128]{2,1,0:T(2,128)(2,1)S(1)} %collective-permute-done.7.refs_2_), custom_call_target="tpu_custom_call" | custom-call | flops 60000000 | bytes 80000 | tf_op jit(solution)/shard_map/spread_entries/pallas_call | solution.py:242
  79.5 0.0 copy-done.7
  79.5 0.0 copy-start
  79.5 2.2 %copy-done = bf16[2,576,2048]{2,1,0:T(8,128)(2,1)} copy-done((bf16[2,576,2048]{2,1,0:T(8,128)(2,1)}, bf16[2,576,2048]{2,1,0:T(8,128)(2,1)S(1)}, u32[]{:S(2)}) %copy-start) | copy-done | bytes 4718616
  81.8 0.0 collective-permute-done.8.other
  81.8 7.3 %pre_partial_0.1 = (bf16[528,768]{1,0:T(8,128)(2,1)}, bf16[512,768]{1,0:T(8,128)(2,1)S(1)}) custom-call(bf16[3,512,768]{2,1,0:T(8,128)(2,1)} %saved.6, bf16[96,768]{1,0:T(8,128)(2,1)S(1)} %collective-permute-done.low, bf16[96,768]{1,0:T(8,128)(2,1)S(1)} %collective-permute-done.2.high, bf16[3,3,768,768]{3,2,1,0:T(8,128)(2,1)} %refs_0_.2), custom_call_target="tpu_custom_call" | custom-call | flops 50000000 | bytes 80000 | tf_op jit(solution)/shard_map/pre_partial_0/pallas_call | solution.py:355
  89.0 0.9 copy-done.11
  89.9 0.0 collective-permute-start.10
  90.0 0.0 collective-permute-done.9.other
  90.0 8.9 %top_gradient.1 = (f32[576,768]{1,0:T(8,128)S(1)}, bf16[576,768]{1,0:T(8,128)(2,1)S(1)}) custom-call(bf16[2,576,2048]{2,1,0:T(8,128)(2,1)} %copy-done, bf16[32,2,64,768]{3,2,1,0:T(8,128)(2,1)} %bitcast.10, bf16[3,768,768]{2,1,0:T(8,128)(2,1)} %refs_1_.3), custom_call_target="tpu_custom_call" | custom-call | flops 50000000 | bytes 140000 | tf_op jit(solution)/shard_map/top_gradient/pallas_call | solution.py:431
  98.8 10.8 %collective-permute-done.10.other = bf16[528,768]{1,0:T(8,128)(2,1)} collective-permute-done((bf16[528,768]{1,0:T(8,128)(2,1)}, bf16[528,768]{1,0:T(8,128)(2,1)}, u32[]{:S(2)}, u32[]{:S(2)}) %collective-permute-start.10) | collective-permute-done | bytes 811040 | tf_op jit(solution)/shard_map/ppermute | solution.py:565
  109.7 0.3 collective-permute-start.11
  110.0 0.1 add_convert_fusion.flags
  110.1 1.2 copy-done.2
  111.2 1.2 copy-done.4
  112.4 1.6 pre_slope_2.1.slope
  114.1 2.4 %stage_weights_2.1 = (bf16[3,768,768]{2,1,0:T(8,128)(2,1)S(1)}, bf16[768,768]{1,0:T(8,128)(2,1)S(1)}) custom-call(bf16[3,3,768,768]{3,2,1,0:T(8,128)(2,1)} %refs_0_.2, bf16[3,768,768]{2,1,0:T(8,128)(2,1)} %refs_1_.3), custom_call_target="tpu_custom_call" | custom-call | flops 10000000 | bytes 10000 | tf_op jit(solution)/shard_map/stage_weights_2/pallas_call | solution.py:268
  116.5 13.3 %collective-permute-done.11.other = bf16[576,768]{1,0:T(8,128)(2,1)S(1)} collective-permute-done((bf16[576,768]{1,0:T(8,128)(2,1)S(1)}, bf16[576,768]{1,0:T(8,128)(2,1)S(1)}, u32[]{:S(2)}, u32[]{:S(2)}) %collective-permute-start.11) | collective-permute-done | bytes 884768 | tf_op jit(solution)/shard_map/ppermute | solution.py:586
  129.8 3.8 %block_step_2.1 = (f32[544,768]{1,0:T(8,128)S(1)}, bf16[544,768]{1,0:T(8,128)(2,1)S(1)}) custom-call(bf16[576,768]{1,0:T(8,128)(2,1)S(1)} %get-tuple-element.54.own, bf16[576,768]{1,0:T(8,128)(2,1)S(1)} %collective-permute-done.11.other, bf16[576,768]{1,0:T(8,128)(2,1)S(1)} %pre_slope_2.1.slope, bf16[3,768,768]{2,1,0:T(8,128)(2,1)S(1)} %get-tuple-element.57.weight, ...), custom_call_target="tpu_custom_call" | custom-call | flops 50000000 | bytes 140000 | tf_op jit(solution)/shard_map/block_step_2/pallas_call | solution.py:493
  133.5 0.9 collective-permute-start.12
  134.4 3.1 %pre_slope_1.1.slope = bf16[544,768]{1,0:T(8,128)(2,1)S(1)} custom-call(s32[2]{0:T(128)S(1)} %add_convert_fusion.flags, bf16[544,768]{1,0:T(8,128)(2,1)S(1)} %copy-done.8, bf16[544,768]{1,0:T(8,128)(2,1)} %collective-permute-done.9.other), custom_call_target="tpu_custom_call" | custom-call | flops 40000000 | bytes 50000 | tf_op jit(solution)/shard_map/pre_slope_1/pallas_call | solution.py:387
  137.5 2.4 %stage_weights_1.1 = (bf16[3,768,768]{2,1,0:T(8,128)(2,1)S(1)}, bf16[768,768]{1,0:T(8,128)(2,1)S(1)}) custom-call(bf16[3,3,768,768]{3,2,1,0:T(8,128)(2,1)} %refs_0_.2, bf16[3,768,768]{2,1,0:T(8,128)(2,1)} %refs_1_.3), custom_call_target="tpu_custom_call" | custom-call | flops 10000000 | bytes 10000 | tf_op jit(solution)/shard_map/stage_weights_1/pallas_call | solution.py:268
  140.0 11.9 %collective-permute-done.12.other = bf16[544,768]{1,0:T(8,128)(2,1)S(1)} collective-permute-done((bf16[544,768]{1,0:T(8,128)(2,1)S(1)}, bf16[544,768]{1,0:T(8,128)(2,1)S(1)}, u32[]{:S(2)}, u32[]{:S(2)}) %collective-permute-start.12) | collective-permute-done | bytes 835616 | tf_op jit(solution)/shard_map/ppermute | solution.py:586
  151.9 3.7 %block_step_1.1 = (f32[528,768]{1,0:T(8,128)S(1)}, bf16[528,768]{1,0:T(8,128)(2,1)S(1)}) custom-call(bf16[544,768]{1,0:T(8,128)(2,1)S(1)} %get-tuple-element.61.own, bf16[544,768]{1,0:T(8,128)(2,1)S(1)} %collective-permute-done.12.other, bf16[544,768]{1,0:T(8,128)(2,1)S(1)} %pre_slope_1.1.slope, bf16[3,768,768]{2,1,0:T(8,128)(2,1)S(1)} %get-tuple-element.64.weight, ...), custom_call_target="tpu_custom_call" | custom-call | flops 50000000 | bytes 140000 | tf_op jit(solution)/shard_map/block_step_1/pallas_call | solution.py:493
  155.6 1.0 collective-permute-start.13
  156.6 3.2 %pre_slope_0.1.slope = bf16[528,768]{1,0:T(8,128)(2,1)S(1)} custom-call(s32[2]{0:T(128)S(1)} %add_convert_fusion.flags, bf16[528,768]{1,0:T(8,128)(2,1)} %get-tuple-element.51.own, bf16[528,768]{1,0:T(8,128)(2,1)} %collective-permute-done.10.other), custom_call_target="tpu_custom_call" | custom-call | flops 40000000 | bytes 50000 | tf_op jit(solution)/shard_map/pre_slope_0/pallas_call | solution.py:387
  159.8 2.1 %stage_weights_0.1.weight = bf16[3,768,768]{2,1,0:T(8,128)(2,1)S(1)} custom-call(bf16[3,3,768,768]{3,2,1,0:T(8,128)(2,1)} %refs_0_.2), custom_call_target="tpu_custom_call" | custom-call | flops 10000000 | bytes 10000 | tf_op jit(solution)/shard_map/stage_weights_0/pallas_call | solution.py:268
  161.9 10.4 %collective-permute-done.13.other = bf16[528,768]{1,0:T(8,128)(2,1)S(1)} collective-permute-done((bf16[528,768]{1,0:T(8,128)(2,1)S(1)}, bf16[528,768]{1,0:T(8,128)(2,1)S(1)}, u32[]{:S(2)}, u32[]{:S(2)}) %collective-permute-start.13) | collective-permute-done | bytes 811040 | tf_op jit(solution)/shard_map/ppermute | solution.py:586
  172.3 0.0 copy-done.12
  172.3 3.1 %block_step_0.1 = bf16[512,768]{1,0:T(8,128)(2,1)} custom-call(bf16[528,768]{1,0:T(8,128)(2,1)S(1)} %get-tuple-element.68.own, bf16[528,768]{1,0:T(8,128)(2,1)S(1)} %collective-permute-done.13.other, bf16[528,768]{1,0:T(8,128)(2,1)S(1)} %pre_slope_0.1.slope, bf16[3,768,768]{2,1,0:T(8,128)(2,1)S(1)} %stage_weights_0.1.weight, ...), custom_call_target="tpu_custom_call" | custom-call | flops 50000000 | bytes 140000 | tf_op jit(solution)/shard_map/block_step_0/pallas_call | solution.py:493
  (24 shorter events, 0.2 us)
Async XLA Ops:
  11.7 19.4 %all-to-all-start = ((bf16[64,2,128]{2,1,0:T(2,128)(2,1)}), bf16[64,2,128]{2,1,0:T(2,128)(2,1)S(1)}, u32[]{:S(2)}, u32[]{:S(2)}) async-start(bf16[64,2,128]{2,1,0:T(2,128)(2,1)} %bucket_entries.1), calls=%async_computation | async-start | bytes 65536 | tf_op jit(solution)/shard_map/all_to_all | solution.py:550
  21.5 68.4 %all-gather.2.cloned.1.call-start = ((), (), s32[]{:S(2)}) async-start(), calls=%async_computation.1 | async-start | bytes 7077888 | tf_op jit(solution)/shard_map/all_gather | solution.py:570
  21.6 9.6 %collective-permute-start.1 = (bf16[64,768]{1,0:T(8,128)(2,1)S(1)}, bf16[64,768]{1,0:T(8,128)(2,1)S(1)}, u32[]{:S(2)}, u32[]{:S(2)}) collective-permute-start(bf16[64,768]{1,0:T(8,128)(2,1)S(1)} %head_vectors.1), channel_id=1, source_target_pairs={{0,8},{2,10},{4,12},{6,14},{8,0},{10,2},{12,4},{14,6},{1,9},{3,11}... | collective-permute-start | bytes 294920 | tf_op jit(solution)/shard_map/ppermute | solution.py:516
  23.2 11.1 %collective-permute-start = (bf16[96,768]{1,0:T(8,128)(2,1)S(1)}, bf16[96,768]{1,0:T(8,128)(2,1)S(1)}, u32[]{:S(2)}, u32[]{:S(2)}) collective-permute-start(bf16[96,768]{1,0:T(8,128)(2,1)S(1)} %get-tuple-element.41), channel_id=1, source_target_pairs={{0,2},{2,4},{4,6},{6,8},{8,10},{10,12},{12,14},{14,16},{16,18},{18... | collective-permute-start | bytes 442376 | tf_op jit(solution)/shard_map/ppermute | solution.py:554
  26.7 8.1 %collective-permute-start.2 = (bf16[96,768]{1,0:T(8,128)(2,1)S(1)}, bf16[96,768]{1,0:T(8,128)(2,1)S(1)}, u32[]{:S(2)}, u32[]{:S(2)}) collective-permute-start(bf16[96,768]{1,0:T(8,128)(2,1)S(1)} %get-tuple-element.42), channel_id=1, source_target_pairs={{2,0},{4,2},{6,4},{8,6},{10,8},{12,10},{14,12},{16,14},{18,16},{20... | collective-permute-start | bytes 442376 | tf_op jit(solution)/shard_map/ppermute | solution.py:555
  31.2 12.5 %collective-permute-start.3 = (bf16[128,768]{1,0:T(8,128)(2,1)S(1)}, bf16[128,768]{1,0:T(8,128)(2,1)S(1)}, u32[]{:S(2)}, u32[]{:S(2)}) collective-permute-start(bf16[128,768]{1,0:T(8,128)(2,1)S(1)} %constant_dynamic-update-slice_fusion), channel_id=1, source_target_pairs={{0,6},{2,0},{4,2},{6,4},{8,14},{10,8},{12,10},{14,12},{1,7},{3,1},... | collective-permute-start | bytes 589832 | tf_op jit(solution)/shard_map/ppermute | solution.py:518
  31.9 12.4 %collective-permute-start.5 = (bf16[128,768]{1,0:T(8,128)(2,1)S(1)}, bf16[128,768]{1,0:T(8,128)(2,1)S(1)}, u32[]{:S(2)}, u32[]{:S(2)}) collective-permute-start(bf16[128,768]{1,0:T(8,128)(2,1)S(1)} %constant_dynamic-update-slice_fusion), channel_id=1, source_target_pairs={{0,2},{2,4},{4,6},{6,0},{8,10},{10,12},{12,14},{14,8},{1,3},{3,5},... | collective-permute-start | bytes 589832 | tf_op jit(solution)/shard_map/ppermute | solution.py:518
  33.3 10.4 %collective-permute-start.4 = (bf16[128,768]{1,0:T(8,128)(2,1)S(1)}, bf16[128,768]{1,0:T(8,128)(2,1)S(1)}, u32[]{:S(2)}, u32[]{:S(2)}) collective-permute-start(bf16[128,768]{1,0:T(8,128)(2,1)S(1)} %constant_dynamic-update-slice_fusion), channel_id=1, source_target_pairs={{0,4},{2,6},{4,0},{6,2},{8,12},{10,14},{12,8},{14,10},{1,5},{3,7},... | collective-permute-start | bytes 589832 | tf_op jit(solution)/shard_map/ppermute | solution.py:518
  41.1 3.4 %copy-start.5 = (bf16[544,768]{1,0:T(8,128)(2,1)}, bf16[544,768]{1,0:T(8,128)(2,1)S(1)}, u32[]{:S(2)}) copy-start(bf16[544,768]{1,0:T(8,128)(2,1)S(1)} %get-tuple-element.59.outer) | copy-start | bytes 2506756
  41.1 4.4 %copy-start.1 = (bf16[576,768]{1,0:T(8,128)(2,1)}, bf16[576,768]{1,0:T(8,128)(2,1)S(1)}, u32[]{:S(2)}) copy-start(bf16[576,768]{1,0:T(8,128)(2,1)S(1)} %get-tuple-element.44.own) | copy-start | bytes 2654212
  45.5 36.3 %collective-permute-start.8 = (bf16[576,768]{1,0:T(8,128)(2,1)S(1)}, bf16[576,768]{1,0:T(8,128)(2,1)S(1)}, u32[]{:S(2)}, u32[]{:S(2)}) collective-permute-start(bf16[576,768]{1,0:T(8,128)(2,1)S(1)} %get-tuple-element.44.own), channel_id=1, source_target_pairs={{0,1},{1,0},{2,3},{3,2},{4,5},{5,4},{6,7},{7,6},{8,9},{9,8},{10,11... | collective-permute-start | bytes 2654216 | tf_op jit(solution)/shard_map/ppermute | solution.py:565
  47.8 20.8 %collective-permute-start.7 = (bf16[64,2,128]{2,1,0:T(2,128)(2,1)S(1)}, bf16[64,2,128]{2,1,0:T(2,128)(2,1)S(1)}, u32[]{:S(2)}, u32[]{:S(2)}) collective-permute-start(bf16[64,2,128]{2,1,0:T(2,128)(2,1)S(1)} %all-to-all-done.refs_0_), channel_id=1, source_target_pairs={{2,0},{4,2},{6,4},{8,6},{10,8},{12,10},{14,12},{16,14},{18,16},{20... | collective-permute-start | bytes 98312 | tf_op jit(solution)/shard_map/ppermute | solution.py:576
  53.0 19.3 %collective-permute-start.6 = (bf16[64,2,128]{2,1,0:T(2,128)(2,1)S(1)}, bf16[64,2,128]{2,1,0:T(2,128)(2,1)S(1)}, u32[]{:S(2)}, u32[]{:S(2)}) collective-permute-start(bf16[64,2,128]{2,1,0:T(2,128)(2,1)S(1)} %all-to-all-done.refs_0_), channel_id=1, source_target_pairs={{0,2},{2,4},{4,6},{6,8},{8,10},{10,12},{12,14},{14,16},{16,18},{18... | collective-permute-start | bytes 98312 | tf_op jit(solution)/shard_map/ppermute | solution.py:575
  61.2 0.9 copy-start.9
  62.1 17.4 %copy-start.7 = (bf16[544,768]{1,0:T(8,128)(2,1)}, bf16[544,768]{1,0:T(8,128)(2,1)S(1)}, u32[]{:S(2)}) copy-start(bf16[544,768]{1,0:T(8,128)(2,1)S(1)} %get-tuple-element.47.own) | copy-start | bytes 2506756
  62.1 27.8 %collective-permute-start.9 = (bf16[544,768]{1,0:T(8,128)(2,1)S(1)}, bf16[544,768]{1,0:T(8,128)(2,1)}, u32[]{:S(2)}, u32[]{:S(2)}) collective-permute-start(bf16[544,768]{1,0:T(8,128)(2,1)S(1)} %get-tuple-element.47.own), channel_id=1, source_target_pairs={{0,1},{1,0},{2,3},{3,2},{4,5},{5,4},{6,7},{7,6},{8,9},{9,8},{10,11... | collective-permute-start | bytes 2506760 | tf_op jit(solution)/shard_map/ppermute | solution.py:565
  79.5 2.2 %copy-start = (bf16[2,576,2048]{2,1,0:T(8,128)(2,1)}, bf16[2,576,2048]{2,1,0:T(8,128)(2,1)S(1)}, u32[]{:S(2)}) copy-start(bf16[2,576,2048]{2,1,0:T(8,128)(2,1)S(1)} %spread_entries.1.spread) | copy-start | bytes 14155780
  81.8 7.3 %copy-start.3 = (bf16[576,768]{1,0:T(8,128)(2,1)}, bf16[576,768]{1,0:T(8,128)(2,1)S(1)}, u32[]{:S(2)}) copy-start(bf16[576,768]{1,0:T(8,128)(2,1)S(1)} %collective-permute-done.8.other) | copy-start | bytes 2654212
  89.0 0.9 copy-start.11
  89.9 19.7 %collective-permute-start.10 = (bf16[528,768]{1,0:T(8,128)(2,1)}, bf16[528,768]{1,0:T(8,128)(2,1)}, u32[]{:S(2)}, u32[]{:S(2)}) collective-permute-start(bf16[528,768]{1,0:T(8,128)(2,1)} %get-tuple-element.51.own), channel_id=1, source_target_pairs={{0,1},{1,0},{2,3},{3,2},{4,5},{5,4},{6,7},{7,6},{8,9},{9,8},{10,11... | collective-permute-start | bytes 2433032 | tf_op jit(solution)/shard_map/ppermute | solution.py:565
  109.7 20.1 %collective-permute-start.11 = (bf16[576,768]{1,0:T(8,128)(2,1)S(1)}, bf16[576,768]{1,0:T(8,128)(2,1)S(1)}, u32[]{:S(2)}, u32[]{:S(2)}) collective-permute-start(bf16[576,768]{1,0:T(8,128)(2,1)S(1)} %get-tuple-element.54.own), channel_id=1, source_target_pairs={{0,1},{1,0},{2,3},{3,2},{4,5},{5,4},{6,7},{7,6},{8,9},{9,8},{10,11... | collective-permute-start | bytes 2654216 | tf_op jit(solution)/shard_map/ppermute | solution.py:586
  110.1 1.2 copy-start.2
  111.2 1.2 copy-start.4
  114.0 15.7 %copy-start.6 = (bf16[544,768]{1,0:T(8,128)(2,1)S(1)}, bf16[544,768]{1,0:T(8,128)(2,1)}, u32[]{:S(2)}) copy-start(bf16[544,768]{1,0:T(8,128)(2,1)} %copy-done.5) | copy-start | bytes 2506756
  129.8 4.7 %copy-start.8 = (bf16[544,768]{1,0:T(8,128)(2,1)S(1)}, bf16[544,768]{1,0:T(8,128)(2,1)}, u32[]{:S(2)}) copy-start(bf16[544,768]{1,0:T(8,128)(2,1)} %copy-done.7) | copy-start | bytes 2506756
  133.5 18.4 %collective-permute-start.12 = (bf16[544,768]{1,0:T(8,128)(2,1)S(1)}, bf16[544,768]{1,0:T(8,128)(2,1)S(1)}, u32[]{:S(2)}, u32[]{:S(2)}) collective-permute-start(bf16[544,768]{1,0:T(8,128)(2,1)S(1)} %get-tuple-element.61.own), channel_id=1, source_target_pairs={{0,1},{1,0},{2,3},{3,2},{4,5},{5,4},{6,7},{7,6},{8,9},{9,8},{10,11... | collective-permute-start | bytes 2506760 | tf_op jit(solution)/shard_map/ppermute | solution.py:586
  137.5 14.4 %copy-start.10 = (bf16[528,768]{1,0:T(8,128)(2,1)S(1)}, bf16[528,768]{1,0:T(8,128)(2,1)}, u32[]{:S(2)}) copy-start(bf16[528,768]{1,0:T(8,128)(2,1)} %copy-done.9) | copy-start | bytes 2433028
  155.6 16.7 %collective-permute-start.13 = (bf16[528,768]{1,0:T(8,128)(2,1)S(1)}, bf16[528,768]{1,0:T(8,128)(2,1)S(1)}, u32[]{:S(2)}, u32[]{:S(2)}) collective-permute-start(bf16[528,768]{1,0:T(8,128)(2,1)S(1)} %get-tuple-element.68.own), channel_id=1, source_target_pairs={{0,1},{1,0},{2,3},{3,2},{4,5},{5,4},{6,7},{7,6},{8,9},{9,8},{10,11... | collective-permute-start | bytes 2433032 | tf_op jit(solution)/shard_map/ppermute | solution.py:586
  159.8 12.5 %copy-start.12 = (bf16[512,768]{1,0:T(8,128)(2,1)S(1)}, bf16[512,768]{1,0:T(8,128)(2,1)}, u32[]{:S(2)}) copy-start(bf16[512,768]{1,0:T(8,128)(2,1)} %copy-done.11) | copy-start | bytes 2359300
Sparse Core Ops, SparseCore 0:
  45.6 42.1 all-gather.1

commit v12 on v11

--- a/solution.py
+++ b/solution.py
@@ -568,16 +568,17 @@
     exchange(levels[0])
     ring = along_head(vectors, place, (arrived, first), (sends[levels[0]],))
     gathered = lax.all_gather(ring, "pos", tiled=True)
+    passed = after(arrived, sends[levels[0]])
+    below = lax.ppermute(passed, GROUP_AXES, up)
+    above = lax.ppermute(passed, GROUP_AXES, down)
     begin(levels[1], ring)
     exchange(levels[1])
     reach = HALO_IN[layers - 1]
-    passed = after(arrived, ring)
-    below = lax.ppermute(passed, GROUP_AXES, up)
-    above = lax.ppermute(passed, GROUP_AXES, down)
+    begin(levels[2], sends[levels[1]], below, above)
     spread = spread_entries(
-        along[None].astype(jnp.int32), after(arrived, sends[levels[1]]), below, above, rows, reach
+        along[None].astype(jnp.int32), after(arrived, sends[levels[2]], others[levels[0]]),
+        below, above, rows, reach,
     )
-    begin(levels[2], spread, others[levels[0]])
     gathered = after(gathered, sends[levels[2]], others[levels[1]])
     grad, send = top_gradient(spread, gathered, expand_weight)
     exchange(levels[2])

time: 183 us -> 189 us (1.033); the launches traced: 182 us -> 185 us
  starting transfers between devices: 33.1 us -> 41 us
  waiting for transfers between devices: 60.3 us -> 55.6 us
    ppermute x1, waiting for transfers between devices: 6.49 us -> 0.01 us  [per_device(): above = lax.ppermute(passed, GROUP_AXES, down)]
    ppermute x3, starting transfers between devices: 2.26 us -> 7.27 us  [per_device(): other = lax.ppermute(send, 'chan', swap)]
    ppermute x1, waiting for transfers between devices: 0.01 us -> 3.37 us  [per_device(): low = lax.ppermute(final, GROUP_AXES, up)]
    ppermute x3, waiting for transfers between devices: 10.8 us -> 7.93 us  [exchange(): others[n] = lax.ppermute(after(sends[n], *earlier), 'chan', swap)]
    ppermute x1, waiting for transfers between devices: 3.59 us -> 5.76 us  [per_device(): below = lax.ppermute(passed, GROUP_AXES, up)]
  transfers between devices with their start and end apart: 16 -> 16, of which waited for: 9 -> 8; matrix products, arithmetic and copies ran while one was open for 0% -> 0% of each run, Pallas kernels for 29% -> 28%
where the time goes in v12:
time: 189 us; the launch traced here: 185 us
  Pallas kernels  67.3 us (36%)
  waiting for transfers between devices  55.6 us (29%)
  starting transfers between devices  41 us (22%)
  between operations  13.8 us (7%)
  local copies, waits for them, and re-layouts  7.47 us (4%)
    ppermute x3, waiting for transfers between devices, per_device(): other = lax.ppermute(send, 'chan', swap)  36.6 us
    pallas_call x3, Pallas kernels, pre_partial(): pl.pallas_call(functools.partial(pre_kernel, level), in_specs=[HBM, VMEM,...  19.6 us
    pallas_call x3, Pallas kernels, block_step(): pl.pallas_call(functools.partial(block_kernel, level), in_specs=[VMEM] *...  10.5 us
    all_to_all x1, starting transfers between devices, per_device(): lax.all_to_all(after(payload, vectors), GROUP_AXES, split_axis=0, concat_...  9.81 us
    pallas_call x1, Pallas kernels, top_gradient(): pl.pallas_call(top_kernel, in_specs=[HBM] * 3, out_specs=[VMEM, VMEM], ou...  8.87 us
    ppermute x3, waiting for transfers between devices, exchange(): others[n] = lax.ppermute(after(sends[n], *earlier), 'chan', swap)  7.93 us
    pallas_call x3, Pallas kernels, pre_slope(): pl.pallas_call(body, grid_spec=pltpu.PrefetchScalarGridSpec(num_scalar_pr...  7.89 us
    pallas_call x1, Pallas kernels, spread_entries(): pl.pallas_call(functools.partial(spread_kernel, rows, reach), grid_spec=p...  7.28 us
  transfers between devices with their start and end apart: 16, of which 8 were waited for; matrix products, arithmetic and copies ran while one was open for 0% of the time, Pallas kernels for 28%

profile of v12, /device:TPU:8, one launch (start us, length us, event | category | flops | bytes accessed | tf_op | source)
XLA Modules:
  0.0 185.2 jit_solution(14100318545270954188)
XLA Ops:
  6.5 3.4 %bucket_entries.1 = bf16[64,2,128]{2,1,0:T(2,128)(2,1)} custom-call(s32[32,64]{1,0:T(8,128)} %bitcast.13, bf16[32,64]{1,0:T(8,128)(2,1)} %bitcast.14), custom_call_target="tpu_custom_call" | custom-call | flops 1000000 | bytes 1000 | tf_op jit(solution)/shard_map/bucket_entries/pallas_call | solution.py:168
  9.9 1.8 head_vectors.1
  11.7 9.8 %all-to-all-start = ((bf16[64,2,128]{2,1,0:T(2,128)(2,1)}), bf16[64,2,128]{2,1,0:T(2,128)(2,1)S(1)}, u32[]{:S(2)}, u32[]{:S(2)}) async-start(bf16[64,2,128]{2,1,0:T(2,128)(2,1)} %bucket_entries.1), calls=%async_computation | async-start | bytes 65536 | tf_op jit(solution)/shard_map/all_to_all | solution.py:550
  21.5 0.0 all-gather.2.cloned.1.call-start
  21.6 0.5 collective-permute-start.1
  22.1 1.1 cut_edges.1
  23.2 5.6 %collective-permute-start.2 = (bf16[96,768]{1,0:T(8,128)(2,1)S(1)}, bf16[96,768]{1,0:T(8,128)(2,1)S(1)}, u32[]{:S(2)}, u32[]{:S(2)}) collective-permute-start(bf16[96,768]{1,0:T(8,128)(2,1)S(1)} %get-tuple-element.42), channel_id=1, source_target_pairs={{2,0},{4,2},{6,4},{8,6},{10,8},{12,10},{14,12},{16,14},{18,16},{20... | collective-permute-start | bytes 442376 | tf_op jit(solution)/shard_map/ppermute | solution.py:555
  28.8 1.9 %collective-permute-start = (bf16[96,768]{1,0:T(8,128)(2,1)S(1)}, bf16[96,768]{1,0:T(8,128)(2,1)S(1)}, u32[]{:S(2)}, u32[]{:S(2)}) collective-permute-start(bf16[96,768]{1,0:T(8,128)(2,1)S(1)} %get-tuple-element.41), channel_id=1, source_target_pairs={{0,2},{2,4},{4,6},{6,8},{8,10},{10,12},{12,14},{14,16},{16,18},{18... | collective-permute-start | bytes 442376 | tf_op jit(solution)/shard_map/ppermute | solution.py:554
  30.7 0.0 all-to-all-done.refs_0_
  30.7 0.0 collective-permute-done.1
  30.8 3.0 %collective-permute-start.3 = (bf16[128,768]{1,0:T(8,128)(2,1)S(1)}, bf16[128,768]{1,0:T(8,128)(2,1)S(1)}, u32[]{:S(2)}, u32[]{:S(2)}) collective-permute-start(bf16[128,768]{1,0:T(8,128)(2,1)S(1)} %constant_dynamic-update-slice_fusion), channel_id=1, source_target_pairs={{0,6},{2,0},{4,2},{6,4},{8,14},{10,8},{12,10},{14,12},{1,7},{3,1},... | collective-permute-start | bytes 589832 | tf_op jit(solution)/shard_map/ppermute | solution.py:518
  33.8 0.0 collective-permute-start.4
  33.8 1.0 collective-permute-start.5
  34.8 3.4 %collective-permute-done.low = bf16[96,768]{1,0:T(8,128)(2,1)S(1)} collective-permute-done((bf16[96,768]{1,0:T(8,128)(2,1)S(1)}, bf16[96,768]{1,0:T(8,128)(2,1)S(1)}, u32[]{:S(2)}, u32[]{:S(2)}) %collective-permute-start) | collective-permute-done | bytes 147488 | tf_op jit(solution)/shard_map/ppermute | solution.py:554
  38.1 0.0 collective-permute-done.2.high
  38.1 6.3 %pre_partial_2.1 = (bf16[576,768]{1,0:T(8,128)(2,1)S(1)}, bf16[544,768]{1,0:T(8,128)(2,1)S(1)}) custom-call(bf16[3,512,768]{2,1,0:T(8,128)(2,1)} %saved.6, bf16[96,768]{1,0:T(8,128)(2,1)S(1)} %collective-permute-done.low, bf16[96,768]{1,0:T(8,128)(2,1)S(1)} %collective-permute-done.2.high, bf16[3,3,768,768]{3,2,1,0:T(8,128)(2,1)} %refs_0_.2), custom_call_target="tpu_custom_call" | custom-call | flops 50000000 | bytes 80000 | tf_op jit(solution)/shard_map/pre_partial_2/pallas_call | solution.py:355
  44.5 0.0 copy-start.5
  44.5 0.0 copy-start.1
  44.5 0.0 collective-permute-done.3
  44.5 0.0 collective-permute-done.4
  44.6 2.0 %collective-permute-done.5 = bf16[128,768]{1,0:T(8,128)(2,1)S(1)} collective-permute-done((bf16[128,768]{1,0:T(8,128)(2,1)S(1)}, bf16[128,768]{1,0:T(8,128)(2,1)S(1)}, u32[]{:S(2)}, u32[]{:S(2)}) %collective-permute-start.5) | collective-permute-done | bytes 196640 | tf_op jit(solution)/shard_map/ppermute | solution.py:518
  46.7 0.9 constant_dynamic-slice_fusion
  47.6 0.0 all-gather.2.cloned.1.call-update
  47.6 2.4 %collective-permute-start.8 = (bf16[576,768]{1,0:T(8,128)(2,1)S(1)}, bf16[576,768]{1,0:T(8,128)(2,1)S(1)}, u32[]{:S(2)}, u32[]{:S(2)}) collective-permute-start(bf16[576,768]{1,0:T(8,128)(2,1)S(1)} %get-tuple-element.44.own), channel_id=1, source_target_pairs={{0,1},{1,0},{2,3},{3,2},{4,5},{5,4},{6,7},{7,6},{8,9},{9,8},{10,11... | collective-permute-start | bytes 2654216 | tf_op jit(solution)/shard_map/ppermute | solution.py:565
  50.0 1.9 %collective-permute-start.6 = (bf16[64,2,128]{2,1,0:T(2,128)(2,1)S(1)}, bf16[64,2,128]{2,1,0:T(2,128)(2,1)S(1)}, u32[]{:S(2)}, u32[]{:S(2)}) collective-permute-start(bf16[64,2,128]{2,1,0:T(2,128)(2,1)S(1)} %all-to-all-done.refs_0_), channel_id=1, source_target_pairs={{0,2},{2,4},{4,6},{6,8},{8,10},{10,12},{12,14},{14,16},{16,18},{18... | collective-permute-start | bytes 98312 | tf_op jit(solution)/shard_map/ppermute | solution.py:572
  51.9 6.0 %collective-permute-start.7 = (bf16[64,2,128]{2,1,0:T(2,128)(2,1)S(1)}, bf16[64,2,128]{2,1,0:T(2,128)(2,1)S(1)}, u32[]{:S(2)}, u32[]{:S(2)}) collective-permute-start(bf16[64,2,128]{2,1,0:T(2,128)(2,1)S(1)} %all-to-all-done.refs_0_), channel_id=1, source_target_pairs={{2,0},{4,2},{6,4},{8,6},{10,8},{12,10},{14,12},{16,14},{18,16},{20... | collective-permute-start | bytes 98312 | tf_op jit(solution)/shard_map/ppermute | solution.py:573
  58.0 6.2 %pre_partial_1.1 = (bf16[544,768]{1,0:T(8,128)(2,1)S(1)}, bf16[528,768]{1,0:T(8,128)(2,1)S(1)}) custom-call(bf16[3,512,768]{2,1,0:T(8,128)(2,1)} %saved.6, bf16[96,768]{1,0:T(8,128)(2,1)S(1)} %collective-permute-done.low, bf16[96,768]{1,0:T(8,128)(2,1)S(1)} %collective-permute-done.2.high, bf16[3,3,768,768]{3,2,1,0:T(8,128)(2,1)} %refs_0_.2), custom_call_target="tpu_custom_call" | custom-call | flops 50000000 | bytes 80000 | tf_op jit(solution)/shard_map/pre_partial_1/pallas_call | solution.py:355
  64.2 0.0 copy-start.9
  64.2 0.9 copy-done.9
  65.1 1.5 collective-permute-start.9
  66.7 5.8 %collective-permute-done.6.refs_1_ = bf16[64,2,128]{2,1,0:T(2,128)(2,1)S(1)} collective-permute-done((bf16[64,2,128]{2,1,0:T(2,128)(2,1)S(1)}, bf16[64,2,128]{2,1,0:T(2,128)(2,1)S(1)}, u32[]{:S(2)}, u32[]{:S(2)}) %collective-permute-start.6) | collective-permute-done | bytes 32800 | tf_op jit(solution)/shard_map/ppermute | solution.py:572
  72.4 0.0 collective-permute-done.7.refs_2_
  72.5 7.0 %pre_partial_0.1 = (bf16[528,768]{1,0:T(8,128)(2,1)}, bf16[512,768]{1,0:T(8,128)(2,1)S(1)}) custom-call(bf16[3,512,768]{2,1,0:T(8,128)(2,1)} %saved.6, bf16[96,768]{1,0:T(8,128)(2,1)S(1)} %collective-permute-done.low, bf16[96,768]{1,0:T(8,128)(2,1)S(1)} %collective-permute-done.2.high, bf16[3,3,768,768]{3,2,1,0:T(8,128)(2,1)} %refs_0_.2), custom_call_target="tpu_custom_call" | custom-call | flops 50000000 | bytes 80000 | tf_op jit(solution)/shard_map/pre_partial_0/pallas_call | solution.py:355
  79.5 0.9 copy-done.11
  80.4 0.0 collective-permute-start.10
  80.4 0.0 collective-permute-done.8.other
  80.4 7.3 %spread_entries.1.spread = bf16[2,576,2048]{2,1,0:T(8,128)(2,1)S(1)} custom-call(s32[1]{0:T(128)} %bitcast.along, bf16[64,2,128]{2,1,0:T(2,128)(2,1)S(1)} %all-to-all-done.refs_0_, bf16[64,2,128]{2,1,0:T(2,128)(2,1)S(1)} %collective-permute-done.6.refs_1_, bf16[64,2,128]{2,1,0:T(2,128)(2,1)S(1)} %collective-permute-done.7.refs_2_), custom_call_target="tpu_custom_call" | custom-call | flops 60000000 | bytes 80000 | tf_op jit(solution)/shard_map/spread_entries/pallas_call | solution.py:242
  87.7 0.0 copy-done.3
  87.7 0.0 copy-start
  87.7 2.2 %copy-done = bf16[2,576,2048]{2,1,0:T(8,128)(2,1)} copy-done((bf16[2,576,2048]{2,1,0:T(8,128)(2,1)}, bf16[2,576,2048]{2,1,0:T(8,128)(2,1)S(1)}, u32[]{:S(2)}) %copy-start) | copy-done | bytes 4718616
  89.9 0.5 collective-permute-done.9.other
  90.5 8.9 %top_gradient.1 = (f32[576,768]{1,0:T(8,128)S(1)}, bf16[576,768]{1,0:T(8,128)(2,1)S(1)}) custom-call(bf16[2,576,2048]{2,1,0:T(8,128)(2,1)} %copy-done, bf16[32,2,64,768]{3,2,1,0:T(8,128)(2,1)} %bitcast.10, bf16[3,768,768]{2,1,0:T(8,128)(2,1)} %refs_1_.3), custom_call_target="tpu_custom_call" | custom-call | flops 50000000 | bytes 140000 | tf_op jit(solution)/shard_map/top_gradient/pallas_call | solution.py:431
  99.3 7.4 %collective-permute-done.10.other = bf16[528,768]{1,0:T(8,128)(2,1)} collective-permute-done((bf16[528,768]{1,0:T(8,128)(2,1)}, bf16[528,768]{1,0:T(8,128)(2,1)}, u32[]{:S(2)}, u32[]{:S(2)}) %collective-permute-start.10) | collective-permute-done | bytes 811040 | tf_op jit(solution)/shard_map/ppermute | solution.py:565
  106.7 2.3 %collective-permute-start.11 = (bf16[576,768]{1,0:T(8,128)(2,1)S(1)}, bf16[576,768]{1,0:T(8,128)(2,1)S(1)}, u32[]{:S(2)}, u32[]{:S(2)}) collective-permute-start(bf16[576,768]{1,0:T(8,128)(2,1)S(1)} %get-tuple-element.54.own), channel_id=1, source_target_pairs={{0,1},{1,0},{2,3},{3,2},{4,5},{5,4},{6,7},{7,6},{8,9},{9,8},{10,11... | collective-permute-start | bytes 2654216 | tf_op jit(solution)/shard_map/ppermute | solution.py:587
  109.0 0.1 add_convert_fusion.flags
  109.1 1.2 copy-done.2
  110.3 1.2 copy-done.4
  111.4 1.6 pre_slope_2.1.slope
  113.1 0.0 copy-start.6
  113.1 2.4 %stage_weights_2.1 = (bf16[3,768,768]{2,1,0:T(8,128)(2,1)S(1)}, bf16[768,768]{1,0:T(8,128)(2,1)S(1)}) custom-call(bf16[3,3,768,768]{3,2,1,0:T(8,128)(2,1)} %refs_0_.2, bf16[3,768,768]{2,1,0:T(8,128)(2,1)} %refs_1_.3), custom_call_target="tpu_custom_call" | custom-call | flops 10000000 | bytes 10000 | tf_op jit(solution)/shard_map/stage_weights_2/pallas_call | solution.py:268
  115.5 13.3 %collective-permute-done.11.other = bf16[576,768]{1,0:T(8,128)(2,1)S(1)} collective-permute-done((bf16[576,768]{1,0:T(8,128)(2,1)S(1)}, bf16[576,768]{1,0:T(8,128)(2,1)S(1)}, u32[]{:S(2)}, u32[]{:S(2)}) %collective-permute-start.11) | collective-permute-done | bytes 884768 | tf_op jit(solution)/shard_map/ppermute | solution.py:587
  128.8 3.8 %block_step_2.1 = (f32[544,768]{1,0:T(8,128)S(1)}, bf16[544,768]{1,0:T(8,128)(2,1)S(1)}) custom-call(bf16[576,768]{1,0:T(8,128)(2,1)S(1)} %get-tuple-element.54.own, bf16[576,768]{1,0:T(8,128)(2,1)S(1)} %collective-permute-done.11.other, bf16[576,768]{1,0:T(8,128)(2,1)S(1)} %pre_slope_2.1.slope, bf16[3,768,768]{2,1,0:T(8,128)(2,1)S(1)} %get-tuple-element.57.weight, ...), custom_call_target="tpu_custom_call" | custom-call | flops 50000000 | bytes 140000 | tf_op jit(solution)/shard_map/block_step_2/pallas_call | solution.py:493
  132.5 2.6 %collective-permute-start.12 = (bf16[544,768]{1,0:T(8,128)(2,1)S(1)}, bf16[544,768]{1,0:T(8,128)(2,1)S(1)}, u32[]{:S(2)}, u32[]{:S(2)}) collective-permute-start(bf16[544,768]{1,0:T(8,128)(2,1)S(1)} %get-tuple-element.61.own), channel_id=1, source_target_pairs={{0,1},{1,0},{2,3},{3,2},{4,5},{5,4},{6,7},{7,6},{8,9},{9,8},{10,11... | collective-permute-start | bytes 2506760 | tf_op jit(solution)/shard_map/ppermute | solution.py:587
  135.1 3.1 %pre_slope_1.1.slope = bf16[544,768]{1,0:T(8,128)(2,1)S(1)} custom-call(s32[2]{0:T(128)S(1)} %add_convert_fusion.flags, bf16[544,768]{1,0:T(8,128)(2,1)S(1)} %copy-done.8, bf16[544,768]{1,0:T(8,128)(2,1)} %collective-permute-done.9.other), custom_call_target="tpu_custom_call" | custom-call | flops 40000000 | bytes 50000 | tf_op jit(solution)/shard_map/pre_slope_1/pallas_call | solution.py:387
  138.2 2.4 %stage_weights_1.1 = (bf16[3,768,768]{2,1,0:T(8,128)(2,1)S(1)}, bf16[768,768]{1,0:T(8,128)(2,1)S(1)}) custom-call(bf16[3,3,768,768]{3,2,1,0:T(8,128)(2,1)} %refs_0_.2, bf16[3,768,768]{2,1,0:T(8,128)(2,1)} %refs_1_.3), custom_call_target="tpu_custom_call" | custom-call | flops 10000000 | bytes 10000 | tf_op jit(solution)/shard_map/stage_weights_1/pallas_call | solution.py:268
  140.7 12.2 %collective-permute-done.12.other = bf16[544,768]{1,0:T(8,128)(2,1)S(1)} collective-permute-done((bf16[544,768]{1,0:T(8,128)(2,1)S(1)}, bf16[544,768]{1,0:T(8,128)(2,1)S(1)}, u32[]{:S(2)}, u32[]{:S(2)}) %collective-permute-start.12) | collective-permute-done | bytes 835616 | tf_op jit(solution)/shard_map/ppermute | solution.py:587
  152.9 0.0 copy-done.10
  152.9 3.7 %block_step_1.1 = (f32[528,768]{1,0:T(8,128)S(1)}, bf16[528,768]{1,0:T(8,128)(2,1)S(1)}) custom-call(bf16[544,768]{1,0:T(8,128)(2,1)S(1)} %get-tuple-element.61.own, bf16[544,768]{1,0:T(8,128)(2,1)S(1)} %collective-permute-done.12.other, bf16[544,768]{1,0:T(8,128)(2,1)S(1)} %pre_slope_1.1.slope, bf16[3,768,768]{2,1,0:T(8,128)(2,1)S(1)} %get-tuple-element.64.weight, ...), custom_call_target="tpu_custom_call" | custom-call | flops 50000000 | bytes 140000 | tf_op jit(solution)/shard_map/block_step_1/pallas_call | solution.py:493
  156.6 2.4 %collective-permute-start.13 = (bf16[528,768]{1,0:T(8,128)(2,1)S(1)}, bf16[528,768]{1,0:T(8,128)(2,1)S(1)}, u32[]{:S(2)}, u32[]{:S(2)}) collective-permute-start(bf16[528,768]{1,0:T(8,128)(2,1)S(1)} %get-tuple-element.68.own), channel_id=1, source_target_pairs={{0,1},{1,0},{2,3},{3,2},{4,5},{5,4},{6,7},{7,6},{8,9},{9,8},{10,11... | collective-permute-start | bytes 2433032 | tf_op jit(solution)/shard_map/ppermute | solution.py:587
  159.0 3.2 %pre_slope_0.1.slope = bf16[528,768]{1,0:T(8,128)(2,1)S(1)} custom-call(s32[2]{0:T(128)S(1)} %add_convert_fusion.flags, bf16[528,768]{1,0:T(8,128)(2,1)} %get-tuple-element.50.own, bf16[528,768]{1,0:T(8,128)(2,1)} %collective-permute-done.10.other), custom_call_target="tpu_custom_call" | custom-call | flops 40000000 | bytes 50000 | tf_op jit(solution)/shard_map/pre_slope_0/pallas_call | solution.py:387
  162.2 2.1 %stage_weights_0.1.weight = bf16[3,768,768]{2,1,0:T(8,128)(2,1)S(1)} custom-call(bf16[3,3,768,768]{3,2,1,0:T(8,128)(2,1)} %refs_0_.2), custom_call_target="tpu_custom_call" | custom-call | flops 10000000 | bytes 10000 | tf_op jit(solution)/shard_map/stage_weights_0/pallas_call | solution.py:268
  164.3 11.0 %collective-permute-done.13.other = bf16[528,768]{1,0:T(8,128)(2,1)S(1)} collective-permute-done((bf16[528,768]{1,0:T(8,128)(2,1)S(1)}, bf16[528,768]{1,0:T(8,128)(2,1)S(1)}, u32[]{:S(2)}, u32[]{:S(2)}) %collective-permute-start.13) | collective-permute-done | bytes 811040 | tf_op jit(solution)/shard_map/ppermute | solution.py:587
  175.3 0.0 copy-done.12
  175.3 3.1 %block_step_0.1 = bf16[512,768]{1,0:T(8,128)(2,1)} custom-call(bf16[528,768]{1,0:T(8,128)(2,1)S(1)} %get-tuple-element.68.own, bf16[528,768]{1,0:T(8,128)(2,1)S(1)} %collective-permute-done.13.other, bf16[528,768]{1,0:T(8,128)(2,1)S(1)} %pre_slope_0.1.slope, bf16[3,768,768]{2,1,0:T(8,128)(2,1)S(1)} %stage_weights_0.1.weight, ...), custom_call_target="tpu_custom_call" | custom-call | flops 50000000 | bytes 140000 | tf_op jit(solution)/shard_map/block_step_0/pallas_call | solution.py:493
  (24 shorter events, 0.2 us)
Async XLA Ops:
  11.7 19.0 %all-to-all-start = ((bf16[64,2,128]{2,1,0:T(2,128)(2,1)}), bf16[64,2,128]{2,1,0:T(2,128)(2,1)S(1)}, u32[]{:S(2)}, u32[]{:S(2)}) async-start(bf16[64,2,128]{2,1,0:T(2,128)(2,1)} %bucket_entries.1), calls=%async_computation | async-start | bytes 65536 | tf_op jit(solution)/shard_map/all_to_all | solution.py:550
  21.5 69.0 %all-gather.2.cloned.1.call-start = ((), (), s32[]{:S(2)}) async-start(), calls=%async_computation.1 | async-start | bytes 7077888 | tf_op jit(solution)/shard_map/all_gather | solution.py:570
  21.6 9.2 %collective-permute-start.1 = (bf16[64,768]{1,0:T(8,128)(2,1)S(1)}, bf16[64,768]{1,0:T(8,128)(2,1)S(1)}, u32[]{:S(2)}, u32[]{:S(2)}) collective-permute-start(bf16[64,768]{1,0:T(8,128)(2,1)S(1)} %head_vectors.1), channel_id=1, source_target_pairs={{0,8},{2,10},{4,12},{6,14},{8,0},{10,2},{12,4},{14,6},{1,9},{3,11}... | collective-permute-start | bytes 294920 | tf_op jit(solution)/shard_map/ppermute | solution.py:516
  23.2 14.9 %collective-permute-start.2 = (bf16[96,768]{1,0:T(8,128)(2,1)S(1)}, bf16[96,768]{1,0:T(8,128)(2,1)S(1)}, u32[]{:S(2)}, u32[]{:S(2)}) collective-permute-start(bf16[96,768]{1,0:T(8,128)(2,1)S(1)} %get-tuple-element.42), channel_id=1, source_target_pairs={{2,0},{4,2},{6,4},{8,6},{10,8},{12,10},{14,12},{16,14},{18,16},{20... | collective-permute-start | bytes 442376 | tf_op jit(solution)/shard_map/ppermute | solution.py:555
  28.8 9.3 %collective-permute-start = (bf16[96,768]{1,0:T(8,128)(2,1)S(1)}, bf16[96,768]{1,0:T(8,128)(2,1)S(1)}, u32[]{:S(2)}, u32[]{:S(2)}) collective-permute-start(bf16[96,768]{1,0:T(8,128)(2,1)S(1)} %get-tuple-element.41), channel_id=1, source_target_pairs={{0,2},{2,4},{4,6},{6,8},{8,10},{10,12},{12,14},{14,16},{16,18},{18... | collective-permute-start | bytes 442376 | tf_op jit(solution)/shard_map/ppermute | solution.py:554
  30.8 13.7 %collective-permute-start.3 = (bf16[128,768]{1,0:T(8,128)(2,1)S(1)}, bf16[128,768]{1,0:T(8,128)(2,1)S(1)}, u32[]{:S(2)}, u32[]{:S(2)}) collective-permute-start(bf16[128,768]{1,0:T(8,128)(2,1)S(1)} %constant_dynamic-update-slice_fusion), channel_id=1, source_target_pairs={{0,6},{2,0},{4,2},{6,4},{8,14},{10,8},{12,10},{14,12},{1,7},{3,1},... | collective-permute-start | bytes 589832 | tf_op jit(solution)/shard_map/ppermute | solution.py:518
  33.8 10.8 %collective-permute-start.4 = (bf16[128,768]{1,0:T(8,128)(2,1)S(1)}, bf16[128,768]{1,0:T(8,128)(2,1)S(1)}, u32[]{:S(2)}, u32[]{:S(2)}) collective-permute-start(bf16[128,768]{1,0:T(8,128)(2,1)S(1)} %constant_dynamic-update-slice_fusion), channel_id=1, source_target_pairs={{0,4},{2,6},{4,0},{6,2},{8,12},{10,14},{12,8},{14,10},{1,5},{3,7},... | collective-permute-start | bytes 589832 | tf_op jit(solution)/shard_map/ppermute | solution.py:518
  33.8 12.8 %collective-permute-start.5 = (bf16[128,768]{1,0:T(8,128)(2,1)S(1)}, bf16[128,768]{1,0:T(8,128)(2,1)S(1)}, u32[]{:S(2)}, u32[]{:S(2)}) collective-permute-start(bf16[128,768]{1,0:T(8,128)(2,1)S(1)} %constant_dynamic-update-slice_fusion), channel_id=1, source_target_pairs={{0,2},{2,4},{4,6},{6,0},{8,10},{10,12},{12,14},{14,8},{1,3},{3,5},... | collective-permute-start | bytes 589832 | tf_op jit(solution)/shard_map/ppermute | solution.py:518
  44.5 2.2 %copy-start.5 = (bf16[544,768]{1,0:T(8,128)(2,1)}, bf16[544,768]{1,0:T(8,128)(2,1)S(1)}, u32[]{:S(2)}) copy-start(bf16[544,768]{1,0:T(8,128)(2,1)S(1)} %get-tuple-element.59.outer) | copy-start | bytes 2506756
  44.5 3.2 %copy-start.1 = (bf16[576,768]{1,0:T(8,128)(2,1)}, bf16[576,768]{1,0:T(8,128)(2,1)S(1)}, u32[]{:S(2)}) copy-start(bf16[576,768]{1,0:T(8,128)(2,1)S(1)} %get-tuple-element.44.own) | copy-start | bytes 2654212
  47.6 32.8 %collective-permute-start.8 = (bf16[576,768]{1,0:T(8,128)(2,1)S(1)}, bf16[576,768]{1,0:T(8,128)(2,1)S(1)}, u32[]{:S(2)}, u32[]{:S(2)}) collective-permute-start(bf16[576,768]{1,0:T(8,128)(2,1)S(1)} %get-tuple-element.44.own), channel_id=1, source_target_pairs={{0,1},{1,0},{2,3},{3,2},{4,5},{5,4},{6,7},{7,6},{8,9},{9,8},{10,11... | collective-permute-start | bytes 2654216 | tf_op jit(solution)/shard_map/ppermute | solution.py:565
  50.0 22.4 %collective-permute-start.6 = (bf16[64,2,128]{2,1,0:T(2,128)(2,1)S(1)}, bf16[64,2,128]{2,1,0:T(2,128)(2,1)S(1)}, u32[]{:S(2)}, u32[]{:S(2)}) collective-permute-start(bf16[64,2,128]{2,1,0:T(2,128)(2,1)S(1)} %all-to-all-done.refs_0_), channel_id=1, source_target_pairs={{0,2},{2,4},{4,6},{6,8},{8,10},{10,12},{12,14},{14,16},{16,18},{18... | collective-permute-start | bytes 98312 | tf_op jit(solution)/shard_map/ppermute | solution.py:572
  51.9 20.5 %collective-permute-start.7 = (bf16[64,2,128]{2,1,0:T(2,128)(2,1)S(1)}, bf16[64,2,128]{2,1,0:T(2,128)(2,1)S(1)}, u32[]{:S(2)}, u32[]{:S(2)}) collective-permute-start(bf16[64,2,128]{2,1,0:T(2,128)(2,1)S(1)} %all-to-all-done.refs_0_), channel_id=1, source_target_pairs={{2,0},{4,2},{6,4},{8,6},{10,8},{12,10},{14,12},{16,14},{18,16},{20... | collective-permute-start | bytes 98312 | tf_op jit(solution)/shard_map/ppermute | solution.py:573
  64.2 0.9 copy-start.9
  65.1 14.3 %copy-start.7 = (bf16[544,768]{1,0:T(8,128)(2,1)}, bf16[544,768]{1,0:T(8,128)(2,1)S(1)}, u32[]{:S(2)}) copy-start(bf16[544,768]{1,0:T(8,128)(2,1)S(1)} %get-tuple-element.47.own) | copy-start | bytes 2506756
  65.1 25.3 %collective-permute-start.9 = (bf16[544,768]{1,0:T(8,128)(2,1)S(1)}, bf16[544,768]{1,0:T(8,128)(2,1)}, u32[]{:S(2)}, u32[]{:S(2)}) collective-permute-start(bf16[544,768]{1,0:T(8,128)(2,1)S(1)} %get-tuple-element.47.own), channel_id=1, source_target_pairs={{0,1},{1,0},{2,3},{3,2},{4,5},{5,4},{6,7},{7,6},{8,9},{9,8},{10,11... | collective-permute-start | bytes 2506760 | tf_op jit(solution)/shard_map/ppermute | solution.py:565
  79.5 0.9 copy-start.11
  80.4 26.3 %collective-permute-start.10 = (bf16[528,768]{1,0:T(8,128)(2,1)}, bf16[528,768]{1,0:T(8,128)(2,1)}, u32[]{:S(2)}, u32[]{:S(2)}) collective-permute-start(bf16[528,768]{1,0:T(8,128)(2,1)} %get-tuple-element.50.own), channel_id=1, source_target_pairs={{0,1},{1,0},{2,3},{3,2},{4,5},{5,4},{6,7},{7,6},{8,9},{9,8},{10,11... | collective-permute-start | bytes 2433032 | tf_op jit(solution)/shard_map/ppermute | solution.py:565
  80.4 7.3 %copy-start.3 = (bf16[576,768]{1,0:T(8,128)(2,1)}, bf16[576,768]{1,0:T(8,128)(2,1)S(1)}, u32[]{:S(2)}) copy-start(bf16[576,768]{1,0:T(8,128)(2,1)S(1)} %collective-permute-done.8.other) | copy-start | bytes 2654212
  87.7 2.2 %copy-start = (bf16[2,576,2048]{2,1,0:T(8,128)(2,1)}, bf16[2,576,2048]{2,1,0:T(8,128)(2,1)S(1)}, u32[]{:S(2)}) copy-start(bf16[2,576,2048]{2,1,0:T(8,128)(2,1)S(1)} %spread_entries.1.spread) | copy-start | bytes 14155780
  106.7 22.1 %collective-permute-start.11 = (bf16[576,768]{1,0:T(8,128)(2,1)S(1)}, bf16[576,768]{1,0:T(8,128)(2,1)S(1)}, u32[]{:S(2)}, u32[]{:S(2)}) collective-permute-start(bf16[576,768]{1,0:T(8,128)(2,1)S(1)} %get-tuple-element.54.own), channel_id=1, source_target_pairs={{0,1},{1,0},{2,3},{3,2},{4,5},{5,4},{6,7},{7,6},{8,9},{9,8},{10,11... | collective-permute-start | bytes 2654216 | tf_op jit(solution)/shard_map/ppermute | solution.py:587
  109.1 1.2 copy-start.2
  110.3 1.2 copy-start.4
  113.1 15.7 %copy-start.6 = (bf16[544,768]{1,0:T(8,128)(2,1)S(1)}, bf16[544,768]{1,0:T(8,128)(2,1)}, u32[]{:S(2)}) copy-start(bf16[544,768]{1,0:T(8,128)(2,1)} %copy-done.5) | copy-start | bytes 2506756
  128.8 6.4 %copy-start.8 = (bf16[544,768]{1,0:T(8,128)(2,1)S(1)}, bf16[544,768]{1,0:T(8,128)(2,1)}, u32[]{:S(2)}) copy-start(bf16[544,768]{1,0:T(8,128)(2,1)} %copy-done.7) | copy-start | bytes 2506756
  132.5 20.4 %collective-permute-start.12 = (bf16[544,768]{1,0:T(8,128)(2,1)S(1)}, bf16[544,768]{1,0:T(8,128)(2,1)S(1)}, u32[]{:S(2)}, u32[]{:S(2)}) collective-permute-start(bf16[544,768]{1,0:T(8,128)(2,1)S(1)} %get-tuple-element.61.own), channel_id=1, source_target_pairs={{0,1},{1,0},{2,3},{3,2},{4,5},{5,4},{6,7},{7,6},{8,9},{9,8},{10,11... | collective-permute-start | bytes 2506760 | tf_op jit(solution)/shard_map/ppermute | solution.py:587
  138.2 14.7 %copy-start.10 = (bf16[528,768]{1,0:T(8,128)(2,1)S(1)}, bf16[528,768]{1,0:T(8,128)(2,1)}, u32[]{:S(2)}) copy-start(bf16[528,768]{1,0:T(8,128)(2,1)} %copy-done.9) | copy-start | bytes 2433028
  156.6 18.7 %collective-permute-start.13 = (bf16[528,768]{1,0:T(8,128)(2,1)S(1)}, bf16[528,768]{1,0:T(8,128)(2,1)S(1)}, u32[]{:S(2)}, u32[]{:S(2)}) collective-permute-start(bf16[528,768]{1,0:T(8,128)(2,1)S(1)} %get-tuple-element.68.own), channel_id=1, source_target_pairs={{0,1},{1,0},{2,3},{3,2},{4,5},{5,4},{6,7},{7,6},{8,9},{9,8},{10,11... | collective-permute-start | bytes 2433032 | tf_op jit(solution)/shard_map/ppermute | solution.py:587
  162.2 13.1 %copy-start.12 = (bf16[512,768]{1,0:T(8,128)(2,1)S(1)}, bf16[512,768]{1,0:T(8,128)(2,1)}, u32[]{:S(2)}) copy-start(bf16[512,768]{1,0:T(8,128)(2,1)} %copy-done.11) | copy-start | bytes 2359300
Sparse Core Ops, SparseCore 0:
  47.8 40.6 all-gather.1

commit v13 on v11

--- a/solution.py
+++ b/solution.py
@@ -564,16 +564,15 @@
     def exchange(n, *earlier):
         others[n] = lax.ppermute(after(sends[n], *earlier), "chan", swap)
 
-    begin(levels[0])
+    below = lax.ppermute(arrived, GROUP_AXES, up)
+    above = lax.ppermute(arrived, GROUP_AXES, down)
+    begin(levels[0], below, above)
     exchange(levels[0])
     ring = along_head(vectors, place, (arrived, first), (sends[levels[0]],))
     gathered = lax.all_gather(ring, "pos", tiled=True)
     begin(levels[1], ring)
     exchange(levels[1])
     reach = HALO_IN[layers - 1]
-    passed = after(arrived, ring)
-    below = lax.ppermute(passed, GROUP_AXES, up)
-    above = lax.ppermute(passed, GROUP_AXES, down)
     spread = spread_entries(
         along[None].astype(jnp.int32), after(arrived, sends[levels[1]]), below, above, rows, reach
     )

time: 183 us -> 191 us (1.044)
  the two profiles are of different devices: /device:TPU:8 before, /device:TPU:64 now
where the time goes in v13:
time: 191 us
  Pallas kernels  67.4 us (35%)
  waiting for transfers between devices  61.2 us (32%)
  starting transfers between devices  40.8 us (21%)
  between operations  13.8 us (7%)
  local copies, waits for them, and re-layouts  7.47 us (4%)
    ppermute x3, waiting for transfers between devices, per_device(): other = lax.ppermute(send, 'chan', swap)  37.7 us
    pallas_call x3, Pallas kernels, pre_partial(): pl.pallas_call(functools.partial(pre_kernel, level), in_specs=[HBM, VMEM,...  19.8 us
    ppermute x3, waiting for transfers between devices, exchange(): others[n] = lax.ppermute(after(sends[n], *earlier), 'chan', swap)  17.3 us
    pallas_call x3, Pallas kernels, block_step(): pl.pallas_call(functools.partial(block_kernel, level), in_specs=[VMEM] *...  10.5 us
    ppermute x3, starting transfers between devices, per_device(): other = lax.ppermute(send, 'chan', swap)  9.09 us
    all_to_all x1, starting transfers between devices, per_device(): lax.all_to_all(after(payload, vectors), GROUP_AXES, split_axis=0, concat_...  9.01 us
    pallas_call x1, Pallas kernels, top_gradient(): pl.pallas_call(top_kernel, in_specs=[HBM] * 3, out_specs=[VMEM, VMEM], ou...  8.86 us
    pallas_call x3, Pallas kernels, pre_slope(): pl.pallas_call(body, grid_spec=pltpu.PrefetchScalarGridSpec(num_scalar_pr...  7.89 us
  transfers between devices with their start and end apart: 16, of which 9 were waited for; matrix products, arithmetic and copies ran while one was open for 0% of the time, Pallas kernels for 27%

profile of v13, /device:TPU:64, one launch (start us, length us, event | category | flops | bytes accessed | tf_op | source)
XLA Modules:
  0.0 190.8 jit_solution(15503708087915033541)
XLA Ops:
  6.5 3.4 %bucket_entries.1 = bf16[64,2,128]{2,1,0:T(2,128)(2,1)} custom-call(s32[32,64]{1,0:T(8,128)} %bitcast.13, bf16[32,64]{1,0:T(8,128)(2,1)} %bitcast.14), custom_call_target="tpu_custom_call" | custom-call | flops 1000000 | bytes 1000 | tf_op jit(solution)/shard_map/bucket_entries/pallas_call | solution.py:168
  9.9 1.8 head_vectors.1
  11.7 9.0 %all-to-all-start = ((bf16[64,2,128]{2,1,0:T(2,128)(2,1)}), bf16[64,2,128]{2,1,0:T(2,128)(2,1)S(1)}, u32[]{:S(2)}, u32[]{:S(2)}) async-start(bf16[64,2,128]{2,1,0:T(2,128)(2,1)} %bucket_entries.1), calls=%async_computation | async-start | bytes 65536 | tf_op jit(solution)/shard_map/all_to_all | solution.py:550
  20.7 0.0 all-gather.2.cloned.1.call-start
  20.8 1.5 collective-permute-start.1
  22.3 1.1 cut_edges.1
  23.4 3.1 %collective-permute-start = (bf16[96,768]{1,0:T(8,128)(2,1)S(1)}, bf16[96,768]{1,0:T(8,128)(2,1)S(1)}, u32[]{:S(2)}, u32[]{:S(2)}) collective-permute-start(bf16[96,768]{1,0:T(8,128)(2,1)S(1)} %get-tuple-element.41), channel_id=1, source_target_pairs={{0,2},{2,4},{4,6},{6,8},{8,10},{10,12},{12,14},{14,16},{16,18},{18... | collective-permute-start | bytes 442376 | tf_op jit(solution)/shard_map/ppermute | solution.py:554
  26.5 2.8 %collective-permute-start.4 = (bf16[96,768]{1,0:T(8,128)(2,1)S(1)}, bf16[96,768]{1,0:T(8,128)(2,1)S(1)}, u32[]{:S(2)}, u32[]{:S(2)}) collective-permute-start(bf16[96,768]{1,0:T(8,128)(2,1)S(1)} %get-tuple-element.42), channel_id=1, source_target_pairs={{2,0},{4,2},{6,4},{8,6},{10,8},{12,10},{14,12},{16,14},{18,16},{20... | collective-permute-start | bytes 442376 | tf_op jit(solution)/shard_map/ppermute | solution.py:555
  29.2 0.0 all-to-all-done.refs_0_
  29.3 0.0 collective-permute-done.1
  29.3 0.6 collective-permute-start.5
  29.9 1.9 %collective-permute-start.3 = (bf16[64,2,128]{2,1,0:T(2,128)(2,1)S(1)}, bf16[64,2,128]{2,1,0:T(2,128)(2,1)S(1)}, u32[]{:S(2)}, u32[]{:S(2)}) collective-permute-start(bf16[64,2,128]{2,1,0:T(2,128)(2,1)S(1)} %all-to-all-done.refs_0_), channel_id=1, source_target_pairs={{2,0},{4,2},{6,4},{8,6},{10,8},{12,10},{14,12},{16,14},{18,16},{20... | collective-permute-start | bytes 98312 | tf_op jit(solution)/shard_map/ppermute | solution.py:568
  31.9 3.9 %collective-permute-start.2 = (bf16[64,2,128]{2,1,0:T(2,128)(2,1)S(1)}, bf16[64,2,128]{2,1,0:T(2,128)(2,1)S(1)}, u32[]{:S(2)}, u32[]{:S(2)}) collective-permute-start(bf16[64,2,128]{2,1,0:T(2,128)(2,1)S(1)} %all-to-all-done.refs_0_), channel_id=1, source_target_pairs={{0,2},{2,4},{4,6},{6,8},{8,10},{10,12},{12,14},{14,16},{16,18},{18... | collective-permute-start | bytes 98312 | tf_op jit(solution)/shard_map/ppermute | solution.py:567
  35.8 2.8 %collective-permute-done.3.refs_2_ = bf16[64,2,128]{2,1,0:T(2,128)(2,1)S(1)} collective-permute-done((bf16[64,2,128]{2,1,0:T(2,128)(2,1)S(1)}, bf16[64,2,128]{2,1,0:T(2,128)(2,1)S(1)}, u32[]{:S(2)}, u32[]{:S(2)}) %collective-permute-start.3) | collective-permute-done | bytes 32800 | tf_op jit(solution)/shard_map/ppermute | solution.py:568
  38.6 0.8 collective-permute-start.7
  39.5 0.0 collective-permute-done.2.refs_1_
  39.5 1.5 collective-permute-start.6
  41.0 0.0 collective-permute-done.low
  41.0 0.0 collective-permute-done.4.high
  41.0 6.3 %pre_partial_2.1 = (bf16[576,768]{1,0:T(8,128)(2,1)S(1)}, bf16[544,768]{1,0:T(8,128)(2,1)S(1)}) custom-call(bf16[3,512,768]{2,1,0:T(8,128)(2,1)} %saved.6, bf16[96,768]{1,0:T(8,128)(2,1)S(1)} %collective-permute-done.low, bf16[96,768]{1,0:T(8,128)(2,1)S(1)} %collective-permute-done.4.high, bf16[3,3,768,768]{3,2,1,0:T(8,128)(2,1)} %refs_0_.2), custom_call_target="tpu_custom_call" | custom-call | flops 50000000 | bytes 80000 | tf_op jit(solution)/shard_map/pre_partial_2/pallas_call | solution.py:355
  47.3 0.0 copy-start.5
  47.3 0.0 collective-permute-done.5
  47.4 1.4 collective-permute-done.6
  48.8 0.0 collective-permute-done.7
  48.9 0.0 copy-done.5
  49.0 0.9 constant_dynamic-slice_fusion
  49.9 0.0 all-gather.2.cloned.1.call-update
  49.9 3.0 %collective-permute-start.8 = (bf16[576,768]{1,0:T(8,128)(2,1)S(1)}, bf16[576,768]{1,0:T(8,128)(2,1)S(1)}, u32[]{:S(2)}, u32[]{:S(2)}) collective-permute-start(bf16[576,768]{1,0:T(8,128)(2,1)S(1)} %get-tuple-element.45.own), channel_id=1, source_target_pairs={{0,1},{1,0},{2,3},{3,2},{4,5},{5,4},{6,7},{7,6},{8,9},{9,8},{10,11... | collective-permute-start | bytes 2654216 | tf_op jit(solution)/shard_map/ppermute | solution.py:565
  52.9 6.1 %pre_partial_1.1 = (bf16[544,768]{1,0:T(8,128)(2,1)S(1)}, bf16[528,768]{1,0:T(8,128)(2,1)S(1)}) custom-call(bf16[3,512,768]{2,1,0:T(8,128)(2,1)} %saved.6, bf16[96,768]{1,0:T(8,128)(2,1)S(1)} %collective-permute-done.low, bf16[96,768]{1,0:T(8,128)(2,1)S(1)} %collective-permute-done.4.high, bf16[3,3,768,768]{3,2,1,0:T(8,128)(2,1)} %refs_0_.2), custom_call_target="tpu_custom_call" | custom-call | flops 50000000 | bytes 80000 | tf_op jit(solution)/shard_map/pre_partial_1/pallas_call | solution.py:355
  59.1 0.9 copy-done.9
  60.0 0.6 collective-permute-start.9
  60.6 7.3 %spread_entries.1.spread = bf16[2,576,2048]{2,1,0:T(8,128)(2,1)S(1)} custom-call(s32[1]{0:T(128)} %bitcast.along, bf16[64,2,128]{2,1,0:T(2,128)(2,1)S(1)} %all-to-all-done.refs_0_, bf16[64,2,128]{2,1,0:T(2,128)(2,1)S(1)} %collective-permute-done.2.refs_1_, bf16[64,2,128]{2,1,0:T(2,128)(2,1)S(1)} %collective-permute-done.3.refs_2_), custom_call_target="tpu_custom_call" | custom-call | flops 60000000 | bytes 80000 | tf_op jit(solution)/shard_map/spread_entries/pallas_call | solution.py:242
  67.9 0.0 copy-done.7
  67.9 0.0 copy-start
  67.9 2.2 %copy-done = bf16[2,576,2048]{2,1,0:T(8,128)(2,1)} copy-done((bf16[2,576,2048]{2,1,0:T(8,128)(2,1)}, bf16[2,576,2048]{2,1,0:T(8,128)(2,1)S(1)}, u32[]{:S(2)}) %copy-start) | copy-done | bytes 4718616
  70.1 3.9 %collective-permute-done.8.other = bf16[576,768]{1,0:T(8,128)(2,1)S(1)} collective-permute-done((bf16[576,768]{1,0:T(8,128)(2,1)S(1)}, bf16[576,768]{1,0:T(8,128)(2,1)S(1)}, u32[]{:S(2)}, u32[]{:S(2)}) %collective-permute-start.8) | collective-permute-done | bytes 884768 | tf_op jit(solution)/shard_map/ppermute | solution.py:565
  74.0 7.3 %pre_partial_0.1 = (bf16[528,768]{1,0:T(8,128)(2,1)}, bf16[512,768]{1,0:T(8,128)(2,1)S(1)}) custom-call(bf16[3,512,768]{2,1,0:T(8,128)(2,1)} %saved.6, bf16[96,768]{1,0:T(8,128)(2,1)S(1)} %collective-permute-done.low, bf16[96,768]{1,0:T(8,128)(2,1)S(1)} %collective-permute-done.4.high, bf16[3,3,768,768]{3,2,1,0:T(8,128)(2,1)} %refs_0_.2), custom_call_target="tpu_custom_call" | custom-call | flops 50000000 | bytes 80000 | tf_op jit(solution)/shard_map/pre_partial_0/pallas_call | solution.py:355
  81.4 0.9 copy-done.11
  82.2 2.9 %collective-permute-start.10 = (bf16[528,768]{1,0:T(8,128)(2,1)}, bf16[528,768]{1,0:T(8,128)(2,1)}, u32[]{:S(2)}, u32[]{:S(2)}) collective-permute-start(bf16[528,768]{1,0:T(8,128)(2,1)} %get-tuple-element.51.own), channel_id=1, source_target_pairs={{0,1},{1,0},{2,3},{3,2},{4,5},{5,4},{6,7},{7,6},{8,9},{9,8},{10,11... | collective-permute-start | bytes 2433032 | tf_op jit(solution)/shard_map/ppermute | solution.py:565
  85.1 6.9 %collective-permute-done.9.other = bf16[544,768]{1,0:T(8,128)(2,1)} collective-permute-done((bf16[544,768]{1,0:T(8,128)(2,1)S(1)}, bf16[544,768]{1,0:T(8,128)(2,1)}, u32[]{:S(2)}, u32[]{:S(2)}) %collective-permute-start.9) | collective-permute-done | bytes 835616 | tf_op jit(solution)/shard_map/ppermute | solution.py:565
  92.0 1.8 all-gather.2.cloned.1.call-done
  93.9 8.9 %top_gradient.1 = (f32[576,768]{1,0:T(8,128)S(1)}, bf16[576,768]{1,0:T(8,128)(2,1)S(1)}) custom-call(bf16[2,576,2048]{2,1,0:T(8,128)(2,1)} %copy-done, bf16[32,2,64,768]{3,2,1,0:T(8,128)(2,1)} %bitcast.10, bf16[3,768,768]{2,1,0:T(8,128)(2,1)} %refs_1_.3), custom_call_target="tpu_custom_call" | custom-call | flops 50000000 | bytes 140000 | tf_op jit(solution)/shard_map/top_gradient/pallas_call | solution.py:431
  102.8 6.5 %collective-permute-done.10.other = bf16[528,768]{1,0:T(8,128)(2,1)} collective-permute-done((bf16[528,768]{1,0:T(8,128)(2,1)}, bf16[528,768]{1,0:T(8,128)(2,1)}, u32[]{:S(2)}, u32[]{:S(2)}) %collective-permute-start.10) | collective-permute-done | bytes 811040 | tf_op jit(solution)/shard_map/ppermute | solution.py:565
  109.3 2.9 %collective-permute-start.11 = (bf16[576,768]{1,0:T(8,128)(2,1)S(1)}, bf16[576,768]{1,0:T(8,128)(2,1)S(1)}, u32[]{:S(2)}, u32[]{:S(2)}) collective-permute-start(bf16[576,768]{1,0:T(8,128)(2,1)S(1)} %get-tuple-element.54.own), channel_id=1, source_target_pairs={{0,1},{1,0},{2,3},{3,2},{4,5},{5,4},{6,7},{7,6},{8,9},{9,8},{10,11... | collective-permute-start | bytes 2654216 | tf_op jit(solution)/shard_map/ppermute | solution.py:585
  112.2 0.1 add_convert_fusion.flags
  112.3 1.2 copy-done.2
  113.4 1.2 copy-done.4
  114.6 1.6 pre_slope_2.1.slope
  116.2 2.4 %stage_weights_2.1 = (bf16[3,768,768]{2,1,0:T(8,128)(2,1)S(1)}, bf16[768,768]{1,0:T(8,128)(2,1)S(1)}) custom-call(bf16[3,3,768,768]{3,2,1,0:T(8,128)(2,1)} %refs_0_.2, bf16[3,768,768]{2,1,0:T(8,128)(2,1)} %refs_1_.3), custom_call_target="tpu_custom_call" | custom-call | flops 10000000 | bytes 10000 | tf_op jit(solution)/shard_map/stage_weights_2/pallas_call | solution.py:268
  118.7 13.6 %collective-permute-done.11.other = bf16[576,768]{1,0:T(8,128)(2,1)S(1)} collective-permute-done((bf16[576,768]{1,0:T(8,128)(2,1)S(1)}, bf16[576,768]{1,0:T(8,128)(2,1)S(1)}, u32[]{:S(2)}, u32[]{:S(2)}) %collective-permute-start.11) | collective-permute-done | bytes 884768 | tf_op jit(solution)/shard_map/ppermute | solution.py:585
  132.3 3.7 %block_step_2.1 = (f32[544,768]{1,0:T(8,128)S(1)}, bf16[544,768]{1,0:T(8,128)(2,1)S(1)}) custom-call(bf16[576,768]{1,0:T(8,128)(2,1)S(1)} %get-tuple-element.54.own, bf16[576,768]{1,0:T(8,128)(2,1)S(1)} %collective-permute-done.11.other, bf16[576,768]{1,0:T(8,128)(2,1)S(1)} %pre_slope_2.1.slope, bf16[3,768,768]{2,1,0:T(8,128)(2,1)S(1)} %get-tuple-element.57.weight, ...), custom_call_target="tpu_custom_call" | custom-call | flops 50000000 | bytes 140000 | tf_op jit(solution)/shard_map/block_step_2/pallas_call | solution.py:493
  136.0 3.2 %collective-permute-start.12 = (bf16[544,768]{1,0:T(8,128)(2,1)S(1)}, bf16[544,768]{1,0:T(8,128)(2,1)S(1)}, u32[]{:S(2)}, u32[]{:S(2)}) collective-permute-start(bf16[544,768]{1,0:T(8,128)(2,1)S(1)} %get-tuple-element.61.own), channel_id=1, source_target_pairs={{0,1},{1,0},{2,3},{3,2},{4,5},{5,4},{6,7},{7,6},{8,9},{9,8},{10,11... | collective-permute-start | bytes 2506760 | tf_op jit(solution)/shard_map/ppermute | solution.py:585
  139.3 3.1 %pre_slope_1.1.slope = bf16[544,768]{1,0:T(8,128)(2,1)S(1)} custom-call(s32[2]{0:T(128)S(1)} %add_convert_fusion.flags, bf16[544,768]{1,0:T(8,128)(2,1)S(1)} %copy-done.8, bf16[544,768]{1,0:T(8,128)(2,1)} %collective-permute-done.9.other), custom_call_target="tpu_custom_call" | custom-call | flops 40000000 | bytes 50000 | tf_op jit(solution)/shard_map/pre_slope_1/pallas_call | solution.py:387
  142.3 2.4 %stage_weights_1.1 = (bf16[3,768,768]{2,1,0:T(8,128)(2,1)S(1)}, bf16[768,768]{1,0:T(8,128)(2,1)S(1)}) custom-call(bf16[3,3,768,768]{3,2,1,0:T(8,128)(2,1)} %refs_0_.2, bf16[3,768,768]{2,1,0:T(8,128)(2,1)} %refs_1_.3), custom_call_target="tpu_custom_call" | custom-call | flops 10000000 | bytes 10000 | tf_op jit(solution)/shard_map/stage_weights_1/pallas_call | solution.py:268
  144.8 12.7 %collective-permute-done.12.other = bf16[544,768]{1,0:T(8,128)(2,1)S(1)} collective-permute-done((bf16[544,768]{1,0:T(8,128)(2,1)S(1)}, bf16[544,768]{1,0:T(8,128)(2,1)S(1)}, u32[]{:S(2)}, u32[]{:S(2)}) %collective-permute-start.12) | collective-permute-done | bytes 835616 | tf_op jit(solution)/shard_map/ppermute | solution.py:585
  157.5 0.0 copy-done.10
  157.5 3.7 %block_step_1.1 = (f32[528,768]{1,0:T(8,128)S(1)}, bf16[528,768]{1,0:T(8,128)(2,1)S(1)}) custom-call(bf16[544,768]{1,0:T(8,128)(2,1)S(1)} %get-tuple-element.61.own, bf16[544,768]{1,0:T(8,128)(2,1)S(1)} %collective-permute-done.12.other, bf16[544,768]{1,0:T(8,128)(2,1)S(1)} %pre_slope_1.1.slope, bf16[3,768,768]{2,1,0:T(8,128)(2,1)S(1)} %get-tuple-element.64.weight, ...), custom_call_target="tpu_custom_call" | custom-call | flops 50000000 | bytes 140000 | tf_op jit(solution)/shard_map/block_step_1/pallas_call | solution.py:493
  161.1 3.0 %collective-permute-start.13 = (bf16[528,768]{1,0:T(8,128)(2,1)S(1)}, bf16[528,768]{1,0:T(8,128)(2,1)S(1)}, u32[]{:S(2)}, u32[]{:S(2)}) collective-permute-start(bf16[528,768]{1,0:T(8,128)(2,1)S(1)} %get-tuple-element.68.own), channel_id=1, source_target_pairs={{0,1},{1,0},{2,3},{3,2},{4,5},{5,4},{6,7},{7,6},{8,9},{9,8},{10,11... | collective-permute-start | bytes 2433032 | tf_op jit(solution)/shard_map/ppermute | solution.py:585
  164.1 3.2 %pre_slope_0.1.slope = bf16[528,768]{1,0:T(8,128)(2,1)S(1)} custom-call(s32[2]{0:T(128)S(1)} %add_convert_fusion.flags, bf16[528,768]{1,0:T(8,128)(2,1)} %get-tuple-element.51.own, bf16[528,768]{1,0:T(8,128)(2,1)} %collective-permute-done.10.other), custom_call_target="tpu_custom_call" | custom-call | flops 40000000 | bytes 50000 | tf_op jit(solution)/shard_map/pre_slope_0/pallas_call | solution.py:387
  167.3 0.0 copy-start.12
  167.3 2.1 %stage_weights_0.1.weight = bf16[3,768,768]{2,1,0:T(8,128)(2,1)S(1)} custom-call(bf16[3,3,768,768]{3,2,1,0:T(8,128)(2,1)} %refs_0_.2), custom_call_target="tpu_custom_call" | custom-call | flops 10000000 | bytes 10000 | tf_op jit(solution)/shard_map/stage_weights_0/pallas_call | solution.py:268
  169.4 11.5 %collective-permute-done.13.other = bf16[528,768]{1,0:T(8,128)(2,1)S(1)} collective-permute-done((bf16[528,768]{1,0:T(8,128)(2,1)S(1)}, bf16[528,768]{1,0:T(8,128)(2,1)S(1)}, u32[]{:S(2)}, u32[]{:S(2)}) %collective-permute-start.13) | collective-permute-done | bytes 811040 | tf_op jit(solution)/shard_map/ppermute | solution.py:585
  180.9 0.0 copy-done.12
  180.9 3.1 %block_step_0.1 = bf16[512,768]{1,0:T(8,128)(2,1)} custom-call(bf16[528,768]{1,0:T(8,128)(2,1)S(1)} %get-tuple-element.68.own, bf16[528,768]{1,0:T(8,128)(2,1)S(1)} %collective-permute-done.13.other, bf16[528,768]{1,0:T(8,128)(2,1)S(1)} %pre_slope_0.1.slope, bf16[3,768,768]{2,1,0:T(8,128)(2,1)S(1)} %stage_weights_0.1.weight, ...), custom_call_target="tpu_custom_call" | custom-call | flops 50000000 | bytes 140000 | tf_op jit(solution)/shard_map/block_step_0/pallas_call | solution.py:493
  (24 shorter events, 0.2 us)
Async XLA Ops:
  11.7 17.5 %all-to-all-start = ((bf16[64,2,128]{2,1,0:T(2,128)(2,1)}), bf16[64,2,128]{2,1,0:T(2,128)(2,1)S(1)}, u32[]{:S(2)}, u32[]{:S(2)}) async-start(bf16[64,2,128]{2,1,0:T(2,128)(2,1)} %bucket_entries.1), calls=%async_computation | async-start | bytes 65536 | tf_op jit(solution)/shard_map/all_to_all | solution.py:550
  20.7 73.2 %all-gather.2.cloned.1.call-start = ((), (), s32[]{:S(2)}) async-start(), calls=%async_computation.1 | async-start | bytes 7077888 | tf_op jit(solution)/shard_map/all_gather | solution.py:572
  20.8 8.5 %collective-permute-start.1 = (bf16[64,768]{1,0:T(8,128)(2,1)S(1)}, bf16[64,768]{1,0:T(8,128)(2,1)S(1)}, u32[]{:S(2)}, u32[]{:S(2)}) collective-permute-start(bf16[64,768]{1,0:T(8,128)(2,1)S(1)} %head_vectors.1), channel_id=1, source_target_pairs={{0,8},{2,10},{4,12},{6,14},{8,0},{10,2},{12,4},{14,6},{1,9},{3,11}... | collective-permute-start | bytes 294920 | tf_op jit(solution)/shard_map/ppermute | solution.py:516
  23.4 17.6 %collective-permute-start = (bf16[96,768]{1,0:T(8,128)(2,1)S(1)}, bf16[96,768]{1,0:T(8,128)(2,1)S(1)}, u32[]{:S(2)}, u32[]{:S(2)}) collective-permute-start(bf16[96,768]{1,0:T(8,128)(2,1)S(1)} %get-tuple-element.41), channel_id=1, source_target_pairs={{0,2},{2,4},{4,6},{6,8},{8,10},{10,12},{12,14},{14,16},{16,18},{18... | collective-permute-start | bytes 442376 | tf_op jit(solution)/shard_map/ppermute | solution.py:554
  26.5 14.5 %collective-permute-start.4 = (bf16[96,768]{1,0:T(8,128)(2,1)S(1)}, bf16[96,768]{1,0:T(8,128)(2,1)S(1)}, u32[]{:S(2)}, u32[]{:S(2)}) collective-permute-start(bf16[96,768]{1,0:T(8,128)(2,1)S(1)} %get-tuple-element.42), channel_id=1, source_target_pairs={{2,0},{4,2},{6,4},{8,6},{10,8},{12,10},{14,12},{16,14},{18,16},{20... | collective-permute-start | bytes 442376 | tf_op jit(solution)/shard_map/ppermute | solution.py:555
  29.3 18.0 %collective-permute-start.5 = (bf16[128,768]{1,0:T(8,128)(2,1)S(1)}, bf16[128,768]{1,0:T(8,128)(2,1)S(1)}, u32[]{:S(2)}, u32[]{:S(2)}) collective-permute-start(bf16[128,768]{1,0:T(8,128)(2,1)S(1)} %constant_dynamic-update-slice_fusion), channel_id=1, source_target_pairs={{0,6},{2,0},{4,2},{6,4},{8,14},{10,8},{12,10},{14,12},{1,7},{3,1},... | collective-permute-start | bytes 589832 | tf_op jit(solution)/shard_map/ppermute | solution.py:518
  29.9 8.7 %collective-permute-start.3 = (bf16[64,2,128]{2,1,0:T(2,128)(2,1)S(1)}, bf16[64,2,128]{2,1,0:T(2,128)(2,1)S(1)}, u32[]{:S(2)}, u32[]{:S(2)}) collective-permute-start(bf16[64,2,128]{2,1,0:T(2,128)(2,1)S(1)} %all-to-all-done.refs_0_), channel_id=1, source_target_pairs={{2,0},{4,2},{6,4},{8,6},{10,8},{12,10},{14,12},{16,14},{18,16},{20... | collective-permute-start | bytes 98312 | tf_op jit(solution)/shard_map/ppermute | solution.py:568
  31.9 7.6 %collective-permute-start.2 = (bf16[64,2,128]{2,1,0:T(2,128)(2,1)S(1)}, bf16[64,2,128]{2,1,0:T(2,128)(2,1)S(1)}, u32[]{:S(2)}, u32[]{:S(2)}) collective-permute-start(bf16[64,2,128]{2,1,0:T(2,128)(2,1)S(1)} %all-to-all-done.refs_0_), channel_id=1, source_target_pairs={{0,2},{2,4},{4,6},{6,8},{8,10},{10,12},{12,14},{14,16},{16,18},{18... | collective-permute-start | bytes 98312 | tf_op jit(solution)/shard_map/ppermute | solution.py:567
  38.6 10.2 %collective-permute-start.7 = (bf16[128,768]{1,0:T(8,128)(2,1)S(1)}, bf16[128,768]{1,0:T(8,128)(2,1)S(1)}, u32[]{:S(2)}, u32[]{:S(2)}) collective-permute-start(bf16[128,768]{1,0:T(8,128)(2,1)S(1)} %constant_dynamic-update-slice_fusion), channel_id=1, source_target_pairs={{0,2},{2,4},{4,6},{6,0},{8,10},{10,12},{12,14},{14,8},{1,3},{3,5},... | collective-permute-start | bytes 589832 | tf_op jit(solution)/shard_map/ppermute | solution.py:518
  39.5 9.3 %collective-permute-start.6 = (bf16[128,768]{1,0:T(8,128)(2,1)S(1)}, bf16[128,768]{1,0:T(8,128)(2,1)S(1)}, u32[]{:S(2)}, u32[]{:S(2)}) collective-permute-start(bf16[128,768]{1,0:T(8,128)(2,1)S(1)} %constant_dynamic-update-slice_fusion), channel_id=1, source_target_pairs={{0,4},{2,6},{4,0},{6,2},{8,12},{10,14},{12,8},{14,10},{1,5},{3,7},... | collective-permute-start | bytes 589832 | tf_op jit(solution)/shard_map/ppermute | solution.py:518
  47.3 1.7 copy-start.5
  47.3 2.6 %copy-start.1 = (bf16[576,768]{1,0:T(8,128)(2,1)}, bf16[576,768]{1,0:T(8,128)(2,1)S(1)}, u32[]{:S(2)}) copy-start(bf16[576,768]{1,0:T(8,128)(2,1)S(1)} %get-tuple-element.45.own) | copy-start | bytes 2654212
  49.9 24.1 %collective-permute-start.8 = (bf16[576,768]{1,0:T(8,128)(2,1)S(1)}, bf16[576,768]{1,0:T(8,128)(2,1)S(1)}, u32[]{:S(2)}, u32[]{:S(2)}) collective-permute-start(bf16[576,768]{1,0:T(8,128)(2,1)S(1)} %get-tuple-element.45.own), channel_id=1, source_target_pairs={{0,1},{1,0},{2,3},{3,2},{4,5},{5,4},{6,7},{7,6},{8,9},{9,8},{10,11... | collective-permute-start | bytes 2654216 | tf_op jit(solution)/shard_map/ppermute | solution.py:565
  59.1 0.9 copy-start.9
  60.0 7.9 %copy-start.7 = (bf16[544,768]{1,0:T(8,128)(2,1)}, bf16[544,768]{1,0:T(8,128)(2,1)S(1)}, u32[]{:S(2)}) copy-start(bf16[544,768]{1,0:T(8,128)(2,1)S(1)} %get-tuple-element.48.own) | copy-start | bytes 2506756
  60.0 32.1 %collective-permute-start.9 = (bf16[544,768]{1,0:T(8,128)(2,1)S(1)}, bf16[544,768]{1,0:T(8,128)(2,1)}, u32[]{:S(2)}, u32[]{:S(2)}) collective-permute-start(bf16[544,768]{1,0:T(8,128)(2,1)S(1)} %get-tuple-element.48.own), channel_id=1, source_target_pairs={{0,1},{1,0},{2,3},{3,2},{4,5},{5,4},{6,7},{7,6},{8,9},{9,8},{10,11... | collective-permute-start | bytes 2506760 | tf_op jit(solution)/shard_map/ppermute | solution.py:565
  67.9 2.2 %copy-start = (bf16[2,576,2048]{2,1,0:T(8,128)(2,1)}, bf16[2,576,2048]{2,1,0:T(8,128)(2,1)S(1)}, u32[]{:S(2)}) copy-start(bf16[2,576,2048]{2,1,0:T(8,128)(2,1)S(1)} %spread_entries.1.spread) | copy-start | bytes 14155780
  74.0 7.3 %copy-start.3 = (bf16[576,768]{1,0:T(8,128)(2,1)}, bf16[576,768]{1,0:T(8,128)(2,1)S(1)}, u32[]{:S(2)}) copy-start(bf16[576,768]{1,0:T(8,128)(2,1)S(1)} %collective-permute-done.8.other) | copy-start | bytes 2654212
  81.3 0.9 copy-start.11
  82.2 27.0 %collective-permute-start.10 = (bf16[528,768]{1,0:T(8,128)(2,1)}, bf16[528,768]{1,0:T(8,128)(2,1)}, u32[]{:S(2)}, u32[]{:S(2)}) collective-permute-start(bf16[528,768]{1,0:T(8,128)(2,1)} %get-tuple-element.51.own), channel_id=1, source_target_pairs={{0,1},{1,0},{2,3},{3,2},{4,5},{5,4},{6,7},{7,6},{8,9},{9,8},{10,11... | collective-permute-start | bytes 2433032 | tf_op jit(solution)/shard_map/ppermute | solution.py:565
  109.3 23.0 %collective-permute-start.11 = (bf16[576,768]{1,0:T(8,128)(2,1)S(1)}, bf16[576,768]{1,0:T(8,128)(2,1)S(1)}, u32[]{:S(2)}, u32[]{:S(2)}) collective-permute-start(bf16[576,768]{1,0:T(8,128)(2,1)S(1)} %get-tuple-element.54.own), channel_id=1, source_target_pairs={{0,1},{1,0},{2,3},{3,2},{4,5},{5,4},{6,7},{7,6},{8,9},{9,8},{10,11... | collective-permute-start | bytes 2654216 | tf_op jit(solution)/shard_map/ppermute | solution.py:585
  112.3 1.2 copy-start.2
  113.4 1.2 copy-start.4
  116.2 16.1 %copy-start.6 = (bf16[544,768]{1,0:T(8,128)(2,1)S(1)}, bf16[544,768]{1,0:T(8,128)(2,1)}, u32[]{:S(2)}) copy-start(bf16[544,768]{1,0:T(8,128)(2,1)} %copy-done.5) | copy-start | bytes 2506756
  132.3 7.0 %copy-start.8 = (bf16[544,768]{1,0:T(8,128)(2,1)S(1)}, bf16[544,768]{1,0:T(8,128)(2,1)}, u32[]{:S(2)}) copy-start(bf16[544,768]{1,0:T(8,128)(2,1)} %copy-done.7) | copy-start | bytes 2506756
  136.0 21.4 %collective-permute-start.12 = (bf16[544,768]{1,0:T(8,128)(2,1)S(1)}, bf16[544,768]{1,0:T(8,128)(2,1)S(1)}, u32[]{:S(2)}, u32[]{:S(2)}) collective-permute-start(bf16[544,768]{1,0:T(8,128)(2,1)S(1)} %get-tuple-element.61.own), channel_id=1, source_target_pairs={{0,1},{1,0},{2,3},{3,2},{4,5},{5,4},{6,7},{7,6},{8,9},{9,8},{10,11... | collective-permute-start | bytes 2506760 | tf_op jit(solution)/shard_map/ppermute | solution.py:585
  142.3 15.1 %copy-start.10 = (bf16[528,768]{1,0:T(8,128)(2,1)S(1)}, bf16[528,768]{1,0:T(8,128)(2,1)}, u32[]{:S(2)}) copy-start(bf16[528,768]{1,0:T(8,128)(2,1)} %copy-done.9) | copy-start | bytes 2433028
  161.1 19.7 %collective-permute-start.13 = (bf16[528,768]{1,0:T(8,128)(2,1)S(1)}, bf16[528,768]{1,0:T(8,128)(2,1)S(1)}, u32[]{:S(2)}, u32[]{:S(2)}) collective-permute-start(bf16[528,768]{1,0:T(8,128)(2,1)S(1)} %get-tuple-element.68.own), channel_id=1, source_target_pairs={{0,1},{1,0},{2,3},{3,2},{4,5},{5,4},{6,7},{7,6},{8,9},{9,8},{10,11... | collective-permute-start | bytes 2433032 | tf_op jit(solution)/shard_map/ppermute | solution.py:585
  167.3 13.6 %copy-start.12 = (bf16[512,768]{1,0:T(8,128)(2,1)S(1)}, bf16[512,768]{1,0:T(8,128)(2,1)}, u32[]{:S(2)}) copy-start(bf16[512,768]{1,0:T(8,128)(2,1)} %copy-done.11) | copy-start | bytes 2359300
Sparse Core Ops, SparseCore 0:
  50.0 43.8 all-gather.1
